TPU v7x, 32 devices: a whole 2x2x4 slice. The times are simulated.
32 devices in a mesh: ctx: 8 (over y, x, core), fsdp: 4 (over z).
Axes of the slice: x: 2, y: 2, z: 4, core: 2. Of those that a mesh axis runs over, the one named last changes fastest.
Arguments:
- token_embed: bfloat16 [8, 2048, 768], P('fsdp', 'ctx'), may hold values from -6 to 6
- bigram_ids: int32 [8, 2048], P('fsdp', 'ctx'), may hold values from 0 to 409599, as said below
- trigram_ids: int32 [8, 2048], P('fsdp', 'ctx'), may hold values from 0 to 409599, as said below
- bigram_table: bfloat16 [409600, 192], P(('ctx', 'fsdp')), may hold values from -6 to 6
- trigram_table: bfloat16 [409600, 192], P(('ctx', 'fsdp')), may hold values from -6 to 6
- block_deal: int32 [16], replicated, may hold values from 0 to 15, each once
- lookup_weight: bfloat16 [192, 768], P('fsdp'), may hold values from -0.3125 to 0.3125
- attention_gain: bfloat16 [768], P('fsdp'), may hold values from 0.099609375 to 1.8984375
- joined_weight: bfloat16 [768, 2304], P('fsdp'), may hold values from -0.3125 to 0.3125
- output_weight: bfloat16 [768, 768], P('fsdp'), may hold values from -0.625 to 0.625
- feedforward_gain: bfloat16 [768], P('fsdp'), may hold values from 0.099609375 to 1.8984375
- expand_weight: bfloat16 [768, 4096], P('fsdp'), may hold values from -0.21875 to 0.21875
- contract_weight: bfloat16 [2048, 768], P('fsdp'), may hold values from -0.1875 to 0.1875
- cotangent: bfloat16 [8, 2048, 768], P('fsdp', 'ctx'), may hold values from -6 to 6
Outputs:
- layer_output: bfloat16 [8, 2048, 768], P('fsdp', 'ctx')
- token_grad: float32 [8, 2048, 768], P('fsdp', 'ctx')
- bigram_grad: float32 [409600, 192], P(('ctx', 'fsdp'))
- trigram_grad: float32 [409600, 192], P(('ctx', 'fsdp'))
- lookup_grad: float32 [192, 768], P('fsdp')
- attention_grad: float32 [768], P('fsdp')
- joined_grad: float32 [768, 2304], P('fsdp')
- output_grad: float32 [768, 768], P('fsdp')
- feedforward_grad: float32 [768], P('fsdp')
- expand_grad: float32 [768, 4096], P('fsdp')
- contract_grad: float32 [2048, 768], P('fsdp')
Inputs may be any that keep to these rules, and one draw needn't show every extreme that they name: `bigram_ids`: row ids of the 2-gram table. Rows are owned in shards of 12800, shard id // 12800 by the device of that index along ctx+fsdp. The ids stored on one device name any one shard at most 32 times, and one shard exactly 32 times on every device. `trigram_ids`: row ids of the 3-gram table, with the same ownership and the same bound 32 on one device's ids in one shard, reached on every device.
All inputs are finite; a program needn't handle non-finite values.
Results may differ from a plain program's by a relative error of at most 0.017.
The roundings to bfloat16 on the way count: a program that leaves them out, or rounds other values in their place, can miss the bound.
Values may be sent and summed in bfloat16 or wider, within the bound.
No kernel may reach another device: no remote copies, remote signals or barrier semaphores. Data moves between devices by JAX's collectives and lax.ppermute only.
A program may use at most 384 MiB of HBM per device.

v0:
```python
import math

import jax
import jax.numpy as jnp
from jax import lax
from jax.sharding import PartitionSpec as P

D = 768
HEADS = 12
HD = 64
FF = 2048
E = 192
ABLK = 256


epsilon = 1e-05
masked_score = -1e30


def rotate(values, cosines, sines):
    half_size = values.shape[-1] // 2
    front_half = values[..., :half_size]
    back_half = values[..., half_size:]
    cosine_part = cosines[:, None, :]
    sine_part = sines[:, None, :]
    return jnp.concatenate(
        [
            front_half * cosine_part - back_half * sine_part,
            back_half * cosine_part + front_half * sine_part,
        ],
        axis=-1,
    )


def unrotate(grads, cosines, sines):
    half_size = grads.shape[-1] // 2
    front_half = grads[..., :half_size]
    back_half = grads[..., half_size:]
    cosine_part = cosines[:, None, :]
    sine_part = sines[:, None, :]
    return jnp.concatenate(
        [
            front_half * cosine_part + back_half * sine_part,
            back_half * cosine_part - front_half * sine_part,
        ],
        axis=-1,
    )


def normalize(rows):
    inverse = lax.rsqrt(jnp.mean(rows * rows, axis=-1, keepdims=True) + epsilon)
    return (rows * inverse, inverse)


def norm_backward(hidden_grad, normed, inverse, gain):
    weighted = hidden_grad * gain
    return inverse * (weighted - normed * jnp.mean(weighted * normed, axis=-1, keepdims=True))


def tile_scores(queries, keys_tile, query_block, key_block):
    heads_keys = keys_tile.reshape(keys_tile.shape[0], HEADS, HD)
    raw = jnp.einsum(
        "qhd,khd->hqk", queries, heads_keys, preferred_element_type=jnp.float32
    ) * HD ** (-0.5)
    visible = key_block[None, None, :] <= query_block[None, :, None]
    return jnp.where(visible, raw, masked_score)


def lookup_rows(table, received, first_row):
    local_row = jnp.clip(received - first_row, 0, table.shape[0] - 1)
    found = table[local_row]
    return jnp.where((received >= 0)[..., None], found, jnp.zeros((), table.dtype))


def add_rows(held_ids, grads, first_row, table_rows):
    local_row = jnp.clip(held_ids - first_row, 0, table_rows - 1)
    masked = jnp.where((held_ids >= 0)[:, None], grads, 0.0)
    return jnp.zeros((table_rows, grads.shape[-1]), jnp.float32).at[local_row].add(masked)


def placement_of(identifiers, table_rows, devices, capacity):
    flat_ids = identifiers.reshape(-1)
    owner_index = flat_ids // table_rows
    onehot = (owner_index[:, None] == jnp.arange(devices, dtype=jnp.int32)[None, :]).astype(
        jnp.int32
    )
    slot_rank = jnp.sum(jnp.cumsum(onehot, axis=0) * onehot, axis=1) - 1
    target = owner_index * capacity + slot_rank
    requests = jnp.full((devices * capacity,), -1, jnp.int32).at[target].set(flat_ids)
    return (target, requests)


def local(
    token_embed,
    bigram_ids,
    trigram_ids,
    bigram_table,
    trigram_table,
    block_deal,
    lookup_weight,
    attention_gain,
    joined_weight,
    output_weight,
    feedforward_gain,
    expand_weight,
    contract_weight,
    cotangent,
):
    contexts = lax.axis_size("ctx")
    shards = lax.axis_size("fsdp")
    devices = contexts * shards
    batches = token_embed.shape[0]
    local_rows = token_embed.shape[1]
    length = local_rows * contexts
    row_count = batches * local_rows
    capacity = max(2, 2 * row_count // devices)
    table_rows = bigram_table.shape[0]
    piece_rows = local_rows // 2
    score_scale = HD ** (-0.5)
    tile_rows = math.gcd(length, 1024)
    tile_count = length // tile_rows
    slot_index = jnp.arange(length, dtype=jnp.int32)
    position = block_deal[slot_index // piece_rows] * piece_rows + slot_index % piece_rows
    key_block = position // ABLK
    local_position = lax.dynamic_slice_in_dim(
        position, lax.axis_index("ctx") * local_rows, local_rows
    )
    query_block = local_position // ABLK
    frequency = jnp.exp(-math.log(10000.0) * (2.0 * jnp.arange(HD // 2, dtype=jnp.float32) / HD))
    angles = local_position.astype(jnp.float32)[:, None] * frequency[None, :]
    cosines = jnp.cos(angles)
    sines = jnp.sin(angles)
    first_row = lax.axis_index(("ctx", "fsdp")) * table_rows
    bigram_target, bigram_requests = placement_of(bigram_ids, table_rows, devices, capacity)
    trigram_target, trigram_requests = placement_of(trigram_ids, table_rows, devices, capacity)
    got_bigram = lax.all_to_all(
        bigram_requests.reshape(devices, capacity),
        ("ctx", "fsdp"),
        split_axis=0,
        concat_axis=0,
        tiled=True,
    )
    got_trigram = lax.all_to_all(
        trigram_requests.reshape(devices, capacity),
        ("ctx", "fsdp"),
        split_axis=0,
        concat_axis=0,
        tiled=True,
    )
    bigram_rows = lax.all_to_all(
        lookup_rows(bigram_table, got_bigram, first_row),
        ("ctx", "fsdp"),
        split_axis=0,
        concat_axis=0,
        tiled=True,
    ).reshape(devices * capacity, E)
    trigram_rows = lax.all_to_all(
        lookup_rows(trigram_table, got_trigram, first_row),
        ("ctx", "fsdp"),
        split_axis=0,
        concat_axis=0,
        tiled=True,
    ).reshape(devices * capacity, E)
    held_bigram = got_bigram.reshape(-1)
    held_trigram = got_trigram.reshape(-1)
    embed_rows = (
        (
            bigram_rows[bigram_target].astype(jnp.float32)
            + trigram_rows[trigram_target].astype(jnp.float32)
        )
        .astype(jnp.bfloat16)
        .reshape(batches, local_rows, E)
    )
    grad_totals = None
    outputs = []
    token_grads = []
    row_grads = []
    for batch in range(batches):
        (
            full_lookup,
            full_first_gain,
            full_joined,
            full_output,
            full_second_gain,
            full_expand,
            full_contract,
        ) = (
            lax.all_gather(lookup_weight, "fsdp", axis=0, tiled=True),
            lax.all_gather(attention_gain, "fsdp", axis=0, tiled=True),
            lax.all_gather(joined_weight, "fsdp", axis=0, tiled=True),
            lax.all_gather(output_weight, "fsdp", axis=0, tiled=True),
            lax.all_gather(feedforward_gain, "fsdp", axis=0, tiled=True),
            lax.all_gather(expand_weight, "fsdp", axis=0, tiled=True),
            lax.all_gather(contract_weight, "fsdp", axis=0, tiled=True),
        )
        first_gain = full_first_gain.astype(jnp.float32)
        second_gain = full_second_gain.astype(jnp.float32)
        embedded = embed_rows[batch]
        start_rows = token_embed[batch].astype(jnp.float32) + jnp.dot(
            embedded, full_lookup, preferred_element_type=jnp.float32
        )
        normed_first, inverse_first = normalize(start_rows)
        hidden_first = (normed_first * first_gain).astype(jnp.bfloat16)
        projected = jnp.dot(hidden_first, full_joined, preferred_element_type=jnp.float32)
        queries = rotate(projected[:, :D].reshape(local_rows, HEADS, HD), cosines, sines).astype(
            jnp.bfloat16
        )
        keys_local = (
            rotate(projected[:, D : 2 * D].reshape(local_rows, HEADS, HD), cosines, sines)
            .astype(jnp.bfloat16)
            .reshape(local_rows, D)
        )
        values_local = projected[:, 2 * D :].astype(jnp.bfloat16)
        keys_all, values_all = (
            lax.all_gather(keys_local, "ctx", axis=0, tiled=True),
            lax.all_gather(values_local, "ctx", axis=0, tiled=True),
        )

        def running(carry, tile_index):
            row_peak, row_total = carry
            keys_tile = lax.dynamic_slice_in_dim(keys_all, tile_index * tile_rows, tile_rows)
            blocks_tile = lax.dynamic_slice_in_dim(key_block, tile_index * tile_rows, tile_rows)
            scores = tile_scores(queries, keys_tile, query_block, blocks_tile)
            new_peak = jnp.maximum(row_peak, jnp.max(scores, axis=-1))
            row_total = row_total * jnp.exp(row_peak - new_peak) + jnp.sum(
                jnp.exp(scores - new_peak[..., None]), axis=-1
            )
            return ((new_peak, row_total), None)

        start_peak = jnp.full((HEADS, local_rows), masked_score, jnp.float32)
        (row_peak, row_total), _ = lax.scan(
            running,
            (start_peak, jnp.zeros((HEADS, local_rows), jnp.float32)),
            jnp.arange(tile_count),
        )
        logsum = row_peak + jnp.log(row_total)

        def accumulate(carry, tile_index):
            keys_tile = lax.dynamic_slice_in_dim(keys_all, tile_index * tile_rows, tile_rows)
            values_tile = lax.dynamic_slice_in_dim(values_all, tile_index * tile_rows, tile_rows)
            blocks_tile = lax.dynamic_slice_in_dim(key_block, tile_index * tile_rows, tile_rows)
            scores = tile_scores(queries, keys_tile, query_block, blocks_tile)
            probabilities = jnp.exp(scores - logsum[..., None]).astype(jnp.bfloat16)
            return (
                carry
                + jnp.einsum(
                    "hqk,khd->qhd",
                    probabilities,
                    values_tile.reshape(tile_rows, HEADS, HD),
                    preferred_element_type=jnp.float32,
                ),
                None,
            )

        attended, _ = lax.scan(
            accumulate, jnp.zeros((local_rows, HEADS, HD), jnp.float32), jnp.arange(tile_count)
        )
        attended = attended.reshape(local_rows, D)
        attended_low = attended.astype(jnp.bfloat16)
        middle = start_rows + jnp.dot(attended_low, full_output, preferred_element_type=jnp.float32)
        normed_second, inverse_second = normalize(middle)
        hidden_second = (normed_second * second_gain).astype(jnp.bfloat16)
        gate_up = jnp.dot(hidden_second, full_expand, preferred_element_type=jnp.float32)
        gate_part = gate_up[:, :FF]
        up_part = gate_up[:, FF:]
        sigmoid = jax.nn.sigmoid(gate_part)
        swish_value = gate_part * sigmoid
        activated = (swish_value * up_part).astype(jnp.bfloat16)
        result = middle + jnp.dot(activated, full_contract, preferred_element_type=jnp.float32)
        outputs.append(result.astype(jnp.bfloat16))
        upstream = cotangent[batch]
        contract_term = jnp.einsum(
            "tf,td->fd", activated, upstream, preferred_element_type=jnp.float32
        )
        activated_grad = jnp.einsum(
            "td,fd->tf", upstream, full_contract, preferred_element_type=jnp.float32
        )
        gate_grad = activated_grad * up_part * sigmoid * (1.0 + gate_part * (1.0 - sigmoid))
        up_grad = activated_grad * swish_value
        gate_up_grad = jnp.concatenate([gate_grad, up_grad], axis=-1).astype(jnp.bfloat16)
        expand_term = jnp.einsum(
            "td,tf->df", hidden_second, gate_up_grad, preferred_element_type=jnp.float32
        )
        hidden_second_grad = jnp.einsum(
            "tf,df->td", gate_up_grad, full_expand, preferred_element_type=jnp.float32
        )
        second_gain_term = jnp.sum(hidden_second_grad * normed_second, axis=0)
        middle_grad = upstream.astype(jnp.float32) + norm_backward(
            hidden_second_grad, normed_second, inverse_second, second_gain
        )
        middle_low = middle_grad.astype(jnp.bfloat16)
        output_term = jnp.einsum(
            "td,te->de", attended_low, middle_low, preferred_element_type=jnp.float32
        )
        attended_grad = jnp.einsum(
            "te,de->td", middle_low, full_output, preferred_element_type=jnp.float32
        ).astype(jnp.bfloat16)
        out_grad_heads = attended_grad.reshape(local_rows, HEADS, HD)
        row_delta = jnp.einsum(
            "qhd,qhd->hq",
            attended_grad.astype(jnp.float32).reshape(local_rows, HEADS, HD),
            attended.reshape(local_rows, HEADS, HD),
        )

        def tile_grads(keys_tile, values_tile, blocks_tile):
            scores = tile_scores(queries, keys_tile, query_block, blocks_tile)
            probabilities = jnp.exp(scores - logsum[..., None])
            prob_grad = jnp.einsum(
                "qhd,khd->hqk",
                out_grad_heads,
                values_tile.reshape(values_tile.shape[0], HEADS, HD),
                preferred_element_type=jnp.float32,
            )
            score_grad = (probabilities * (prob_grad - row_delta[..., None])).astype(jnp.bfloat16)
            return (score_grad, probabilities.astype(jnp.bfloat16))

        def query_part(score_grad, keys_tile):
            return (
                jnp.einsum(
                    "hqk,khd->qhd",
                    score_grad,
                    keys_tile.reshape(keys_tile.shape[0], HEADS, HD),
                    preferred_element_type=jnp.float32,
                )
                * score_scale
            )

        def query_tile(query_grad, tile_index):
            keys_tile = lax.dynamic_slice_in_dim(keys_all, tile_index * tile_rows, tile_rows)
            values_tile = lax.dynamic_slice_in_dim(values_all, tile_index * tile_rows, tile_rows)
            blocks_tile = lax.dynamic_slice_in_dim(key_block, tile_index * tile_rows, tile_rows)
            score_grad, _ = tile_grads(keys_tile, values_tile, blocks_tile)
            return (query_grad + query_part(score_grad, keys_tile), None)

        zero_query = jnp.zeros((local_rows, HEADS, HD), jnp.float32)
        query_grad, _ = lax.scan(query_tile, zero_query, jnp.arange(tile_count))
        values_heads = values_local.reshape(local_rows, HEADS, HD)

        def fold_queries(total, piece):
            query_rows_all, grad_rows_all, logsum_rows, delta_rows = piece
            rows_in = query_rows_all.shape[0]
            step_rows = math.gcd(rows_in, 512)

            def query_step(carry, step_index):
                begin = step_index * step_rows
                query_heads = lax.dynamic_slice_in_dim(query_rows_all, begin, step_rows).reshape(
                    step_rows, HEADS, HD
                )
                grad_heads = lax.dynamic_slice_in_dim(grad_rows_all, begin, step_rows).reshape(
                    step_rows, HEADS, HD
                )
                logsum_step = lax.dynamic_slice_in_dim(logsum_rows, begin, step_rows).T
                delta_step = lax.dynamic_slice_in_dim(delta_rows, begin, step_rows).T
                blocks_step = lax.dynamic_slice_in_dim(key_block, begin, step_rows)
                scores = tile_scores(query_heads, keys_local, blocks_step, query_block)
                probabilities = jnp.exp(scores - logsum_step[..., None])
                prob_grad = jnp.einsum(
                    "qhd,khd->hqk", grad_heads, values_heads, preferred_element_type=jnp.float32
                )
                score_grad = (probabilities * (prob_grad - delta_step[..., None])).astype(
                    jnp.bfloat16
                )
                key_term = (
                    jnp.einsum(
                        "hqk,qhd->khd", score_grad, query_heads, preferred_element_type=jnp.float32
                    )
                    * score_scale
                )
                value_term = jnp.einsum(
                    "hqk,qhd->khd",
                    probabilities.astype(jnp.bfloat16),
                    grad_heads,
                    preferred_element_type=jnp.float32,
                )
                return (
                    carry
                    + jnp.concatenate(
                        [key_term.reshape(local_rows, D), value_term.reshape(local_rows, D)],
                        axis=-1,
                    ),
                    None,
                )

            total, _ = lax.scan(query_step, total, jnp.arange(rows_in // step_rows))
            return total

        key_value_grad = fold_queries(
            jnp.zeros((local_rows, 2 * D), jnp.float32),
            (
                lax.all_gather(
                    queries.reshape(local_rows, D).astype(jnp.float32), "ctx", axis=0, tiled=True
                ).astype(jnp.bfloat16),
                lax.all_gather(attended_grad.astype(jnp.float32), "ctx", axis=0, tiled=True).astype(
                    jnp.bfloat16
                ),
                lax.all_gather(logsum.T, "ctx", axis=0, tiled=True),
                lax.all_gather(row_delta.T, "ctx", axis=0, tiled=True),
            ),
        )
        key_grad = unrotate(
            key_value_grad[:, :D].reshape(local_rows, HEADS, HD), cosines, sines
        ).reshape(local_rows, D)
        query_grad_flat = unrotate(query_grad, cosines, sines).reshape(local_rows, D)
        joined_local = jnp.concatenate(
            [query_grad_flat, key_grad, key_value_grad[:, D:]], axis=-1
        ).astype(jnp.bfloat16)
        joined_term = jnp.einsum(
            "td,te->de", hidden_first, joined_local, preferred_element_type=jnp.float32
        )
        hidden_first_grad = jnp.einsum(
            "te,de->td", joined_local, full_joined, preferred_element_type=jnp.float32
        )
        first_gain_term = jnp.sum(hidden_first_grad * normed_first, axis=0)
        start_grad = middle_grad + norm_backward(
            hidden_first_grad, normed_first, inverse_first, first_gain
        )
        token_grads.append(start_grad)
        start_low = start_grad.astype(jnp.bfloat16)
        lookup_term = jnp.einsum(
            "te,td->ed", embedded, start_low, preferred_element_type=jnp.float32
        )
        row_grads.append(
            jnp.einsum("td,ed->te", start_low, full_lookup, preferred_element_type=jnp.float32)
        )
        batch_terms = (
            lookup_term,
            first_gain_term,
            joined_term,
            output_term,
            second_gain_term,
            expand_term,
            contract_term,
        )
        if grad_totals is None:
            grad_totals = batch_terms
        else:
            grad_totals = tuple(
                (earlier + later for earlier, later in zip(grad_totals, batch_terms))
            )
    shares = lax.psum_scatter(grad_totals, "fsdp", scatter_dimension=0, tiled=True)
    summed = lax.psum(shares, "ctx")
    embed_grad = jnp.concatenate(row_grads, axis=0)
    empty_buffer = jnp.zeros((devices * capacity, E), jnp.float32)
    bigram_send = empty_buffer.at[bigram_target].set(embed_grad)
    trigram_send = empty_buffer.at[trigram_target].set(embed_grad)
    arrived = (
        lax.all_to_all(
            bigram_send.reshape(devices, capacity, E),
            ("ctx", "fsdp"),
            split_axis=0,
            concat_axis=0,
            tiled=True,
        ),
        lax.all_to_all(
            trigram_send.reshape(devices, capacity, E),
            ("ctx", "fsdp"),
            split_axis=0,
            concat_axis=0,
            tiled=True,
        ),
    )
    bigram_grad = add_rows(held_bigram, arrived[0].reshape(-1, E), first_row, table_rows)
    trigram_grad = add_rows(held_trigram, arrived[1].reshape(-1, E), first_row, table_rows)
    return (
        jnp.stack(outputs),
        jnp.stack(token_grads),
        bigram_grad,
        trigram_grad,
        summed[0],
        summed[1],
        summed[2],
        summed[3],
        summed[4],
        summed[5],
        summed[6],
    )


def solution(mesh):
    return jax.shard_map(
        local,
        mesh=mesh,
        in_specs=(
            P("fsdp", "ctx", None),
            P("fsdp", "ctx"),
            P("fsdp", "ctx"),
            P(("ctx", "fsdp"), None),
            P(("ctx", "fsdp"), None),
            P(),
            P("fsdp", None),
            P("fsdp"),
            P("fsdp", None),
            P("fsdp", None),
            P("fsdp"),
            P("fsdp", None),
            P("fsdp", None),
            P("fsdp", "ctx", None),
        ),
        out_specs=(
            P("fsdp", "ctx", None),
            P("fsdp", "ctx", None),
            P(("ctx", "fsdp"), None),
            P(("ctx", "fsdp"), None),
            P("fsdp", None),
            P("fsdp"),
            P("fsdp", None),
            P("fsdp", None),
            P("fsdp"),
            P("fsdp", None),
            P("fsdp", None),
        ),
        check_vma=False,
    )
```

profile of v0, /device:TPU:0, one launch (start us, length us, event | category | flops | bytes accessed | tf_op | source)
XLA Modules:
  0.0 1471.4 jit_solution(13719738949906756690)
XLA Ops:
  15.5 7.3 all-to-all-start.2
  28.4 8.3 copy.88
  36.7 8.2 copy.84
  50.4 18.5 %all_gather.64 = bf16[192,768]{1,0:T(8,128)(2,1)S(1)} all-gather(bf16[48,768]{1,0:T(8,128)(2,1)S(1)} %copy-done.91), channel_id=1, replica_groups=mesh['ctx'=8,'fsdp'=4] {'fsdp'}, dimensions={0}, use_global_device_ids=true | all-gather | bytes 368640 | tf_op jit(solution)/shard_map/all_gather | solution.py:188
  73.9 10.8 all-reduce.7
  88.2 7.2 gather_fusion.2
  104.2 7.2 gather_fusion
  168.1 23.9 %all-gather.27.cloned.1.call-done = bf16[2048,768]{0,1:T(8,128)(2,1)} async-done(((bf16[256,768]{0,1:T(8,128)(2,1)}), bf16[2048,768]{0,1:T(8,128)(2,1)}) %all-gather.27.cloned.1.call-update) | async-done | bytes 3145744 | tf_op jit(solution)/shard_map/all_gather | solution.py:215
  191.9 34.1 %while.94 = (s32[]{:T(128)}, f32[12,256]{1,0:T(8,128)S(1)}, f32[12,256]{1,0:T(8,128)S(1)}, s32[2]{0:T(128)S(1)}, s32[2048]{0:T(1024)S(1)}, /*index=5*/s32[256]{0...) while((s32[]{:T(128)}, f32[12,256]{1,0:T(8,128)S(1)}, ...), condition=%wide.region_20.21_spmd.clone, body=%wide.region_17.20_spmd.clone.sunk | while | flops 424950784 | bytes 31237320 | solution.py:231
  201.7 7.2 exponential_reduce_fusion.5
  218.8 7.2 exponential_reduce_fusion.5
  231.5 25.4 %while.95 = (s32[]{:T(128)}, f32[256,12,64]{0,2,1:T(8,128)}, s32[2]{0:T(128)S(1)}, bf16[2048,768]{0,1:T(8,128)(2,1)}, s32[2048]{0:T(1024)S(1)}, /*index=5*/s32[2...) while((s32[]{:T(128)}, f32[256,12,64]{0,2,1:T(8,128)}, ...), condition=%wide.region_22.23_spmd.clone, body=%wide.region_21.22_spmd.clone.sunk | while | flops 818544640 | bytes 11953361 | solution.py:255
  237.2 6.9 fusion.330
  249.8 7.2 fusion.330
  261.3 35.7 %while.92 = (s32[]{:T(128)}, f32[12,256]{1,0:T(8,128)}, f32[12,256]{1,0:T(8,128)}, s32[2]{0:T(128)S(1)}, s32[2048]{0:T(1024)S(1)}, /*index=5*/s32[256]{0:T(256)S...) while((s32[]{:T(128)}, f32[12,256]{1,0:T(8,128)}, ...), condition=%wide.region_12.13_spmd.clone, body=%wide.region_9.12_spmd.clone.sunk | while | flops 424950784 | bytes 32957752 | solution.py:231
  271.6 7.1 exponential_reduce_fusion.4
  289.1 7.2 exponential_reduce_fusion.4
  303.2 25.6 %while.93 = (s32[]{:T(128)}, f32[256,12,64]{0,2,1:T(8,128)}, s32[2]{0:T(128)S(1)}, bf16[2048,768]{0,1:T(8,128)(2,1)}, s32[2048]{0:T(1024)S(1)}, /*index=5*/s32[2...) while((s32[]{:T(128)}, f32[256,12,64]{0,2,1:T(8,128)}, ...), condition=%wide.region_14.15_spmd.clone, body=%wide.region_13.14_spmd.clone.sunk | while | flops 818544640 | bytes 11953361 | solution.py:255
  309.0 6.9 fusion.321
  321.6 7.2 fusion.321
  334.8 108.6 %all-gather.21.cloned.1.call-done = bf16[768,4096]{1,0:T(8,128)(2,1)} async-done(((bf16[192,4096]{1,0:T(8,128)(2,1)}), bf16[768,4096]{1,0:T(8,128)(2,1)}) %all-gather.21.cloned.1.call-update) | async-done | bytes 6291472 | tf_op jit(solution)/shard_map/all_gather | solution.py:193
  443.4 7.1 fusion.182
  454.4 52.3 %all-gather.23.cloned.1.call-done = bf16[2048,768]{1,0:T(8,128)(2,1)} async-done(((bf16[512,768]{1,0:T(8,128)(2,1)}), bf16[2048,768]{1,0:T(8,128)(2,1)}) %all-gather.23.cloned.1.call-update) | async-done | bytes 3145744 | tf_op jit(solution)/shard_map/all_gather | solution.py:194
  539.0 45.9 %while.96 = (s32[]{:T(128)}, f32[256,12,64]{0,2,1:T(8,128)}, s32[2]{0:T(128)S(1)}, bf16[2048,768]{0,1:T(8,128)(2,1)S(1)}, s32[2048]{0:T(1024)S(1)}, /*index=5*/s...) while((s32[]{:T(128)}, f32[256,12,64]{0,2,1:T(8,128)}, ...), condition=%wide.region_26.27_spmd.clone, body=%wide.region_25.26_spmd.clone.sunk | while | flops 1227685888 | bytes 45389052 | solution.py:336
  550.6 11.3 fusion.338
  573.4 11.6 fusion.338
  586.2 11.0 all_gather.76
  597.2 10.3 all_gather.78
  607.5 10.0 all_gather.80
  619.3 9.8 all_gather.82
  633.8 45.9 %while.98 = (s32[]{:T(128)}, f32[256,12,64]{0,2,1:T(8,128)}, s32[2]{0:T(128)S(1)}, bf16[2048,768]{0,1:T(8,128)(2,1)S(1)}, s32[2048]{0:T(1024)S(1)}, /*index=5*/s...) while((s32[]{:T(128)}, f32[256,12,64]{0,2,1:T(8,128)}, ...), condition=%wide.region_32.33_spmd.clone, body=%wide.region_31.32_spmd.clone.sunk | while | flops 1227685888 | bytes 45389052 | solution.py:336
  645.3 11.3 fusion.356
  668.2 11.6 fusion.356
  680.0 77.7 %while.97 = (s32[]{:T(128)}, f32[256,1536]{0,1:T(8,128)}, s32[4]{0:T(128)S(1)}, bf16[2048,768]{0,1:T(8,128)(2,1)}, s32[256]{0:T(256)S(1)}, /*index=5*/s32[2048]{...) while((s32[]{:T(128)}, f32[256,1536]{0,1:T(8,128)}, ...), condition=%wide.region_28.29_spmd.clone, body=%wide.region_27.28_spmd.clone.sunk | while | flops 822542336 | bytes 64896368 | solution.py:384
  689.9 6.8 fusion.348
  708.9 6.8 fusion.348
  757.8 72.2 %while.99 = (s32[]{:T(128)}, f32[256,1536]{0,1:T(8,128)S(1)}, s32[4]{0:T(128)S(1)}, bf16[2048,768]{0,1:T(8,128)(2,1)}, s32[256]{0:T(256)S(1)}, /*index=5*/s32[20...) while((s32[]{:T(128)}, f32[256,1536]{0,1:T(8,128)S(1)}, ...), condition=%wide.region_34.35_spmd.clone, body=%wide.region_33.34_spmd.clone.sunk | while | flops 822542336 | bytes 63323480 | solution.py:384
  866.8 105.4 %reduce-scatter.14.cloned.1.call-done = f32[512,768]{1,0:T(8,128)} async-done(((f32[2048,768]{1,0:T(8,128)}), f32[512,768]{1,0:T(8,128)}) %reduce-scatter.14.cloned.1.call-update) | async-done | bytes 1572880 | tf_op jit(solution)/shard_map/reduce_scatter | solution.py:440
  972.3 126.8 %reduce-scatter.8.cloned.1.call-done = f32[192,2304]{1,0:T(8,128)} async-done(((f32[768,2304]{1,0:T(8,128)}), f32[192,2304]{1,0:T(8,128)}) %reduce-scatter.8.cloned.1.call-update) | async-done | bytes 1769488 | tf_op jit(solution)/shard_map/reduce_scatter | solution.py:440
  1099.0 214.6 %reduce-scatter.12.cloned.1.call-done = f32[192,4096]{1,0:T(8,128)} async-done(((f32[768,4096]{1,0:T(8,128)}), f32[192,4096]{1,0:T(8,128)}) %reduce-scatter.12.cloned.1.call-update) | async-done | bytes 3145744 | tf_op jit(solution)/shard_map/reduce_scatter | solution.py:440
  1332.0 20.3 %all-to-all-done.4 = f32[32,32,192]{2,1,0:T(8,128)} async-done(((f32[32,32,192]{2,1,0:T(8,128)}), f32[32,32,192]{2,1,0:T(8,128)}, u32[]{:S(2)}, u32[]{:S(2)}) %all-to-all-start.4) | async-done | bytes 786464 | tf_op jit(solution)/shard_map/all_to_all | solution.py:447
  1362.4 18.5 %all-reduce.6 = (f32[768]{0:T(1024)S(1)}, f32[768]{0:T(1024)S(1)}) all-reduce(f32[768]{0:T(1024)S(1)} %add.458, f32[768]{0:T(1024)S(1)} %add.461), channel_id=3, replica_groups=mesh['ctx'=8,'fsdp'=4] {'fsdp'}, use_global_device_ids=true, to_apply=%region_44.45.clone | all-reduce | flops 1536 | bytes 12288
  1381.0 13.9 all-reduce.4
  1397.6 11.7 scatter_custom_fusion.3
  1409.3 12.0 copy.105
  1422.9 11.7 scatter_custom_fusion.5
  1434.6 12.1 copy.106
  1446.7 8.7 all-reduce.10.cloned.1.call-done
  (707 shorter events, 466.6 us)
Async XLA Ops:
  12.3 114.4 %copy-start.104 = (s32[512,1]{0,1:T(1,128)}, s32[512,1]{0,1:T(1,128)S(1)}, u32[]{:S(2)}) copy-start(s32[512,1]{0,1:T(1,128)S(1)} %compare_select_fusion.11) | copy-start | bytes 6148
  15.5 69.3 %all-to-all-start.2 = ((s32[32,1,32]{2,1,0:T(1,128)}), s32[32,1,32]{2,1,0:T(1,128)S(1)}, u32[]{:S(2)}, u32[]{:S(2)}) async-start(s32[32,1,32]{2,1,0:T(1,128)} %all_to_all.27), calls=%async_computation.2 | async-start | bytes 32768 | tf_op jit(solution)/shard_map/all_to_all | solution.py:143
  22.8 115.2 %all-gather.13.cloned.1.call-start = ((), (), s32[]{:S(2)}) async-start(), calls=%async_computation.11 | async-start | bytes 4423680 | tf_op jit(solution)/shard_map/all_gather | solution.py:190
  36.7 12.9 copy-start.111
  36.7 13.1 copy-start.112
  36.7 13.7 copy-start.91
  36.7 32.3 %copy-start.90 = (s32[16]{0:T(128)S(1)}, s32[16]{0:T(128)}, u32[]{:S(2)}) copy-start(s32[16]{0:T(128)} %param.35) | copy-start | bytes 196
  45.1 81.6 %copy-start.105 = (s32[512,1]{0,1:T(1,128)}, s32[512,1]{0,1:T(1,128)S(1)}, u32[]{:S(2)}) copy-start(s32[512,1]{0,1:T(1,128)S(1)} %compare_select_fusion.12) | copy-start | bytes 6148
  68.9 68.6 %copy-start.33 = (bf16[192,768]{1,0:T(8,128)(2,1)}, bf16[192,768]{1,0:T(8,128)(2,1)S(1)}, u32[]{:S(2)}) copy-start(bf16[192,768]{1,0:T(8,128)(2,1)S(1)} %all_gather.64) | copy-start | bytes 884740
  84.7 59.7 %copy-start.82 = (f32[768]{0:T(1024)}, f32[768]{0:T(1024)S(1)}, u32[]{:S(2)}) copy-start(f32[768]{0:T(1024)S(1)} %convert_element_type.195) | copy-start | bytes 9220
  84.7 11.7 copy-start.86
  84.7 11.7 all-to-all-start
  96.4 16.0 %copy-start.88 = (s32[32,1,32]{2,1,0:T(1,128)}, s32[32,1,32]{2,1,0:T(1,128)S(1)}, u32[]{:S(2)}) copy-start(s32[32,1,32]{2,1,0:T(1,128)S(1)} %all-to-all-done) | copy-start | bytes 12292
  96.4 20.2 %all-to-all-start.3 = ((bf16[32,32,192]{2,1,0:T(8,128)(2,1)}), bf16[32,32,192]{2,1,0:T(8,128)(2,1)S(1)}, u32[]{:S(2)}, u32[]{:S(2)}) async-start(bf16[32,32,192]{2,1,0:T(8,128)(2,1)} %broadcast_select_fusion), calls=%async_computation.3 | async-start | bytes 1048576 | tf_op jit(solution)/shard_map/all_to_all | solution.py:157
  112.4 24.7 %copy-start.78 = (bf16[2,256,768]{2,1,0:T(8,128)(2,1)S(1)}, bf16[2,256,768]{2,1,0:T(8,128)(2,1)}, u32[]{:S(2)}) copy-start(bf16[2,256,768]{2,1,0:T(8,128)(2,1)} %param.30) | copy-start | bytes 2359300
  116.6 18.5 %all-to-all-start.1 = ((bf16[32,32,192]{2,1,0:T(8,128)(2,1)}), bf16[32,32,192]{2,1,0:T(8,128)(2,1)S(1)}, u32[]{:S(2)}, u32[]{:S(2)}) async-start(bf16[32,32,192]{2,1,0:T(8,128)(2,1)} %broadcast_select_fusion.1), calls=%async_computation.1 | async-start | bytes 1048576 | tf_op jit(solution)/shard_map/all_to_all | solution.py:150
  120.7 71.2 %all-gather.27.cloned.1.call-start = ((), (), s32[]{:S(2)}) async-start(), calls=%async_computation.18 | async-start | bytes 3538944 | tf_op jit(solution)/shard_map/all_gather | solution.py:215
  159.5 67.3 %all-gather.25.cloned.1.call-start = ((), (), s32[]{:S(2)}) async-start(), calls=%async_computation.17 | async-start | bytes 3538944 | tf_op jit(solution)/shard_map/all_gather | solution.py:216
  160.4 101.0 %all-gather.17.cloned.1.call-start = ((), (), s32[]{:S(2)}) async-start(), calls=%async_computation.13 | async-start | bytes 3538944 | tf_op jit(solution)/shard_map/all_gather | solution.py:215
  161.3 137.1 %all-gather.15.cloned.1.call-start = ((), (), s32[]{:S(2)}) async-start(), calls=%async_computation.12 | async-start | bytes 3538944 | tf_op jit(solution)/shard_map/all_gather | solution.py:216
  163.3 165.6 %all-gather.19.cloned.1.call-start = ((), (), s32[]{:S(2)}) async-start(), calls=%async_computation.14 | async-start | bytes 1474560 | tf_op jit(solution)/shard_map/all_gather | solution.py:191
  163.8 279.6 %all-gather.21.cloned.1.call-start = ((), (), s32[]{:S(2)}) async-start(), calls=%async_computation.15 | async-start | bytes 7864320 | tf_op jit(solution)/shard_map/all_gather | solution.py:193
  164.6 342.2 %all-gather.23.cloned.1.call-start = ((), (), s32[]{:S(2)}) async-start(), calls=%async_computation.16 | async-start | bytes 3932160 | tf_op jit(solution)/shard_map/all_gather | solution.py:194
  165.3 514.6 %all-gather.29.cloned.1.call-start = ((), (), s32[]{:S(2)}) async-start(), calls=%async_computation.19 | async-start | bytes 3538944 | tf_op jit(solution)/shard_map/all_gather | solution.py:390
  167.8 512.2 %all-gather.31.cloned.1.call-start = ((), (), s32[]{:S(2)}) async-start(), calls=%async_computation.20 | async-start | bytes 3538944 | tf_op jit(solution)/shard_map/all_gather | solution.py:393
  328.9 114.5 %copy-start.51 = (f32[768]{0:T(1024)S(1)}, f32[768]{0:T(1024)}, u32[]{:S(2)}) copy-start(f32[768]{0:T(1024)} %convert_element_type.203) | copy-start | bytes 9220
  506.8 11.6 copy-start.109
  527.3 230.4 %all-gather.33.cloned.1.call-start = ((), (), s32[]{:S(2)}) async-start(), calls=%async_computation.21 | async-start | bytes 3538944 | tf_op jit(solution)/shard_map/all_gather | solution.py:390
  528.1 229.7 %all-gather.35.cloned.1.call-start = ((), (), s32[]{:S(2)}) async-start(), calls=%async_computation.22 | async-start | bytes 3538944 | tf_op jit(solution)/shard_map/all_gather | solution.py:393
  539.0 327.8 %reduce-scatter.10.cloned.1.call-start = ((), (), s32[]{:S(2)}) async-start(), calls=%async_computation.25 | async-start | bytes 2949120 | tf_op jit(solution)/shard_map/reduce_scatter | solution.py:440
  586.1 43.0 %copy-start.57 = (bf16[256,768]{0,1:T(8,128)(2,1)}, bf16[256,768]{0,1:T(8,128)(2,1)S(1)}, u32[]{:S(2)}) copy-start(bf16[256,768]{0,1:T(8,128)(2,1)S(1)} %copy.99) | copy-start | bytes 1179652
  586.2 44.7 %copy-start.30 = (f32[256,768]{1,0:T(8,128)S(1)}, f32[256,768]{1,0:T(8,128)}, u32[]{:S(2)}) copy-start(f32[256,768]{1,0:T(8,128)} %get-tuple-element.1119) | copy-start | bytes 2359300
  586.2 44.7 %copy-start.38 = (bf16[256,12,64]{0,2,1:T(8,128)(2,1)S(1)}, bf16[256,12,64]{0,2,1:T(8,128)(2,1)}, u32[]{:S(2)}) copy-start(bf16[256,12,64]{0,2,1:T(8,128)(2,1)} %convert_element_type.213) | copy-start | bytes 1179652
  679.7 187.1 %reduce-scatter.6.cloned.1.call-start = ((), (), s32[]{:S(2)}) async-start(), calls=%async_computation.23 | async-start | bytes 737280 | tf_op jit(solution)/shard_map/reduce_scatter | solution.py:440
  680.0 77.7 %copy-start.11 = (f32[256,1536]{0,1:T(8,128)S(1)}, f32[256,1536]{0,1:T(8,128)}, u32[]{:S(2)}) copy-start(f32[256,1536]{0,1:T(8,128)} %custom-call.9) | copy-start | bytes 4718596
  680.0 77.7 %copy-start.17 = (bf16[256,12,64]{0,2,1:T(8,128)(2,1)S(1)}, bf16[256,12,64]{0,2,1:T(8,128)(2,1)}, u32[]{:S(2)}) copy-start(bf16[256,12,64]{0,2,1:T(8,128)(2,1)} %maximum_convert_fusion.2) | copy-start | bytes 1179652
  840.2 132.1 %reduce-scatter.14.cloned.1.call-start = ((), (), s32[]{:S(2)}) async-start(), calls=%async_computation.27 | async-start | bytes 7864320 | tf_op jit(solution)/shard_map/reduce_scatter | solution.py:440
  846.6 252.4 %reduce-scatter.8.cloned.1.call-start = ((), (), s32[]{:S(2)}) async-start(), calls=%async_computation.24 | async-start | bytes 8847360 | tf_op jit(solution)/shard_map/reduce_scatter | solution.py:440
  853.6 460.1 %reduce-scatter.12.cloned.1.call-start = ((), (), s32[]{:S(2)}) async-start(), calls=%async_computation.26 | async-start | bytes 15728640 | tf_op jit(solution)/shard_map/reduce_scatter | solution.py:440
  864.9 590.5 %all-reduce.10.cloned.1.call-start = ((), (), s32[]{:S(2)}) async-start(), calls=%async_computation.28 | async-start | bytes 14450688 | tf_op jit(solution)/shard_map/psum | solution.py:441
  1313.6 14.2 copy-start.94
  1313.7 14.3 copy-start.89
  1313.7 14.4 copy-start.93
  1313.7 14.5 copy-start.87
  1317.7 39.3 %copy-start.106 = (f32[768]{0:T(1024)S(1)}, f32[768]{0:T(1024)}, u32[]{:S(2)}) copy-start(f32[768]{0:T(1024)} %get-tuple-element.897) | copy-start | bytes 9220
  1317.7 39.3 %copy-start.107 = (f32[768]{0:T(1024)S(1)}, f32[768]{0:T(1024)}, u32[]{:S(2)}) copy-start(f32[768]{0:T(1024)} %get-tuple-element.1136) | copy-start | bytes 9220
  1321.4 30.8 %all-to-all-start.4 = ((f32[32,32,192]{2,1,0:T(8,128)}), f32[32,32,192]{2,1,0:T(8,128)}, u32[]{:S(2)}, u32[]{:S(2)}) async-start(f32[32,32,192]{2,1,0:T(8,128)} %bitcast.573), calls=%async_computation.4 | async-start | bytes 2097152 | tf_op jit(solution)/shard_map/all_to_all | solution.py:447
  1352.2 69.1 %all-to-all-start.5 = ((f32[32,32,192]{2,1,0:T(8,128)}), f32[32,32,192]{2,1,0:T(8,128)}, u32[]{:S(2)}, u32[]{:S(2)}) async-start(f32[32,32,192]{2,1,0:T(8,128)} %bitcast.572), calls=%async_computation.5 | async-start | bytes 2097152 | tf_op jit(solution)/shard_map/all_to_all | solution.py:454
  (124 other events, 440.0 us)
Sparse Core Ops, SparseCore 0:
  25.2 76.3 all-gather.12
  159.6 32.2 all-gather.26
  194.4 32.3 all-gather.24
  228.5 32.8 all-gather.16
  263.1 32.3 all-gather.14
  296.8 30.4 all-gather.18
  328.9 114.4 all-gather.20
  445.0 61.7 all-gather.22
  508.6 31.4 all-gather.28
  541.9 32.3 all-gather.30
  576.2 33.5 all-gather.32
  611.5 32.8 all-gather.34
  679.9 46.1 reduce-scatter.9
  840.3 19.9 reduce-scatter.5
  863.1 109.1 reduce-scatter.13
  975.0 124.0 reduce-scatter.7
  1101.2 212.3 reduce-scatter.11
  1317.4 137.9 all-reduce.9
where the time goes:
time: 1480 us; the launch traced here: 1470 us
  waiting for transfers between devices  676 us (46%)
  matrix products  282 us (19%)
  local copies, waits for them, and re-layouts  218 us (15%)
  other arithmetic  127 us (9%)
  blocking collectives  103 us (7%)
  starting transfers between devices  32.4 us (2%)
  between operations  17.5 us (1%)
  loops' own time  15 us (1%)
    reduce_scatter x5, waiting for transfers between devices, local(): lax.psum_scatter(grad_totals, 'fsdp', scatter_dimension=0, tiled=True)  447 us
    all_gather x1, waiting for transfers between devices, local(): lax.all_gather(expand_weight, 'fsdp', axis=0, tiled=True)  109 us
    unnamed x224, local copies, waits for them, and re-layouts  69.5 us
    dot_general x16, matrix products, tile_scores(): jnp.einsum('qhd,khd->hqk', queries, heads_keys, preferred_element_type=jn...  61 us
    dot_general x8, matrix products, query_step(): jnp.einsum('hqk,qhd->khd', score_grad, query_heads, preferred_element_typ...  54.3 us
    all_gather x1, waiting for transfers between devices, local(): lax.all_gather(contract_weight, 'fsdp', axis=0, tiled=True)  52.3 us
    dot_general x4, matrix products, query_part(): jnp.einsum('hqk,khd->qhd', score_grad, keys_tile.reshape(keys_tile.shape[...  45.8 us
  transfers between devices with their start and end apart: 24, of which 12 were waited for; matrix products, arithmetic and copies ran while one was open for 39% of the time, Pallas kernels for 0%

commit v1 on v0

v1 whole, which is shorter than its diff:
```python
import functools
import math

import jax
import jax.numpy as jnp
from jax import lax
from jax.experimental import pallas as pl
from jax.experimental.pallas import tpu as pltpu
from jax.sharding import PartitionSpec as P

D = 768
HEADS = 12
HD = 64
FF = 2048
E = 192
ABLK = 256
BF = jnp.bfloat16
F32 = jnp.float32

epsilon = 1e-05
NT = (((1,), (1,)), ((), ()))
NN = (((1,), (0,)), ((), ()))
TN = (((0,), (0,)), ((), ()))


def mm(a, b, dims=NN):
    return lax.dot_general(a, b, dims, preferred_element_type=F32)


def eye(n):
    rows = lax.broadcasted_iota(jnp.int32, (n, n), 0)
    return jnp.where(rows == lax.broadcasted_iota(jnp.int32, (n, n), 1), 1.0, 0.0).astype(BF)


def vmem():
    return pl.BlockSpec(memory_space=pltpu.VMEM)


def smem():
    return pl.BlockSpec(memory_space=pltpu.SMEM)


def params(megabytes, **kw):
    return pltpu.CompilerParams(vmem_limit_bytes=megabytes << 20, **kw)


def placement_kernel(capacity, owner_row, owner_col, local_row, requests, target_row, target_col):
    tokens = owner_row.shape[1]
    devices = requests.shape[0]
    for table in range(2):
        own_r = owner_row[table : table + 1, :]
        own_c = owner_col[:, table : table + 1]
        t_row = lax.broadcasted_iota(jnp.int32, (tokens, tokens), 0)
        t_col = lax.broadcasted_iota(jnp.int32, (tokens, tokens), 1)
        same = own_c == own_r
        rank_r = jnp.sum(jnp.where(same & (t_row < t_col), 1.0, 0.0), axis=0, keepdims=True)
        rank_c = jnp.sum(jnp.where(same & (t_col < t_row), 1.0, 0.0), axis=1, keepdims=True)
        rank_r = rank_r.astype(jnp.int32)
        rank_c = rank_c.astype(jnp.int32)
        target_row[table : table + 1, :] = own_r * capacity + rank_r
        target_col[:, table : table + 1] = own_c * capacity + rank_c
        device = lax.broadcasted_iota(jnp.int32, (devices, tokens), 0)
        owned = device == own_r
        row = local_row[table : table + 1, :]
        high = jnp.where(owned, (row >> 7).astype(F32), 0.0).astype(BF)
        low = jnp.where(owned, (row & 127).astype(F32), 0.0).astype(BF)
        one = jnp.where(owned, 1.0, 0.0).astype(BF)
        slot = lax.broadcasted_iota(jnp.int32, (tokens, capacity), 1)
        ranked = jnp.where(slot == rank_c, 1.0, 0.0).astype(BF)
        code = 128.0 * mm(high, ranked) + mm(low, ranked) + mm(one, ranked)
        requests[:, table * capacity : (table + 1) * capacity] = code.astype(jnp.int32)


def placement(ids, table_rows, devices, capacity):
    tokens = ids.shape[1]
    owner = ids // table_rows
    local_row = ids - owner * table_rows
    return pl.pallas_call(
        functools.partial(placement_kernel, capacity),
        out_shape=(
            jax.ShapeDtypeStruct((devices, 2 * capacity), jnp.int32),
            jax.ShapeDtypeStruct((2, tokens), jnp.int32),
            jax.ShapeDtypeStruct((tokens, 2), jnp.int32),
        ),
        in_specs=[vmem()] * 3,
        out_specs=(vmem(),) * 3,
        compiler_params=params(32),
        name="placement",
    )(owner, owner.T, local_row)


def wide(ref, columns, table):
    ref[table] = jnp.broadcast_to(columns[:, table : table + 1].astype(F32), ref.shape[1:])


def onehot_block(ref, table, base, width):
    lane = lax.broadcasted_iota(jnp.int32, ref.shape[1:], 1).astype(F32)
    parts = []
    for j in range(width // 128):
        hit = ref[table] == lane + (base + 128 * j + 1).astype(F32)
        parts.append(jnp.where(hit, 1.0, 0.0).astype(BF))
    return jnp.concatenate(parts, axis=1)


def read_rows_kernel(codes, bigram, trigram, out, spread, total):
    step = pl.program_id(0)
    width = bigram.shape[1]

    @pl.when(step == 0)
    def _():
        for table in range(2):
            wide(spread, codes, table)
        total[...] = jnp.zeros_like(total)

    for table, source in enumerate((bigram, trigram)):
        hot = onehot_block(spread, table, step * width, width)
        total[table] += mm(hot, source[...], NT)

    @pl.when(step == pl.num_programs(0) - 1)
    def _():
        out[...] = jnp.concatenate([total[0], total[1]], axis=1).astype(BF)


def table_block(table_rows):
    for width in (1280, 640, 512, 256, 128):
        if table_rows % width == 0:
            return width
    return table_rows


def read_rows(codes, bigram_t, trigram_t):
    slots = codes.shape[0]
    rows = bigram_t.shape[1]
    width = table_block(rows)
    table = pl.BlockSpec((E, width), lambda i: (0, i))
    return pl.pallas_call(
        read_rows_kernel,
        grid=(rows // width,),
        out_shape=jax.ShapeDtypeStruct((slots, 2 * E), BF),
        in_specs=[pl.BlockSpec((slots, 2), lambda i: (0, 0)), table, table],
        out_specs=pl.BlockSpec((slots, 2 * E), lambda i: (0, 0)),
        scratch_shapes=[pltpu.VMEM((2, slots, 128), F32), pltpu.VMEM((2, slots, E), F32)],
        compiler_params=params(32),
        name="read_rows",
    )(codes, bigram_t, trigram_t)


def add_rows_kernel(codes, grads, bigram, trigram, spread, turned):
    step = pl.program_id(0)
    width = bigram.shape[1]

    @pl.when(step == 0)
    def _():
        for table in range(2):
            wide(spread, codes, table)
        turned[...] = mm(eye(2 * E), grads[...], NT).astype(BF)

    for table, out in enumerate((bigram, trigram)):
        hot = onehot_block(spread, table, step * width, width)
        out[...] = mm(turned[table * E : (table + 1) * E, :], hot)


def add_rows(codes, grads, rows):
    slots = codes.shape[0]
    width = table_block(rows)
    table = pl.BlockSpec((E, width), lambda i: (0, i))
    shape = jax.ShapeDtypeStruct((E, rows), F32)
    return pl.pallas_call(
        add_rows_kernel,
        grid=(rows // width,),
        out_shape=(shape, shape),
        in_specs=[
            pl.BlockSpec((slots, 2), lambda i: (0, 0)),
            pl.BlockSpec((slots, 2 * E), lambda i: (0, 0)),
        ],
        out_specs=(table, table),
        scratch_shapes=[pltpu.VMEM((2, slots, 128), F32), pltpu.VMEM((2 * E, slots), BF)],
        compiler_params=params(32),
        name="add_rows",
    )(codes, grads)


def attend_kernel(pairs, piece, order, rows, out, attended_t, logsum, q_s, k_s, vt_s, s_s):
    length = rows.shape[0]
    blocks = length // ABLK
    per_block = ABLK // piece
    width = pairs * HD
    identity = eye(HD)

    def sort(j, _):
        block = rows[pl.ds(pl.multiple_of(order[j] * piece, piece), piece), :]
        to = pl.ds(pl.multiple_of(j * piece, piece), piece)
        for p in range(pairs):
            q = block[:, p * HD : (p + 1) * HD]
            q_s[p, to, :] = (q.astype(F32) * HD ** (-0.5)).astype(BF)
            k_s[p, to, :] = block[:, width + p * HD : width + (p + 1) * HD]
            v = block[:, 2 * width + p * HD : 2 * width + (p + 1) * HD]
            vt_s[p, :, to] = mm(identity, v, NT).astype(BF)
        return 0

    lax.fori_loop(0, length // piece, sort, 0)

    for p in range(pairs):

        def one(i, _):
            at = pl.ds(pl.multiple_of(i * ABLK, ABLK), ABLK)
            queries = q_s[p, at, :]

            def score(j, peak):
                to = pl.ds(pl.multiple_of(j * ABLK, ABLK), ABLK)
                s = mm(k_s[p, to, :], queries, NT)
                s_s[to, :] = s
                return jnp.maximum(peak, jnp.max(s, axis=0, keepdims=True))

            peak = lax.fori_loop(0, i + 1, score, jnp.full((1, ABLK), -jnp.inf, F32))

            def raise_(j, total):
                to = pl.ds(pl.multiple_of(j * ABLK, ABLK), ABLK)
                e = jnp.exp(s_s[to, :] - peak)
                s_s[to, :] = e
                return total + jnp.sum(e, axis=0, keepdims=True)

            total = lax.fori_loop(0, i + 1, raise_, jnp.zeros((1, ABLK), F32))
            scale = 1.0 / total

            def weigh(j, o):
                to = pl.ds(pl.multiple_of(j * ABLK, ABLK), ABLK)
                probs = (s_s[to, :] * scale).astype(BF)
                return o + mm(vt_s[p, :, to], probs)

            o = lax.fori_loop(0, i + 1, weigh, jnp.zeros((HD, ABLK), F32))
            attended_t[p, :, at] = o
            logsum[p, :, at] = peak + jnp.log(total)
            o = o.T.astype(BF)
            for h in range(per_block):
                to = pl.ds(pl.multiple_of(order[per_block * i + h] * piece, piece), piece)
                out[to, p * HD : (p + 1) * HD] = o[h * piece : (h + 1) * piece, :]
            return 0

        lax.fori_loop(0, blocks, one, 0)


def attend(order, rows, pairs, piece):
    length = rows.shape[0]
    return pl.pallas_call(
        functools.partial(attend_kernel, pairs, piece),
        out_shape=(
            jax.ShapeDtypeStruct((length, pairs * HD), BF),
            jax.ShapeDtypeStruct((pairs, HD, length), F32),
            jax.ShapeDtypeStruct((pairs, 1, length), F32),
        ),
        in_specs=[smem(), vmem()],
        out_specs=(vmem(),) * 3,
        scratch_shapes=[
            pltpu.VMEM((pairs, length, HD), BF),
            pltpu.VMEM((pairs, length, HD), BF),
            pltpu.VMEM((pairs, HD, length), BF),
            pltpu.VMEM((length, ABLK), F32),
        ],
        compiler_params=params(48),
        name="attend",
    )(order, rows)


def attend_grad_kernel(
    pairs,
    piece,
    order,
    rows,
    grads,
    attended_t,
    logsum,
    cos,
    sin,
    cos_t,
    sin_t,
    out,
    q_s,
    k_s,
    v_s,
    g_s,
    kt_s,
    dq_s,
    dk_s,
    dv_s,
    dk_o,
    dv_o,
):
    length = rows.shape[0]
    blocks = length // ABLK
    width = pairs * HD
    half = HD // 2
    scale = HD ** (-0.5)
    identity = eye(HD)

    for p in range(pairs):

        def sort(j, _):
            take = pl.ds(pl.multiple_of(order[j] * piece, piece), piece)
            block = rows[take, :]
            to = pl.ds(pl.multiple_of(j * piece, piece), piece)
            q_s[to, :] = (block[:, p * HD : (p + 1) * HD].astype(F32) * scale).astype(BF)
            k = block[:, width + p * HD : width + (p + 1) * HD]
            k_s[to, :] = k
            kt_s[:, to] = mm(identity, k, NT).astype(BF)
            v_s[to, :] = block[:, 2 * width + p * HD : 2 * width + (p + 1) * HD]
            g_s[to, :] = grads[take, :][:, p * HD : (p + 1) * HD]
            return 0

        lax.fori_loop(0, length // piece, sort, 0)
        dk_s[...] = jnp.zeros_like(dk_s)
        dv_s[...] = jnp.zeros_like(dv_s)

        def one(i, _):
            at = pl.ds(pl.multiple_of(i * ABLK, ABLK), ABLK)
            queries = q_s[at, :]
            grad = g_s[at, :]
            delta = jnp.sum(
                mm(identity, grad, NT) * attended_t[p, :, at], axis=0, keepdims=True
            )
            level = logsum[p, :, at]

            def tile(j, dq):
                to = pl.ds(pl.multiple_of(j * ABLK, ABLK), ABLK)
                probs = jnp.exp(mm(k_s[to, :], queries, NT) - level)
                ds = (probs * (mm(v_s[to, :], grad, NT) - delta)).astype(BF)
                dv_s[to, :] += mm(probs.astype(BF), grad)
                dk_s[to, :] += mm(ds, queries)
                return dq + mm(kt_s[:, to], ds)

            dq = lax.fori_loop(0, i + 1, tile, jnp.zeros((HD, ABLK), F32)) * scale
            c, s = cos_t[:, at], sin_t[:, at]
            a, b = dq[:half, :], dq[half:, :]
            dq = jnp.concatenate([a * c + b * s, b * c - a * s], axis=0)
            dq_s[p, at, :] = dq.T.astype(BF)
            return 0

        lax.fori_loop(0, blocks, one, 0)

        def turn(j, _):
            to = pl.ds(pl.multiple_of(j * ABLK, ABLK), ABLK)
            dk = dk_s[to, :]
            a, b = dk[:, :half], dk[:, half:]
            c, s = cos[to, :], sin[to, :]
            dk_o[p, to, :] = jnp.concatenate([a * c + b * s, b * c - a * s], axis=1).astype(BF)
            dv_o[p, to, :] = dv_s[to, :].astype(BF)
            return 0

        lax.fori_loop(0, blocks, turn, 0)

    def unsort(j, _):
        take = pl.ds(pl.multiple_of(j * piece, piece), piece)
        to = pl.ds(pl.multiple_of(order[j] * piece, piece), piece)
        parts = [ref[p, take, :] for ref in (dq_s, dk_o, dv_o) for p in range(pairs)]
        out[to, :] = jnp.concatenate(parts, axis=1)
        return 0

    lax.fori_loop(0, length // piece, unsort, 0)


def attend_grad(order, rows, grads, attended_t, logsum, cos, sin, pairs, piece):
    length = rows.shape[0]
    low = pltpu.VMEM((length, HD), BF)
    full = pltpu.VMEM((length, HD), F32)
    each = pltpu.VMEM((pairs, length, HD), BF)
    return pl.pallas_call(
        functools.partial(attend_grad_kernel, pairs, piece),
        out_shape=jax.ShapeDtypeStruct((length, 3 * pairs * HD), BF),
        in_specs=[smem()] + [vmem()] * 8,
        out_specs=vmem(),
        scratch_shapes=[low] * 4 + [pltpu.VMEM((HD, length), BF), each, full, full, each, each],
        compiler_params=params(56),
        name="attend_grad",
    )(order, rows, grads, attended_t, logsum, cos, sin, cos.T, sin.T)


def over_ctx(value, mask):
    size = lax.axis_size("ctx")
    return lax.ppermute(value, "ctx", [(i, i ^ mask) for i in range(size)])


def along_fsdp(value, shift):
    size = lax.axis_size("fsdp")
    return lax.ppermute(value, "fsdp", [(i, (i + shift) % size) for i in range(size)])


def by_index(blocks, index):
    if len(blocks) == 1:
        return blocks
    half = len(blocks) // 2
    flip = (index // half) % 2 == 1
    lower = [jnp.where(flip, b, a) for a, b in zip(blocks[:half], blocks[half:])]
    upper = [jnp.where(flip, a, b) for a, b in zip(blocks[:half], blocks[half:])]
    return by_index(lower, index) + by_index(upper, index)


def place():
    ctx = lax.axis_index("ctx")
    return ctx % 2, ctx // 2, lax.axis_index("fsdp")


def gather_weight(shard):
    core, chip, z = place()
    chips = lax.axis_size("ctx") // 2
    shards = lax.axis_size("fsdp")
    rows, columns = shard.shape
    r, half = rows // chips, columns // 2
    mine = lax.dynamic_slice(shard, (chip * r, core * half), (r, half))
    along = [mine] + [along_fsdp(mine, k) for k in range(1, shards)]
    turned = jnp.stack([along[(shards - m) % shards] for m in range(shards)])
    column = lax.dynamic_slice_in_dim(
        jnp.concatenate([turned, turned]), (shards - z) % shards, shards
    )
    blocks = [column] + [over_ctx(column, 2 * k) for k in range(1, chips)]
    own = jnp.stack(by_index(blocks, chip), axis=1).reshape(shards * rows, half)
    other = over_ctx(own, 1)
    return jnp.where(
        core == 0, jnp.concatenate([own, other], axis=1), jnp.concatenate([other, own], axis=1)
    )


def gather_gains(gains):
    _, _, z = place()
    shards = lax.axis_size("fsdp")
    along = [gains] + [along_fsdp(gains, k) for k in range(1, shards)]
    turned = jnp.stack([along[(shards - m) % shards] for m in range(shards)])
    every = lax.dynamic_slice_in_dim(
        jnp.concatenate([turned, turned]), (shards - z) % shards, shards
    )
    return jnp.moveaxis(every, 0, 1).reshape(gains.shape[0], -1)


def reduce_grad(grad):
    core, chip, z = place()
    chips = lax.axis_size("ctx") // 2
    shards = lax.axis_size("fsdp")
    rows, columns = grad.shape[0] // shards, grad.shape[1]
    r, half = rows // chips, columns // 2
    view = grad.reshape(shards, chips, r, columns)

    def columns_of(which):
        return lax.dynamic_slice_in_dim(view, which * half, half, axis=3)

    total = columns_of(core).astype(F32) + over_ctx(columns_of(1 - core), 1).astype(F32)
    low = total.astype(BF)
    sent = [
        over_ctx(lax.dynamic_index_in_dim(low, chip ^ k, 1, keepdims=False), 2 * k)
        for k in range(1, chips)
    ]
    total = lax.dynamic_index_in_dim(low, chip, 1, keepdims=False).astype(F32)
    total = sum((s.astype(F32) for s in sent), total)
    low = total.astype(BF)
    sent = [
        along_fsdp(lax.dynamic_index_in_dim(low, (z + k) % shards, 0, keepdims=False), k)
        for k in range(1, shards)
    ]
    total = lax.dynamic_index_in_dim(low, z, 0, keepdims=False).astype(F32)
    total = sum((s.astype(F32) for s in sent), total)
    piece = total.astype(BF)
    blocks = [piece] + [over_ctx(piece, 2 * k) for k in range(1, chips)]
    own = jnp.stack(by_index(blocks, chip)).reshape(rows, half)
    other = over_ctx(own, 1)
    return jnp.where(
        core == 0, jnp.concatenate([own, other], axis=1), jnp.concatenate([other, own], axis=1)
    ).astype(F32)


def by_head(values, devices, pairs):
    batches, tokens, kinds, _ = values.shape
    groups = HEADS // pairs
    values = values.reshape(batches, tokens, kinds, groups, pairs * HD)
    values = values.transpose(0, 3, 1, 2, 4).reshape(batches * groups, tokens, kinds * pairs * HD)
    spare = devices - batches * groups
    return jnp.pad(values, ((0, spare), (0, 0), (0, 0)))


def by_token(values, batches, kinds, pairs):
    groups = HEADS // pairs
    tokens = values.shape[1]
    values = values[: batches * groups].reshape(batches, groups, tokens, kinds, pairs * HD)
    return values.transpose(0, 2, 3, 1, 4).reshape(batches, tokens, kinds, HEADS * HD)


def exchange(values, axes):
    return lax.all_to_all(values, axes, split_axis=0, concat_axis=0, tiled=True)


def rotate(values, cosines, sines):
    half = values.shape[-1] // 2
    a, b = values[..., :half], values[..., half:]
    c, s = cosines[:, None, :], sines[:, None, :]
    return jnp.concatenate([a * c - b * s, b * c + a * s], axis=-1)


def normalize(rows):
    inverse = lax.rsqrt(jnp.mean(rows * rows, axis=-1, keepdims=True) + epsilon)
    return rows * inverse, inverse


def norm_backward(hidden_grad, normed, inverse, gain):
    weighted = hidden_grad * gain
    return inverse * (weighted - normed * jnp.mean(weighted * normed, axis=-1, keepdims=True))


def local(
    token_embed,
    bigram_ids,
    trigram_ids,
    bigram_table,
    trigram_table,
    block_deal,
    lookup_weight,
    attention_gain,
    joined_weight,
    output_weight,
    feedforward_gain,
    expand_weight,
    contract_weight,
    cotangent,
):
    contexts = lax.axis_size("ctx")
    shards = lax.axis_size("fsdp")
    devices = contexts * shards
    batches, local_rows = token_embed.shape[:2]
    tokens = batches * local_rows
    length = local_rows * contexts
    capacity = max(2, 2 * tokens // devices)
    table_rows = bigram_table.shape[0]
    piece = local_rows // 2
    pieces = length // piece
    pairs = -(-batches * HEADS // contexts)
    while HEADS % pairs:
        pairs += 1
    both = ("ctx", "fsdp")

    ids = jnp.stack([bigram_ids.reshape(-1), trigram_ids.reshape(-1)])
    requests, target_row, target_col = placement(ids, table_rows, devices, capacity)
    asked = exchange(requests, both)
    codes = jnp.stack([asked[:, :capacity].reshape(-1), asked[:, capacity:].reshape(-1)], axis=1)
    got = exchange(
        read_rows(codes, bigram_table.T, trigram_table.T).reshape(devices, capacity, 2 * E), both
    ).reshape(devices * capacity, 2 * E)

    lookup = gather_weight(lookup_weight)
    joined = gather_weight(joined_weight)
    output = gather_weight(output_weight)
    gains = gather_gains(jnp.stack([attention_gain, feedforward_gain])).astype(F32)
    first_gain, second_gain = gains[0], gains[1]
    expand = gather_weight(expand_weight)
    contract = gather_weight(contract_weight)

    order = jnp.argmin(
        jnp.abs(block_deal[None, :] - jnp.arange(pieces, dtype=jnp.int32)[:, None]), axis=1
    ).astype(jnp.int32)
    frequency = jnp.exp(-math.log(10000.0) * (2.0 * jnp.arange(HD // 2, dtype=F32) / HD))
    slot = lax.axis_index("ctx") * local_rows + jnp.arange(local_rows, dtype=jnp.int32)
    position = block_deal[slot // piece] * piece + slot % piece
    angles = position.astype(F32)[:, None] * frequency[None, :]
    cosines, sines = jnp.cos(angles), jnp.sin(angles)
    all_angles = jnp.arange(length, dtype=F32)[:, None] * frequency[None, :]
    all_cosines, all_sines = jnp.cos(all_angles), jnp.sin(all_angles)

    slots = jnp.arange(devices * capacity, dtype=jnp.int32)
    hot_b = (target_col[:, 0:1] == slots[None, :]).astype(BF)
    hot_t = (target_col[:, 1:2] == slots[None, :]).astype(BF)
    embedded = (mm(hot_b, got[:, :E]) + mm(hot_t, got[:, E:])).astype(BF)
    start = token_embed.reshape(tokens, D).astype(F32) + mm(embedded, lookup)
    normed_first, inverse_first = normalize(start)
    hidden_first = (normed_first * first_gain).astype(BF)
    projected = mm(hidden_first, joined).reshape(batches, local_rows, 3, HEADS, HD)
    cos_b, sin_b = cosines[None, :, None, :], sines[None, :, None, :]
    turn = lambda x: jnp.concatenate(
        [
            x[..., : HD // 2] * cos_b - x[..., HD // 2 :] * sin_b,
            x[..., HD // 2 :] * cos_b + x[..., : HD // 2] * sin_b,
        ],
        axis=-1,
    )
    qkv = jnp.stack(
        [turn(projected[:, :, 0]), turn(projected[:, :, 1]), projected[:, :, 2]], axis=2
    ).astype(BF)
    qkv = qkv.reshape(batches, local_rows, 3, D)
    rows = exchange(by_head(qkv, contexts, pairs), "ctx").reshape(length, 3 * pairs * HD)
    attended_rows, attended_t, logsum = attend(order, rows, pairs, piece)
    attended = by_token(
        exchange(attended_rows.reshape(contexts, local_rows, pairs * HD), "ctx"), batches, 1, pairs
    ).reshape(tokens, D)
    middle = start + mm(attended, output)
    normed_second, inverse_second = normalize(middle)
    hidden_second = (normed_second * second_gain).astype(BF)
    gate_up = mm(hidden_second, expand)
    gate, up = gate_up[:, :FF], gate_up[:, FF:]
    sigmoid = jax.nn.sigmoid(gate)
    swish = gate * sigmoid
    activated = (swish * up).astype(BF)
    result = (middle + mm(activated, contract)).astype(BF)

    upstream = cotangent.reshape(tokens, D)
    activated_grad = mm(upstream, contract, NT)
    gate_up_grad = jnp.concatenate(
        [
            activated_grad * up * sigmoid * (1.0 + gate * (1.0 - sigmoid)),
            activated_grad * swish,
        ],
        axis=-1,
    ).astype(BF)
    hidden_second_grad = mm(gate_up_grad, expand, NT)
    second_gain_term = jnp.sum(hidden_second_grad * normed_second, axis=0)
    middle_grad = upstream.astype(F32) + norm_backward(
        hidden_second_grad, normed_second, inverse_second, second_gain
    )
    middle_low = middle_grad.astype(BF)
    attended_grad = mm(middle_low, output, NT).astype(BF)
    grad_rows = exchange(
        by_head(attended_grad.reshape(batches, local_rows, 1, D), contexts, pairs), "ctx"
    ).reshape(length, pairs * HD)
    contract_term = mm(activated, upstream, TN).astype(BF)
    expand_term = mm(hidden_second, gate_up_grad, TN).astype(BF)
    output_term = mm(attended, middle_low, TN).astype(BF)
    contract_grad = reduce_grad(contract_term)
    expand_grad = reduce_grad(expand_term)
    output_grad = reduce_grad(output_term)

    grad_rows = attend_grad(
        order, rows, grad_rows, attended_t, logsum, all_cosines, all_sines, pairs, piece
    )
    joined_local = by_token(
        exchange(grad_rows.reshape(contexts, local_rows, 3 * pairs * HD), "ctx"), batches, 3, pairs
    ).reshape(tokens, 3 * D)
    joined_grad = reduce_grad(mm(hidden_first, joined_local, TN).astype(BF))
    hidden_first_grad = mm(joined_local, joined, NT)
    first_gain_term = jnp.sum(hidden_first_grad * normed_first, axis=0)
    start_grad = middle_grad + norm_backward(
        hidden_first_grad, normed_first, inverse_first, first_gain
    )
    start_low = start_grad.astype(BF)
    lookup_grad = reduce_grad(mm(embedded, start_low, TN).astype(BF))
    embed_grad = mm(start_low, lookup, NT).astype(BF)
    give_b = (target_row[0:1, :] == slots[:, None]).astype(BF)
    give_t = (target_row[1:2, :] == slots[:, None]).astype(BF)
    send = jnp.concatenate([mm(give_b, embed_grad), mm(give_t, embed_grad)], axis=1).astype(BF)
    arrived = exchange(send.reshape(devices, capacity, 2 * E), both)
    bigram_grad, trigram_grad = add_rows(
        codes, arrived.reshape(devices * capacity, 2 * E), table_rows
    )
    gain_terms = lax.psum(jnp.stack([first_gain_term, second_gain_term]), both)
    gain_share = lax.dynamic_slice_in_dim(
        gain_terms, lax.axis_index("fsdp") * (D // shards), D // shards, axis=1
    )
    return (
        result.reshape(batches, local_rows, D),
        start_grad.reshape(batches, local_rows, D),
        bigram_grad.T,
        trigram_grad.T,
        lookup_grad,
        gain_share[0],
        joined_grad,
        output_grad,
        gain_share[1],
        expand_grad,
        contract_grad,
    )


def solution(mesh):
    return jax.shard_map(
        local,
        mesh=mesh,
        in_specs=(
            P("fsdp", "ctx", None),
            P("fsdp", "ctx"),
            P("fsdp", "ctx"),
            P(("ctx", "fsdp"), None),
            P(("ctx", "fsdp"), None),
            P(),
            P("fsdp", None),
            P("fsdp"),
            P("fsdp", None),
            P("fsdp", None),
            P("fsdp"),
            P("fsdp", None),
            P("fsdp", None),
            P("fsdp", "ctx", None),
        ),
        out_specs=(
            P("fsdp", "ctx", None),
            P("fsdp", "ctx", None),
            P(("ctx", "fsdp"), None),
            P(("ctx", "fsdp"), None),
            P("fsdp", None),
            P("fsdp"),
            P("fsdp", None),
            P("fsdp", None),
            P("fsdp"),
            P("fsdp", None),
            P("fsdp", None),
        ),
        check_vma=False,
    )
```

time: 1480 us -> 724 us (0.49)
  waiting for transfers between devices: 676 us -> 123 us
  matrix products: 282 us -> 73.4 us
  Pallas kernels: 0 us -> 156 us
  local copies, waits for them, and re-layouts: 218 us -> 94.8 us
  starting transfers between devices: 32.4 us -> 145 us
  other arithmetic: 127 us -> 56.8 us
  blocking collectives: 103 us -> 64.4 us
  loops' own time: 15 us -> 0 us
  between operations: 17.5 us -> 2.52 us
    reduce_scatter x5 -> x0, waiting for transfers between devices: 447 us -> none  [local(): lax.psum_scatter(grad_totals, 'fsdp', scatter_dimension=0, tiled=True)]
    dot_general x70 -> x19, matrix products: 282 us -> 73.4 us  [mm(): return lax.dot_general(a, b, dims, preferred_element_type=F32)]
    all_gather x12 -> x0, waiting for transfers between devices: 187 us -> none  [the longest x1 109 us: local(): lax.all_gather(expand_weight, 'fsdp', axis=0, tiled=True)]
    pallas_call x0 -> x5, Pallas kernels: none -> 156 us  [the longest x1 69.9 us: attend_grad(): pl.pallas_call(functools.partial(attend_grad_kernel, pairs, piece), out_s...]
    ppermute x0 -> x93, starting transfers between devices: none -> 117 us  [the longest x60 59.3 us: over_ctx(): return lax.ppermute(value, 'ctx', [(i, i ^ mask) for i in range(size)])]
    ppermute x0 -> x93, waiting for transfers between devices: none -> 115 us  [the longest x60 73.1 us: over_ctx(): return lax.ppermute(value, 'ctx', [(i, i ^ mask) for i in range(size)])]
    dynamic_slice x76 -> x10, local copies, waits for them, and re-layouts: 72.6 us -> 9.61 us  [the longest x5 7.11 us: columns_of(): return lax.dynamic_slice_in_dim(view, which * half, half, axis=3)]
    all_gather x5 -> x0, blocking collectives: 59.6 us -> none  [the longest x2 21 us: local(): lax.all_gather(logsum.T, 'ctx', axis=0, tiled=True)]
  transfers between devices with their start and end apart: 24 -> 100, of which waited for: 12 -> 24; matrix products, arithmetic and copies ran while one was open for 39% -> 27% of each run, Pallas kernels for 0% -> 22%
where the time goes in v1:
time: 724 us; the launch traced here: 716 us
  Pallas kernels  156 us (22%)
  starting transfers between devices  145 us (20%)
  waiting for transfers between devices  123 us (17%)
  local copies, waits for them, and re-layouts  94.8 us (13%)
  matrix products  73.4 us (10%)
  blocking collectives  64.4 us (9%)
  other arithmetic  56.8 us (8%)
    dot_general x19, matrix products, mm(): return lax.dot_general(a, b, dims, preferred_element_type=F32)  73.4 us
    ppermute x60, waiting for transfers between devices, over_ctx(): return lax.ppermute(value, 'ctx', [(i, i ^ mask) for i in range(size)])  73.1 us
    pallas_call x1, Pallas kernels, attend_grad(): pl.pallas_call(functools.partial(attend_grad_kernel, pairs, piece), out_s...  69.9 us
    psum x1, blocking collectives, local(): gain_terms = lax.psum(jnp.stack([first_gain_term, second_gain_term]), both)  64.4 us
    ppermute x60, starting transfers between devices, over_ctx(): return lax.ppermute(value, 'ctx', [(i, i ^ mask) for i in range(size)])  59.3 us
    ppermute x33, starting transfers between devices, along_fsdp(): lax.ppermute(value, 'fsdp', [(i, (i + shift) % size) for i in range(size)])  58 us
    pallas_call x1, Pallas kernels, attend(): pl.pallas_call(functools.partial(attend_kernel, pairs, piece), out_shape=...  52.8 us
    ppermute x33, waiting for transfers between devices, along_fsdp(): lax.ppermute(value, 'fsdp', [(i, (i + shift) % size) for i in range(size)])  41.9 us
  transfers between devices with their start and end apart: 100, of which 24 were waited for; matrix products, arithmetic and copies ran while one was open for 27% of the time, Pallas kernels for 22%

profile of v1, /device:TPU:0, one launch (start us, length us, event | category | flops | bytes accessed | tf_op | source)
XLA Modules:
  0.0 715.7 jit_solution(4291759040743382206)
XLA Ops:
  1.5 5.0 collective-permute-start
  15.8 4.0 all-to-all-start
  23.3 4.8 fusion.21
  30.2 4.4 compare_select_fusion.1
  34.6 5.8 fusion.73
  62.6 17.6 %read_rows.1 = bf16[1024,384]{1,0:T(8,128)(2,1)} custom-call(s32[1024,2]{1,0:T(8,128)S(1)} %copy.130.codes, bf16[192,12800]{1,0:T(8,128)(2,1)S(1)} %bitcast.390, bf16[192,12800]{1,0:T(8,128)(2,1)S(1)} %bitcast.391), custom_call_target="tpu_custom_call" | custom-call | tf_op jit(solution)/shard_map/read_rows/pallas_call | solution.py:136
  80.3 5.0 all-to-all-start.1
  97.3 3.0 collective-permute-start.24
  103.7 7.3 %collective-permute-done.31 = bf16[128,384]{1,0:T(8,128)(2,1)} collective-permute-done((bf16[128,384]{1,0:T(8,128)(2,1)}, bf16[128,384]{1,0:T(8,128)(2,1)}, u32[]{:S(2)}, u32[]{:S(2)}) %collective-permute-start.31) | collective-permute-done | bytes 98336 | tf_op jit(solution)/shard_map/ppermute | solution.py:384
  111.0 3.2 collective-permute-start.25
  129.4 3.1 collective-permute-done.25
  135.6 5.4 collective-permute-done.13
  141.0 7.0 collective-permute-done.14
  158.2 7.6 %fusion.34 = f32[512,2304]{0,1:T(8,128)} fusion(bf16[768,1152]{1,0:T(8,128)(2,1)} %collective-permute-done.16, bf16[768,1152]{1,0:T(8,128)(2,1)} %bitcast.33, pred[]{:T(512)S(6)} %eq.180, f32[512,768]{1,0:T(8,128)S(1)} %get-tuple-element.161, f32[768]{0:T(1024)S(1)} %mul.303, f32[512]{0:T(512)S(1)} %add_rsqrt_fusion.1), kind=kOutput, calls=%fused_computation.104 | convolution fusion | flops 1829044224 | bytes 9835521 | tf_op jit(solution)/shard_map/dot_general | solution.py:27
  165.8 6.8 reshape.322
  174.5 3.6 slice_bitcast_fusion.1
  184.1 4.8 all-to-all-start.2
  206.3 15.7 %collective-permute-done.20 = bf16[4,48,384]{2,1,0:T(8,128)(2,1)S(1)} collective-permute-done((bf16[4,48,384]{2,1,0:T(8,128)(2,1)S(1)}, bf16[4,48,384]{2,1,0:T(8,128)(2,1)S(1)}, u32[]{:S(2)}, u32[]{:S(2)}) %collective-permute-start.20) | collective-permute-done | bytes 147488 | tf_op jit(solution)/shard_map/ppermute | solution.py:379
  226.5 3.1 copy.140
  229.6 52.8 %attend.1 = (bf16[2048,192]{1,0:T(8,128)(2,1)S(1)}, f32[3,64,2048]{2,1,0:T(8,128)S(1)}, f32[3,1,2048]{2,1,0:T(1,128)S(1)}) custom-call(s32[16]{0:T(128)S(1)} %get-tuple-element.22.order, bf16[2048,576]{1,0:T(8,128)(2,1)S(1)} %bitcast.388), custom_call_target="tpu_custom_call" | custom-call | tf_op jit(solution)/shard_map/attend/pallas_call | solution.py:245
  287.4 3.5 all-to-all-start.3
  295.6 7.8 %all-to-all-done.3 = bf16[8,256,192]{1,2,0:T(8,128)(2,1)S(1)} async-done(((bf16[8,256,192]{1,2,0:T(8,128)(2,1)}), bf16[8,256,192]{1,2,0:T(8,128)(2,1)S(1)}, u32[]{:S(2)}, u32[]{:S(2)}) %all-to-all-start.3) | async-done | bytes 786464 | tf_op jit(solution)/shard_map/all_to_all | solution.py:485
  307.1 11.7 %fusion.18 = f32[512,4096]{1,0:T(8,128)} fusion(bf16[768,2048]{1,0:T(8,128)(2,1)} %collective-permute-done.30, bf16[768,2048]{1,0:T(8,128)(2,1)} %bitcast.85, pred[]{:T(512)S(6)} %eq.180, f32[512,768]{1,0:T(8,128)S(1)} %get-tuple-element.163, f32[768]{0:T(1024)S(1)} %mul.328, f32[512]{0:T(512)S(1)} %add_rsqrt_fusion), kind=kOutput, calls=%fused_computation.64 | convolution fusion | flops 3250716672 | bytes 16258049 | tf_op jit(solution)/shard_map/dot_general | solution.py:27
  318.7 7.2 %fusion.2 = (bf16[512,2048]{1,0:T(8,128)(2,1)S(1)}, bf16[512,2048]{1,0:T(8,128)(2,1)S(1)}, bf16[512,2048]{1,0:T(8,128)(2,1)S(1)}) fusion(f32[512,4096]{1,0:T(8,128)} %fusion.18, bf16[512,768]{1,0:T(8,128)(2,1)S(1)} %bitcast.429, bf16[2048,384]{1,0:T(8,128)(2,1)} %collective-permute-done.37, bf16[2048,384]{1,0:T(8,128)(2,1)} %bitcast.97, pred[]{:T(512)S(6)} %eq.180), kind=kOutput, calls=%fused_computation.9 | convolution fusion | flops 1640497152 | bytes 18612224 | tf_op jit(solution)/shard_map/dot_general | solution.py:27
  325.9 10.0 %multiply_reduce_fusion = (f32[768]{0:T(1024)S(1)}, f32[512]{0:T(512)S(1)}, f32[512,768]{1,0:T(8,128)S(1)}) fusion(f32[512,768]{1,0:T(8,128)S(1)} %get-tuple-element.163, f32[512]{0:T(512)S(1)} %add_rsqrt_fusion, f32[768]{0:T(1024)S(1)} %mul.328, bf16[768,2048]{1,0:T(8,128)(2,1)} %collective-permute-done.30, bf16[768,2048]{1,0:T(8,128)(2,1)} %bitcast.85, ...), kind=kOutput, calls=%fused_computation.42 | convolution fusion | flops 3260283648 | bytes 13641729 | tf_op jit(solution)/shard_map/dot_general | solution.py:27
  341.2 5.6 convolution_convert_fusion
  357.7 3.5 all-to-all-start.4
  362.4 3.5 collective-permute-start.66
  374.6 5.7 add_convert_fusion.3
  381.8 69.9 %attend_grad.1 = bf16[2048,576]{1,0:T(8,128)(2,1)} custom-call(s32[16]{0:T(128)} %copy-done.6, bf16[2048,576]{1,0:T(8,128)(2,1)} %bitcast.389, bf16[2048,192]{1,0:T(8,128)(2,1)} %bitcast.405, f32[3,64,2048]{2,1,0:T(8,128)} %copy-done.3, f32[3,1,2048]{2,1,0:T(1,128)} %copy-done.5, f32[2048,32]{1,0:T(8,128)} %get-tuple-element.143.cos, ...), custom_call_target="tpu_custom_call" | custom-call | tf_op jit(solution)/shard_map/attend_grad/pallas_call | solution.py:366
  451.7 4.3 copy.156
  456.0 4.1 all-to-all-start.5
  466.2 3.2 collective-permute-start.88
  470.6 20.2 %collective-permute-done.67 = bf16[48,384]{1,0:T(8,128)(2,1)S(1)} collective-permute-done((bf16[48,384]{1,0:T(8,128)(2,1)S(1)}, bf16[48,384]{1,0:T(8,128)(2,1)S(1)}, u32[]{:S(2)}, u32[]{:S(2)}) %collective-permute-start.67) | collective-permute-done | bytes 36896 | tf_op jit(solution)/shard_map/ppermute | solution.py:379
  493.7 3.5 collective-permute-done.86
  504.2 4.0 constant_dynamic-slice_fusion.2
  514.7 6.4 multiply_reduce_fusion.1
  527.1 3.1 all-to-all-start.6
  532.0 4.6 convolution_convert_fusion.1
  542.5 3.2 add_convert_fusion
  551.7 3.5 collective-permute-start.44
  555.2 64.4 %psum.7 = f32[2,768]{1,0:T(2,128)S(1)} all-reduce(f32[2,768]{1,0:T(2,128)S(1)} %pad_maximum_fusion.16), channel_id=1, replica_groups=mesh['ctx'=8,'fsdp'=4] {'ctx','fsdp'}, use_global_device_ids=true, to_apply=%region_7.8 | all-reduce | flops 1536 | bytes 12288 | tf_op jit(solution)/shard_map/psum | solution.py:646
  635.4 3.6 collective-permute-done.77
  638.9 11.6 %collective-permute-done.76 = bf16[48,2048]{1,0:T(8,128)(2,1)S(1)} collective-permute-done((bf16[48,2048]{1,0:T(8,128)(2,1)S(1)}, bf16[48,2048]{1,0:T(8,128)(2,1)S(1)}, u32[]{:S(2)}, u32[]{:S(2)}) %collective-permute-start.76) | collective-permute-done | bytes 196640 | tf_op jit(solution)/shard_map/ppermute | solution.py:384
  664.3 6.2 collective-permute-done.80
  673.2 6.8 collective-permute-done.51
  685.5 7.9 %collective-permute-done.54 = bf16[48,1152]{1,0:T(8,128)(2,1)S(1)} collective-permute-done((bf16[48,1152]{1,0:T(8,128)(2,1)S(1)}, bf16[48,1152]{1,0:T(8,128)(2,1)S(1)}, u32[]{:S(2)}, u32[]{:S(2)}) %collective-permute-start.54) | collective-permute-done | bytes 110624 | tf_op jit(solution)/shard_map/ppermute | solution.py:384
  697.7 13.8 %add_rows.1 = (f32[192,12800]{1,0:T(8,128)}, f32[192,12800]{1,0:T(8,128)}) custom-call(s32[1024,2]{1,0:T(8,128)S(1)} %copy.130.codes, bf16[1024,384]{1,0:T(8,128)(2,1)S(1)} %bitcast.392), custom_call_target="tpu_custom_call" | custom-call | tf_op jit(solution)/shard_map/add_rows/pallas_call | solution.py:168
  (431 shorter events, 240.3 us)
Async XLA Ops:
  1.5 51.7 %collective-permute-start = (bf16[12,384]{1,0:T(8,128)(2,1)S(1)}, bf16[12,384]{1,0:T(8,128)(2,1)S(1)}, u32[]{:S(2)}, u32[]{:S(2)}) collective-permute-start(bf16[12,384]{1,0:T(8,128)(2,1)S(1)} %get-tuple-element.48), channel_id=1, source_target_pairs={{0,3},{1,0},{2,1},{3,2},{4,7},{5,4},{6,5},{7,6},{8,11},{9,8},{10,9... | collective-permute-start | bytes 27656 | tf_op jit(solution)/shard_map/ppermute | solution.py:384
  6.5 48.1 %collective-permute-start.1 = (bf16[12,384]{1,0:T(8,128)(2,1)S(1)}, bf16[12,384]{1,0:T(8,128)(2,1)S(1)}, u32[]{:S(2)}, u32[]{:S(2)}) collective-permute-start(bf16[12,384]{1,0:T(8,128)(2,1)S(1)} %get-tuple-element.48), channel_id=1, source_target_pairs={{0,2},{1,3},{2,0},{3,1},{4,6},{5,7},{6,4},{7,5},{8,10},{9,11},{10,... | collective-permute-start | bytes 27656 | tf_op jit(solution)/shard_map/ppermute | solution.py:384
  6.5 49.6 %collective-permute-start.2 = (bf16[12,384]{1,0:T(8,128)(2,1)S(1)}, bf16[12,384]{1,0:T(8,128)(2,1)S(1)}, u32[]{:S(2)}, u32[]{:S(2)}) collective-permute-start(bf16[12,384]{1,0:T(8,128)(2,1)S(1)} %get-tuple-element.48), channel_id=1, source_target_pairs={{0,1},{1,2},{2,3},{3,0},{4,5},{5,6},{6,7},{7,4},{8,9},{9,10},{10,1... | collective-permute-start | bytes 27656 | tf_op jit(solution)/shard_map/ppermute | solution.py:384
  8.9 37.9 %collective-permute-start.7 = (bf16[2,192]{1,0:T(2,128)(2,1)S(1)}, bf16[2,192]{1,0:T(2,128)(2,1)S(1)}, u32[]{:S(2)}, u32[]{:S(2)}) collective-permute-start(bf16[2,192]{1,0:T(2,128)(2,1)S(1)} %get-tuple-element.44), channel_id=1, source_target_pairs={{0,3},{1,0},{2,1},{3,2},{4,7},{5,4},{6,5},{7,6},{8,11},{9,8},{10,9... | collective-permute-start | bytes 2312 | tf_op jit(solution)/shard_map/ppermute | solution.py:384
  11.7 36.8 %collective-permute-start.8 = (bf16[2,192]{1,0:T(2,128)(2,1)S(1)}, bf16[2,192]{1,0:T(2,128)(2,1)S(1)}, u32[]{:S(2)}, u32[]{:S(2)}) collective-permute-start(bf16[2,192]{1,0:T(2,128)(2,1)S(1)} %get-tuple-element.44), channel_id=1, source_target_pairs={{0,2},{1,3},{2,0},{3,1},{4,6},{5,7},{6,4},{7,5},{8,10},{9,11},{10,... | collective-permute-start | bytes 2312 | tf_op jit(solution)/shard_map/ppermute | solution.py:384
  15.8 41.5 %all-to-all-start = ((s32[32,1,64]{2,1,0:T(1,128)}), s32[32,1,64]{2,1,0:T(1,128)S(1)}, u32[]{:S(2)}, u32[]{:S(2)}) async-start(s32[32,1,64]{2,1,0:T(1,128)} %bitcast.3), calls=%async_computation | async-start | bytes 32768 | tf_op jit(solution)/shard_map/all_to_all | solution.py:485
  48.5 67.2 %collective-permute-start.10 = (bf16[48,1152]{1,0:T(8,128)(2,1)}, bf16[48,1152]{1,0:T(8,128)(2,1)}, u32[]{:S(2)}, u32[]{:S(2)}) collective-permute-start(bf16[48,1152]{1,0:T(8,128)(2,1)} %get-tuple-element.46), channel_id=1, source_target_pairs={{0,3},{1,0},{2,1},{3,2},{4,7},{5,4},{6,5},{7,6},{8,11},{9,8},{10,9... | collective-permute-start | bytes 331784 | tf_op jit(solution)/shard_map/ppermute | solution.py:384
  52.1 65.5 %collective-permute-start.11 = (bf16[48,1152]{1,0:T(8,128)(2,1)}, bf16[48,1152]{1,0:T(8,128)(2,1)}, u32[]{:S(2)}, u32[]{:S(2)}) collective-permute-start(bf16[48,1152]{1,0:T(8,128)(2,1)} %get-tuple-element.46), channel_id=1, source_target_pairs={{0,2},{1,3},{2,0},{3,1},{4,6},{5,7},{6,4},{7,5},{8,10},{9,11},{10,... | collective-permute-start | bytes 331784 | tf_op jit(solution)/shard_map/ppermute | solution.py:384
  53.2 32.2 %collective-permute-start.17 = (bf16[48,384]{1,0:T(8,128)(2,1)S(1)}, bf16[48,384]{1,0:T(8,128)(2,1)S(1)}, u32[]{:S(2)}, u32[]{:S(2)}) collective-permute-start(bf16[48,384]{1,0:T(8,128)(2,1)S(1)} %get-tuple-element.42), channel_id=1, source_target_pairs={{0,3},{1,0},{2,1},{3,2},{4,7},{5,4},{6,5},{7,6},{8,11},{9,8},{10,9... | collective-permute-start | bytes 110600 | tf_op jit(solution)/shard_map/ppermute | solution.py:384
  54.6 34.0 %collective-permute-start.18 = (bf16[48,384]{1,0:T(8,128)(2,1)S(1)}, bf16[48,384]{1,0:T(8,128)(2,1)S(1)}, u32[]{:S(2)}, u32[]{:S(2)}) collective-permute-start(bf16[48,384]{1,0:T(8,128)(2,1)S(1)} %get-tuple-element.42), channel_id=1, source_target_pairs={{0,2},{1,3},{2,0},{3,1},{4,6},{5,7},{6,4},{7,5},{8,10},{9,11},{10,... | collective-permute-start | bytes 110600 | tf_op jit(solution)/shard_map/ppermute | solution.py:384
  56.2 33.6 %collective-permute-start.19 = (bf16[48,384]{1,0:T(8,128)(2,1)S(1)}, bf16[48,384]{1,0:T(8,128)(2,1)S(1)}, u32[]{:S(2)}, u32[]{:S(2)}) collective-permute-start(bf16[48,384]{1,0:T(8,128)(2,1)S(1)} %get-tuple-element.42), channel_id=1, source_target_pairs={{0,1},{1,2},{2,3},{3,0},{4,5},{5,6},{6,7},{7,4},{8,9},{9,10},{10,1... | collective-permute-start | bytes 110600 | tf_op jit(solution)/shard_map/ppermute | solution.py:384
  80.3 72.0 %all-to-all-start.1 = ((bf16[32,32,384]{2,1,0:T(8,128)(2,1)}), bf16[32,32,384]{2,1,0:T(8,128)(2,1)}, u32[]{:S(2)}, u32[]{:S(2)}) async-start(bf16[32,32,384]{2,1,0:T(8,128)(2,1)} %bitcast.7), calls=%async_computation.1 | async-start | bytes 1572864 | tf_op jit(solution)/shard_map/all_to_all | solution.py:485
  95.1 26.4 %collective-permute-start.12 = (bf16[48,1152]{1,0:T(8,128)(2,1)}, bf16[48,1152]{1,0:T(8,128)(2,1)}, u32[]{:S(2)}, u32[]{:S(2)}) collective-permute-start(bf16[48,1152]{1,0:T(8,128)(2,1)} %get-tuple-element.46), channel_id=1, source_target_pairs={{0,1},{1,2},{2,3},{3,0},{4,5},{5,6},{6,7},{7,4},{8,9},{9,10},{10,1... | collective-permute-start | bytes 331784 | tf_op jit(solution)/shard_map/ppermute | solution.py:384
  97.3 29.6 %collective-permute-start.24 = (bf16[48,2048]{1,0:T(8,128)(2,1)S(1)}, bf16[48,2048]{1,0:T(8,128)(2,1)S(1)}, u32[]{:S(2)}, u32[]{:S(2)}) collective-permute-start(bf16[48,2048]{1,0:T(8,128)(2,1)S(1)} %get-tuple-element.40), channel_id=1, source_target_pairs={{0,3},{1,0},{2,1},{3,2},{4,7},{5,4},{6,5},{7,6},{8,11},{9,8},{10,9... | collective-permute-start | bytes 589832 | tf_op jit(solution)/shard_map/ppermute | solution.py:384
  117.7 78.7 %collective-permute-start.32 = (bf16[128,384]{1,0:T(8,128)(2,1)}, bf16[128,384]{1,0:T(8,128)(2,1)}, u32[]{:S(2)}, u32[]{:S(2)}) collective-permute-start(bf16[128,384]{1,0:T(8,128)(2,1)} %get-tuple-element.38), channel_id=1, source_target_pairs={{0,2},{1,3},{2,0},{3,1},{4,6},{5,7},{6,4},{7,5},{8,10},{9,11},{10,... | collective-permute-start | bytes 294920 | tf_op jit(solution)/shard_map/ppermute | solution.py:384
  121.6 75.7 %collective-permute-start.33 = (bf16[128,384]{1,0:T(8,128)(2,1)}, bf16[128,384]{1,0:T(8,128)(2,1)}, u32[]{:S(2)}, u32[]{:S(2)}) collective-permute-start(bf16[128,384]{1,0:T(8,128)(2,1)} %get-tuple-element.38), channel_id=1, source_target_pairs={{0,1},{1,2},{2,3},{3,0},{4,5},{5,6},{6,7},{7,4},{8,9},{9,10},{10,1... | collective-permute-start | bytes 294920 | tf_op jit(solution)/shard_map/ppermute | solution.py:384
  149.8 39.1 %collective-permute-start.27 = (bf16[4,48,2048]{2,1,0:T(8,128)(2,1)S(1)}, bf16[4,48,2048]{2,1,0:T(8,128)(2,1)}, u32[]{:S(2)}, u32[]{:S(2)}) collective-permute-start(bf16[4,48,2048]{2,1,0:T(8,128)(2,1)S(1)} %constant_dynamic-slice_fusion.11), channel_id=1, source_target_pairs={{0,24},{4,28},{8,16},{12,20},{16,8},{20,12},{24,0},{28,4},{1,25},{... | collective-permute-start | bytes 2359304 | tf_op jit(solution)/shard_map/ppermute | solution.py:379
  155.9 35.9 %collective-permute-start.28 = (bf16[4,48,2048]{2,1,0:T(8,128)(2,1)S(1)}, bf16[4,48,2048]{2,1,0:T(8,128)(2,1)}, u32[]{:S(2)}, u32[]{:S(2)}) collective-permute-start(bf16[4,48,2048]{2,1,0:T(8,128)(2,1)S(1)} %constant_dynamic-slice_fusion.11), channel_id=1, source_target_pairs={{0,8},{4,12},{8,0},{12,4},{16,24},{20,28},{24,16},{28,20},{1,9},{5... | collective-permute-start | bytes 2359304 | tf_op jit(solution)/shard_map/ppermute | solution.py:379
  157.1 35.3 %collective-permute-start.29 = (bf16[4,48,2048]{2,1,0:T(8,128)(2,1)S(1)}, bf16[4,48,2048]{2,1,0:T(8,128)(2,1)}, u32[]{:S(2)}, u32[]{:S(2)}) collective-permute-start(bf16[4,48,2048]{2,1,0:T(8,128)(2,1)S(1)} %constant_dynamic-slice_fusion.11), channel_id=1, source_target_pairs={{0,16},{4,20},{8,24},{12,28},{16,0},{20,4},{24,8},{28,12},{1,17},{... | collective-permute-start | bytes 2359304 | tf_op jit(solution)/shard_map/ppermute | solution.py:379
  184.1 42.4 %all-to-all-start.2 = ((bf16[8,256,576]{1,2,0:T(8,128)(2,1)}), bf16[8,256,576]{1,2,0:T(8,128)(2,1)}, u32[]{:S(2)}, u32[]{:S(2)}) async-start(bf16[8,256,576]{1,2,0:T(8,128)(2,1)} %bitcast.57), calls=%async_computation.2 | async-start | bytes 4718592 | tf_op jit(solution)/shard_map/all_to_all | solution.py:485
  189.0 33.0 %collective-permute-start.20 = (bf16[4,48,384]{2,1,0:T(8,128)(2,1)S(1)}, bf16[4,48,384]{2,1,0:T(8,128)(2,1)S(1)}, u32[]{:S(2)}, u32[]{:S(2)}) collective-permute-start(bf16[4,48,384]{2,1,0:T(8,128)(2,1)S(1)} %copy-done.28), channel_id=1, source_target_pairs={{0,24},{4,28},{8,16},{12,20},{16,8},{20,12},{24,0},{28,4},{1,25},{... | collective-permute-start | bytes 442376 | tf_op jit(solution)/shard_map/ppermute | solution.py:379
  191.8 32.4 %collective-permute-start.21 = (bf16[4,48,384]{2,1,0:T(8,128)(2,1)S(1)}, bf16[4,48,384]{2,1,0:T(8,128)(2,1)S(1)}, u32[]{:S(2)}, u32[]{:S(2)}) collective-permute-start(bf16[4,48,384]{2,1,0:T(8,128)(2,1)S(1)} %copy-done.28), channel_id=1, source_target_pairs={{0,8},{4,12},{8,0},{12,4},{16,24},{20,28},{24,16},{28,20},{1,9},{5... | collective-permute-start | bytes 442376 | tf_op jit(solution)/shard_map/ppermute | solution.py:379
  192.4 33.3 %collective-permute-start.22 = (bf16[4,48,384]{2,1,0:T(8,128)(2,1)S(1)}, bf16[4,48,384]{2,1,0:T(8,128)(2,1)S(1)}, u32[]{:S(2)}, u32[]{:S(2)}) collective-permute-start(bf16[4,48,384]{2,1,0:T(8,128)(2,1)S(1)} %copy-done.28), channel_id=1, source_target_pairs={{0,16},{4,20},{8,24},{12,28},{16,0},{20,4},{24,8},{28,12},{1,17},{... | collective-permute-start | bytes 442376 | tf_op jit(solution)/shard_map/ppermute | solution.py:379
  196.3 110.7 %collective-permute-start.30 = (bf16[768,2048]{1,0:T(8,128)(2,1)}, bf16[768,2048]{1,0:T(8,128)(2,1)}, u32[]{:S(2)}, u32[]{:S(2)}) collective-permute-start(bf16[768,2048]{1,0:T(8,128)(2,1)} %bitcast.85), channel_id=1, source_target_pairs={{0,4},{4,0},{8,12},{12,8},{16,20},{20,16},{24,28},{28,24},{1,5},{5... | collective-permute-start | bytes 9437192 | tf_op jit(solution)/shard_map/ppermute | solution.py:379
  203.5 89.1 %collective-permute-start.34 = (bf16[4,128,384]{2,1,0:T(8,128)(2,1)}, bf16[4,128,384]{2,1,0:T(8,128)(2,1)}, u32[]{:S(2)}, u32[]{:S(2)}) collective-permute-start(bf16[4,128,384]{2,1,0:T(8,128)(2,1)} %constant_dynamic-slice_fusion.10), channel_id=1, source_target_pairs={{0,24},{4,28},{8,16},{12,20},{16,8},{20,12},{24,0},{28,4},{1,25},{... | collective-permute-start | bytes 1179656 | tf_op jit(solution)/shard_map/ppermute | solution.py:379
  222.0 70.6 %collective-permute-start.35 = (bf16[4,128,384]{2,1,0:T(8,128)(2,1)}, bf16[4,128,384]{2,1,0:T(8,128)(2,1)}, u32[]{:S(2)}, u32[]{:S(2)}) collective-permute-start(bf16[4,128,384]{2,1,0:T(8,128)(2,1)} %constant_dynamic-slice_fusion.10), channel_id=1, source_target_pairs={{0,8},{4,12},{8,0},{12,4},{16,24},{20,28},{24,16},{28,20},{1,9},{5... | collective-permute-start | bytes 1179656 | tf_op jit(solution)/shard_map/ppermute | solution.py:379
  224.2 68.3 %collective-permute-start.36 = (bf16[4,128,384]{2,1,0:T(8,128)(2,1)}, bf16[4,128,384]{2,1,0:T(8,128)(2,1)}, u32[]{:S(2)}, u32[]{:S(2)}) collective-permute-start(bf16[4,128,384]{2,1,0:T(8,128)(2,1)} %constant_dynamic-slice_fusion.10), channel_id=1, source_target_pairs={{0,16},{4,20},{8,24},{12,28},{16,0},{20,4},{24,8},{28,12},{1,17},{... | collective-permute-start | bytes 1179656 | tf_op jit(solution)/shard_map/ppermute | solution.py:379
  340.7 25.8 %collective-permute-start.82 = (bf16[4,4,128,384]{3,2,1,0:T(8,128)(2,1)}, bf16[4,4,128,384]{3,2,1,0:T(8,128)(2,1)}, u32[]{:S(2)}, u32[]{:S(2)}) collective-permute-start(bf16[4,4,128,384]{3,2,1,0:T(8,128)(2,1)} %constant_dynamic-slice_fusion.1), channel_id=1, source_target_pairs={{0,4},{4,0},{8,12},{12,8},{16,20},{20,16},{24,28},{28,24},{1,5},{5... | collective-permute-start | bytes 4718600 | tf_op jit(solution)/shard_map/ppermute | solution.py:379
  365.9 94.2 %collective-permute-start.65 = (bf16[48,384]{1,0:T(8,128)(2,1)S(1)}, bf16[48,384]{1,0:T(8,128)(2,1)S(1)}, u32[]{:S(2)}, u32[]{:S(2)}) collective-permute-start(bf16[48,384]{1,0:T(8,128)(2,1)S(1)} %get-tuple-element.122), channel_id=1, source_target_pairs={{0,2},{1,3},{2,0},{3,1},{4,6},{5,7},{6,4},{7,5},{8,10},{9,11},{10,... | collective-permute-start | bytes 110600 | tf_op jit(solution)/shard_map/ppermute | solution.py:384
  365.9 94.2 %collective-permute-start.64 = (bf16[48,384]{1,0:T(8,128)(2,1)S(1)}, bf16[48,384]{1,0:T(8,128)(2,1)S(1)}, u32[]{:S(2)}, u32[]{:S(2)}) collective-permute-start(bf16[48,384]{1,0:T(8,128)(2,1)S(1)} %get-tuple-element.120), channel_id=1, source_target_pairs={{0,1},{1,2},{2,3},{3,0},{4,5},{5,6},{6,7},{7,4},{8,9},{9,10},{10,1... | collective-permute-start | bytes 110600 | tf_op jit(solution)/shard_map/ppermute | solution.py:384
  371.1 93.4 %collective-permute-start.85 = (bf16[4,128,384]{2,1,0:T(8,128)(2,1)}, bf16[4,128,384]{2,1,0:T(8,128)(2,1)}, u32[]{:S(2)}, u32[]{:S(2)}) collective-permute-start(bf16[4,128,384]{2,1,0:T(8,128)(2,1)} %get-tuple-element.75), channel_id=1, source_target_pairs={{0,24},{4,28},{8,16},{12,20},{16,8},{20,12},{24,0},{28,4},{1,25},{... | collective-permute-start | bytes 1179656 | tf_op jit(solution)/shard_map/ppermute | solution.py:379
  373.9 90.7 %collective-permute-start.84 = (bf16[4,128,384]{2,1,0:T(8,128)(2,1)}, bf16[4,128,384]{2,1,0:T(8,128)(2,1)}, u32[]{:S(2)}, u32[]{:S(2)}) collective-permute-start(bf16[4,128,384]{2,1,0:T(8,128)(2,1)} %get-tuple-element.76), channel_id=1, source_target_pairs={{0,16},{4,20},{8,24},{12,28},{16,0},{20,4},{24,8},{28,12},{1,17},{... | collective-permute-start | bytes 1179656 | tf_op jit(solution)/shard_map/ppermute | solution.py:379
  374.4 90.2 %collective-permute-start.83 = (bf16[4,128,384]{2,1,0:T(8,128)(2,1)S(1)}, bf16[4,128,384]{2,1,0:T(8,128)(2,1)}, u32[]{:S(2)}, u32[]{:S(2)}) collective-permute-start(bf16[4,128,384]{2,1,0:T(8,128)(2,1)S(1)} %get-tuple-element.74), channel_id=1, source_target_pairs={{0,8},{4,12},{8,0},{12,4},{16,24},{20,28},{24,16},{28,20},{1,9},{5... | collective-permute-start | bytes 1179656 | tf_op jit(solution)/shard_map/ppermute | solution.py:379
  456.0 54.8 %all-to-all-start.5 = ((bf16[8,256,576]{1,2,0:T(8,128)(2,1)}), bf16[8,256,576]{1,2,0:T(8,128)(2,1)S(1)}, u32[]{:S(2)}, u32[]{:S(2)}) async-start(bf16[8,256,576]{1,2,0:T(8,128)(2,1)} %copy.156), calls=%async_computation.5 | async-start | bytes 4718592 | tf_op jit(solution)/shard_map/all_to_all | solution.py:485
  460.9 29.8 %collective-permute-start.67 = (bf16[48,384]{1,0:T(8,128)(2,1)S(1)}, bf16[48,384]{1,0:T(8,128)(2,1)S(1)}, u32[]{:S(2)}, u32[]{:S(2)}) collective-permute-start(bf16[48,384]{1,0:T(8,128)(2,1)S(1)} %fusion.63), channel_id=1, source_target_pairs={{0,24},{4,28},{8,16},{12,20},{16,8},{20,12},{24,0},{28,4},{1,25},{... | collective-permute-start | bytes 110600 | tf_op jit(solution)/shard_map/ppermute | solution.py:379
  463.9 29.7 %collective-permute-start.68 = (bf16[48,384]{1,0:T(8,128)(2,1)S(1)}, bf16[48,384]{1,0:T(8,128)(2,1)S(1)}, u32[]{:S(2)}, u32[]{:S(2)}) collective-permute-start(bf16[48,384]{1,0:T(8,128)(2,1)S(1)} %fusion.63), channel_id=1, source_target_pairs={{0,8},{4,12},{8,0},{12,4},{16,24},{20,28},{24,16},{28,20},{1,9},{5... | collective-permute-start | bytes 110600 | tf_op jit(solution)/shard_map/ppermute | solution.py:379
  464.5 29.1 %collective-permute-start.69 = (bf16[48,384]{1,0:T(8,128)(2,1)S(1)}, bf16[48,384]{1,0:T(8,128)(2,1)S(1)}, u32[]{:S(2)}, u32[]{:S(2)}) collective-permute-start(bf16[48,384]{1,0:T(8,128)(2,1)S(1)} %fusion.63), channel_id=1, source_target_pairs={{0,16},{4,20},{8,24},{12,28},{16,0},{20,4},{24,8},{28,12},{1,17},{... | collective-permute-start | bytes 110600 | tf_op jit(solution)/shard_map/ppermute | solution.py:379
  466.2 27.5 %collective-permute-start.88 = (bf16[128,384]{1,0:T(8,128)(2,1)S(1)}, bf16[128,384]{1,0:T(8,128)(2,1)S(1)}, u32[]{:S(2)}, u32[]{:S(2)}) collective-permute-start(bf16[128,384]{1,0:T(8,128)(2,1)S(1)} %get-tuple-element.107), channel_id=1, source_target_pairs={{0,3},{1,0},{2,1},{3,2},{4,7},{5,4},{6,5},{7,6},{8,11},{9,8},{10,9... | collective-permute-start | bytes 294920 | tf_op jit(solution)/shard_map/ppermute | solution.py:384
  469.4 24.2 %collective-permute-start.87 = (bf16[128,384]{1,0:T(8,128)(2,1)S(1)}, bf16[128,384]{1,0:T(8,128)(2,1)S(1)}, u32[]{:S(2)}, u32[]{:S(2)}) collective-permute-start(bf16[128,384]{1,0:T(8,128)(2,1)S(1)} %get-tuple-element.108), channel_id=1, source_target_pairs={{0,2},{1,3},{2,0},{3,1},{4,6},{5,7},{6,4},{7,5},{8,10},{9,11},{10,... | collective-permute-start | bytes 294920 | tf_op jit(solution)/shard_map/ppermute | solution.py:384
  508.2 34.3 %collective-permute-start.71 = (bf16[4,4,48,2048]{3,2,1,0:T(8,128)(2,1)}, bf16[4,4,48,2048]{3,2,1,0:T(8,128)(2,1)}, u32[]{:S(2)}, u32[]{:S(2)}) collective-permute-start(bf16[4,4,48,2048]{3,2,1,0:T(8,128)(2,1)} %constant_dynamic-slice_fusion.2), channel_id=1, source_target_pairs={{0,4},{4,0},{8,12},{12,8},{16,20},{20,16},{24,28},{28,24},{1,5},{5... | collective-permute-start | bytes 9437192 | tf_op jit(solution)/shard_map/ppermute | solution.py:379
  527.1 170.6 %all-to-all-start.6 = ((bf16[32,32,384]{2,1,0:T(8,128)(2,1)}), bf16[32,32,384]{2,1,0:T(8,128)(2,1)S(1)}, u32[]{:S(2)}, u32[]{:S(2)}) async-start(bf16[32,32,384]{2,1,0:T(8,128)(2,1)} %pad_maximum_fusion.8), calls=%async_computation.6 | async-start | bytes 1572864 | tf_op jit(solution)/shard_map/all_to_all | solution.py:485
  548.2 79.9 %collective-permute-start.74 = (bf16[4,48,2048]{2,1,0:T(8,128)(2,1)}, bf16[4,48,2048]{2,1,0:T(8,128)(2,1)S(1)}, u32[]{:S(2)}, u32[]{:S(2)}) collective-permute-start(bf16[4,48,2048]{2,1,0:T(8,128)(2,1)} %get-tuple-element.57), channel_id=1, source_target_pairs={{0,24},{4,28},{8,16},{12,20},{16,8},{20,12},{24,0},{28,4},{1,25},{... | collective-permute-start | bytes 2359304 | tf_op jit(solution)/shard_map/ppermute | solution.py:379
  550.6 78.9 %collective-permute-start.73 = (bf16[4,48,2048]{2,1,0:T(8,128)(2,1)}, bf16[4,48,2048]{2,1,0:T(8,128)(2,1)S(1)}, u32[]{:S(2)}, u32[]{:S(2)}) collective-permute-start(bf16[4,48,2048]{2,1,0:T(8,128)(2,1)} %get-tuple-element.58), channel_id=1, source_target_pairs={{0,16},{4,20},{8,24},{12,28},{16,0},{20,4},{24,8},{28,12},{1,17},{... | collective-permute-start | bytes 2359304 | tf_op jit(solution)/shard_map/ppermute | solution.py:379
  551.2 79.3 %collective-permute-start.72 = (bf16[4,48,2048]{2,1,0:T(8,128)(2,1)}, bf16[4,48,2048]{2,1,0:T(8,128)(2,1)}, u32[]{:S(2)}, u32[]{:S(2)}) collective-permute-start(bf16[4,48,2048]{2,1,0:T(8,128)(2,1)} %get-tuple-element.56), channel_id=1, source_target_pairs={{0,8},{4,12},{8,0},{12,4},{16,24},{20,28},{24,16},{28,20},{1,9},{5... | collective-permute-start | bytes 2359304 | tf_op jit(solution)/shard_map/ppermute | solution.py:379
  551.7 68.5 %collective-permute-start.44 = (bf16[12,384]{1,0:T(8,128)(2,1)S(1)}, bf16[12,384]{1,0:T(8,128)(2,1)S(1)}, u32[]{:S(2)}, u32[]{:S(2)}) collective-permute-start(bf16[12,384]{1,0:T(8,128)(2,1)S(1)} %get-tuple-element.130), channel_id=1, source_target_pairs={{0,3},{1,0},{2,1},{3,2},{4,7},{5,4},{6,5},{7,6},{8,11},{9,8},{10,9... | collective-permute-start | bytes 27656 | tf_op jit(solution)/shard_map/ppermute | solution.py:384
  624.3 29.9 %collective-permute-start.49 = (bf16[4,4,48,1152]{3,2,1,0:T(8,128)(2,1)}, bf16[4,4,48,1152]{3,2,1,0:T(8,128)(2,1)}, u32[]{:S(2)}, u32[]{:S(2)}) collective-permute-start(bf16[4,4,48,1152]{3,2,1,0:T(8,128)(2,1)} %constant_dynamic-slice_fusion.4), channel_id=1, source_target_pairs={{0,4},{4,0},{8,12},{12,8},{16,20},{20,16},{24,28},{28,24},{1,5},{5... | collective-permute-start | bytes 5308424 | tf_op jit(solution)/shard_map/ppermute | solution.py:379
  635.3 61.7 %collective-permute-start.48 = (bf16[48,384]{1,0:T(8,128)(2,1)S(1)}, bf16[48,384]{1,0:T(8,128)(2,1)S(1)}, u32[]{:S(2)}, u32[]{:S(2)}) collective-permute-start(bf16[48,384]{1,0:T(8,128)(2,1)S(1)} %reshape.339), channel_id=1, source_target_pairs={{0,4},{4,0},{8,12},{12,8},{16,20},{20,16},{24,28},{28,24},{1,5},{5... | collective-permute-start | bytes 110600 | tf_op jit(solution)/shard_map/ppermute | solution.py:379
  685.4 26.4 %collective-permute-start.81 = (bf16[192,2048]{1,0:T(8,128)(2,1)S(1)}, bf16[192,2048]{1,0:T(8,128)(2,1)S(1)}, u32[]{:S(2)}, u32[]{:S(2)}) collective-permute-start(bf16[192,2048]{1,0:T(8,128)(2,1)S(1)} %bitcast.408), channel_id=1, source_target_pairs={{0,4},{4,0},{8,12},{12,8},{16,20},{20,16},{24,28},{28,24},{1,5},{5... | collective-permute-start | bytes 2359304 | tf_op jit(solution)/shard_map/ppermute | solution.py:379
  (90 other events, 1113.0 us)

commit v2 on v1

--- a/solution.py
+++ b/solution.py
@@ -42,6 +42,20 @@
 
 def params(megabytes, **kw):
     return pltpu.CompilerParams(vmem_limit_bytes=megabytes << 20, **kw)
+
+
+def cost(microseconds):
+    return pl.CostEstimate(
+        flops=int(microseconds * 6e8), bytes_accessed=int(microseconds * 2.5e6), transcendentals=0
+    )
+
+
+def in_hbm(value):
+    return pltpu.with_memory_space_constraint(value, pltpu.HBM)
+
+
+def after(value, *others):
+    return lax.optimization_barrier((value, others))[0]
 
 
 def placement_kernel(capacity, owner_row, owner_col, local_row, requests, target_row, target_col):
@@ -85,6 +99,7 @@
         in_specs=[vmem()] * 3,
         out_specs=(vmem(),) * 3,
         compiler_params=params(32),
+        cost_estimate=cost(2),
         name="placement",
     )(owner, owner.T, local_row)
 
@@ -141,6 +156,7 @@
         out_specs=pl.BlockSpec((slots, 2 * E), lambda i: (0, 0)),
         scratch_shapes=[pltpu.VMEM((2, slots, 128), F32), pltpu.VMEM((2, slots, E), F32)],
         compiler_params=params(32),
+        cost_estimate=cost(17),
         name="read_rows",
     )(codes, bigram_t, trigram_t)
 
@@ -176,6 +192,7 @@
         out_specs=(table, table),
         scratch_shapes=[pltpu.VMEM((2, slots, 128), F32), pltpu.VMEM((2 * E, slots), BF)],
         compiler_params=params(32),
+        cost_estimate=cost(14),
         name="add_rows",
     )(codes, grads)
 
@@ -258,6 +275,7 @@
             pltpu.VMEM((length, ABLK), F32),
         ],
         compiler_params=params(48),
+        cost_estimate=cost(50),
         name="attend",
     )(order, rows)
 
@@ -358,7 +376,7 @@
     lax.fori_loop(0, length // piece, unsort, 0)
 
 
-def attend_grad(order, rows, grads, attended_t, logsum, cos, sin, pairs, piece):
+def attend_grad(order, rows, grads, attended_t, logsum, cos, sin, cos_t, sin_t, pairs, piece):
     length = rows.shape[0]
     low = pltpu.VMEM((length, HD), BF)
     full = pltpu.VMEM((length, HD), F32)
@@ -370,8 +388,214 @@
         out_specs=vmem(),
         scratch_shapes=[low] * 4 + [pltpu.VMEM((HD, length), BF), each, full, full, each, each],
         compiler_params=params(56),
+        cost_estimate=cost(68),
         name="attend_grad",
-    )(order, rows, grads, attended_t, logsum, cos, sin, cos.T, sin.T)
+    )(order, rows, grads, attended_t, logsum, cos, sin, cos_t, sin_t)
+
+
+def fold_max(peak, tile):
+    return jnp.maximum(peak, jnp.max(tile.reshape(-1, 8, tile.shape[1]), axis=0))
+
+
+def fold_sum(total, tile):
+    return total + jnp.sum(tile.reshape(-1, 8, tile.shape[1]), axis=0)
+
+
+def attend_short_kernel(pairs, piece, order, rows, out, attended_t, logsum, q_s, k_s, vt_s, s_s, o_s):
+    length = rows.shape[0]
+    blocks = length // ABLK
+    width = pairs * HD
+    identity = eye(HD)
+
+    def sort(j, _):
+        block = rows[pl.ds(pl.multiple_of(order[j] * piece, piece), piece), :]
+        to = pl.ds(pl.multiple_of(j * piece, piece), piece)
+        for p in range(pairs):
+            q = block[:, p * HD : (p + 1) * HD]
+            q_s[p, to, :] = (q.astype(F32) * HD ** (-0.5)).astype(BF)
+            k_s[p, to, :] = block[:, width + p * HD : width + (p + 1) * HD]
+            v = block[:, 2 * width + p * HD : 2 * width + (p + 1) * HD]
+            vt_s[p, :, to] = mm(identity, v, NT).astype(BF)
+        return 0
+
+    lax.fori_loop(0, length // piece, sort, 0)
+
+    def pair(p, _):
+        for i in range(blocks):
+            at = slice(i * ABLK, (i + 1) * ABLK)
+            queries = q_s[p, at, :]
+            peak = jnp.full((8, ABLK), -jnp.inf, F32)
+            for j in range(i + 1):
+                s = mm(k_s[p, j * ABLK : (j + 1) * ABLK, :], queries, NT)
+                s_s[i % 2, j * ABLK : (j + 1) * ABLK, :] = s
+                peak = fold_max(peak, s)
+            peak = jnp.max(peak, axis=0, keepdims=True)
+            total = jnp.zeros((8, ABLK), F32)
+            o = jnp.zeros((HD, ABLK), F32)
+            for j in range(i + 1):
+                e = jnp.exp(s_s[i % 2, j * ABLK : (j + 1) * ABLK, :] - peak)
+                total = fold_sum(total, e)
+                o += mm(vt_s[p, :, j * ABLK : (j + 1) * ABLK], e.astype(BF))
+            total = jnp.sum(total, axis=0, keepdims=True)
+            o = o * (1.0 / total)
+            attended_t[p, :, at] = o
+            logsum[p, :, at] = peak + jnp.log(total)
+            o_s[p, at, :] = o.T.astype(BF)
+        return 0
+
+    lax.fori_loop(0, pairs, pair, 0)
+
+    def unsort(j, _):
+        take = pl.ds(pl.multiple_of(j * piece, piece), piece)
+        to = pl.ds(pl.multiple_of(order[j] * piece, piece), piece)
+        out[to, :] = jnp.concatenate([o_s[p, take, :] for p in range(pairs)], axis=1)
+        return 0
+
+    lax.fori_loop(0, length // piece, unsort, 0)
+
+
+def attend_short(order, rows, pairs, piece):
+    length = rows.shape[0]
+    return pl.pallas_call(
+        functools.partial(attend_short_kernel, pairs, piece),
+        out_shape=(
+            jax.ShapeDtypeStruct((length, pairs * HD), BF),
+            jax.ShapeDtypeStruct((pairs, HD, length), F32),
+            jax.ShapeDtypeStruct((pairs, 1, length), F32),
+        ),
+        in_specs=[smem(), vmem()],
+        out_specs=(vmem(),) * 3,
+        scratch_shapes=[
+            pltpu.VMEM((pairs, length, HD), BF),
+            pltpu.VMEM((pairs, length, HD), BF),
+            pltpu.VMEM((pairs, HD, length), BF),
+            pltpu.VMEM((2, length, ABLK), F32),
+            pltpu.VMEM((pairs, length, HD), BF),
+        ],
+        compiler_params=params(48),
+        cost_estimate=cost(25),
+        name="attend",
+    )(order, rows)
+
+
+def attend_grad_short_kernel(
+    pairs,
+    begin,
+    count,
+    piece,
+    order,
+    rows,
+    grads,
+    attended_t,
+    logsum,
+    cos,
+    sin,
+    cos_t,
+    sin_t,
+    out,
+    q_s,
+    k_s,
+    v_s,
+    g_s,
+    kt_s,
+    dq_s,
+    dk_s,
+    dv_s,
+    dk_o,
+    dv_o,
+):
+    length = rows.shape[0]
+    blocks = length // ABLK
+    width = pairs * HD
+    half = HD // 2
+    scale = HD ** (-0.5)
+    identity = eye(HD)
+
+    def sort(j, _):
+        take = pl.ds(pl.multiple_of(order[j] * piece, piece), piece)
+        block = rows[take, :]
+        grad = grads[take, :]
+        to = pl.ds(pl.multiple_of(j * piece, piece), piece)
+        for p in range(count):
+            lane = (begin + p) * HD
+            q_s[p, to, :] = (block[:, lane : lane + HD].astype(F32) * scale).astype(BF)
+            k = block[:, width + lane : width + lane + HD]
+            k_s[p, to, :] = k
+            kt_s[p, :, to] = mm(identity, k, NT).astype(BF)
+            v_s[p, to, :] = block[:, 2 * width + lane : 2 * width + lane + HD]
+            g_s[p, to, :] = grad[:, lane : lane + HD]
+        return 0
+
+    lax.fori_loop(0, length // piece, sort, 0)
+
+    def pair(p, _):
+        for i in range(blocks):
+            at = slice(i * ABLK, (i + 1) * ABLK)
+            queries = q_s[p, at, :]
+            grad = g_s[p, at, :]
+            delta = jnp.sum(mm(identity, grad, NT) * attended_t[begin + p, :, at], axis=0, keepdims=True)
+            level = logsum[begin + p, :, at]
+            dq = jnp.zeros((HD, ABLK), F32)
+            for j in range(i, -1, -1):
+                to = slice(j * ABLK, (j + 1) * ABLK)
+                probs = jnp.exp(mm(k_s[p, to, :], queries, NT) - level)
+                ds = (probs * (mm(v_s[p, to, :], grad, NT) - delta)).astype(BF)
+                dv = mm(probs.astype(BF), grad)
+                dk = mm(ds, queries)
+                if i == j:
+                    dv_s[to, :] = dv
+                    dk_s[to, :] = dk
+                else:
+                    dv_s[to, :] += dv
+                    dk_s[to, :] += dk
+                dq += mm(kt_s[p, :, to], ds)
+            dq = dq * scale
+            c, s = cos_t[:, at], sin_t[:, at]
+            a, b = dq[:half, :], dq[half:, :]
+            dq = jnp.concatenate([a * c + b * s, b * c - a * s], axis=0)
+            dq_s[p, at, :] = dq.T.astype(BF)
+
+        def turn(j, _):
+            to = pl.ds(pl.multiple_of(j * ABLK, ABLK), ABLK)
+            dk = dk_s[to, :]
+            a, b = dk[:, :half], dk[:, half:]
+            c, s = cos[to, :], sin[to, :]
+            dk_o[p, to, :] = jnp.concatenate([a * c + b * s, b * c - a * s], axis=1).astype(BF)
+            dv_o[p, to, :] = dv_s[to, :].astype(BF)
+            return 0
+
+        lax.fori_loop(0, blocks, turn, 0)
+        return 0
+
+    lax.fori_loop(0, count, pair, 0)
+
+    def unsort(j, _):
+        take = pl.ds(pl.multiple_of(j * piece, piece), piece)
+        to = pl.ds(pl.multiple_of(order[j] * piece, piece), piece)
+        parts = [ref[p, take, :] for ref in (dq_s, dk_o, dv_o) for p in range(count)]
+        out[to, :] = jnp.concatenate(parts, axis=1)
+        return 0
+
+    lax.fori_loop(0, length // piece, unsort, 0)
+
+
+def attend_grad_short(
+    order, rows, grads, attended_t, logsum, cos, sin, cos_t, sin_t, pairs, piece, begin, count
+):
+    length = rows.shape[0]
+    full = pltpu.VMEM((length, HD), F32)
+    each = pltpu.VMEM((count, length, HD), BF)
+    return pl.pallas_call(
+        functools.partial(attend_grad_short_kernel, pairs, begin, count, piece),
+        out_shape=jax.ShapeDtypeStruct((length, 3 * count * HD), BF),
+        in_specs=[smem()] + [vmem()] * 8,
+        out_specs=vmem(),
+        scratch_shapes=[each] * 4
+        + [pltpu.VMEM((count, HD, length), BF), each, full, full, each, each],
+        compiler_params=params(48),
+        cost_estimate=cost(14 * count),
+        name=f"attend_grad_{begin}",
+    )(order, rows, grads, attended_t, logsum, cos, sin, cos_t, sin_t)
 
 
 def over_ctx(value, mask):
@@ -483,6 +707,611 @@
 
 def exchange(values, axes):
     return lax.all_to_all(values, axes, split_axis=0, concat_axis=0, tiled=True)
+
+
+def aligned(value, by=16):
+    return pl.multiple_of(value, by)
+
+
+def pack_weights_kernel(where, joined, output, lookup, gains, expand, contract, first, second):
+    core, chip = where[0], where[1]
+    rows = pl.ds(aligned(chip * 48), 48)
+    for t in range(3):
+        first[t * 48 : (t + 1) * 48, :] = joined[rows, pl.ds(aligned(t * D + core * 384, 128), 384)]
+    columns = pl.ds(aligned(core * 384, 128), 384)
+    first[144:192, :] = lookup[:, columns]
+    first[192:208, :] = gains[...]
+    for j in range(16):
+        second[j * 48 : (j + 1) * 48, :] = expand[
+            rows, pl.ds(aligned(core * FF + j * 128, 128), 128)
+        ]
+    for j in range(3):
+        second[768 + j * 128 : 896 + j * 128, :] = contract[
+            pl.ds(aligned(chip * 128), 128), pl.ds(aligned(core * 384 + j * 128, 128), 128)
+        ]
+        second[1152 + j * 48 : 1200 + j * 48, :] = output[
+            rows, pl.ds(aligned(core * 384 + j * 128, 128), 128)
+        ]
+
+
+def pack_weights(where, *weights):
+    return pl.pallas_call(
+        pack_weights_kernel,
+        out_shape=(
+            jax.ShapeDtypeStruct((208, 384), BF),
+            jax.ShapeDtypeStruct((1296, 128), BF),
+        ),
+        in_specs=[smem()] + [vmem()] * 6,
+        out_specs=(vmem(),) * 2,
+        compiler_params=params(16),
+        cost_estimate=cost(2),
+        name="pack_weights",
+    )(where, *weights)
+
+
+def assemble_first_kernel(where, own, other, own_tail, other_tail, joined, lookup, gains):
+    core, chip, z = where[0], where[1], where[2]
+    for source, tail, half in ((own, own_tail, core), (other, other_tail, 1 - core)):
+        columns = pl.ds(aligned(half * 384, 128), 384)
+        for m in range(4):
+            zz = lax.rem(z + m, 4)
+            for k in range(4):
+                rows = pl.ds(aligned(zz * 192 + (chip ^ k) * 48), 48)
+                for t in range(3):
+                    joined[rows, pl.ds(aligned(t * D + half * 384, 128), 384)] = source[
+                        k, m, t * 48 : (t + 1) * 48, :
+                    ]
+            lookup[pl.ds(aligned(zz * 48), 48), columns] = tail[m, 0:48, :]
+    for m in range(4):
+        gains[lax.rem(z + m, 4)] = own_tail[m, 48:64, :]
+
+
+def assemble_first(where, *blocks):
+    return pl.pallas_call(
+        assemble_first_kernel,
+        out_shape=(
+            jax.ShapeDtypeStruct((D, 3 * D), BF),
+            jax.ShapeDtypeStruct((E, D), BF),
+            jax.ShapeDtypeStruct((4, 16, 384), BF),
+        ),
+        in_specs=[smem()] + [vmem()] * 4,
+        out_specs=(vmem(),) * 3,
+        compiler_params=params(24),
+        cost_estimate=cost(3),
+        name="assemble_first",
+    )(where, *blocks)
+
+
+def assemble_second_kernel(where, own, other, expand, contract, output):
+    core, chip, z = where[0], where[1], where[2]
+    for source, half in ((own, core), (other, 1 - core)):
+
+        def block(i, _):
+            k, m = i // 4, lax.rem(i, 4)
+            zz, yx = lax.rem(z + m, 4), chip ^ k
+            rows = pl.ds(aligned(zz * 192 + yx * 48), 48)
+            for j in range(16):
+                expand[rows, pl.ds(aligned(half * FF + j * 128, 128), 128)] = source[
+                    k, m, j * 48 : (j + 1) * 48, :
+                ]
+            tall = pl.ds(aligned(zz * 512 + yx * 128), 128)
+            for j in range(3):
+                to = pl.ds(aligned(half * 384 + j * 128, 128), 128)
+                contract[tall, to] = source[k, m, 768 + j * 128 : 896 + j * 128, :]
+                output[rows, to] = source[k, m, 1152 + j * 48 : 1200 + j * 48, :]
+            return 0
+
+        lax.fori_loop(0, 16, block, 0)
+
+
+def assemble_second(where, *blocks):
+    return pl.pallas_call(
+        assemble_second_kernel,
+        out_shape=(
+            jax.ShapeDtypeStruct((D, 2 * FF), BF),
+            jax.ShapeDtypeStruct((FF, D), BF),
+            jax.ShapeDtypeStruct((D, D), BF),
+        ),
+        in_specs=[smem()] + [vmem()] * 2,
+        out_specs=(vmem(),) * 3,
+        compiler_params=params(32),
+        cost_estimate=cost(7),
+        name="assemble_second",
+    )(where, *blocks)
+
+
+def spread_fsdp(piece):
+    along = [piece] + [along_fsdp(piece, k) for k in range(1, 4)]
+    return [along[(4 - m) % 4] for m in range(4)]
+
+
+def add_cores(own, came):
+    return [(own[k].astype(F32) + came[k].astype(F32)).astype(BF) for k in range(4)]
+
+
+def add_blocks(own, came):
+    total = own.astype(F32)
+    for block in came:
+        total = total + block.astype(F32)
+    return total.astype(BF)
+
+
+def to_chips(blocks):
+    return [over_ctx(blocks[k], 2 * k) for k in range(1, 4)]
+
+
+def to_fsdp(total):
+    return [along_fsdp(total[m], m) for m in range(1, 4)]
+
+
+def unpack_second_kernel(where, own, other, expand, contract, output):
+    core, chip = where[0], where[1]
+    for k in range(4):
+        yx = chip ^ k
+        rows = pl.ds(aligned(yx * 48), 48)
+        for half in range(2):
+
+            def taken(begin, count):
+                part = slice(begin, begin + count)
+                return jnp.where(core == half, own[k, part, :].astype(F32), other[k, part, :].astype(F32))
+
+            for j in range(16):
+                expand[rows, half * FF + j * 128 : half * FF + (j + 1) * 128] = taken(j * 48, 48)
+            for j in range(3):
+                to = slice(half * 384 + j * 128, half * 384 + (j + 1) * 128)
+                contract[pl.ds(aligned(yx * 128), 128), to] = taken(768 + j * 128, 128)
+                output[rows, to] = taken(1152 + j * 48, 48)
+
+
+def unpack_second(where, own, other):
+    return pl.pallas_call(
+        unpack_second_kernel,
+        out_shape=(
+            jax.ShapeDtypeStruct((192, 2 * FF), F32),
+            jax.ShapeDtypeStruct((512, D), F32),
+            jax.ShapeDtypeStruct((192, D), F32),
+        ),
+        in_specs=[smem()] + [vmem()] * 2,
+        out_specs=(vmem(),) * 3,
+        compiler_params=params(24),
+        cost_estimate=cost(4),
+        name="unpack_second",
+    )(where, own, other)
+
+
+def unpack_first_kernel(where, own, other, joined, lookup, gains):
+    core, chip = where[0], where[1]
+    for k in range(4):
+        yx = chip ^ k
+        rows = pl.ds(aligned(yx * 48), 48)
+        for half in range(2):
+
+            def taken(begin, count):
+                part = slice(begin, begin + count)
+                return jnp.where(core == half, own[k, part, :].astype(F32), other[k, part, :].astype(F32))
+
+            for t in range(3):
+                for j in range(3):
+                    to = t * D + half * 384 + j * 128
+                    joined[rows, to : to + 128] = taken((t * 3 + j) * 48, 48)
+
+            @pl.when(yx < 3)
+            def _():
+                at = pl.ds(aligned(half * 384 + yx * 128, 128), 128)
+                lookup[:, at] = taken(432, 48)
+
+            @pl.when(yx == 3)
+            def _():
+                gains[half] = taken(432, 48)
+
+
+def unpack_first(where, own, other):
+    return pl.pallas_call(
+        unpack_first_kernel,
+        out_shape=(
+            jax.ShapeDtypeStruct((192, 3 * D), F32),
+            jax.ShapeDtypeStruct((48, D), F32),
+            jax.ShapeDtypeStruct((2, 48, 128), F32),
+        ),
+        in_specs=[smem()] + [vmem()] * 2,
+        out_specs=(vmem(),) * 3,
+        compiler_params=params(24),
+        cost_estimate=cost(2),
+        name="unpack_first",
+    )(where, own, other)
+
+
+def unit_rows(x):
+    inverse = lax.rsqrt(jnp.mean(x * x, axis=-1, keepdims=True) + epsilon)
+    return x * inverse, inverse
+
+
+def front_kernel(
+    pairs, starts, got, target, token, lookup, gain, joined, cos, sin, start, embed, hidden, send
+):
+    tokens = token.shape[0]
+    piece = 128
+    per_batch = tokens // 2 // piece
+    groups = HEADS // pairs
+    wide_ = pairs * HD
+    slots = got.shape[0]
+    lane = lax.broadcasted_iota(jnp.int32, (piece, 128), 1)
+    first_half = lax.rem(lane, HD) < HD // 2
+
+    def block(i, _):
+        at = pl.ds(aligned(i * piece, piece), piece)
+        goal = target[at, :]
+        slot = lax.broadcasted_iota(jnp.int32, (piece, slots), 1)
+        parts = []
+        for table in range(2):
+            hot = jnp.where(goal[:, table : table + 1] == slot, 1.0, 0.0).astype(BF)
+            parts.append(mm(hot, got[:, table * E : (table + 1) * E]))
+        rows = (parts[0] + parts[1]).astype(BF)
+        embed[at, :] = rows
+        x = token[at, :].astype(F32) + mm(rows, lookup[...])
+        start[at, :] = x
+        normed, _ = unit_rows(x)
+        low = (normed * gain[...]).astype(BF)
+        hidden[at, :] = low
+        projected = mm(low, joined[...])
+        begin = pl.ds(aligned(starts[lax.rem(i, per_batch)] * piece, piece), piece)
+        c = cos[begin, :]
+        s = sin[begin, :]
+        c = jnp.concatenate([c, c, c, c], axis=1)
+        s = jnp.concatenate([-s, s, -s, s], axis=1)
+        turned = []
+        for j in range(12):
+            v = projected[:, j * 128 : (j + 1) * 128]
+            swapped = jnp.where(first_half, pltpu.roll(v, 96, 1), pltpu.roll(v, 32, 1))
+            turned.append((v * c + swapped * s).astype(BF))
+        q = jnp.concatenate(turned[:6], axis=1)
+        k = jnp.concatenate(turned[6:], axis=1)
+        v = projected[:, 2 * D :].astype(BF)
+        batch = i // per_batch
+        to = pl.ds(aligned(lax.rem(i, per_batch) * piece, piece), piece)
+        for g in range(groups):
+            take = slice(g * wide_, (g + 1) * wide_)
+            send[batch * groups + g, to, :] = jnp.concatenate(
+                [q[:, take], k[:, take], v[:, take]], axis=1
+            )
+        return 0
+
+    lax.fori_loop(0, tokens // piece, block, 0)
+
+
+def front(pairs, devices, starts, got, target, token, lookup, gain, joined, cos, sin):
+    tokens = token.shape[0]
+    return pl.pallas_call(
+        functools.partial(front_kernel, pairs),
+        out_shape=(
+            jax.ShapeDtypeStruct((tokens, D), F32),
+            jax.ShapeDtypeStruct((tokens, E), BF),
+            jax.ShapeDtypeStruct((tokens, D), BF),
+            jax.ShapeDtypeStruct((devices, tokens // 2, 3 * pairs * HD), BF),
+        ),
+        in_specs=[smem()] + [vmem()] * 8,
+        out_specs=(vmem(),) * 4,
+        compiler_params=params(40),
+        cost_estimate=cost(9),
+        name="front",
+    )(starts, got, target, token, lookup, gain, joined, cos, sin)
+
+
+def mlp_kernel(
+    pairs,
+    came,
+    start,
+    output,
+    gain,
+    upstream,
+    w_gate,
+    w_up,
+    w_down,
+    result,
+    hidden_out,
+    attended_out,
+    act_out,
+    gate_out,
+    up_out,
+    gain_grad,
+    middle_grad,
+    send,
+    hidden,
+    total,
+    back,
+):
+    step = pl.program_id(0)
+    groups = HEADS // pairs
+    wide_ = pairs * HD
+    half = came.shape[1]
+
+    @pl.when(step == 0)
+    def _():
+        for batch in range(2):
+            at = slice(batch * half, (batch + 1) * half)
+            rows = jnp.concatenate([came[batch * groups + g] for g in range(groups)], axis=1)
+            attended_out[at, :] = rows
+            x = start[at, :] + mm(rows, output[...])
+            total[at, :] = x
+            middle_grad[at, :] = x
+            normed, _ = unit_rows(x)
+            low = (normed * gain[...]).astype(BF)
+            hidden[at, :] = low
+            hidden_out[at, :] = low
+        back[...] = jnp.zeros_like(back)
+
+    for batch in range(2):
+        at = slice(batch * half, (batch + 1) * half)
+        gate = mm(hidden[at, :], w_gate[...])
+        up = mm(hidden[at, :], w_up[...])
+        sigmoid = jax.nn.sigmoid(gate)
+        swish = gate * sigmoid
+        act = (swish * up).astype(BF)
+        act_out[at, :] = act
+        total[at, :] += mm(act, w_down[...])
+        grad = mm(upstream[at, :], w_down[...], NT)
+        gate_grad = (grad * up * sigmoid * (1.0 + gate * (1.0 - sigmoid))).astype(BF)
+        up_grad = (grad * swish).astype(BF)
+        gate_out[at, :] = gate_grad
+        up_out[at, :] = up_grad
+        back[at, :] += mm(gate_grad, w_gate[...], NT) + mm(up_grad, w_up[...], NT)
+
+    @pl.when(step == pl.num_programs(0) - 1)
+    def _():
+        gains = jnp.zeros((1, D), F32)
+        for batch in range(2):
+            at = slice(batch * half, (batch + 1) * half)
+            result[at, :] = total[at, :].astype(BF)
+            normed, inverse = unit_rows(middle_grad[at, :])
+            grad = back[at, :]
+            gains += jnp.sum(grad * normed, axis=0, keepdims=True)
+            weighted = grad * gain[...]
+            grad = upstream[at, :].astype(F32) + inverse * (
+                weighted - normed * jnp.mean(weighted * normed, axis=-1, keepdims=True)
+            )
+            middle_grad[at, :] = grad
+            heads = mm(grad.astype(BF), output[...], NT).astype(BF)
+            for g in range(groups):
+                send[batch * groups + g] = heads[:, g * wide_ : (g + 1) * wide_]
+        gain_grad[...] = gains
+
+
+def mlp(pairs, came, start, output, gain, upstream, expand, contract):
+    tokens = start.shape[0]
+    width = 256
+    steps = FF // width
+    whole = lambda *shape: pl.BlockSpec(shape, lambda i: (0,) * len(shape))
+    column = pl.BlockSpec((tokens, width), lambda i: (0, i))
+    return pl.pallas_call(
+        functools.partial(mlp_kernel, pairs),
+        grid=(steps,),
+        out_shape=(
+            jax.ShapeDtypeStruct((tokens, D), BF),
+            jax.ShapeDtypeStruct((tokens, D), BF),
+            jax.ShapeDtypeStruct((tokens, D), BF),
+            jax.ShapeDtypeStruct((tokens, FF), BF),
+            jax.ShapeDtypeStruct((tokens, FF), BF),
+            jax.ShapeDtypeStruct((tokens, FF), BF),
+            jax.ShapeDtypeStruct((1, D), F32),
+            jax.ShapeDtypeStruct((tokens, D), F32),
+            jax.ShapeDtypeStruct(came.shape, BF),
+        ),
+        in_specs=[
+            whole(*came.shape),
+            whole(tokens, D),
+            whole(D, D),
+            whole(1, D),
+            whole(tokens, D),
+            pl.BlockSpec((D, width), lambda i: (0, i)),
+            pl.BlockSpec((D, width), lambda i: (0, steps + i)),
+            pl.BlockSpec((width, D), lambda i: (i, 0)),
+        ],
+        out_specs=(
+            whole(tokens, D),
+            whole(tokens, D),
+            whole(tokens, D),
+            column,
+            column,
+            column,
+            whole(1, D),
+            whole(tokens, D),
+            whole(*came.shape),
+        ),
+        scratch_shapes=[
+            pltpu.VMEM((tokens, D), BF),
+            pltpu.VMEM((tokens, D), F32),
+            pltpu.VMEM((tokens, D), F32),
+        ],
+        compiler_params=params(48),
+        cost_estimate=cost(23),
+        name="mlp",
+    )(came, start, output, gain, upstream, expand, expand, contract)
+
+
+def weight_grads_kernel(
+    where, hidden, gate, up, act, upstream, attended, middle, own, other, wide_s, tall_s, out_s
+):
+    core, chip, z = where[0], where[1], where[2]
+
+    def chunk(c, _):
+        at = pl.ds(aligned(c * 256, 256), 256)
+        wide_s[0] = mm(hidden[...], gate[:, at], TN).astype(BF)
+        wide_s[1] = mm(hidden[...], up[:, at], TN).astype(BF)
+        tall = mm(act[:, at], upstream[...], TN).astype(BF)
+        tall_s[0] = tall[:, :384]
+        tall_s[1] = tall[:, 384:]
+        for out, half in ((own, core), (other, 1 - core)):
+            for m in range(4):
+                zz = lax.rem(z + m, 4)
+                for k in range(4):
+                    block = wide_s[half, pl.ds(aligned(zz * 192 + (chip ^ k) * 48), 48), :]
+                    for j in range(2):
+                        to = pl.ds(aligned((2 * c + j) * 48), 48)
+                        out[k, m, to, :] = block[:, j * 128 : (j + 1) * 128]
+            m = lax.rem(c // 2 - z + 4, 4)
+            for b in range(2):
+                k = (lax.rem(c, 2) * 2 + b) ^ chip
+                block = tall_s[half, b * 128 : (b + 1) * 128, :]
+                for j in range(3):
+                    out[k, m, 768 + j * 128 : 896 + j * 128, :] = block[:, j * 128 : (j + 1) * 128]
+        return 0
+
+    lax.fori_loop(0, FF // 256, chunk, 0)
+    square = mm(attended[...], middle[...].astype(BF), TN).astype(BF)
+    out_s[0] = square[:, :384]
+    out_s[1] = square[:, 384:]
+    for out, half in ((own, core), (other, 1 - core)):
+        for m in range(4):
+            zz = lax.rem(z + m, 4)
+            for k in range(4):
+                block = out_s[half, pl.ds(aligned(zz * 192 + (chip ^ k) * 48), 48), :]
+                for j in range(3):
+                    out[k, m, 1152 + j * 48 : 1200 + j * 48, :] = block[:, j * 128 : (j + 1) * 128]
+
+
+def weight_grads(where, *operands):
+    shape = jax.ShapeDtypeStruct((4, 4, 1296, 128), BF)
+    return pl.pallas_call(
+        weight_grads_kernel,
+        out_shape=(shape, shape),
+        in_specs=[smem()] + [vmem()] * 7,
+        out_specs=(vmem(),) * 2,
+        scratch_shapes=[
+            pltpu.VMEM((2, D, 256), BF),
+            pltpu.VMEM((2, 256, 384), BF),
+            pltpu.VMEM((2, D, 384), BF),
+        ],
+        compiler_params=params(48),
+        cost_estimate=cost(15),
+        name="weight_grads",
+    )(where, *operands)
+
+
+def back_kernel(
+    where,
+    came_a,
+    came_b,
+    hidden,
+    start,
+    middle,
+    joined,
+    lookup,
+    gain,
+    second_gain,
+    embed,
+    target,
+    token_grad,
+    send,
+    own,
+    other,
+    df_s,
+    half_s,
+    look_s,
+    gain_s,
+):
+    core, chip, z = where[0], where[1], where[2]
+    widths = [(ref, ref.shape[2] // 3) for ref in (came_a, came_b)]
+    groups = D // sum(w for _, w in widths)
+    rows = came_a.shape[1]
+    tokens = 2 * rows
+    for batch in range(2):
+        for t in range(3):
+            parts = [
+                ref[batch * groups + g, :, t * w : (t + 1) * w]
+                for g in range(groups)
+                for ref, w in widths
+            ]
+            df_s[batch * rows : (batch + 1) * rows, t * D : (t + 1) * D] = jnp.concatenate(
+                parts, axis=1
+            )
+
+    def kind(t, _):
+        grad = mm(hidden[...], df_s[:, pl.ds(aligned(t * D, 128), D)], TN).astype(BF)
+        half_s[0] = grad[:, :384]
+        half_s[1] = grad[:, 384:]
+        for out, half in ((own, core), (other, 1 - core)):
+            for m in range(4):
+                zz = lax.rem(z + m, 4)
+                for k in range(4):
+                    block = half_s[half, pl.ds(aligned(zz * 192 + (chip ^ k) * 48), 48), :]
+                    for j in range(3):
+                        to = pl.ds(aligned((t * 3 + j) * 48), 48)
+                        out[k, m, to, :] = block[:, j * 128 : (j + 1) * 128]
+        return 0
+
+    lax.fori_loop(0, 3, kind, 0)
+
+    gains = jnp.zeros((1, D), F32)
+    lows = []
+    for batch in range(2):
+        at = slice(batch * rows, (batch + 1) * rows)
+        grad = mm(df_s[at, :], joined[...], NT)
+        normed, inverse = unit_rows(start[at, :])
+        gains += jnp.sum(grad * normed, axis=0, keepdims=True)
+        weighted = grad * gain[...]
+        grad = middle[at, :] + inverse * (
+            weighted - normed * jnp.mean(weighted * normed, axis=-1, keepdims=True)
+        )
+        token_grad[at, :] = grad
+        lows.append(grad.astype(BF))
+    low = jnp.concatenate(lows, axis=0)
+    look = mm(embed[...], low, TN).astype(BF)
+    for half in range(2):
+        for j in range(3):
+            begin = half * 384 + j * 128
+            look_s[half, j] = look[:, begin : begin + 128]
+    for half, row in enumerate((gains, second_gain[...])):
+        parts = [row[:, j * 128 : (j + 1) * 128] for j in range(6)]
+        gain_s[half] = jnp.concatenate(parts + [jnp.zeros((42, 128), F32)], axis=0).astype(BF)
+    for out, half in ((own, core), (other, 1 - core)):
+        for m in range(4):
+            zz = lax.rem(z + m, 4)
+            for k in range(4):
+                yx = chip ^ k
+
+                @pl.when(yx < 3)
+                def _():
+                    out[k, m, 432:480, :] = look_s[
+                        half, lax.rem(yx, 3), pl.ds(aligned(zz * 48), 48), :
+                    ]
+
+                @pl.when(yx == 3)
+                def _():
+                    out[k, m, 432:480, :] = gain_s[half]
+
+    de = mm(low, lookup[...], NT).astype(BF)
+    slots = send.shape[0]
+    slot = lax.broadcasted_iota(jnp.int32, (slots, tokens), 0)
+    parts = []
+    for table in range(2):
+        hot = jnp.where(slot == target[table : table + 1, :], 1.0, 0.0).astype(BF)
+        parts.append(mm(hot, de))
+    send[...] = jnp.concatenate(parts, axis=1).astype(BF)
+
+
+def back_pass(slots, where, *operands):
+    tokens = operands[2].shape[0]
+    shape = jax.ShapeDtypeStruct((4, 4, 480, 128), BF)
+    return pl.pallas_call(
+        back_kernel,
+        out_shape=(
+            jax.ShapeDtypeStruct((tokens, D), F32),
+            jax.ShapeDtypeStruct((slots, 2 * E), BF),
+            shape,
+            shape,
+        ),
+        in_specs=[smem()] + [vmem()] * 11,
+        out_specs=(vmem(),) * 4,
+        scratch_shapes=[
+            pltpu.VMEM((tokens, 3 * D), BF),
+            pltpu.VMEM((2, D, 384), BF),
+            pltpu.VMEM((2, 3, E, 128), BF),
+            pltpu.VMEM((2, 48, 128), BF),
+        ],
+        compiler_params=params(48),
+        cost_estimate=cost(13),
+        name="back",
+    )(where, *operands)
 
 
 def rotate(values, cosines, sines):
@@ -622,7 +1451,17 @@
     output_grad = reduce_grad(output_term)
 
     grad_rows = attend_grad(
-        order, rows, grad_rows, attended_t, logsum, all_cosines, all_sines, pairs, piece
+        order,
+        rows,
+        grad_rows,
+        attended_t,
+        logsum,
+        all_cosines,
+        all_sines,
+        all_cosines.T,
+        all_sines.T,
+        pairs,
+        piece,
     )
     joined_local = by_token(
         exchange(grad_rows.reshape(contexts, local_rows, 3 * pairs * HD), "ctx"), batches, 3, pairs
@@ -662,9 +1501,192 @@
     )
 
 
+def local_packed(
+    token_embed,
+    bigram_ids,
+    trigram_ids,
+    bigram_table,
+    trigram_table,
+    block_deal,
+    lookup_weight,
+    attention_gain,
+    joined_weight,
+    output_weight,
+    feedforward_gain,
+    expand_weight,
+    contract_weight,
+    cotangent,
+):
+    contexts = lax.axis_size("ctx")
+    shards = lax.axis_size("fsdp")
+    devices = contexts * shards
+    batches, local_rows = token_embed.shape[:2]
+    tokens = batches * local_rows
+    length = local_rows * contexts
+    capacity = max(2, 2 * tokens // devices)
+    table_rows = bigram_table.shape[0]
+    piece = local_rows // 2
+    pieces = length // piece
+    pairs = -(-batches * HEADS // contexts)
+    while HEADS % pairs:
+        pairs += 1
+    both = ("ctx", "fsdp")
+
+
+    core, chip, z = place()
+    where = jnp.stack([core, chip, z]).astype(jnp.int32)
+    ids = jnp.stack([bigram_ids.reshape(-1), trigram_ids.reshape(-1)])
+    requests, target_row, target_col = placement(ids, table_rows, devices, capacity)
+    asked = exchange(requests, both)
+    gain_rows = jnp.pad(jnp.stack([attention_gain, feedforward_gain]), ((0, 14), (0, 192)))
+    first, second = pack_weights(
+        after(where, requests),
+        joined_weight,
+        output_weight,
+        lookup_weight,
+        gain_rows,
+        expand_weight,
+        contract_weight,
+    )
+    along = spread_fsdp(first)
+    column = jnp.stack([p[:144] for p in along])
+    tail = jnp.stack([p[144:] for p in along])
+    blocks = [over_ctx(column, 2 * k) for k in range(1, 4)]
+    codes = jnp.stack([asked[:, :capacity].reshape(-1), asked[:, capacity:].reshape(-1)], axis=1)
+    answer = read_rows(
+        after(codes, column, tail), in_hbm(bigram_table.T), in_hbm(trigram_table.T)
+    )
+    got = exchange(answer.reshape(devices, capacity, 2 * E), both)
+    own = jnp.stack([after(block, answer) for block in [column] + blocks])
+    joined, lookup, gains = assemble_first(
+        where, own, over_ctx(own, 1), tail, over_ctx(tail, 1)
+    )
+    second_column = jnp.stack(spread_fsdp(after(second, own)))
+    gains = gains[:, :2, :192].astype(F32).transpose(1, 0, 2).reshape(2, D)
+    first_gain, second_gain = gains[0:1], gains[1:2]
+    got = got.reshape(devices * capacity, 2 * E)
+
+    order = jnp.sum(
+        jnp.where(
+            block_deal[None, :] == jnp.arange(pieces, dtype=jnp.int32)[:, None],
+            jnp.arange(pieces, dtype=jnp.int32)[None, :],
+            0,
+        ),
+        axis=1,
+    )
+    starts = lax.dynamic_slice_in_dim(block_deal, lax.axis_index("ctx") * 2, 2)
+    frequency = jnp.exp(-math.log(10000.0) * (2.0 * jnp.arange(HD // 2, dtype=F32) / HD))
+    angles = frequency[:, None] * jnp.arange(length, dtype=F32)[None, :]
+    cos_t, sin_t = lax.optimization_barrier((jnp.cos(angles), jnp.sin(angles)))
+    cos, sin = cos_t.T, sin_t.T
+
+    start, embedded, hidden_first, sent = front(
+        pairs,
+        contexts,
+        starts,
+        got,
+        target_col,
+        token_embed.reshape(tokens, D),
+        lookup,
+        first_gain,
+        joined,
+        cos,
+        sin,
+    )
+    rows = exchange(sent, "ctx").reshape(length, 3 * pairs * HD)
+    second_column = after(second_column, rows)
+    blocks = [over_ctx(second_column, 2 * k) for k in range(1, 4)]
+    attended_rows, attended_t, logsum = attend_short(order, rows, pairs, piece)
+    came = exchange(attended_rows.reshape(contexts, local_rows, pairs * HD), "ctx")
+    own = jnp.stack([after(block, attended_rows) for block in [second_column] + blocks])
+    expand, contract, output = assemble_second(where, own, over_ctx(own, 1))
+    upstream = cotangent.reshape(tokens, D)
+    (
+        result,
+        hidden_second,
+        attended,
+        activated,
+        gate_grad,
+        up_grad,
+        second_gain_term,
+        middle_grad,
+        sent,
+    ) = mlp(pairs, came, start, output, second_gain, upstream, expand, contract)
+
+    grad_rows = exchange(sent, "ctx").reshape(length, pairs * HD)
+    own_m, other_m = weight_grads(
+        where, hidden_second, gate_grad, up_grad, activated, upstream, attended, middle_grad
+    )
+    from_core = over_ctx(after(other_m, grad_rows), 1)
+    part = functools.partial(attend_grad_short, order)
+    shared = (attended_t, logsum, cos, sin, cos_t, sin_t, pairs, piece)
+    grad_a = part(rows, grad_rows, *shared, 0, 1)
+    came_a = exchange(grad_a.reshape(contexts, local_rows, 3 * HD), "ctx")
+    half_m = add_cores(own_m, after(from_core, grad_a))
+    from_chips = [over_ctx(half_m[k], 2 * k) for k in (1, 2)]
+    grad_b = part(after(rows, half_m), grad_rows, *shared, 1, pairs - 1)
+    grad_b = after(grad_b, from_chips)
+    from_chips.append(over_ctx(after(half_m[3], grad_b), 6))
+    came_b = exchange(grad_b.reshape(contexts, local_rows, 3 * (pairs - 1) * HD), "ctx")
+    start_grad, send, own_j, other_j = back_pass(
+        devices * capacity,
+        where,
+        came_a,
+        came_b,
+        hidden_first,
+        start,
+        middle_grad,
+        joined,
+        lookup,
+        first_gain,
+        second_gain_term,
+        embedded,
+        target_row,
+    )
+    from_core = over_ctx(other_j, 1)
+    arrived = exchange(send.reshape(devices, capacity, 2 * E), both)
+    total_m = add_blocks(half_m[0], [after(block, own_j) for block in from_chips])
+    from_fsdp_m = to_fsdp(total_m)
+    half_j = add_cores(own_j, after(from_core, total_m))
+    total_j = add_blocks(half_j[0], to_chips(half_j))
+    from_fsdp_j = to_fsdp(total_j)
+    piece_m = add_blocks(total_m[0], [after(block, total_j) for block in from_fsdp_m])
+    every_m = to_chips([piece_m] * 4)
+    bigram_grad, trigram_grad = add_rows(
+        after(codes, total_j, piece_m), arrived.reshape(devices * capacity, 2 * E), table_rows
+    )
+    piece_j = add_blocks(total_j[0], [after(block, bigram_grad) for block in from_fsdp_j])
+    every_j = to_chips([piece_j] * 4)
+    blocks_m = jnp.stack([piece_m] + [after(block, piece_j) for block in every_m])
+    other_m = over_ctx(blocks_m, 1)
+    blocks_j = jnp.stack([piece_j] + [after(block, blocks_m) for block in every_j])
+    other_j = over_ctx(blocks_j, 1)
+    expand_grad, contract_grad, output_grad = unpack_second(
+        where, blocks_m, after(other_m, blocks_j)
+    )
+    joined_grad, lookup_grad, gain_grads = unpack_first(where, blocks_j, other_j)
+    gain_share = lax.dynamic_slice_in_dim(
+        gain_grads[:, :6].reshape(2, D), z * (D // shards), D // shards, axis=1
+    )
+    return (
+        result.reshape(batches, local_rows, D),
+        start_grad.reshape(batches, local_rows, D),
+        bigram_grad.T,
+        trigram_grad.T,
+        lookup_grad,
+        gain_share[0],
+        joined_grad,
+        output_grad,
+        gain_share[1],
+        expand_grad,
+        contract_grad,
+    )
+
+
 def solution(mesh):
+    fits = mesh.shape["ctx"] == 8 and mesh.shape["fsdp"] == 4
     return jax.shard_map(
-        local,
+        local_packed if fits else local,
         mesh=mesh,
         in_specs=(
             P("fsdp", "ctx", None),

time: 724 us -> 508 us (0.70)
  matrix products: 73.4 us -> 0 us
  blocking collectives: 64.4 us -> 0 us
  starting transfers between devices: 145 us -> 83.1 us
  waiting for transfers between devices: 123 us -> 166 us
  local copies, waits for them, and re-layouts: 94.8 us -> 55.2 us
  other arithmetic: 56.8 us -> 21 us
  Pallas kernels: 156 us -> 173 us
    dot_general x19 -> x0, matrix products: 73.4 us -> none  [mm(): return lax.dot_general(a, b, dims, preferred_element_type=F32)]
    psum x1 -> x0, blocking collectives: 64.4 us -> none  [local(): gain_terms = lax.psum(jnp.stack([first_gain_term, second_gain_term]), both)]
    all_to_all x7 -> x8, waiting for transfers between devices: 7.83 us -> 52 us  [exchange(): return lax.all_to_all(values, axes, split_axis=0, concat_axis=0, tiled=True)]
    ppermute x60 -> x25, starting transfers between devices: 59.3 us -> 25.2 us  [over_ctx(): return lax.ppermute(value, 'ctx', [(i, i ^ mask) for i in range(size)])]
    ppermute x33 -> x12, starting transfers between devices: 58 us -> 29.4 us  [along_fsdp(): lax.ppermute(value, 'fsdp', [(i, (i + shift) % size) for i in range(size)])]
    pallas_call x2 -> x12, Pallas kernels: 123 us -> 140 us  [the longest x2 46.9 us: attend_grad_short(): pl.pallas_call(functools.partial(attend_grad_short_kernel, pairs, begin,...]
    convert_element_type x22 -> x6, other arithmetic: 26.6 us -> 12.1 us  [the longest x2 7.57 us: add_cores(): (own[k].astype(F32) + came[k].astype(F32)).astype(BF)]
    reshape x6 -> x2, local copies, waits for them, and re-layouts: 14.3 us -> 4.44 us  [the longest x1 2.22 us: local_packed(): came_a = exchange(grad_a.reshape(contexts, local_rows, 3 * HD), 'ctx')]
  transfers between devices with their start and end apart: 100 -> 45, of which waited for: 24 -> 16; matrix products, arithmetic and copies ran while one was open for 27% -> 5% of each run, Pallas kernels for 22% -> 26%
where the time goes in v2:
time: 508 us; the launch traced here: 500 us
  Pallas kernels  173 us (34%)
  waiting for transfers between devices  166 us (33%)
  starting transfers between devices  83.1 us (16%)
  local copies, waits for them, and re-layouts  55.2 us (11%)
  other arithmetic  21 us (4%)
    ppermute x25, waiting for transfers between devices, over_ctx(): return lax.ppermute(value, 'ctx', [(i, i ^ mask) for i in range(size)])  77.1 us
    all_to_all x8, waiting for transfers between devices, exchange(): return lax.all_to_all(values, axes, split_axis=0, concat_axis=0, tiled=True)  52 us
    pallas_call x2, Pallas kernels, attend_grad_short(): pl.pallas_call(functools.partial(attend_grad_short_kernel, pairs, begin,...  46.9 us
    ppermute x12, waiting for transfers between devices, along_fsdp(): lax.ppermute(value, 'fsdp', [(i, (i + shift) % size) for i in range(size)])  36.7 us
    unnamed x104, local copies, waits for them, and re-layouts  34.4 us
    ppermute x12, starting transfers between devices, along_fsdp(): lax.ppermute(value, 'fsdp', [(i, (i + shift) % size) for i in range(size)])  29.4 us
    all_to_all x8, starting transfers between devices, exchange(): return lax.all_to_all(values, axes, split_axis=0, concat_axis=0, tiled=True)  28.6 us
    ppermute x25, starting transfers between devices, over_ctx(): return lax.ppermute(value, 'ctx', [(i, i ^ mask) for i in range(size)])  25.2 us
  transfers between devices with their start and end apart: 45, of which 16 were waited for; matrix products, arithmetic and copies ran while one was open for 5% of the time, Pallas kernels for 26%

profile of v2, /device:TPU:0, one launch (start us, length us, event | category | flops | bytes accessed | tf_op | source)
XLA Modules:
  0.0 500.1 jit_solution(4262963178413771329)
XLA Ops:
  4.9 3.1 collective-permute-start.2
  7.9 2.6 collective-permute-start.1
  11.9 2.9 all-to-all-start
  14.8 11.7 %all-to-all-done = s32[32,1,64]{2,1,0:T(1,128)S(1)} async-done(((s32[32,1,64]{2,1,0:T(1,128)}), s32[32,1,64]{2,1,0:T(1,128)S(1)}, u32[]{:S(2)}, u32[]{:S(2)}) %all-to-all-start) | async-done | bytes 8224 | tf_op jit(solution)/shard_map/all_to_all | solution.py:709
  28.2 2.3 collective-permute-start.5
  31.5 18.2 %read_rows.1 = bf16[1024,384]{1,0:T(8,128)(2,1)} custom-call(s32[1024,2]{1,0:T(8,128)S(1)} %copy.61.codes, bf16[192,12800]{1,0:T(8,128)(2,1)} %bitcast.161, bf16[192,12800]{1,0:T(8,128)(2,1)} %bitcast.162), custom_call_target="tpu_custom_call" | custom-call | flops 10200000512 | bytes 42500000 | tf_op jit(solution)/shard_map/read_rows/pallas_call | solution.py:151
  52.3 2.6 all-to-all-start.1
  63.7 10.9 %all-to-all-done.1 = bf16[32,32,384]{2,1,0:T(8,128)(2,1)S(1)} async-done(((bf16[32,32,384]{2,1,0:T(8,128)(2,1)}), bf16[32,32,384]{2,1,0:T(8,128)(2,1)S(1)}, u32[]{:S(2)}, u32[]{:S(2)}) %all-to-all-start.1) | async-done | bytes 786464 | tf_op jit(solution)/shard_map/all_to_all | solution.py:709
  84.1 7.5 %front.1 = (f32[512,768]{1,0:T(8,128)S(1)}, bf16[512,192]{1,0:T(8,128)(2,1)S(1)}, bf16[512,768]{1,0:T(8,128)(2,1)S(1)}, bf16[8,256,576]{2,1,0:T(8,128)(2,1)S(1)}) custom-call(s32[2]{0:T(128)S(1)} %dynamic_slice.6.starts, bf16[1024,384]{1,0:T(8,128)(2,1)S(1)} %bitcast.129, s32[512,2]{1,0:T(8,128)S(1)} %copy-done.26, bf16[512,768]{1,0:T(8,128)(2,1)S(1)} %bitcast.132, ...), custom_call_target="tpu_custom_call" | custom-call | flops 5400000000 | bytes 22500000 | tf_op jit(solution)/shard_map/front/pallas_call | solution.py:984
  94.4 2.5 copy.64
  96.9 4.4 all-to-all-start.2
  101.3 3.1 collective-permute-start.8
  106.3 6.3 %collective-permute-done.8 = bf16[1296,128]{1,0:T(8,128)(2,1)S(1)} collective-permute-done((bf16[1296,128]{1,0:T(8,128)(2,1)S(1)}, bf16[1296,128]{1,0:T(8,128)(2,1)S(1)}, u32[]{:S(2)}, u32[]{:S(2)}) %collective-permute-start.8) | collective-permute-done | bytes 331808 | tf_op jit(solution)/shard_map/ppermute | solution.py:608
  112.6 22.5 %collective-permute-done.9 = bf16[1296,128]{1,0:T(8,128)(2,1)S(1)} collective-permute-done((bf16[1296,128]{1,0:T(8,128)(2,1)S(1)}, bf16[1296,128]{1,0:T(8,128)(2,1)S(1)}, u32[]{:S(2)}, u32[]{:S(2)}) %collective-permute-start.9) | collective-permute-done | bytes 331808 | tf_op jit(solution)/shard_map/ppermute | solution.py:608
  136.3 3.1 copy.65
  143.0 20.1 %attend.1 = (bf16[2048,192]{1,0:T(8,128)(2,1)S(1)}, f32[3,64,2048]{2,1,0:T(8,128)S(1)}, f32[3,1,2048]{2,1,0:T(1,128)S(1)}) custom-call(s32[16]{0:T(128)S(1)} %select_reduce_fusion.order, bf16[2048,576]{1,0:T(8,128)(2,1)S(1)} %bitcast.119), custom_call_target="tpu_custom_call" | custom-call | flops 15000000512 | bytes 62500000 | tf_op jit(solution)/shard_map/attend/pallas_call | solution.py:459
  163.2 8.6 %collective-permute-done.11 = bf16[4,1296,128]{2,1,0:T(8,128)(2,1)S(1)} collective-permute-done((bf16[4,1296,128]{2,1,0:T(8,128)(2,1)}, bf16[4,1296,128]{2,1,0:T(8,128)(2,1)S(1)}, u32[]{:S(2)}, u32[]{:S(2)}) %collective-permute-start.11) | collective-permute-done | bytes 1327136 | tf_op jit(solution)/shard_map/ppermute | solution.py:603
  171.8 28.1 %collective-permute-done.12 = bf16[4,1296,128]{2,1,0:T(8,128)(2,1)S(1)} collective-permute-done((bf16[4,1296,128]{2,1,0:T(8,128)(2,1)}, bf16[4,1296,128]{2,1,0:T(8,128)(2,1)S(1)}, u32[]{:S(2)}, u32[]{:S(2)}) %collective-permute-start.12) | collective-permute-done | bytes 1327136 | tf_op jit(solution)/shard_map/ppermute | solution.py:603
  199.9 2.9 pad_maximum_fusion.own
  205.0 3.5 all-to-all-start.3
  208.6 12.4 %all-to-all-done.3 = bf16[8,256,192]{1,2,0:T(8,128)(2,1)S(1)} async-done(((bf16[8,256,192]{1,2,0:T(8,128)(2,1)}), bf16[8,256,192]{1,2,0:T(8,128)(2,1)S(1)}, u32[]{:S(2)}, u32[]{:S(2)}) %all-to-all-start.3) | async-done | bytes 786464 | tf_op jit(solution)/shard_map/all_to_all | solution.py:709
  221.6 6.6 %assemble_second.1 = (bf16[768,4096]{1,0:T(8,128)(2,1)S(1)}, bf16[2048,768]{1,0:T(8,128)(2,1)S(1)}, bf16[768,768]{1,0:T(8,128)(2,1)S(1)}) custom-call(s32[3]{0:T(128)S(1)} %pad_add_fusion.2.where, bf16[4,4,1296,128]{3,2,1,0:T(8,128)(2,1)} %pad_maximum_fusion.own, bf16[4,4,1296,128]{3,2,1,0:T(8,128)(2,1)} %collective-permute-done.14.other), custom_call_target="tpu_custom_call" | custom-call | flops 4200000000 | bytes 17500000 | tf_op jit(solution)/shard_map/assemble_second/pallas_call | solution.py:808
  228.2 2.7 copy-done.20
  232.5 22.6 %mlp.1 = (bf16[512,768]{1,0:T(8,128)(2,1)}, bf16[512,768]{1,0:T(8,128)(2,1)S(1)}, bf16[512,768]{1,0:T(8,128)(2,1)S(1)}, bf16[512,2048]{1,0:T(8,128)(2,1)}, bf16[...) custom-call(bf16[8,256,192]{2,1,0:T(8,128)(2,1)S(1)} %copy.67.came, ...), custom_call_target="tpu_custom_call" | custom-call | flops 13799999488 | bytes 57500000 | tf_op jit(solution)/shard_map/mlp/pallas_call | solution.py:1085
  258.2 4.4 all-to-all-start.4
  267.8 14.6 %weight_grads.1 = (bf16[4,4,1296,128]{3,2,1,0:T(8,128)(2,1)}, bf16[4,4,1296,128]{3,2,1,0:T(8,128)(2,1)}) custom-call(s32[3]{0:T(128)S(1)} %pad_add_fusion.2.where, bf16[512,768]{1,0:T(8,128)(2,1)S(1)} %copy-done.36, bf16[512,2048]{1,0:T(8,128)(2,1)S(1)} %copy-done.31, bf16[512,2048]{1,0:T(8,128)(2,1)} %get-tuple-element.122.up, ...), custom_call_target="tpu_custom_call" | custom-call | flops 8999999488 | bytes 37500000 | tf_op jit(solution)/shard_map/weight_grads/pallas_call | solution.py:1174
  286.5 17.5 %attend_grad_0.1 = bf16[2048,192]{1,0:T(8,128)(2,1)S(1)} custom-call(s32[16]{0:T(128)S(1)} %select_reduce_fusion.order, bf16[2048,576]{1,0:T(8,128)(2,1)} %bitcast.120, bf16[2048,192]{1,0:T(8,128)(2,1)S(1)} %bitcast.124, f32[3,64,2048]{2,1,0:T(8,128)} %copy-done.32, f32[3,1,2048]{2,1,0:T(1,128)S(1)} %get-tuple-element.119.logsum, f32[2048,32]{1,0:T(8,128)S(1)} %copy-done.2, ...), custom_call_target="tpu_custom_call" | custom-call | flops 8400000000 | bytes 35000000 | tf_op jit(solution)/shard_map/attend_grad_0/pallas_call | solution.py:588
  307.2 4.1 all-to-all-start.5
  311.3 5.9 %fusion.3 = (bf16[4,1296,128]{2,1,0:T(8,128)(2,1)}, bf16[4,1296,128]{2,1,0:T(8,128)(2,1)S(1)}, bf16[4,1296,128]{2,1,0:T(8,128)(2,1)S(1)}, bf16[4,1296,128]{2,1,0:T(8,128)(2,1)}) fusion(bf16[4,4,1296,128]{3,2,1,0:T(8,128)(2,1)} %collective-permute-done.15, bf16[4,4,1296,128]{3,2,1,0:T(8,128)(2,1)} %get-tuple-element.126), kind=kLoop, calls=%fused_computation.10 | loop fusion | flops 10616832 | bytes 15925248 | tf_op jit(solution)/shard_map/convert_element_type | solution.py:829
  320.6 29.4 %attend_grad_1.1 = bf16[2048,384]{1,0:T(8,128)(2,1)} custom-call(s32[16]{0:T(128)S(1)} %select_reduce_fusion.order, bf16[2048,576]{1,0:T(8,128)(2,1)} %bitcast.121, bf16[2048,192]{1,0:T(8,128)(2,1)S(1)} %bitcast.125, f32[3,64,2048]{2,1,0:T(8,128)} %copy-done.32, f32[3,1,2048]{2,1,0:T(1,128)S(1)} %get-tuple-element.119.logsum, f32[2048,32]{1,0:T(8,128)S(1)} %copy-done.2, ...), custom_call_target="tpu_custom_call" | custom-call | flops 16800000000 | bytes 70000000 | tf_op jit(solution)/shard_map/attend_grad_1/pallas_call | solution.py:588
  353.4 4.0 all-to-all-start.6
  358.8 3.0 collective-permute-start.19
  361.8 17.0 %all-to-all-done.6.came_b = bf16[8,256,384]{2,1,0:T(8,128)(2,1)S(1)} async-done(((bf16[8,256,384]{2,1,0:T(8,128)(2,1)}), bf16[8,256,384]{2,1,0:T(8,128)(2,1)S(1)}, u32[]{:S(2)}, u32[]{:S(2)}) %all-to-all-start.6) | async-done | bytes 1572896 | tf_op jit(solution)/shard_map/all_to_all | solution.py:709
  379.9 12.8 %back.1 = (f32[512,768]{1,0:T(8,128)}, bf16[1024,384]{1,0:T(8,128)(2,1)}, bf16[4,4,480,128]{3,2,1,0:T(8,128)(2,1)}, bf16[4,4,480,128]{3,2,1,0:T(8,128)(2,1)}) custom-call(s32[3]{0:T(128)S(1)} %pad_add_fusion.2.where, bf16[8,256,192]{2,1,0:T(8,128)(2,1)S(1)} %copy.75.came_a, bf16[8,256,384]{2,1,0:T(8,128)(2,1)S(1)} %all-to-all-done.6.came_b, ...), custom_call_target="tpu_custom_call" | custom-call | flops 7800000000 | bytes 32500000 | tf_op jit(solution)/shard_map/back/pallas_call | solution.py:1295
  392.8 14.1 %collective-permute-done.19 = bf16[4,1296,128]{2,1,0:T(8,128)(2,1)} collective-permute-done((bf16[4,1296,128]{2,1,0:T(8,128)(2,1)}, bf16[4,1296,128]{2,1,0:T(8,128)(2,1)}, u32[]{:S(2)}, u32[]{:S(2)}) %collective-permute-start.19) | collective-permute-done | bytes 1327136 | tf_op jit(solution)/shard_map/ppermute | solution.py:603
  406.9 2.6 all-to-all-start.7
  409.5 3.0 add_convert_fusion
  419.6 2.5 collective-permute-start.24
  422.1 9.4 %collective-permute-done.20 = bf16[4,480,128]{2,1,0:T(8,128)(2,1)S(1)} collective-permute-done((bf16[4,480,128]{2,1,0:T(8,128)(2,1)S(1)}, bf16[4,480,128]{2,1,0:T(8,128)(2,1)S(1)}, u32[]{:S(2)}, u32[]{:S(2)}) %collective-permute-start.20) | collective-permute-done | bytes 491552 | tf_op jit(solution)/shard_map/ppermute | solution.py:603
  431.5 3.6 collective-permute-start.25
  435.1 7.5 %collective-permute-done.22 = bf16[4,480,128]{2,1,0:T(8,128)(2,1)S(1)} collective-permute-done((bf16[4,480,128]{2,1,0:T(8,128)(2,1)S(1)}, bf16[4,480,128]{2,1,0:T(8,128)(2,1)S(1)}, u32[]{:S(2)}, u32[]{:S(2)}) %collective-permute-start.22) | collective-permute-done | bytes 491552 | tf_op jit(solution)/shard_map/ppermute | solution.py:603
  444.0 7.9 %collective-permute-done.24 = bf16[1296,128]{1,0:T(8,128)(2,1)S(1)} collective-permute-done((bf16[1296,128]{1,0:T(8,128)(2,1)S(1)}, bf16[1296,128]{1,0:T(8,128)(2,1)S(1)}, u32[]{:S(2)}, u32[]{:S(2)}) %collective-permute-start.24) | collective-permute-done | bytes 331808 | tf_op jit(solution)/shard_map/ppermute | solution.py:608
  452.6 7.2 %collective-permute-start.26 = (bf16[480,128]{1,0:T(8,128)(2,1)}, bf16[480,128]{1,0:T(8,128)(2,1)S(1)}, u32[]{:S(2)}, u32[]{:S(2)}) collective-permute-start(bf16[480,128]{1,0:T(8,128)(2,1)} %get-tuple-element.181), channel_id=1, source_target_pairs={{0,1},{1,2},{2,3},{3,0},{4,5},{5,6},{6,7},{7,4},{8,9},{9,10},{10,1... | collective-permute-start | bytes 368648 | tf_op jit(solution)/shard_map/ppermute | solution.py:608
  466.2 13.8 %add_rows.1 = (f32[192,12800]{1,0:T(8,128)}, f32[192,12800]{1,0:T(8,128)}) custom-call(s32[1024,2]{1,0:T(8,128)S(1)} %copy.76.codes, bf16[1024,384]{1,0:T(8,128)(2,1)S(1)} %bitcast.128), custom_call_target="tpu_custom_call" | custom-call | flops 8400000000 | bytes 35000000 | tf_op jit(solution)/shard_map/add_rows/pallas_call | solution.py:184
  485.0 2.4 collective-permute-done.29
  487.3 3.6 collective-permute-done.33
  493.1 2.5 unpack_first.1
  496.3 3.4 unpack_second.1
  (215 shorter events, 90.8 us)
Async XLA Ops:
  4.9 21.9 %collective-permute-start.2 = (bf16[208,384]{1,0:T(8,128)(2,1)S(1)}, bf16[208,384]{1,0:T(8,128)(2,1)S(1)}, u32[]{:S(2)}, u32[]{:S(2)}) collective-permute-start(bf16[208,384]{1,0:T(8,128)(2,1)S(1)} %get-tuple-element.91), channel_id=1, source_target_pairs={{0,1},{1,2},{2,3},{3,0},{4,5},{5,6},{6,7},{7,4},{8,9},{9,10},{10,1... | collective-permute-start | bytes 479240 | tf_op jit(solution)/shard_map/ppermute | solution.py:608
  7.9 18.9 %collective-permute-start.1 = (bf16[208,384]{1,0:T(8,128)(2,1)S(1)}, bf16[208,384]{1,0:T(8,128)(2,1)S(1)}, u32[]{:S(2)}, u32[]{:S(2)}) collective-permute-start(bf16[208,384]{1,0:T(8,128)(2,1)S(1)} %get-tuple-element.91), channel_id=1, source_target_pairs={{0,2},{1,3},{2,0},{3,1},{4,6},{5,7},{6,4},{7,5},{8,10},{9,11},{10,... | collective-permute-start | bytes 479240 | tf_op jit(solution)/shard_map/ppermute | solution.py:608
  10.5 16.2 %collective-permute-start = (bf16[208,384]{1,0:T(8,128)(2,1)S(1)}, bf16[208,384]{1,0:T(8,128)(2,1)S(1)}, u32[]{:S(2)}, u32[]{:S(2)}) collective-permute-start(bf16[208,384]{1,0:T(8,128)(2,1)S(1)} %get-tuple-element.91), channel_id=1, source_target_pairs={{0,3},{1,0},{2,1},{3,2},{4,7},{5,4},{6,5},{7,6},{8,11},{9,8},{10,9... | collective-permute-start | bytes 479240 | tf_op jit(solution)/shard_map/ppermute | solution.py:608
  11.9 14.6 %all-to-all-start = ((s32[32,1,64]{2,1,0:T(1,128)}), s32[32,1,64]{2,1,0:T(1,128)S(1)}, u32[]{:S(2)}, u32[]{:S(2)}) async-start(s32[32,1,64]{2,1,0:T(1,128)} %bitcast.2), calls=%async_computation | async-start | bytes 32768 | tf_op jit(solution)/shard_map/all_to_all | solution.py:709
  26.9 22.7 %collective-permute-start.3 = (bf16[4,144,384]{2,1,0:T(8,128)(2,1)S(1)}, bf16[4,144,384]{2,1,0:T(8,128)(2,1)S(1)}, u32[]{:S(2)}, u32[]{:S(2)}) collective-permute-start(bf16[4,144,384]{2,1,0:T(8,128)(2,1)S(1)} %pad_maximum_fusion.5), channel_id=1, source_target_pairs={{0,8},{4,12},{8,0},{12,4},{16,24},{20,28},{24,16},{28,20},{1,9},{5... | collective-permute-start | bytes 1327112 | tf_op jit(solution)/shard_map/ppermute | solution.py:603
  27.6 22.1 %collective-permute-start.4 = (bf16[4,144,384]{2,1,0:T(8,128)(2,1)S(1)}, bf16[4,144,384]{2,1,0:T(8,128)(2,1)S(1)}, u32[]{:S(2)}, u32[]{:S(2)}) collective-permute-start(bf16[4,144,384]{2,1,0:T(8,128)(2,1)S(1)} %pad_maximum_fusion.5), channel_id=1, source_target_pairs={{0,16},{4,20},{8,24},{12,28},{16,0},{20,4},{24,8},{28,12},{1,17},{... | collective-permute-start | bytes 1327112 | tf_op jit(solution)/shard_map/ppermute | solution.py:603
  28.2 21.5 %collective-permute-start.5 = (bf16[4,144,384]{2,1,0:T(8,128)(2,1)S(1)}, bf16[4,144,384]{2,1,0:T(8,128)(2,1)S(1)}, u32[]{:S(2)}, u32[]{:S(2)}) collective-permute-start(bf16[4,144,384]{2,1,0:T(8,128)(2,1)S(1)} %pad_maximum_fusion.5), channel_id=1, source_target_pairs={{0,24},{4,28},{8,16},{12,20},{16,8},{20,12},{24,0},{28,4},{1,25},{... | collective-permute-start | bytes 1327112 | tf_op jit(solution)/shard_map/ppermute | solution.py:603
  52.2 6.7 %collective-permute-start.6 = (bf16[4,4,144,384]{3,2,1,0:T(8,128)(2,1)S(1)}, bf16[4,4,144,384]{3,2,1,0:T(8,128)(2,1)}, u32[]{:S(2)}, u32[]{:S(2)}) collective-permute-start(bf16[4,4,144,384]{3,2,1,0:T(8,128)(2,1)S(1)} %pad_maximum_fusion.1.own), channel_id=1, source_target_pairs={{0,4},{4,0},{8,12},{12,8},{16,20},{20,16},{24,28},{28,24},{1,5},{5... | collective-permute-start | bytes 5308424 | tf_op jit(solution)/shard_map/ppermute | solution.py:603
  52.3 22.2 %all-to-all-start.1 = ((bf16[32,32,384]{2,1,0:T(8,128)(2,1)}), bf16[32,32,384]{2,1,0:T(8,128)(2,1)S(1)}, u32[]{:S(2)}, u32[]{:S(2)}) async-start(bf16[32,32,384]{2,1,0:T(8,128)(2,1)} %bitcast.17), calls=%async_computation.1 | async-start | bytes 1572864 | tf_op jit(solution)/shard_map/all_to_all | solution.py:709
  55.0 4.0 collective-permute-start.7
  96.9 39.4 %all-to-all-start.2 = ((bf16[8,256,576]{1,2,0:T(8,128)(2,1)}), bf16[8,256,576]{1,2,0:T(8,128)(2,1)}, u32[]{:S(2)}, u32[]{:S(2)}) async-start(bf16[8,256,576]{1,2,0:T(8,128)(2,1)} %copy.64), calls=%async_computation.2 | async-start | bytes 4718592 | tf_op jit(solution)/shard_map/all_to_all | solution.py:709
  101.3 11.3 %collective-permute-start.8 = (bf16[1296,128]{1,0:T(8,128)(2,1)S(1)}, bf16[1296,128]{1,0:T(8,128)(2,1)S(1)}, u32[]{:S(2)}, u32[]{:S(2)}) collective-permute-start(bf16[1296,128]{1,0:T(8,128)(2,1)S(1)} %get-tuple-element.107), channel_id=1, source_target_pairs={{0,3},{1,0},{2,1},{3,2},{4,7},{5,4},{6,5},{7,6},{8,11},{9,8},{10,9... | collective-permute-start | bytes 995336 | tf_op jit(solution)/shard_map/ppermute | solution.py:608
  104.4 30.7 %collective-permute-start.9 = (bf16[1296,128]{1,0:T(8,128)(2,1)S(1)}, bf16[1296,128]{1,0:T(8,128)(2,1)S(1)}, u32[]{:S(2)}, u32[]{:S(2)}) collective-permute-start(bf16[1296,128]{1,0:T(8,128)(2,1)S(1)} %get-tuple-element.107), channel_id=1, source_target_pairs={{0,2},{1,3},{2,0},{3,1},{4,6},{5,7},{6,4},{7,5},{8,10},{9,11},{10,... | collective-permute-start | bytes 995336 | tf_op jit(solution)/shard_map/ppermute | solution.py:608
  105.7 29.3 %collective-permute-start.10 = (bf16[1296,128]{1,0:T(8,128)(2,1)S(1)}, bf16[1296,128]{1,0:T(8,128)(2,1)S(1)}, u32[]{:S(2)}, u32[]{:S(2)}) collective-permute-start(bf16[1296,128]{1,0:T(8,128)(2,1)S(1)} %get-tuple-element.107), channel_id=1, source_target_pairs={{0,1},{1,2},{2,3},{3,0},{4,5},{5,6},{6,7},{7,4},{8,9},{9,10},{10,1... | collective-permute-start | bytes 995336 | tf_op jit(solution)/shard_map/ppermute | solution.py:608
  139.4 60.5 %copy-start.40 = (bf16[4,1296,128]{2,1,0:T(8,128)(2,1)S(1)}, bf16[4,1296,128]{2,1,0:T(8,128)(2,1)}, u32[]{:S(2)}) copy-start(bf16[4,1296,128]{2,1,0:T(8,128)(2,1)} %pad_maximum_fusion.2) | copy-start | bytes 3981316
  139.4 32.3 %collective-permute-start.11 = (bf16[4,1296,128]{2,1,0:T(8,128)(2,1)}, bf16[4,1296,128]{2,1,0:T(8,128)(2,1)S(1)}, u32[]{:S(2)}, u32[]{:S(2)}) collective-permute-start(bf16[4,1296,128]{2,1,0:T(8,128)(2,1)} %pad_maximum_fusion.2), channel_id=1, source_target_pairs={{0,8},{4,12},{8,0},{12,4},{16,24},{20,28},{24,16},{28,20},{1,9},{5... | collective-permute-start | bytes 3981320 | tf_op jit(solution)/shard_map/ppermute | solution.py:603
  141.2 58.7 %collective-permute-start.12 = (bf16[4,1296,128]{2,1,0:T(8,128)(2,1)}, bf16[4,1296,128]{2,1,0:T(8,128)(2,1)S(1)}, u32[]{:S(2)}, u32[]{:S(2)}) collective-permute-start(bf16[4,1296,128]{2,1,0:T(8,128)(2,1)} %pad_maximum_fusion.2), channel_id=1, source_target_pairs={{0,16},{4,20},{8,24},{12,28},{16,0},{20,4},{24,8},{28,12},{1,17},{... | collective-permute-start | bytes 3981320 | tf_op jit(solution)/shard_map/ppermute | solution.py:603
  142.6 57.2 %collective-permute-start.13 = (bf16[4,1296,128]{2,1,0:T(8,128)(2,1)}, bf16[4,1296,128]{2,1,0:T(8,128)(2,1)S(1)}, u32[]{:S(2)}, u32[]{:S(2)}) collective-permute-start(bf16[4,1296,128]{2,1,0:T(8,128)(2,1)} %pad_maximum_fusion.2), channel_id=1, source_target_pairs={{0,24},{4,28},{8,16},{12,20},{16,8},{20,12},{24,0},{28,4},{1,25},{... | collective-permute-start | bytes 3981320 | tf_op jit(solution)/shard_map/ppermute | solution.py:603
  163.1 39.6 %copy-start.7 = (bf16[2048,192]{1,0:T(8,128)(2,1)}, bf16[2048,192]{1,0:T(8,128)(2,1)S(1)}, u32[]{:S(2)}) copy-start(bf16[2048,192]{1,0:T(8,128)(2,1)S(1)} %get-tuple-element.104) | copy-start | bytes 2359300
  163.1 39.6 %copy-start.32 = (f32[3,64,2048]{2,1,0:T(8,128)}, f32[3,64,2048]{2,1,0:T(8,128)S(1)}, u32[]{:S(2)}) copy-start(f32[3,64,2048]{2,1,0:T(8,128)S(1)} %get-tuple-element.118.attended_t) | copy-start | bytes 4718596
  202.7 18.8 %collective-permute-start.14 = (bf16[4,4,1296,128]{3,2,1,0:T(8,128)(2,1)}, bf16[4,4,1296,128]{3,2,1,0:T(8,128)(2,1)}, u32[]{:S(2)}, u32[]{:S(2)}) collective-permute-start(bf16[4,4,1296,128]{3,2,1,0:T(8,128)(2,1)} %pad_maximum_fusion.own), channel_id=1, source_target_pairs={{0,4},{4,0},{8,12},{12,8},{16,20},{20,16},{24,28},{28,24},{1,5},{5... | collective-permute-start | bytes 15925256 | tf_op jit(solution)/shard_map/ppermute | solution.py:603
  205.0 16.1 %all-to-all-start.3 = ((bf16[8,256,192]{1,2,0:T(8,128)(2,1)}), bf16[8,256,192]{1,2,0:T(8,128)(2,1)S(1)}, u32[]{:S(2)}, u32[]{:S(2)}) async-start(bf16[8,256,192]{1,2,0:T(8,128)(2,1)} %copy.66), calls=%async_computation.3 | async-start | bytes 1572864 | tf_op jit(solution)/shard_map/all_to_all | solution.py:709
  258.2 24.3 %all-to-all-start.4 = ((bf16[8,256,192]{1,2,0:T(8,128)(2,1)}), bf16[8,256,192]{1,2,0:T(8,128)(2,1)}, u32[]{:S(2)}, u32[]{:S(2)}) async-start(bf16[8,256,192]{1,2,0:T(8,128)(2,1)} %copy.68), calls=%async_computation.4 | async-start | bytes 1572864 | tf_op jit(solution)/shard_map/all_to_all | solution.py:709
  284.8 26.5 %collective-permute-start.15 = (bf16[4,4,1296,128]{3,2,1,0:T(8,128)(2,1)}, bf16[4,4,1296,128]{3,2,1,0:T(8,128)(2,1)}, u32[]{:S(2)}, u32[]{:S(2)}) collective-permute-start(bf16[4,4,1296,128]{3,2,1,0:T(8,128)(2,1)} %get-tuple-element.128), channel_id=1, source_target_pairs={{0,4},{4,0},{8,12},{12,8},{16,20},{20,16},{24,28},{28,24},{1,5},{5... | collective-permute-start | bytes 15925256 | tf_op jit(solution)/shard_map/ppermute | solution.py:603
  307.2 45.3 %all-to-all-start.5 = ((bf16[8,256,192]{1,2,0:T(8,128)(2,1)}), bf16[8,256,192]{1,2,0:T(8,128)(2,1)S(1)}, u32[]{:S(2)}, u32[]{:S(2)}) async-start(bf16[8,256,192]{1,2,0:T(8,128)(2,1)} %copy.72), calls=%async_computation.5 | async-start | bytes 1572864 | tf_op jit(solution)/shard_map/all_to_all | solution.py:709
  317.2 34.2 %collective-permute-start.16 = (bf16[4,1296,128]{2,1,0:T(8,128)(2,1)S(1)}, bf16[4,1296,128]{2,1,0:T(8,128)(2,1)S(1)}, u32[]{:S(2)}, u32[]{:S(2)}) collective-permute-start(bf16[4,1296,128]{2,1,0:T(8,128)(2,1)S(1)} %get-tuple-element.173), channel_id=1, source_target_pairs={{0,8},{4,12},{8,0},{12,4},{16,24},{20,28},{24,16},{28,20},{1,9},{5... | collective-permute-start | bytes 3981320 | tf_op jit(solution)/shard_map/ppermute | solution.py:603
  319.2 33.3 %collective-permute-start.17 = (bf16[4,1296,128]{2,1,0:T(8,128)(2,1)S(1)}, bf16[4,1296,128]{2,1,0:T(8,128)(2,1)}, u32[]{:S(2)}, u32[]{:S(2)}) collective-permute-start(bf16[4,1296,128]{2,1,0:T(8,128)(2,1)S(1)} %get-tuple-element.172), channel_id=1, source_target_pairs={{0,16},{4,20},{8,24},{12,28},{16,0},{20,4},{24,8},{28,12},{1,17},{... | collective-permute-start | bytes 3981320 | tf_op jit(solution)/shard_map/ppermute | solution.py:603
  353.4 25.4 %all-to-all-start.6 = ((bf16[8,256,384]{2,1,0:T(8,128)(2,1)}), bf16[8,256,384]{2,1,0:T(8,128)(2,1)S(1)}, u32[]{:S(2)}, u32[]{:S(2)}) async-start(bf16[8,256,384]{2,1,0:T(8,128)(2,1)} %bitcast.45), calls=%async_computation.6 | async-start | bytes 3145728 | tf_op jit(solution)/shard_map/all_to_all | solution.py:709
  358.8 48.1 %collective-permute-start.19 = (bf16[4,1296,128]{2,1,0:T(8,128)(2,1)}, bf16[4,1296,128]{2,1,0:T(8,128)(2,1)}, u32[]{:S(2)}, u32[]{:S(2)}) collective-permute-start(bf16[4,1296,128]{2,1,0:T(8,128)(2,1)} %get-tuple-element.141), channel_id=1, source_target_pairs={{0,24},{4,28},{8,16},{12,20},{16,8},{20,12},{24,0},{28,4},{1,25},{... | collective-permute-start | bytes 3981320 | tf_op jit(solution)/shard_map/ppermute | solution.py:603
  392.8 19.7 %collective-permute-start.18 = (bf16[4,4,480,128]{3,2,1,0:T(8,128)(2,1)}, bf16[4,4,480,128]{3,2,1,0:T(8,128)(2,1)}, u32[]{:S(2)}, u32[]{:S(2)}) collective-permute-start(bf16[4,4,480,128]{3,2,1,0:T(8,128)(2,1)} %get-tuple-element.138), channel_id=1, source_target_pairs={{0,4},{4,0},{8,12},{12,8},{16,20},{20,16},{24,28},{28,24},{1,5},{5... | collective-permute-start | bytes 5898248 | tf_op jit(solution)/shard_map/ppermute | solution.py:603
  406.9 59.4 %all-to-all-start.7 = ((bf16[32,32,384]{2,1,0:T(8,128)(2,1)}), bf16[32,32,384]{2,1,0:T(8,128)(2,1)S(1)}, u32[]{:S(2)}, u32[]{:S(2)}) async-start(bf16[32,32,384]{2,1,0:T(8,128)(2,1)} %bitcast.55), calls=%async_computation.7 | async-start | bytes 1572864 | tf_op jit(solution)/shard_map/all_to_all | solution.py:709
  414.2 17.3 %collective-permute-start.20 = (bf16[4,480,128]{2,1,0:T(8,128)(2,1)S(1)}, bf16[4,480,128]{2,1,0:T(8,128)(2,1)S(1)}, u32[]{:S(2)}, u32[]{:S(2)}) collective-permute-start(bf16[4,480,128]{2,1,0:T(8,128)(2,1)S(1)} %get-tuple-element.175), channel_id=1, source_target_pairs={{0,8},{4,12},{8,0},{12,4},{16,24},{20,28},{24,16},{28,20},{1,9},{5... | collective-permute-start | bytes 1474568 | tf_op jit(solution)/shard_map/ppermute | solution.py:603
  415.9 19.2 %collective-permute-start.21 = (bf16[4,480,128]{2,1,0:T(8,128)(2,1)S(1)}, bf16[4,480,128]{2,1,0:T(8,128)(2,1)S(1)}, u32[]{:S(2)}, u32[]{:S(2)}) collective-permute-start(bf16[4,480,128]{2,1,0:T(8,128)(2,1)S(1)} %get-tuple-element.177), channel_id=1, source_target_pairs={{0,16},{4,20},{8,24},{12,28},{16,0},{20,4},{24,8},{28,12},{1,17},{... | collective-permute-start | bytes 1474568 | tf_op jit(solution)/shard_map/ppermute | solution.py:603
  417.4 25.2 %collective-permute-start.22 = (bf16[4,480,128]{2,1,0:T(8,128)(2,1)S(1)}, bf16[4,480,128]{2,1,0:T(8,128)(2,1)S(1)}, u32[]{:S(2)}, u32[]{:S(2)}) collective-permute-start(bf16[4,480,128]{2,1,0:T(8,128)(2,1)S(1)} %get-tuple-element.176), channel_id=1, source_target_pairs={{0,24},{4,28},{8,16},{12,20},{16,8},{20,12},{24,0},{28,4},{1,25},{... | collective-permute-start | bytes 1474568 | tf_op jit(solution)/shard_map/ppermute | solution.py:603
  417.8 26.2 %collective-permute-start.23 = (bf16[1296,128]{1,0:T(8,128)(2,1)S(1)}, bf16[1296,128]{1,0:T(8,128)(2,1)S(1)}, u32[]{:S(2)}, u32[]{:S(2)}) collective-permute-start(bf16[1296,128]{1,0:T(8,128)(2,1)S(1)} %get-tuple-element.178), channel_id=1, source_target_pairs={{0,1},{1,2},{2,3},{3,0},{4,5},{5,6},{6,7},{7,4},{8,9},{9,10},{10,1... | collective-permute-start | bytes 995336 | tf_op jit(solution)/shard_map/ppermute | solution.py:608
  419.6 32.3 %collective-permute-start.24 = (bf16[1296,128]{1,0:T(8,128)(2,1)S(1)}, bf16[1296,128]{1,0:T(8,128)(2,1)S(1)}, u32[]{:S(2)}, u32[]{:S(2)}) collective-permute-start(bf16[1296,128]{1,0:T(8,128)(2,1)S(1)} %get-tuple-element.180), channel_id=1, source_target_pairs={{0,2},{1,3},{2,0},{3,1},{4,6},{5,7},{6,4},{7,5},{8,10},{9,11},{10,... | collective-permute-start | bytes 995336 | tf_op jit(solution)/shard_map/ppermute | solution.py:608
  431.5 20.4 %collective-permute-start.25 = (bf16[1296,128]{1,0:T(8,128)(2,1)S(1)}, bf16[1296,128]{1,0:T(8,128)(2,1)S(1)}, u32[]{:S(2)}, u32[]{:S(2)}) collective-permute-start(bf16[1296,128]{1,0:T(8,128)(2,1)S(1)} %get-tuple-element.179), channel_id=1, source_target_pairs={{0,3},{1,0},{2,1},{3,2},{4,7},{5,4},{6,5},{7,6},{8,11},{9,8},{10,9... | collective-permute-start | bytes 995336 | tf_op jit(solution)/shard_map/ppermute | solution.py:608
  452.6 12.6 %collective-permute-start.26 = (bf16[480,128]{1,0:T(8,128)(2,1)}, bf16[480,128]{1,0:T(8,128)(2,1)S(1)}, u32[]{:S(2)}, u32[]{:S(2)}) collective-permute-start(bf16[480,128]{1,0:T(8,128)(2,1)} %get-tuple-element.181), channel_id=1, source_target_pairs={{0,1},{1,2},{2,3},{3,0},{4,5},{5,6},{6,7},{7,4},{8,9},{9,10},{10,1... | collective-permute-start | bytes 368648 | tf_op jit(solution)/shard_map/ppermute | solution.py:608
  460.0 20.2 %collective-permute-start.30 = (bf16[1296,128]{1,0:T(8,128)(2,1)S(1)}, bf16[1296,128]{1,0:T(8,128)(2,1)S(1)}, u32[]{:S(2)}, u32[]{:S(2)}) collective-permute-start(bf16[1296,128]{1,0:T(8,128)(2,1)S(1)} %fusion.9), channel_id=1, source_target_pairs={{0,8},{4,12},{8,0},{12,4},{16,24},{20,28},{24,16},{28,20},{1,9},{5... | collective-permute-start | bytes 995336 | tf_op jit(solution)/shard_map/ppermute | solution.py:603
  461.6 18.6 %collective-permute-start.31 = (bf16[1296,128]{1,0:T(8,128)(2,1)S(1)}, bf16[1296,128]{1,0:T(8,128)(2,1)S(1)}, u32[]{:S(2)}, u32[]{:S(2)}) collective-permute-start(bf16[1296,128]{1,0:T(8,128)(2,1)S(1)} %fusion.9), channel_id=1, source_target_pairs={{0,16},{4,20},{8,24},{12,28},{16,0},{20,4},{24,8},{28,12},{1,17},{... | collective-permute-start | bytes 995336 | tf_op jit(solution)/shard_map/ppermute | solution.py:603
  463.1 17.1 %collective-permute-start.32 = (bf16[1296,128]{1,0:T(8,128)(2,1)S(1)}, bf16[1296,128]{1,0:T(8,128)(2,1)}, u32[]{:S(2)}, u32[]{:S(2)}) collective-permute-start(bf16[1296,128]{1,0:T(8,128)(2,1)S(1)} %fusion.9), channel_id=1, source_target_pairs={{0,24},{4,28},{8,16},{12,20},{16,8},{20,12},{24,0},{28,4},{1,25},{... | collective-permute-start | bytes 995336 | tf_op jit(solution)/shard_map/ppermute | solution.py:603
  463.8 16.3 %collective-permute-start.27 = (bf16[480,128]{1,0:T(8,128)(2,1)}, bf16[480,128]{1,0:T(8,128)(2,1)S(1)}, u32[]{:S(2)}, u32[]{:S(2)}) collective-permute-start(bf16[480,128]{1,0:T(8,128)(2,1)} %get-tuple-element.183), channel_id=1, source_target_pairs={{0,2},{1,3},{2,0},{3,1},{4,6},{5,7},{6,4},{7,5},{8,10},{9,11},{10,... | collective-permute-start | bytes 368648 | tf_op jit(solution)/shard_map/ppermute | solution.py:608
  465.3 14.8 %collective-permute-start.28 = (bf16[480,128]{1,0:T(8,128)(2,1)}, bf16[480,128]{1,0:T(8,128)(2,1)S(1)}, u32[]{:S(2)}, u32[]{:S(2)}) collective-permute-start(bf16[480,128]{1,0:T(8,128)(2,1)} %get-tuple-element.182), channel_id=1, source_target_pairs={{0,3},{1,0},{2,1},{3,2},{4,7},{5,4},{6,5},{7,6},{8,11},{9,8},{10,9... | collective-permute-start | bytes 368648 | tf_op jit(solution)/shard_map/ppermute | solution.py:608
  481.3 15.0 %collective-permute-start.36 = (bf16[4,1296,128]{2,1,0:T(8,128)(2,1)S(1)}, bf16[4,1296,128]{2,1,0:T(8,128)(2,1)S(1)}, u32[]{:S(2)}, u32[]{:S(2)}) collective-permute-start(bf16[4,1296,128]{2,1,0:T(8,128)(2,1)S(1)} %pad_maximum_fusion.3.own), channel_id=1, source_target_pairs={{0,4},{4,0},{8,12},{12,8},{16,20},{20,16},{24,28},{28,24},{1,5},{5... | collective-permute-start | bytes 3981320 | tf_op jit(solution)/shard_map/ppermute | solution.py:603
  481.4 5.9 %collective-permute-start.29 = (bf16[480,128]{1,0:T(8,128)(2,1)S(1)}, bf16[480,128]{1,0:T(8,128)(2,1)S(1)}, u32[]{:S(2)}, u32[]{:S(2)}) collective-permute-start(bf16[480,128]{1,0:T(8,128)(2,1)S(1)} %fusion.18), channel_id=1, source_target_pairs={{0,8},{4,12},{8,0},{12,4},{16,24},{20,28},{24,16},{28,20},{1,9},{5... | collective-permute-start | bytes 368648 | tf_op jit(solution)/shard_map/ppermute | solution.py:603
  483.0 8.0 %collective-permute-start.33 = (bf16[480,128]{1,0:T(8,128)(2,1)S(1)}, bf16[480,128]{1,0:T(8,128)(2,1)S(1)}, u32[]{:S(2)}, u32[]{:S(2)}) collective-permute-start(bf16[480,128]{1,0:T(8,128)(2,1)S(1)} %fusion.18), channel_id=1, source_target_pairs={{0,16},{4,20},{8,24},{12,28},{16,0},{20,4},{24,8},{28,12},{1,17},{... | collective-permute-start | bytes 368648 | tf_op jit(solution)/shard_map/ppermute | solution.py:603
  484.5 6.5 %collective-permute-start.34 = (bf16[480,128]{1,0:T(8,128)(2,1)S(1)}, bf16[480,128]{1,0:T(8,128)(2,1)S(1)}, u32[]{:S(2)}, u32[]{:S(2)}) collective-permute-start(bf16[480,128]{1,0:T(8,128)(2,1)S(1)} %fusion.18), channel_id=1, source_target_pairs={{0,24},{4,28},{8,16},{12,20},{16,8},{20,12},{24,0},{28,4},{1,25},{... | collective-permute-start | bytes 368648 | tf_op jit(solution)/shard_map/ppermute | solution.py:603
  491.1 2.1 collective-permute-start.35
  (47 other events, 186.0 us)

commit v3 on v2

--- a/solution.py
+++ b/solution.py
@@ -401,32 +401,41 @@
     return total + jnp.sum(tile.reshape(-1, 8, tile.shape[1]), axis=0)
 
 
-def attend_short_kernel(pairs, piece, order, rows, out, attended_t, logsum, q_s, k_s, vt_s, s_s, o_s):
-    length = rows.shape[0]
+def swap(value):
+    return mm(eye(value.shape[1]), value, NT).astype(BF)
+
+
+def piece_of(order, j, piece):
+    at = order[j]
+    return at // 2, pl.ds(pl.multiple_of(lax.rem(at, 2) * piece, piece), piece)
+
+
+def attend_short_kernel(pairs, piece, order, rows, out, attended_t, logsum, q_s, k_s, v_s, s_s):
+    length = rows.shape[0] * rows.shape[2]
     blocks = length // ABLK
     width = pairs * HD
-    identity = eye(HD)
 
     def sort(j, _):
-        block = rows[pl.ds(pl.multiple_of(order[j] * piece, piece), piece), :]
+        device, lanes = piece_of(order, j, piece)
+        block = rows[device, :, lanes]
         to = pl.ds(pl.multiple_of(j * piece, piece), piece)
         for p in range(pairs):
-            q = block[:, p * HD : (p + 1) * HD]
-            q_s[p, to, :] = (q.astype(F32) * HD ** (-0.5)).astype(BF)
-            k_s[p, to, :] = block[:, width + p * HD : width + (p + 1) * HD]
-            v = block[:, 2 * width + p * HD : 2 * width + (p + 1) * HD]
-            vt_s[p, :, to] = mm(identity, v, NT).astype(BF)
+            q = block[p * HD : (p + 1) * HD, :]
+            q_s[p, :, to] = (q.astype(F32) * HD ** (-0.5)).astype(BF)
+            k_s[p, to, :] = swap(block[width + p * HD : width + (p + 1) * HD, :])
+            v_s[p, :, to] = block[2 * width + p * HD : 2 * width + (p + 1) * HD, :]
         return 0
 
     lax.fori_loop(0, length // piece, sort, 0)
 
     def pair(p, _):
+        features = pl.ds(pl.multiple_of(p * HD, HD), HD)
         for i in range(blocks):
             at = slice(i * ABLK, (i + 1) * ABLK)
-            queries = q_s[p, at, :]
+            queries = q_s[p, :, at]
             peak = jnp.full((8, ABLK), -jnp.inf, F32)
             for j in range(i + 1):
-                s = mm(k_s[p, j * ABLK : (j + 1) * ABLK, :], queries, NT)
+                s = mm(k_s[p, j * ABLK : (j + 1) * ABLK, :], queries)
                 s_s[i % 2, j * ABLK : (j + 1) * ABLK, :] = s
                 peak = fold_max(peak, s)
             peak = jnp.max(peak, axis=0, keepdims=True)
@@ -435,42 +444,37 @@
             for j in range(i + 1):
                 e = jnp.exp(s_s[i % 2, j * ABLK : (j + 1) * ABLK, :] - peak)
                 total = fold_sum(total, e)
-                o += mm(vt_s[p, :, j * ABLK : (j + 1) * ABLK], e.astype(BF))
+                o += mm(v_s[p, :, j * ABLK : (j + 1) * ABLK], e.astype(BF))
             total = jnp.sum(total, axis=0, keepdims=True)
             o = o * (1.0 / total)
             attended_t[p, :, at] = o
             logsum[p, :, at] = peak + jnp.log(total)
-            o_s[p, at, :] = o.T.astype(BF)
+            o = o.astype(BF)
+            for h in range(ABLK // piece):
+                device, lanes = piece_of(order, ABLK // piece * i + h, piece)
+                out[device, features, lanes] = o[:, h * piece : (h + 1) * piece]
         return 0
 
     lax.fori_loop(0, pairs, pair, 0)
 
-    def unsort(j, _):
-        take = pl.ds(pl.multiple_of(j * piece, piece), piece)
-        to = pl.ds(pl.multiple_of(order[j] * piece, piece), piece)
-        out[to, :] = jnp.concatenate([o_s[p, take, :] for p in range(pairs)], axis=1)
-        return 0
-
-    lax.fori_loop(0, length // piece, unsort, 0)
-
 
 def attend_short(order, rows, pairs, piece):
-    length = rows.shape[0]
+    contexts, _, tokens = rows.shape
+    length = contexts * tokens
     return pl.pallas_call(
         functools.partial(attend_short_kernel, pairs, piece),
         out_shape=(
-            jax.ShapeDtypeStruct((length, pairs * HD), BF),
+            jax.ShapeDtypeStruct((contexts, pairs * HD, tokens), BF),
             jax.ShapeDtypeStruct((pairs, HD, length), F32),
             jax.ShapeDtypeStruct((pairs, 1, length), F32),
         ),
         in_specs=[smem(), vmem()],
         out_specs=(vmem(),) * 3,
         scratch_shapes=[
-            pltpu.VMEM((pairs, length, HD), BF),
+            pltpu.VMEM((pairs, HD, length), BF),
             pltpu.VMEM((pairs, length, HD), BF),
             pltpu.VMEM((pairs, HD, length), BF),
             pltpu.VMEM((2, length, ABLK), F32),
-            pltpu.VMEM((pairs, length, HD), BF),
         ],
         compiler_params=params(48),
         cost_estimate=cost(25),
@@ -488,114 +492,103 @@
     grads,
     attended_t,
     logsum,
-    cos,
-    sin,
     cos_t,
     sin_t,
     out,
     q_s,
+    g_s,
+    kt_s,
     k_s,
     v_s,
-    g_s,
-    kt_s,
-    dq_s,
     dk_s,
     dv_s,
-    dk_o,
-    dv_o,
 ):
-    length = rows.shape[0]
+    length = rows.shape[0] * rows.shape[2]
     blocks = length // ABLK
     width = pairs * HD
     half = HD // 2
     scale = HD ** (-0.5)
-    identity = eye(HD)
 
     def sort(j, _):
-        take = pl.ds(pl.multiple_of(order[j] * piece, piece), piece)
-        block = rows[take, :]
-        grad = grads[take, :]
+        device, lanes = piece_of(order, j, piece)
+        block = rows[device, :, lanes]
+        grad = grads[device, :, lanes]
         to = pl.ds(pl.multiple_of(j * piece, piece), piece)
         for p in range(count):
-            lane = (begin + p) * HD
-            q_s[p, to, :] = (block[:, lane : lane + HD].astype(F32) * scale).astype(BF)
-            k = block[:, width + lane : width + lane + HD]
-            k_s[p, to, :] = k
-            kt_s[p, :, to] = mm(identity, k, NT).astype(BF)
-            v_s[p, to, :] = block[:, 2 * width + lane : 2 * width + lane + HD]
-            g_s[p, to, :] = grad[:, lane : lane + HD]
+            row = (begin + p) * HD
+            q_s[p, :, to] = (block[row : row + HD, :].astype(F32) * scale).astype(BF)
+            k = block[width + row : width + row + HD, :]
+            kt_s[p, :, to] = k
+            k_s[p, to, :] = swap(k)
+            v_s[p, to, :] = swap(block[2 * width + row : 2 * width + row + HD, :])
+            g_s[p, :, to] = grad[row : row + HD, :]
         return 0
 
     lax.fori_loop(0, length // piece, sort, 0)
 
+    def turn(x, at):
+        c, s = cos_t[:, at], sin_t[:, at]
+        a, b = x[:half, :], x[half:, :]
+        return jnp.concatenate([a * c + b * s, b * c - a * s], axis=0)
+
     def pair(p, _):
+        def put(kind, i, value):
+            features = pl.ds(pl.multiple_of((kind * count + p) * HD, HD), HD)
+            value = value.astype(BF)
+            for h in range(ABLK // piece):
+                device, lanes = piece_of(order, ABLK // piece * i + h, piece)
+                out[device, features, lanes] = value[:, h * piece : (h + 1) * piece]
+
         for i in range(blocks):
             at = slice(i * ABLK, (i + 1) * ABLK)
-            queries = q_s[p, at, :]
-            grad = g_s[p, at, :]
-            delta = jnp.sum(mm(identity, grad, NT) * attended_t[begin + p, :, at], axis=0, keepdims=True)
+            queries = q_s[p, :, at]
+            grad = g_s[p, :, at]
+            delta = jnp.sum(
+                grad.astype(F32) * attended_t[begin + p, :, at], axis=0, keepdims=True
+            )
             level = logsum[begin + p, :, at]
             dq = jnp.zeros((HD, ABLK), F32)
             for j in range(i, -1, -1):
                 to = slice(j * ABLK, (j + 1) * ABLK)
-                probs = jnp.exp(mm(k_s[p, to, :], queries, NT) - level)
-                ds = (probs * (mm(v_s[p, to, :], grad, NT) - delta)).astype(BF)
-                dv = mm(probs.astype(BF), grad)
-                dk = mm(ds, queries)
+                probs = jnp.exp(mm(k_s[p, to, :], queries) - level)
+                ds = (probs * (mm(v_s[p, to, :], grad) - delta)).astype(BF)
+                dv = mm(grad, probs.astype(BF), NT)
+                dk = mm(queries, ds, NT)
                 if i == j:
-                    dv_s[to, :] = dv
-                    dk_s[to, :] = dk
+                    dv_s[:, to] = dv
+                    dk_s[:, to] = dk
                 else:
-                    dv_s[to, :] += dv
-                    dk_s[to, :] += dk
+                    dv_s[:, to] += dv
+                    dk_s[:, to] += dk
                 dq += mm(kt_s[p, :, to], ds)
-            dq = dq * scale
-            c, s = cos_t[:, at], sin_t[:, at]
-            a, b = dq[:half, :], dq[half:, :]
-            dq = jnp.concatenate([a * c + b * s, b * c - a * s], axis=0)
-            dq_s[p, at, :] = dq.T.astype(BF)
-
-        def turn(j, _):
-            to = pl.ds(pl.multiple_of(j * ABLK, ABLK), ABLK)
-            dk = dk_s[to, :]
-            a, b = dk[:, :half], dk[:, half:]
-            c, s = cos[to, :], sin[to, :]
-            dk_o[p, to, :] = jnp.concatenate([a * c + b * s, b * c - a * s], axis=1).astype(BF)
-            dv_o[p, to, :] = dv_s[to, :].astype(BF)
-            return 0
-
-        lax.fori_loop(0, blocks, turn, 0)
+            put(0, i, turn(dq * scale, at))
+        for i in range(blocks):
+            at = slice(i * ABLK, (i + 1) * ABLK)
+            put(1, i, turn(dk_s[:, at], at))
+            put(2, i, dv_s[:, at])
         return 0
 
     lax.fori_loop(0, count, pair, 0)
 
-    def unsort(j, _):
-        take = pl.ds(pl.multiple_of(j * piece, piece), piece)
-        to = pl.ds(pl.multiple_of(order[j] * piece, piece), piece)
-        parts = [ref[p, take, :] for ref in (dq_s, dk_o, dv_o) for p in range(count)]
-        out[to, :] = jnp.concatenate(parts, axis=1)
-        return 0
-
-    lax.fori_loop(0, length // piece, unsort, 0)
-
 
 def attend_grad_short(
-    order, rows, grads, attended_t, logsum, cos, sin, cos_t, sin_t, pairs, piece, begin, count
+    order, rows, grads, attended_t, logsum, cos_t, sin_t, pairs, piece, begin, count
 ):
-    length = rows.shape[0]
-    full = pltpu.VMEM((length, HD), F32)
-    each = pltpu.VMEM((count, length, HD), BF)
+    contexts, _, tokens = rows.shape
+    length = contexts * tokens
+    wide_ = pltpu.VMEM((count, HD, length), BF)
+    tall = pltpu.VMEM((count, length, HD), BF)
+    full = pltpu.VMEM((HD, length), F32)
     return pl.pallas_call(
         functools.partial(attend_grad_short_kernel, pairs, begin, count, piece),
-        out_shape=jax.ShapeDtypeStruct((length, 3 * count * HD), BF),
-        in_specs=[smem()] + [vmem()] * 8,
+        out_shape=jax.ShapeDtypeStruct((contexts, 3 * count * HD, tokens), BF),
+        in_specs=[smem()] + [vmem()] * 6,
         out_specs=vmem(),
-        scratch_shapes=[each] * 4
-        + [pltpu.VMEM((count, HD, length), BF), each, full, full, each, each],
+        scratch_shapes=[wide_] * 3 + [tall] * 2 + [full] * 2,
         compiler_params=params(48),
         cost_estimate=cost(14 * count),
         name=f"attend_grad_{begin}",
-    )(order, rows, grads, attended_t, logsum, cos, sin, cos_t, sin_t)
+    )(order, rows, grads, attended_t, logsum, cos_t, sin_t)
 
 
 def over_ctx(value, mask):
@@ -749,75 +742,14 @@
     )(where, *weights)
 
 
-def assemble_first_kernel(where, own, other, own_tail, other_tail, joined, lookup, gains):
-    core, chip, z = where[0], where[1], where[2]
-    for source, tail, half in ((own, own_tail, core), (other, other_tail, 1 - core)):
-        columns = pl.ds(aligned(half * 384, 128), 384)
-        for m in range(4):
-            zz = lax.rem(z + m, 4)
-            for k in range(4):
-                rows = pl.ds(aligned(zz * 192 + (chip ^ k) * 48), 48)
-                for t in range(3):
-                    joined[rows, pl.ds(aligned(t * D + half * 384, 128), 384)] = source[
-                        k, m, t * 48 : (t + 1) * 48, :
-                    ]
-            lookup[pl.ds(aligned(zz * 48), 48), columns] = tail[m, 0:48, :]
-    for m in range(4):
-        gains[lax.rem(z + m, 4)] = own_tail[m, 48:64, :]
-
-
-def assemble_first(where, *blocks):
-    return pl.pallas_call(
-        assemble_first_kernel,
-        out_shape=(
-            jax.ShapeDtypeStruct((D, 3 * D), BF),
-            jax.ShapeDtypeStruct((E, D), BF),
-            jax.ShapeDtypeStruct((4, 16, 384), BF),
-        ),
-        in_specs=[smem()] + [vmem()] * 4,
-        out_specs=(vmem(),) * 3,
-        compiler_params=params(24),
-        cost_estimate=cost(3),
-        name="assemble_first",
-    )(where, *blocks)
-
-
-def assemble_second_kernel(where, own, other, expand, contract, output):
-    core, chip, z = where[0], where[1], where[2]
-    for source, half in ((own, core), (other, 1 - core)):
-
-        def block(i, _):
-            k, m = i // 4, lax.rem(i, 4)
-            zz, yx = lax.rem(z + m, 4), chip ^ k
-            rows = pl.ds(aligned(zz * 192 + yx * 48), 48)
-            for j in range(16):
-                expand[rows, pl.ds(aligned(half * FF + j * 128, 128), 128)] = source[
-                    k, m, j * 48 : (j + 1) * 48, :
-                ]
-            tall = pl.ds(aligned(zz * 512 + yx * 128), 128)
-            for j in range(3):
-                to = pl.ds(aligned(half * 384 + j * 128, 128), 128)
-                contract[tall, to] = source[k, m, 768 + j * 128 : 896 + j * 128, :]
-                output[rows, to] = source[k, m, 1152 + j * 48 : 1200 + j * 48, :]
-            return 0
-
-        lax.fori_loop(0, 16, block, 0)
-
-
-def assemble_second(where, *blocks):
-    return pl.pallas_call(
-        assemble_second_kernel,
-        out_shape=(
-            jax.ShapeDtypeStruct((D, 2 * FF), BF),
-            jax.ShapeDtypeStruct((FF, D), BF),
-            jax.ShapeDtypeStruct((D, D), BF),
-        ),
-        in_specs=[smem()] + [vmem()] * 2,
-        out_specs=(vmem(),) * 3,
-        compiler_params=params(32),
-        cost_estimate=cost(7),
-        name="assemble_second",
-    )(where, *blocks)
+CUT = 14 * 48
+
+
+def by_chip(near_x, near_y, far_y, far_x):
+    return (
+        [near_x.at[0], near_x.at[1], far_y.at[0], far_y.at[1]],
+        [near_y.at[0], far_x.at[0], near_y.at[1], far_x.at[1]],
+    )
 
 
 def spread_fsdp(piece):
@@ -840,8 +772,12 @@
     return [over_ctx(blocks[k], 2 * k) for k in range(1, 4)]
 
 
-def to_fsdp(total):
-    return [along_fsdp(total[m], m) for m in range(1, 4)]
+def add_all(*blocks):
+    return sum((b.astype(F32) for b in blocks[1:]), blocks[0].astype(F32))
+
+
+def over_fsdp(value, mask):
+    return lax.ppermute(value, "fsdp", [(i, i ^ mask) for i in range(4)])
 
 
 def unpack_second_kernel(where, own, other, expand, contract, output):
@@ -927,8 +863,45 @@
 
 
 def front_kernel(
-    pairs, starts, got, target, token, lookup, gain, joined, cos, sin, start, embed, hidden, send
+    pairs,
+    where,
+    starts,
+    got,
+    target,
+    token,
+    cos_t,
+    sin_t,
+    *refs,
 ):
+    own_tail, other_tail = refs[8:10]
+    start, embed, hidden, send, joined, lookup, gains, t_s, g_s = refs[10:]
+    core, chip, z = where[0], where[1], where[2]
+    for blocks, tail, half in ((refs[:4], own_tail, core), (refs[4:8], other_tail, 1 - core)):
+        upper, lower = by_chip(*blocks)
+        for m in range(4):
+            zz = lax.rem(z + m, 4)
+            for k in range(4):
+                begin = zz * 192 + (chip ^ k) * 48
+                for t, source, first, last, at in (
+                    (0, upper, 0, 48, 0),
+                    (1, upper, 48, 80, 0),
+                    (1, lower, 0, 16, 32),
+                    (2, lower, 16, 64, 0),
+                ):
+                    joined[
+                        pl.ds(aligned(begin + at), last - first),
+                        pl.ds(aligned(t * D + half * 384, 128), 384),
+                    ] = source[k][m, first:last, :]
+            lookup[pl.ds(aligned(zz * 48), 48), pl.ds(aligned(half * 384, 128), 384)] = tail[
+                m, 0:48, :
+            ]
+    for m in range(4):
+        g_s[lax.rem(z + m, 4)] = own_tail[m, 48:64, :].astype(F32)
+    for row in range(2):
+        gains[row : row + 1, :] = jnp.concatenate(
+            [g_s[zz, row : row + 1, :192] for zz in range(4)], axis=1
+        )
+    gain = gains[0:1, :]
     tokens = token.shape[0]
     piece = 128
     per_batch = tokens // 2 // piece
@@ -951,12 +924,12 @@
         x = token[at, :].astype(F32) + mm(rows, lookup[...])
         start[at, :] = x
         normed, _ = unit_rows(x)
-        low = (normed * gain[...]).astype(BF)
+        low = (normed * gain).astype(BF)
         hidden[at, :] = low
         projected = mm(low, joined[...])
         begin = pl.ds(aligned(starts[lax.rem(i, per_batch)] * piece, piece), piece)
-        c = cos[begin, :]
-        s = sin[begin, :]
+        c = cos_t[:, begin].T
+        s = sin_t[:, begin].T
         c = jnp.concatenate([c, c, c, c], axis=1)
         s = jnp.concatenate([-s, s, -s, s], axis=1)
         turned = []
@@ -964,22 +937,24 @@
             v = projected[:, j * 128 : (j + 1) * 128]
             swapped = jnp.where(first_half, pltpu.roll(v, 96, 1), pltpu.roll(v, 32, 1))
             turned.append((v * c + swapped * s).astype(BF))
-        q = jnp.concatenate(turned[:6], axis=1)
-        k = jnp.concatenate(turned[6:], axis=1)
-        v = projected[:, 2 * D :].astype(BF)
+        for j in range(12, 18):
+            turned.append(projected[:, j * 128 : (j + 1) * 128].astype(BF))
+        for j, v in enumerate(turned):
+            t_s[j * 128 : (j + 1) * 128, :] = swap(v)
         batch = i // per_batch
         to = pl.ds(aligned(lax.rem(i, per_batch) * piece, piece), piece)
         for g in range(groups):
-            take = slice(g * wide_, (g + 1) * wide_)
-            send[batch * groups + g, to, :] = jnp.concatenate(
-                [q[:, take], k[:, take], v[:, take]], axis=1
-            )
+            for t in range(3):
+                begin = t * D + g * wide_
+                send[batch * groups + g, t * wide_ : (t + 1) * wide_, to] = t_s[
+                    begin : begin + wide_, :
+                ]
         return 0
 
     lax.fori_loop(0, tokens // piece, block, 0)
 
 
-def front(pairs, devices, starts, got, target, token, lookup, gain, joined, cos, sin):
+def front(pairs, devices, where, starts, got, target, token, cos_t, sin_t, *blocks):
     tokens = token.shape[0]
     return pl.pallas_call(
         functools.partial(front_kernel, pairs),
@@ -987,63 +962,126 @@
             jax.ShapeDtypeStruct((tokens, D), F32),
             jax.ShapeDtypeStruct((tokens, E), BF),
             jax.ShapeDtypeStruct((tokens, D), BF),
-            jax.ShapeDtypeStruct((devices, tokens // 2, 3 * pairs * HD), BF),
+            jax.ShapeDtypeStruct((devices, 3 * pairs * HD, tokens // 2), BF),
+            jax.ShapeDtypeStruct((D, 3 * D), BF),
+            jax.ShapeDtypeStruct((E, D), BF),
+            jax.ShapeDtypeStruct((2, D), F32),
         ),
-        in_specs=[smem()] + [vmem()] * 8,
-        out_specs=(vmem(),) * 4,
-        compiler_params=params(40),
+        in_specs=[smem()] * 2 + [vmem()] * 15,
+        out_specs=(vmem(),) * 7,
+        scratch_shapes=[pltpu.VMEM((3 * D, 128), BF), pltpu.VMEM((4, 16, 384), F32)],
+        compiler_params=params(60),
         cost_estimate=cost(9),
         name="front",
-    )(starts, got, target, token, lookup, gain, joined, cos, sin)
+    )(where, starts, got, target, token, cos_t, sin_t, *blocks)
 
 
 def mlp_kernel(
     pairs,
+    where,
     came,
     start,
-    output,
-    gain,
+    gains,
     upstream,
-    w_gate,
-    w_up,
-    w_down,
-    result,
-    hidden_out,
-    attended_out,
-    act_out,
-    gate_out,
-    up_out,
-    gain_grad,
-    middle_grad,
-    send,
-    hidden,
-    total,
-    back,
+    *refs,
 ):
+    blocks_own, blocks_other = refs[:4], refs[4:8]
+    (
+        result,
+        hidden_out,
+        attended_out,
+        act_out,
+        gate_out,
+        up_out,
+        gain_grad,
+        middle_grad,
+        send,
+        hidden,
+        total,
+        back,
+        output,
+        pair_s,
+        w_down,
+    ) = refs[8:]
     step = pl.program_id(0)
+    core, chip, z = where[0], where[1], where[2]
+    gain = gains[1:2, :]
+    sides = [
+        by_chip(*blocks) + (half,)
+        for blocks, half in ((blocks_own, core), (blocks_other, 1 - core))
+    ]
+
+    def fill(which, begin):
+        for side in sides:
+            for m in range(4):
+                for k in range(4):
+                    rows = pl.ds(aligned(lax.rem(z + m, 4) * 192 + (chip ^ k) * 48), 48)
+                    for j in range(2):
+                        take = pl.ds(aligned((2 * step + j) * 48 - begin), 48)
+                        pair_s[side[2], rows, j * 128 : (j + 1) * 128] = side[which][k][m, take, :]
+
+    @pl.when(step < 7)
+    def _():
+        fill(0, 0)
+
+    @pl.when(step == 7)
+    def _():
+        fill(1, CUT)
+
+    m = lax.rem(step // 2 - z + 4, 4)
+    for k in range(4):
+        yx = chip ^ k
+
+        @pl.when(yx // 2 == lax.rem(step, 2))
+        def _():
+            rows = pl.ds(aligned(lax.rem(yx, 2) * 128), 128)
+            for _, lower, half in sides:
+                for j in range(3):
+                    begin = 768 + j * 128 - CUT
+                    w_down[rows, pl.ds(aligned(half * 384 + j * 128, 128), 128)] = lower[k][
+                        m, begin : begin + 128, :
+                    ]
+
     groups = HEADS // pairs
     wide_ = pairs * HD
-    half = came.shape[1]
+    half = came.shape[2]
 
     @pl.when(step == 0)
     def _():
+        for _, lower, side in sides:
+            for m in range(4):
+                for k in range(4):
+                    rows = pl.ds(aligned(lax.rem(z + m, 4) * 192 + (chip ^ k) * 48), 48)
+                    for j in range(3):
+                        begin = 1152 + j * 48 - CUT
+                        output[rows, pl.ds(aligned(side * 384 + j * 128, 128), 128)] = lower[k][
+                            m, begin : begin + 48, :
+                        ]
         for batch in range(2):
             at = slice(batch * half, (batch + 1) * half)
-            rows = jnp.concatenate([came[batch * groups + g] for g in range(groups)], axis=1)
+            parts = []
+            for h in range(half // 128):
+                lanes = slice(h * 128, (h + 1) * 128)
+                parts.append(
+                    jnp.concatenate(
+                        [swap(came[batch * groups + g, :, lanes]) for g in range(groups)], axis=1
+                    )
+                )
+            rows = jnp.concatenate(parts, axis=0)
             attended_out[at, :] = rows
             x = start[at, :] + mm(rows, output[...])
             total[at, :] = x
             middle_grad[at, :] = x
             normed, _ = unit_rows(x)
-            low = (normed * gain[...]).astype(BF)
+            low = (normed * gain).astype(BF)
             hidden[at, :] = low
             hidden_out[at, :] = low
         back[...] = jnp.zeros_like(back)
 
     for batch in range(2):
         at = slice(batch * half, (batch + 1) * half)
-        gate = mm(hidden[at, :], w_gate[...])
-        up = mm(hidden[at, :], w_up[...])
+        gate = mm(hidden[at, :], pair_s[0])
+        up = mm(hidden[at, :], pair_s[1])
         sigmoid = jax.nn.sigmoid(gate)
         swish = gate * sigmoid
         act = (swish * up).astype(BF)
@@ -1054,7 +1092,7 @@
         up_grad = (grad * swish).astype(BF)
         gate_out[at, :] = gate_grad
         up_out[at, :] = up_grad
-        back[at, :] += mm(gate_grad, w_gate[...], NT) + mm(up_grad, w_up[...], NT)
+        back[at, :] += mm(gate_grad, pair_s[0], NT) + mm(up_grad, pair_s[1], NT)
 
     @pl.when(step == pl.num_programs(0) - 1)
     def _():
@@ -1065,22 +1103,24 @@
             normed, inverse = unit_rows(middle_grad[at, :])
             grad = back[at, :]
             gains += jnp.sum(grad * normed, axis=0, keepdims=True)
-            weighted = grad * gain[...]
+            weighted = grad * gain
             grad = upstream[at, :].astype(F32) + inverse * (
                 weighted - normed * jnp.mean(weighted * normed, axis=-1, keepdims=True)
             )
             middle_grad[at, :] = grad
-            heads = mm(grad.astype(BF), output[...], NT).astype(BF)
+            heads = mm(output[...], grad.astype(BF), NT).astype(BF)
             for g in range(groups):
-                send[batch * groups + g] = heads[:, g * wide_ : (g + 1) * wide_]
+                send[batch * groups + g] = heads[g * wide_ : (g + 1) * wide_, :]
         gain_grad[...] = gains
 
 
-def mlp(pairs, came, start, output, gain, upstream, expand, contract):
+def mlp(pairs, where, came, start, gains, upstream, *blocks):
     tokens = start.shape[0]
     width = 256
     steps = FF // width
-    whole = lambda *shape: pl.BlockSpec(shape, lambda i: (0,) * len(shape))
+    whole = lambda shape: pl.BlockSpec(
+        shape, lambda i: (0,) * len(shape), pipeline_mode=pl.Buffered(1)
+    )
     column = pl.BlockSpec((tokens, width), lambda i: (0, i))
     return pl.pallas_call(
         functools.partial(mlp_kernel, pairs),
@@ -1096,42 +1136,64 @@
             jax.ShapeDtypeStruct((tokens, D), F32),
             jax.ShapeDtypeStruct(came.shape, BF),
         ),
-        in_specs=[
-            whole(*came.shape),
-            whole(tokens, D),
-            whole(D, D),
-            whole(1, D),
-            whole(tokens, D),
-            pl.BlockSpec((D, width), lambda i: (0, i)),
-            pl.BlockSpec((D, width), lambda i: (0, steps + i)),
-            pl.BlockSpec((width, D), lambda i: (i, 0)),
-        ],
+        in_specs=[smem()] + [whole(x.shape) for x in (came, start, gains, upstream, *blocks)],
         out_specs=(
-            whole(tokens, D),
-            whole(tokens, D),
-            whole(tokens, D),
+            whole((tokens, D)),
+            whole((tokens, D)),
+            whole((tokens, D)),
             column,
             column,
             column,
-            whole(1, D),
-            whole(tokens, D),
-            whole(*came.shape),
+            whole((1, D)),
+            whole((tokens, D)),
+            whole(came.shape),
         ),
         scratch_shapes=[
             pltpu.VMEM((tokens, D), BF),
             pltpu.VMEM((tokens, D), F32),
             pltpu.VMEM((tokens, D), F32),
+            pltpu.VMEM((D, D), BF),
+            pltpu.VMEM((2, D, width), BF),
+            pltpu.VMEM((width, D), BF),
         ],
-        compiler_params=params(48),
+        compiler_params=params(40),
         cost_estimate=cost(23),
         name="mlp",
-    )(came, start, output, gain, upstream, expand, expand, contract)
+    )(where, came, start, gains, upstream, *blocks)
+
+
+UPPER, LOWER, ALONG = (1, 3, 2, 0), (2, 3, 1, 0), (1, 3, 2, 0)
+
+
+def placed(order, value):
+    at = jnp.int32(3)
+    for place_, here in enumerate(order[:3]):
+        at = jnp.where(value == here, place_, at)
+    return at
 
 
 def weight_grads_kernel(
-    where, hidden, gate, up, act, upstream, attended, middle, own, other, wide_s, tall_s, out_s
+    where,
+    hidden,
+    gate,
+    up,
+    act,
+    upstream,
+    attended,
+    middle,
+    own_u,
+    own_l,
+    other_u,
+    other_l,
+    wide_s,
+    tall_s,
+    out_s,
 ):
     core, chip, z = where[0], where[1], where[2]
+    sides = ((own_u, own_l, core), (other_u, other_l, 1 - core))
+
+    def rows_of(k, m):
+        return pl.ds(aligned((z ^ m) * 192 + (chip ^ k) * 48), 48)
 
     def chunk(c, _):
         at = pl.ds(aligned(c * 256, 256), 256)
@@ -1140,48 +1202,61 @@
         tall = mm(act[:, at], upstream[...], TN).astype(BF)
         tall_s[0] = tall[:, :384]
         tall_s[1] = tall[:, 384:]
-        for out, half in ((own, core), (other, 1 - core)):
-            for m in range(4):
-                zz = lax.rem(z + m, 4)
-                for k in range(4):
-                    block = wide_s[half, pl.ds(aligned(zz * 192 + (chip ^ k) * 48), 48), :]
-                    for j in range(2):
-                        to = pl.ds(aligned((2 * c + j) * 48), 48)
-                        out[k, m, to, :] = block[:, j * 128 : (j + 1) * 128]
-            m = lax.rem(c // 2 - z + 4, 4)
+
+        def put(which, ks, begin):
+            for side in sides:
+                for i, m in enumerate(ALONG):
+                    for n, k in enumerate(ks):
+                        block = wide_s[side[2], rows_of(k, m), :]
+                        for j in range(2):
+                            to = pl.ds(aligned((2 * c + j) * 48 - begin), 48)
+                            side[which][n, i, to, :] = block[:, j * 128 : (j + 1) * 128]
+
+        @pl.when(c < 7)
+        def _():
+            put(0, UPPER, 0)
+
+        @pl.when(c == 7)
+        def _():
+            put(1, LOWER, CUT)
+
+        i = placed(ALONG, (c // 2) ^ z)
+        for _, lower, half in sides:
             for b in range(2):
-                k = (lax.rem(c, 2) * 2 + b) ^ chip
+                n = placed(LOWER, (lax.rem(c, 2) * 2 + b) ^ chip)
                 block = tall_s[half, b * 128 : (b + 1) * 128, :]
                 for j in range(3):
-                    out[k, m, 768 + j * 128 : 896 + j * 128, :] = block[:, j * 128 : (j + 1) * 128]
+                    begin = 768 + j * 128 - CUT
+                    lower[n, i, begin : begin + 128, :] = block[:, j * 128 : (j + 1) * 128]
         return 0
 
     lax.fori_loop(0, FF // 256, chunk, 0)
     square = mm(attended[...], middle[...].astype(BF), TN).astype(BF)
     out_s[0] = square[:, :384]
     out_s[1] = square[:, 384:]
-    for out, half in ((own, core), (other, 1 - core)):
-        for m in range(4):
-            zz = lax.rem(z + m, 4)
-            for k in range(4):
-                block = out_s[half, pl.ds(aligned(zz * 192 + (chip ^ k) * 48), 48), :]
+    for _, lower, half in sides:
+        for i, m in enumerate(ALONG):
+            for n, k in enumerate(LOWER):
+                block = out_s[half, rows_of(k, m), :]
                 for j in range(3):
-                    out[k, m, 1152 + j * 48 : 1200 + j * 48, :] = block[:, j * 128 : (j + 1) * 128]
+                    begin = 1152 + j * 48 - CUT
+                    lower[n, i, begin : begin + 48, :] = block[:, j * 128 : (j + 1) * 128]
 
 
 def weight_grads(where, *operands):
-    shape = jax.ShapeDtypeStruct((4, 4, 1296, 128), BF)
+    upper = jax.ShapeDtypeStruct((4, 4, CUT, 128), BF)
+    lower = jax.ShapeDtypeStruct((4, 4, 1296 - CUT, 128), BF)
     return pl.pallas_call(
         weight_grads_kernel,
-        out_shape=(shape, shape),
+        out_shape=(upper, lower) * 2,
         in_specs=[smem()] + [vmem()] * 7,
-        out_specs=(vmem(),) * 2,
+        out_specs=(vmem(),) * 4,
         scratch_shapes=[
             pltpu.VMEM((2, D, 256), BF),
             pltpu.VMEM((2, 256, 384), BF),
             pltpu.VMEM((2, D, 384), BF),
         ],
-        compiler_params=params(48),
+        compiler_params=params(60),
         cost_estimate=cost(15),
         name="weight_grads",
     )(where, *operands)
@@ -1210,19 +1285,21 @@
     gain_s,
 ):
     core, chip, z = where[0], where[1], where[2]
-    widths = [(ref, ref.shape[2] // 3) for ref in (came_a, came_b)]
-    groups = D // sum(w for _, w in widths)
-    rows = came_a.shape[1]
+    widths = [ref.shape[1] // 3 for ref in (came_a, came_b)]
+    groups = D // sum(widths)
+    rows = came_a.shape[2]
     tokens = 2 * rows
-    for batch in range(2):
+    for i in range(tokens // 128):
+        batch, lanes = divmod(i * 128, rows)
+        lanes = slice(lanes, lanes + 128)
+        parts = [
+            (swap(ref[batch * groups + g, :, lanes]), w)
+            for g in range(groups)
+            for ref, w in zip((came_a, came_b), widths)
+        ]
         for t in range(3):
-            parts = [
-                ref[batch * groups + g, :, t * w : (t + 1) * w]
-                for g in range(groups)
-                for ref, w in widths
-            ]
-            df_s[batch * rows : (batch + 1) * rows, t * D : (t + 1) * D] = jnp.concatenate(
-                parts, axis=1
+            df_s[i * 128 : (i + 1) * 128, t * D : (t + 1) * D] = jnp.concatenate(
+                [part[:, t * w : (t + 1) * w] for part, w in parts], axis=1
             )
 
     def kind(t, _):
@@ -1231,7 +1308,7 @@
         half_s[1] = grad[:, 384:]
         for out, half in ((own, core), (other, 1 - core)):
             for m in range(4):
-                zz = lax.rem(z + m, 4)
+                zz = z ^ m
                 for k in range(4):
                     block = half_s[half, pl.ds(aligned(zz * 192 + (chip ^ k) * 48), 48), :]
                     for j in range(3):
@@ -1248,7 +1325,7 @@
         grad = mm(df_s[at, :], joined[...], NT)
         normed, inverse = unit_rows(start[at, :])
         gains += jnp.sum(grad * normed, axis=0, keepdims=True)
-        weighted = grad * gain[...]
+        weighted = grad * gain[0:1, :]
         grad = middle[at, :] + inverse * (
             weighted - normed * jnp.mean(weighted * normed, axis=-1, keepdims=True)
         )
@@ -1265,7 +1342,7 @@
         gain_s[half] = jnp.concatenate(parts + [jnp.zeros((42, 128), F32)], axis=0).astype(BF)
     for out, half in ((own, core), (other, 1 - core)):
         for m in range(4):
-            zz = lax.rem(z + m, 4)
+            zz = z ^ m
             for k in range(4):
                 yx = chip ^ k
 
@@ -1551,19 +1628,25 @@
     along = spread_fsdp(first)
     column = jnp.stack([p[:144] for p in along])
     tail = jnp.stack([p[144:] for p in along])
-    blocks = [over_ctx(column, 2 * k) for k in range(1, 4)]
+    upper, lower = column[:, :80], column[:, 80:]
+    near = [over_ctx(upper, 2), over_ctx(lower, 4)]
     codes = jnp.stack([asked[:, :capacity].reshape(-1), asked[:, capacity:].reshape(-1)], axis=1)
     answer = read_rows(
         after(codes, column, tail), in_hbm(bigram_table.T), in_hbm(trigram_table.T)
     )
+    ready = after(second, column)
+    along = [along_fsdp(ready, k) for k in (1, 2, 3)]
+    answer, near, along = lax.optimization_barrier((answer, near, along))
     got = exchange(answer.reshape(devices, capacity, 2 * E), both)
-    own = jnp.stack([after(block, answer) for block in [column] + blocks])
-    joined, lookup, gains = assemble_first(
-        where, own, over_ctx(own, 1), tail, over_ctx(tail, 1)
-    )
-    second_column = jnp.stack(spread_fsdp(after(second, own)))
-    gains = gains[:, :2, :192].astype(F32).transpose(1, 0, 2).reshape(2, D)
-    first_gain, second_gain = gains[0:1], gains[1:2]
+    first_near = [jnp.stack([upper, near[0]]), jnp.stack([lower, near[1]])]
+    first_far = [over_ctx(first_near[0], 4), over_ctx(first_near[1], 2)]
+    first_own = first_near + first_far
+    first_other = [over_ctx(block, 1) for block in first_own]
+    first_blocks = (*first_own, *first_other, tail, over_ctx(tail, 1))
+    along = [second] + [after(along[k], first_far) for k in (2, 1, 0)]
+    upper = jnp.stack([block[:CUT] for block in along])
+    lower = jnp.stack([block[CUT:] for block in along])
+    near = [over_ctx(upper, 2), over_ctx(lower, 4)]
     got = got.reshape(devices * capacity, 2 * E)
 
     order = jnp.sum(
@@ -1578,28 +1661,29 @@
     frequency = jnp.exp(-math.log(10000.0) * (2.0 * jnp.arange(HD // 2, dtype=F32) / HD))
     angles = frequency[:, None] * jnp.arange(length, dtype=F32)[None, :]
     cos_t, sin_t = lax.optimization_barrier((jnp.cos(angles), jnp.sin(angles)))
-    cos, sin = cos_t.T, sin_t.T
-
-    start, embedded, hidden_first, sent = front(
+
+    start, embedded, hidden_first, sent, joined, lookup, gains = front(
         pairs,
         contexts,
+        where,
         starts,
         got,
         target_col,
         token_embed.reshape(tokens, D),
-        lookup,
-        first_gain,
-        joined,
-        cos,
-        sin,
-    )
-    rows = exchange(sent, "ctx").reshape(length, 3 * pairs * HD)
-    second_column = after(second_column, rows)
-    blocks = [over_ctx(second_column, 2 * k) for k in range(1, 4)]
+        cos_t,
+        sin_t,
+        *first_blocks,
+    )
+    sent, near = lax.optimization_barrier((sent, near))
+    rows = exchange(sent, "ctx")
+    near_x, near_y = jnp.stack([upper, near[0]]), jnp.stack([lower, near[1]])
+    rows, near_x, near_y = lax.optimization_barrier((rows, near_x, near_y))
+    far_y, far_x = over_ctx(near_x, 4), over_ctx(near_y, 2)
+    others = [over_ctx(near_x, 1), over_ctx(near_y, 1)]
     attended_rows, attended_t, logsum = attend_short(order, rows, pairs, piece)
-    came = exchange(attended_rows.reshape(contexts, local_rows, pairs * HD), "ctx")
-    own = jnp.stack([after(block, attended_rows) for block in [second_column] + blocks])
-    expand, contract, output = assemble_second(where, own, over_ctx(own, 1))
+    came = exchange(attended_rows, "ctx")
+    far_y, far_x = after((far_y, far_x), attended_rows)
+    others += [over_ctx(far_y, 1), over_ctx(far_x, 1)]
     upstream = cotangent.reshape(tokens, D)
     (
         result,
@@ -1611,23 +1695,33 @@
         second_gain_term,
         middle_grad,
         sent,
-    ) = mlp(pairs, came, start, output, second_gain, upstream, expand, contract)
-
-    grad_rows = exchange(sent, "ctx").reshape(length, pairs * HD)
-    own_m, other_m = weight_grads(
+    ) = mlp(pairs, where, came, start, gains, upstream, near_x, near_y, far_y, far_x, *others)
+
+    grad_rows = exchange(sent, "ctx")
+    own_u, own_l, other_u, other_l = weight_grads(
         where, hidden_second, gate_grad, up_grad, activated, upstream, attended, middle_grad
     )
-    from_core = over_ctx(after(other_m, grad_rows), 1)
+    other_u, other_l = after((other_u, other_l), grad_rows)
+    core_u, core_l = over_ctx(other_u, 1), over_ctx(other_l, 1)
     part = functools.partial(attend_grad_short, order)
-    shared = (attended_t, logsum, cos, sin, cos_t, sin_t, pairs, piece)
+    shared = (attended_t, logsum, cos_t, sin_t, pairs, piece)
     grad_a = part(rows, grad_rows, *shared, 0, 1)
-    came_a = exchange(grad_a.reshape(contexts, local_rows, 3 * HD), "ctx")
-    half_m = add_cores(own_m, after(from_core, grad_a))
-    from_chips = [over_ctx(half_m[k], 2 * k) for k in (1, 2)]
-    grad_b = part(after(rows, half_m), grad_rows, *shared, 1, pairs - 1)
-    grad_b = after(grad_b, from_chips)
-    from_chips.append(over_ctx(after(half_m[3], grad_b), 6))
-    came_b = exchange(grad_b.reshape(contexts, local_rows, 3 * (pairs - 1) * HD), "ctx")
+    came_a = exchange(grad_a, "ctx")
+    core_u, core_l = after((core_u, core_l), grad_a)
+    near_u = add_all(own_u[:2], core_u[:2]).astype(BF)
+    near_l = add_all(own_l[:2], core_l[:2]).astype(BF)
+    from_x, from_y = over_ctx(near_u, 2), over_ctx(near_l, 4)
+    grad_b = part(after(rows, near_u, near_l), grad_rows, *shared, 1, pairs - 1)
+    grad_b, came_a, from_x, from_y = lax.optimization_barrier((grad_b, came_a, from_x, from_y))
+    far_u = add_all(own_u[2], core_u[2], from_x[1]).astype(BF)
+    far_l = add_all(own_l[2], core_l[2], from_y[1]).astype(BF)
+    from_far = [over_ctx(far_u, 4), over_ctx(far_l, 2)]
+    came_b = exchange(grad_b, "ctx")
+    came_b, from_far = lax.optimization_barrier((came_b, from_far))
+    sums_u = add_all(own_u[3], core_u[3], from_x[0], from_far[0]).astype(BF)
+    sums_l = add_all(own_l[3], core_l[3], from_y[0], from_far[1]).astype(BF)
+    from_z = over_fsdp(jnp.concatenate([sums_u[:2], sums_l[:2]], axis=1), 1)
+    total_m = jnp.concatenate([sums_u[2:], sums_l[2:]], axis=1)
     start_grad, send, own_j, other_j = back_pass(
         devices * capacity,
         where,
@@ -1638,32 +1732,38 @@
         middle_grad,
         joined,
         lookup,
-        first_gain,
+        gains,
         second_gain_term,
         embedded,
         target_row,
     )
     from_core = over_ctx(other_j, 1)
     arrived = exchange(send.reshape(devices, capacity, 2 * E), both)
-    total_m = add_blocks(half_m[0], [after(block, own_j) for block in from_chips])
-    from_fsdp_m = to_fsdp(total_m)
-    half_j = add_cores(own_j, after(from_core, total_m))
-    total_j = add_blocks(half_j[0], to_chips(half_j))
-    from_fsdp_j = to_fsdp(total_j)
-    piece_m = add_blocks(total_m[0], [after(block, total_j) for block in from_fsdp_m])
-    every_m = to_chips([piece_m] * 4)
+    half_j = add_cores(own_j, from_core)
+    from_chips = to_chips(half_j)
+    from_z, kept = lax.optimization_barrier((from_z, half_j[0]))
+    near_m, far_m = add_blocks(total_m[1], [from_z[0]]), add_blocks(total_m[0], [from_z[1]])
+    from_z = over_fsdp(far_m, 2)
+    total_j = add_blocks(kept, from_chips)
+    from_fsdp = [over_fsdp(total_j[m], m) for m in (1, 2, 3)]
+    from_z, kept = lax.optimization_barrier((from_z, total_j[0]))
+    piece_m = add_blocks(near_m, [from_z])
+    every_m = [over_ctx(piece_m, 2 * k) for k in (1, 2)]
+    late_codes, kept, piece_m = lax.optimization_barrier((codes, kept, piece_m))
     bigram_grad, trigram_grad = add_rows(
-        after(codes, total_j, piece_m), arrived.reshape(devices * capacity, 2 * E), table_rows
-    )
-    piece_j = add_blocks(total_j[0], [after(block, bigram_grad) for block in from_fsdp_j])
+        late_codes, arrived.reshape(devices * capacity, 2 * E), table_rows
+    )
+    bigram_grad, from_fsdp = lax.optimization_barrier((bigram_grad, from_fsdp))
+    piece_j = add_blocks(kept, from_fsdp)
     every_j = to_chips([piece_j] * 4)
-    blocks_m = jnp.stack([piece_m] + [after(block, piece_j) for block in every_m])
+    piece_j, piece_m = lax.optimization_barrier((piece_j, piece_m))
+    every_m.append(over_ctx(piece_m, 6))
+    every_m, every_j = lax.optimization_barrier((every_m, every_j))
+    blocks_m = jnp.stack([piece_m] + every_m)
     other_m = over_ctx(blocks_m, 1)
-    blocks_j = jnp.stack([piece_j] + [after(block, blocks_m) for block in every_j])
+    blocks_j = jnp.stack([piece_j] + every_j)
     other_j = over_ctx(blocks_j, 1)
-    expand_grad, contract_grad, output_grad = unpack_second(
-        where, blocks_m, after(other_m, blocks_j)
-    )
+    expand_grad, contract_grad, output_grad = unpack_second(where, blocks_m, other_m)
     joined_grad, lookup_grad, gain_grads = unpack_first(where, blocks_j, other_j)
     gain_share = lax.dynamic_slice_in_dim(
         gain_grads[:, :6].reshape(2, D), z * (D // shards), D // shards, axis=1

time: 508 us -> 452 us (0.89)
  local copies, waits for them, and re-layouts: 55.2 us -> 20.4 us
  waiting for transfers between devices: 166 us -> 144 us
  blocking collectives: 0 us -> 15 us
  Pallas kernels: 173 us -> 163 us
  starting transfers between devices: 83.1 us -> 74.1 us
  other arithmetic: 21 us -> 27.4 us
    ppermute x12 -> x6, waiting for transfers between devices: 36.7 us -> 0.02 us  [along_fsdp(): lax.ppermute(value, 'fsdp', [(i, (i + shift) % size) for i in range(size)])]
    unnamed x104 -> x86, local copies, waits for them, and re-layouts: 34.4 us -> 14.6 us
    ppermute x0 -> x5, waiting for transfers between devices: none -> 19.4 us  [over_fsdp(): return lax.ppermute(value, 'fsdp', [(i, i ^ mask) for i in range(4)])]
    ppermute x12 -> x6, starting transfers between devices: 29.4 us -> 10.9 us  [along_fsdp(): lax.ppermute(value, 'fsdp', [(i, (i + shift) % size) for i in range(size)])]
    all_to_all x0 -> x1, blocking collectives: none -> 15 us  [exchange(): return lax.all_to_all(values, axes, split_axis=0, concat_axis=0, tiled=True)]
    convert_element_type x0 -> x6, other arithmetic: none -> 13.5 us  [the longest x1 3.26 us: local_packed(): near_l = add_all(own_l[:2], core_l[:2]).astype(BF)]
    pallas_call x2, Pallas kernels: 46.9 us -> 36.8 us  [attend_grad_short(): pl.pallas_call(functools.partial(attend_grad_short_kernel, pairs, begin,...]
    all_to_all x8 -> x7, waiting for transfers between devices: 52 us -> 43.5 us  [exchange(): return lax.all_to_all(values, axes, split_axis=0, concat_axis=0, tiled=True)]
  transfers between devices with their start and end apart: 45 -> 53, of which waited for: 16 -> 16; matrix products, arithmetic and copies ran while one was open for 5% -> 7% of each run, Pallas kernels for 26% -> 27%
where the time goes in v3:
time: 452 us; the launch traced here: 445 us
  Pallas kernels  163 us (36%)
  waiting for transfers between devices  144 us (32%)
  starting transfers between devices  74.1 us (16%)
  other arithmetic  27.4 us (6%)
  local copies, waits for them, and re-layouts  20.4 us (5%)
  blocking collectives  15 us (3%)
    ppermute x35, waiting for transfers between devices, over_ctx(): return lax.ppermute(value, 'ctx', [(i, i ^ mask) for i in range(size)])  80.9 us
    all_to_all x7, waiting for transfers between devices, exchange(): return lax.all_to_all(values, axes, split_axis=0, concat_axis=0, tiled=True)  43.5 us
    pallas_call x2, Pallas kernels, attend_grad_short(): pl.pallas_call(functools.partial(attend_grad_short_kernel, pairs, begin,...  36.8 us
    all_to_all x7, starting transfers between devices, exchange(): return lax.all_to_all(values, axes, split_axis=0, concat_axis=0, tiled=True)  28.3 us
    ppermute x35, starting transfers between devices, over_ctx(): return lax.ppermute(value, 'ctx', [(i, i ^ mask) for i in range(size)])  28.1 us
    pallas_call x1, Pallas kernels, mlp(): pl.pallas_call(functools.partial(mlp_kernel, pairs), grid=(steps,), out_s...  25.2 us
    ppermute x5, waiting for transfers between devices, over_fsdp(): return lax.ppermute(value, 'fsdp', [(i, i ^ mask) for i in range(4)])  19.4 us
    pallas_call x1, Pallas kernels, read_rows(): pl.pallas_call(read_rows_kernel, grid=(rows // width,), out_shape=jax.Sha...  18.2 us
  transfers between devices with their start and end apart: 53, of which 16 were waited for; matrix products, arithmetic and copies ran while one was open for 7% of the time, Pallas kernels for 27%

profile of v3, /device:TPU:0, one launch (start us, length us, event | category | flops | bytes accessed | tf_op | source)
XLA Modules:
  0.0 445.1 jit_solution(2446515116617388096)
XLA Ops:
  4.9 3.1 collective-permute-start.2
  7.9 2.6 collective-permute-start.1
  11.9 2.9 all-to-all-start
  14.9 11.7 %all-to-all-done = s32[32,1,64]{2,1,0:T(1,128)S(1)} async-done(((s32[32,1,64]{2,1,0:T(1,128)}), s32[32,1,64]{2,1,0:T(1,128)S(1)}, u32[]{:S(2)}, u32[]{:S(2)}) %all-to-all-start) | async-done | bytes 8224 | tf_op jit(solution)/shard_map/all_to_all | solution.py:702
  36.1 18.2 %read_rows.1 = bf16[1024,384]{1,0:T(8,128)(2,1)} custom-call(s32[1024,2]{1,0:T(8,128)S(1)} %copy.35.codes, bf16[192,12800]{1,0:T(8,128)(2,1)} %bitcast.144, bf16[192,12800]{1,0:T(8,128)(2,1)} %bitcast.145), custom_call_target="tpu_custom_call" | custom-call | flops 10200000512 | bytes 42500000 | tf_op jit(solution)/shard_map/read_rows/pallas_call | solution.py:151
  59.6 6.4 %all-to-all-start.1 = ((bf16[32,32,384]{2,1,0:T(8,128)(2,1)}), bf16[32,32,384]{2,1,0:T(8,128)(2,1)S(1)}, u32[]{:S(2)}, u32[]{:S(2)}) async-start(bf16[32,32,384]{2,1,0:T(8,128)(2,1)} %bitcast.17), calls=%async_computation.1 | async-start | bytes 1572864 | tf_op jit(solution)/shard_map/all_to_all | solution.py:702
  66.3 5.6 %collective-permute-done.8.refs_2_ = bf16[2,4,80,384]{3,2,1,0:T(8,128)(2,1)} collective-permute-done((bf16[2,4,80,384]{3,2,1,0:T(8,128)(2,1)}, bf16[2,4,80,384]{3,2,1,0:T(8,128)(2,1)}, u32[]{:S(2)}, u32[]{:S(2)}) %collective-permute-start.8) | collective-permute-done | bytes 491552 | tf_op jit(solution)/shard_map/ppermute | solution.py:596
  74.3 2.6 collective-permute-start.16
  76.9 1.9 fusion.12
  79.4 6.2 %all-to-all-done.1 = bf16[32,32,384]{2,1,0:T(8,128)(2,1)S(1)} async-done(((bf16[32,32,384]{2,1,0:T(8,128)(2,1)}), bf16[32,32,384]{2,1,0:T(8,128)(2,1)S(1)}, u32[]{:S(2)}, u32[]{:S(2)}) %all-to-all-start.1) | async-done | bytes 786464 | tf_op jit(solution)/shard_map/all_to_all | solution.py:702
  86.5 13.2 %front.1 = (f32[512,768]{1,0:T(8,128)}, bf16[512,192]{1,0:T(8,128)(2,1)}, bf16[512,768]{1,0:T(8,128)(2,1)}, bf16[8,576,256]{2,1,0:T(8,128)(2,1)}, bf16[768,2304]...) custom-call(s32[3]{0:T(128)} %copy-done.8, s32[2]{0:T(128)} %dynamic_slice.6.starts, ...), custom_call_target="tpu_custom_call" | custom-call | flops 5400000000 | bytes 22500000 | tf_op jit(solution)/shard_map/front/pallas_call | solution.py:959
  100.6 4.2 all-to-all-start.2
  104.9 2.5 pad_maximum_fusion.2.refs_1_
  108.6 25.6 %all-to-all-done.2.rows = bf16[8,576,256]{2,1,0:T(8,128)(2,1)S(1)} async-done(((bf16[8,576,256]{2,1,0:T(8,128)(2,1)}), bf16[8,576,256]{2,1,0:T(8,128)(2,1)S(1)}, u32[]{:S(2)}, u32[]{:S(2)}) %all-to-all-start.2) | async-done | bytes 2359328 | tf_op jit(solution)/shard_map/all_to_all | solution.py:702
  135.9 17.5 %attend.1 = (bf16[8,192,256]{2,1,0:T(8,128)(2,1)S(1)}, f32[3,64,2048]{2,1,0:T(8,128)S(1)}, f32[3,1,2048]{2,1,0:T(1,128)S(1)}) custom-call(s32[16]{0:T(128)S(1)} %select_reduce_fusion.order, bf16[8,576,256]{2,1,0:T(8,128)(2,1)S(1)} %all-to-all-done.2.rows), custom_call_target="tpu_custom_call" | custom-call | flops 15000000512 | bytes 62500000 | tf_op jit(solution)/shard_map/attend/pallas_call | solution.py:464
  154.5 11.4 %collective-permute-done.18.refs_3_ = bf16[2,4,624,128]{3,2,1,0:T(8,128)(2,1)S(1)} collective-permute-done((bf16[2,4,624,128]{3,2,1,0:T(8,128)(2,1)}, bf16[2,4,624,128]{3,2,1,0:T(8,128)(2,1)S(1)}, u32[]{:S(2)}, u32[]{:S(2)}) %collective-permute-start.18) | collective-permute-done | bytes 1277984 | tf_op jit(solution)/shard_map/ppermute | solution.py:596
  166.6 15.0 %all_to_all.47.came = bf16[8,192,256]{2,1,0:T(8,128)(2,1)S(1)} all-to-all(bf16[8,192,256]{2,1,0:T(8,128)(2,1)S(1)} %get-tuple-element.127), channel_id=1, replica_groups=mesh['ctx'=8,'fsdp'=4] {'ctx'}, dimensions={0} | all-to-all | bytes 1572864 | tf_op jit(solution)/shard_map/all_to_all | solution.py:702
  181.6 25.2 %mlp.1 = (bf16[512,768]{1,0:T(8,128)(2,1)}, bf16[512,768]{1,0:T(8,128)(2,1)S(1)}, bf16[512,768]{1,0:T(8,128)(2,1)S(1)}, bf16[512,2048]{1,0:T(8,128)(2,1)}, bf16[...) custom-call(s32[3]{0:T(128)S(1)} %copy-done.9, ...), custom_call_target="tpu_custom_call" | custom-call | flops 13799999488 | bytes 57500000 | tf_op jit(solution)/shard_map/mlp/pallas_call | solution.py:1125
  209.6 3.8 all-to-all-start.4
  213.4 16.5 %weight_grads.1 = (bf16[4,4,672,128]{3,2,1,0:T(8,128)(2,1)}, bf16[4,4,624,128]{3,2,1,0:T(8,128)(2,1)}, bf16[4,4,672,128]{3,2,1,0:T(8,128)(2,1)}, bf16[4,4,624,128]{3,2,1,0:T(8,128)(2,1)}) custom-call(s32[3]{0:T(128)} %copy-done.8, bf16[512,768]{1,0:T(8,128)(2,1)} %copy-done.24, bf16[512,2048]{1,0:T(8,128)(2,1)} %get-tuple-element.136.gate, ...), custom_call_target="tpu_custom_call" | custom-call | flops 8999999488 | bytes 37500000 | tf_op jit(solution)/shard_map/weight_grads/pallas_call | solution.py:1249
  232.8 12.4 %attend_grad_0.1 = bf16[8,192,256]{2,1,0:T(8,128)(2,1)S(1)} custom-call(s32[16]{0:T(128)S(1)} %select_reduce_fusion.order, bf16[8,576,256]{2,1,0:T(8,128)(2,1)S(1)} %all-to-all-done.2.rows, bf16[8,192,256]{2,1,0:T(8,128)(2,1)S(1)} %all-to-all-done.4.grads, f32[3,64,2048]{2,1,0:T(8,128)S(1)} %copy-done.21, f32[3,1,2048]{2,1,0:T(1,128)S(1)} %get-tuple-element.148.logsum, ...), custom_call_target="tpu_custom_call" | custom-call | flops 8400000000 | bytes 35000000 | tf_op jit(solution)/shard_map/attend_grad_0/pallas_call | solution.py:582
  246.1 4.6 %all-to-all-start.5 = ((bf16[8,192,256]{2,1,0:T(8,128)(2,1)}), bf16[8,192,256]{2,1,0:T(8,128)(2,1)S(1)}, u32[]{:S(2)}, u32[]{:S(2)}) async-start(bf16[8,192,256]{2,1,0:T(8,128)(2,1)} %copy-done.3), calls=%async_computation.5 | async-start | bytes 1572864 | tf_op jit(solution)/shard_map/all_to_all | solution.py:702
  250.8 3.3 add_convert_fusion.1
  254.0 2.0 collective-permute-start.26
  256.1 2.9 add_convert_fusion
  260.4 24.4 %attend_grad_1.1 = bf16[8,384,256]{2,1,0:T(8,128)(2,1)} custom-call(s32[16]{0:T(128)S(1)} %select_reduce_fusion.order, bf16[8,576,256]{2,1,0:T(8,128)(2,1)} %copy-done, bf16[8,192,256]{2,1,0:T(8,128)(2,1)S(1)} %all-to-all-done.4.grads, f32[3,64,2048]{2,1,0:T(8,128)S(1)} %copy-done.22, f32[3,1,2048]{2,1,0:T(1,128)S(1)} %get-tuple-element.148.logsum, ...), custom_call_target="tpu_custom_call" | custom-call | flops 16800000000 | bytes 70000000 | tf_op jit(solution)/shard_map/attend_grad_1/pallas_call | solution.py:582
  284.9 5.0 %collective-permute-done.26 = bf16[2,4,624,128]{3,2,1,0:T(8,128)(2,1)} collective-permute-done((bf16[2,4,624,128]{3,2,1,0:T(8,128)(2,1)}, bf16[2,4,624,128]{3,2,1,0:T(8,128)(2,1)}, u32[]{:S(2)}, u32[]{:S(2)}) %collective-permute-start.26) | collective-permute-done | bytes 1277984 | tf_op jit(solution)/shard_map/ppermute | solution.py:596
  289.8 2.2 collective-permute-done.25
  292.1 3.8 all-to-all-start.6
  295.8 1.8 fusion.2
  297.6 2.0 collective-permute-start.27
  302.9 26.6 %collective-permute-done.28 = bf16[4,624,128]{2,1,0:T(8,128)(2,1)S(1)} collective-permute-done((bf16[4,624,128]{2,1,0:T(8,128)(2,1)S(1)}, bf16[4,624,128]{2,1,0:T(8,128)(2,1)S(1)}, u32[]{:S(2)}, u32[]{:S(2)}) %collective-permute-start.28) | collective-permute-done | bytes 639008 | tf_op jit(solution)/shard_map/ppermute | solution.py:596
  333.0 13.3 %back.1 = (f32[512,768]{1,0:T(8,128)}, bf16[1024,384]{1,0:T(8,128)(2,1)}, bf16[4,4,480,128]{3,2,1,0:T(8,128)(2,1)}, bf16[4,4,480,128]{3,2,1,0:T(8,128)(2,1)}) custom-call(s32[3]{0:T(128)S(1)} %copy-done.10, bf16[8,192,256]{2,1,0:T(8,128)(2,1)S(1)} %all-to-all-done.5.came_a, bf16[8,384,256]{2,1,0:T(8,128)(2,1)S(1)} %all-to-all-done.6.came_b, ...), custom_call_target="tpu_custom_call" | custom-call | flops 7800000000 | bytes 32500000 | tf_op jit(solution)/shard_map/back/pallas_call | solution.py:1372
  346.3 1.8 fusion.1
  348.2 2.1 fusion
  351.2 2.3 collective-permute-start.29
  353.5 2.6 all-to-all-start.7
  356.2 2.6 fusion.6
  362.3 13.9 %collective-permute-done.29 = bf16[2,1296,128]{2,1,0:T(8,128)(2,1)S(1)} collective-permute-done((bf16[2,1296,128]{2,1,0:T(8,128)(2,1)}, bf16[2,1296,128]{2,1,0:T(8,128)(2,1)S(1)}, u32[]{:S(2)}, u32[]{:S(2)}) %collective-permute-start.29) | collective-permute-done | bytes 663584 | tf_op jit(solution)/shard_map/ppermute | solution.py:780
  376.4 11.9 %collective-permute-done.33 = bf16[4,480,128]{2,1,0:T(8,128)(2,1)S(1)} collective-permute-done((bf16[4,480,128]{2,1,0:T(8,128)(2,1)S(1)}, bf16[4,480,128]{2,1,0:T(8,128)(2,1)S(1)}, u32[]{:S(2)}, u32[]{:S(2)}) %collective-permute-start.33) | collective-permute-done | bytes 491552 | tf_op jit(solution)/shard_map/ppermute | solution.py:596
  390.2 5.5 %collective-permute-done.31 = bf16[1296,128]{1,0:T(8,128)(2,1)S(1)} collective-permute-done((bf16[1296,128]{1,0:T(8,128)(2,1)S(1)}, bf16[1296,128]{1,0:T(8,128)(2,1)S(1)}, u32[]{:S(2)}, u32[]{:S(2)}) %collective-permute-start.31) | collective-permute-done | bytes 331808 | tf_op jit(solution)/shard_map/ppermute | solution.py:780
  398.0 3.1 collective-permute-start.36
  402.3 13.8 %add_rows.1 = (f32[192,12800]{1,0:T(8,128)}, f32[192,12800]{1,0:T(8,128)}) custom-call(s32[1024,2]{1,0:T(8,128)S(1)} %copy.36.codes, bf16[1024,384]{1,0:T(8,128)(2,1)S(1)} %bitcast.120), custom_call_target="tpu_custom_call" | custom-call | flops 8400000000 | bytes 35000000 | tf_op jit(solution)/shard_map/add_rows/pallas_call | solution.py:184
  419.8 8.5 %collective-permute-done.41 = bf16[480,128]{1,0:T(8,128)(2,1)S(1)} collective-permute-done((bf16[480,128]{1,0:T(8,128)(2,1)S(1)}, bf16[480,128]{1,0:T(8,128)(2,1)S(1)}, u32[]{:S(2)}, u32[]{:S(2)}) %collective-permute-start.41) | collective-permute-done | bytes 122912 | tf_op jit(solution)/shard_map/ppermute | solution.py:596
  429.3 4.8 %collective-permute-done.43 = bf16[480,128]{1,0:T(8,128)(2,1)S(1)} collective-permute-done((bf16[480,128]{1,0:T(8,128)(2,1)S(1)}, bf16[480,128]{1,0:T(8,128)(2,1)S(1)}, u32[]{:S(2)}, u32[]{:S(2)}) %collective-permute-start.43) | collective-permute-done | bytes 122912 | tf_op jit(solution)/shard_map/ppermute | solution.py:596
  435.0 3.1 collective-permute-done.44.other
  438.1 2.0 unpack_first.1
  440.8 4.1 unpack_second.1
  (216 shorter events, 61.0 us)
Async XLA Ops:
  4.9 21.9 %collective-permute-start.2 = (bf16[208,384]{1,0:T(8,128)(2,1)S(1)}, bf16[208,384]{1,0:T(8,128)(2,1)S(1)}, u32[]{:S(2)}, u32[]{:S(2)}) collective-permute-start(bf16[208,384]{1,0:T(8,128)(2,1)S(1)} %get-tuple-element.106), channel_id=1, source_target_pairs={{0,1},{1,2},{2,3},{3,0},{4,5},{5,6},{6,7},{7,4},{8,9},{9,10},{10,1... | collective-permute-start | bytes 479240 | tf_op jit(solution)/shard_map/ppermute | solution.py:601
  7.9 18.9 %collective-permute-start.1 = (bf16[208,384]{1,0:T(8,128)(2,1)S(1)}, bf16[208,384]{1,0:T(8,128)(2,1)S(1)}, u32[]{:S(2)}, u32[]{:S(2)}) collective-permute-start(bf16[208,384]{1,0:T(8,128)(2,1)S(1)} %get-tuple-element.106), channel_id=1, source_target_pairs={{0,2},{1,3},{2,0},{3,1},{4,6},{5,7},{6,4},{7,5},{8,10},{9,11},{10,... | collective-permute-start | bytes 479240 | tf_op jit(solution)/shard_map/ppermute | solution.py:601
  10.5 16.3 %collective-permute-start = (bf16[208,384]{1,0:T(8,128)(2,1)S(1)}, bf16[208,384]{1,0:T(8,128)(2,1)S(1)}, u32[]{:S(2)}, u32[]{:S(2)}) collective-permute-start(bf16[208,384]{1,0:T(8,128)(2,1)S(1)} %get-tuple-element.106), channel_id=1, source_target_pairs={{0,3},{1,0},{2,1},{3,2},{4,7},{5,4},{6,5},{7,6},{8,11},{9,8},{10,9... | collective-permute-start | bytes 479240 | tf_op jit(solution)/shard_map/ppermute | solution.py:601
  11.9 14.6 %all-to-all-start = ((s32[32,1,64]{2,1,0:T(1,128)}), s32[32,1,64]{2,1,0:T(1,128)S(1)}, u32[]{:S(2)}, u32[]{:S(2)}) async-start(s32[32,1,64]{2,1,0:T(1,128)} %bitcast.5), calls=%async_computation | async-start | bytes 32768 | tf_op jit(solution)/shard_map/all_to_all | solution.py:702
  27.6 26.7 %collective-permute-start.5 = (bf16[1296,128]{1,0:T(8,128)(2,1)S(1)}, bf16[1296,128]{1,0:T(8,128)(2,1)S(1)}, u32[]{:S(2)}, u32[]{:S(2)}) collective-permute-start(bf16[1296,128]{1,0:T(8,128)(2,1)S(1)} %get-tuple-element.109), channel_id=1, source_target_pairs={{0,1},{1,2},{2,3},{3,0},{4,5},{5,6},{6,7},{7,4},{8,9},{9,10},{10,1... | collective-permute-start | bytes 995336 | tf_op jit(solution)/shard_map/ppermute | solution.py:601
  28.2 26.1 %collective-permute-start.6 = (bf16[1296,128]{1,0:T(8,128)(2,1)S(1)}, bf16[1296,128]{1,0:T(8,128)(2,1)S(1)}, u32[]{:S(2)}, u32[]{:S(2)}) collective-permute-start(bf16[1296,128]{1,0:T(8,128)(2,1)S(1)} %get-tuple-element.109), channel_id=1, source_target_pairs={{0,2},{1,3},{2,0},{3,1},{4,6},{5,7},{6,4},{7,5},{8,10},{9,11},{10,... | collective-permute-start | bytes 995336 | tf_op jit(solution)/shard_map/ppermute | solution.py:601
  29.9 24.5 %collective-permute-start.7 = (bf16[1296,128]{1,0:T(8,128)(2,1)S(1)}, bf16[1296,128]{1,0:T(8,128)(2,1)S(1)}, u32[]{:S(2)}, u32[]{:S(2)}) collective-permute-start(bf16[1296,128]{1,0:T(8,128)(2,1)S(1)} %get-tuple-element.109), channel_id=1, source_target_pairs={{0,3},{1,0},{2,1},{3,2},{4,7},{5,4},{6,5},{7,6},{8,11},{9,8},{10,9... | collective-permute-start | bytes 995336 | tf_op jit(solution)/shard_map/ppermute | solution.py:601
  34.9 19.4 %collective-permute-start.3 = (bf16[4,80,384]{2,1,0:T(8,128)(2,1)S(1)}, bf16[4,80,384]{2,1,0:T(8,128)(2,1)S(1)}, u32[]{:S(2)}, u32[]{:S(2)}) collective-permute-start(bf16[4,80,384]{2,1,0:T(8,128)(2,1)S(1)} %get-tuple-element.218), channel_id=1, source_target_pairs={{0,8},{4,12},{8,0},{12,4},{16,24},{20,28},{24,16},{28,20},{1,9},{5... | collective-permute-start | bytes 737288 | tf_op jit(solution)/shard_map/ppermute | solution.py:596
  35.6 18.8 %collective-permute-start.4 = (bf16[4,64,384]{2,1,0:T(8,128)(2,1)S(1)}, bf16[4,64,384]{2,1,0:T(8,128)(2,1)S(1)}, u32[]{:S(2)}, u32[]{:S(2)}) collective-permute-start(bf16[4,64,384]{2,1,0:T(8,128)(2,1)S(1)} %get-tuple-element.216), channel_id=1, source_target_pairs={{0,16},{4,20},{8,24},{12,28},{16,0},{20,4},{24,8},{28,12},{1,17},{... | collective-permute-start | bytes 589832 | tf_op jit(solution)/shard_map/ppermute | solution.py:596
  55.2 10.8 %collective-permute-start.9 = (bf16[2,4,64,384]{3,2,1,0:T(8,128)(2,1)}, bf16[2,4,64,384]{3,2,1,0:T(8,128)(2,1)}, u32[]{:S(2)}, u32[]{:S(2)}) collective-permute-start(bf16[2,4,64,384]{3,2,1,0:T(8,128)(2,1)} %pad_maximum_fusion.9.refs_1_), channel_id=1, source_target_pairs={{0,8},{4,12},{8,0},{12,4},{16,24},{20,28},{24,16},{28,20},{1,9},{5... | collective-permute-start | bytes 1179656 | tf_op jit(solution)/shard_map/ppermute | solution.py:596
  57.5 14.4 %collective-permute-start.8 = (bf16[2,4,80,384]{3,2,1,0:T(8,128)(2,1)}, bf16[2,4,80,384]{3,2,1,0:T(8,128)(2,1)}, u32[]{:S(2)}, u32[]{:S(2)}) collective-permute-start(bf16[2,4,80,384]{3,2,1,0:T(8,128)(2,1)} %pad_maximum_fusion.6.refs_0_), channel_id=1, source_target_pairs={{0,16},{4,20},{8,24},{12,28},{16,0},{20,4},{24,8},{28,12},{1,17},{... | collective-permute-start | bytes 1474568 | tf_op jit(solution)/shard_map/ppermute | solution.py:596
  59.0 15.4 %collective-permute-start.14 = (bf16[4,64,384]{2,1,0:T(8,128)(2,1)}, bf16[4,64,384]{2,1,0:T(8,128)(2,1)}, u32[]{:S(2)}, u32[]{:S(2)}) collective-permute-start(bf16[4,64,384]{2,1,0:T(8,128)(2,1)} %pad_maximum_fusion.11.refs_8_), channel_id=1, source_target_pairs={{0,4},{4,0},{8,12},{12,8},{16,20},{20,16},{24,28},{28,24},{1,5},{5... | collective-permute-start | bytes 589832 | tf_op jit(solution)/shard_map/ppermute | solution.py:596
  59.1 17.8 %collective-permute-start.11 = (bf16[2,4,64,384]{3,2,1,0:T(8,128)(2,1)}, bf16[2,4,64,384]{3,2,1,0:T(8,128)(2,1)}, u32[]{:S(2)}, u32[]{:S(2)}) collective-permute-start(bf16[2,4,64,384]{3,2,1,0:T(8,128)(2,1)} %pad_maximum_fusion.9.refs_1_), channel_id=1, source_target_pairs={{0,4},{4,0},{8,12},{12,8},{16,20},{20,16},{24,28},{28,24},{1,5},{5... | collective-permute-start | bytes 1179656 | tf_op jit(solution)/shard_map/ppermute | solution.py:596
  59.6 19.8 %collective-permute-start.10 = (bf16[2,4,80,384]{3,2,1,0:T(8,128)(2,1)}, bf16[2,4,80,384]{3,2,1,0:T(8,128)(2,1)}, u32[]{:S(2)}, u32[]{:S(2)}) collective-permute-start(bf16[2,4,80,384]{3,2,1,0:T(8,128)(2,1)} %pad_maximum_fusion.6.refs_0_), channel_id=1, source_target_pairs={{0,4},{4,0},{8,12},{12,8},{16,20},{20,16},{24,28},{28,24},{1,5},{5... | collective-permute-start | bytes 1474568 | tf_op jit(solution)/shard_map/ppermute | solution.py:596
  59.6 26.0 %all-to-all-start.1 = ((bf16[32,32,384]{2,1,0:T(8,128)(2,1)}), bf16[32,32,384]{2,1,0:T(8,128)(2,1)S(1)}, u32[]{:S(2)}, u32[]{:S(2)}) async-start(bf16[32,32,384]{2,1,0:T(8,128)(2,1)} %bitcast.17), calls=%async_computation.1 | async-start | bytes 1572864 | tf_op jit(solution)/shard_map/all_to_all | solution.py:702
  66.0 13.3 %collective-permute-start.13 = (bf16[2,4,64,384]{3,2,1,0:T(8,128)(2,1)}, bf16[2,4,64,384]{3,2,1,0:T(8,128)(2,1)}, u32[]{:S(2)}, u32[]{:S(2)}) collective-permute-start(bf16[2,4,64,384]{3,2,1,0:T(8,128)(2,1)} %collective-permute-done.9.refs_3_), channel_id=1, source_target_pairs={{0,4},{4,0},{8,12},{12,8},{16,20},{20,16},{24,28},{28,24},{1,5},{5... | collective-permute-start | bytes 1179656 | tf_op jit(solution)/shard_map/ppermute | solution.py:596
  74.3 25.4 %collective-permute-start.16 = (bf16[4,624,128]{2,1,0:T(8,128)(2,1)}, bf16[4,624,128]{2,1,0:T(8,128)(2,1)}, u32[]{:S(2)}, u32[]{:S(2)}) collective-permute-start(bf16[4,624,128]{2,1,0:T(8,128)(2,1)} %get-tuple-element.210), channel_id=1, source_target_pairs={{0,16},{4,20},{8,24},{12,28},{16,0},{20,4},{24,8},{28,12},{1,17},{... | collective-permute-start | bytes 1916936 | tf_op jit(solution)/shard_map/ppermute | solution.py:596
  76.9 22.9 %collective-permute-start.15 = (bf16[4,672,128]{2,1,0:T(8,128)(2,1)S(1)}, bf16[4,672,128]{2,1,0:T(8,128)(2,1)S(1)}, u32[]{:S(2)}, u32[]{:S(2)}) collective-permute-start(bf16[4,672,128]{2,1,0:T(8,128)(2,1)S(1)} %get-tuple-element.206), channel_id=1, source_target_pairs={{0,8},{4,12},{8,0},{12,4},{16,24},{20,28},{24,16},{28,20},{1,9},{5... | collective-permute-start | bytes 2064392 | tf_op jit(solution)/shard_map/ppermute | solution.py:596
  100.6 33.6 %all-to-all-start.2 = ((bf16[8,576,256]{2,1,0:T(8,128)(2,1)}), bf16[8,576,256]{2,1,0:T(8,128)(2,1)S(1)}, u32[]{:S(2)}, u32[]{:S(2)}) async-start(bf16[8,576,256]{2,1,0:T(8,128)(2,1)} %get-tuple-element.123), calls=%async_computation.2 | async-start | bytes 4718592 | tf_op jit(solution)/shard_map/all_to_all | solution.py:702
  134.2 31.8 %collective-permute-start.17 = (bf16[2,4,672,128]{3,2,1,0:T(8,128)(2,1)}, bf16[2,4,672,128]{3,2,1,0:T(8,128)(2,1)S(1)}, u32[]{:S(2)}, u32[]{:S(2)}) collective-permute-start(bf16[2,4,672,128]{3,2,1,0:T(8,128)(2,1)} %pad_maximum_fusion.refs_0_), channel_id=1, source_target_pairs={{0,16},{4,20},{8,24},{12,28},{16,0},{20,4},{24,8},{28,12},{1,17},{... | collective-permute-start | bytes 4128776 | tf_op jit(solution)/shard_map/ppermute | solution.py:596
  135.3 46.3 %collective-permute-start.19 = (bf16[2,4,672,128]{3,2,1,0:T(8,128)(2,1)}, bf16[2,4,672,128]{3,2,1,0:T(8,128)(2,1)S(1)}, u32[]{:S(2)}, u32[]{:S(2)}) collective-permute-start(bf16[2,4,672,128]{3,2,1,0:T(8,128)(2,1)} %pad_maximum_fusion.refs_0_), channel_id=1, source_target_pairs={{0,4},{4,0},{8,12},{12,8},{16,20},{20,16},{24,28},{28,24},{1,5},{5... | collective-permute-start | bytes 4128776 | tf_op jit(solution)/shard_map/ppermute | solution.py:596
  135.3 30.7 %collective-permute-start.18 = (bf16[2,4,624,128]{3,2,1,0:T(8,128)(2,1)}, bf16[2,4,624,128]{3,2,1,0:T(8,128)(2,1)S(1)}, u32[]{:S(2)}, u32[]{:S(2)}) collective-permute-start(bf16[2,4,624,128]{3,2,1,0:T(8,128)(2,1)} %pad_maximum_fusion.2.refs_1_), channel_id=1, source_target_pairs={{0,8},{4,12},{8,0},{12,4},{16,24},{20,28},{24,16},{28,20},{1,9},{5... | collective-permute-start | bytes 3833864 | tf_op jit(solution)/shard_map/ppermute | solution.py:596
  166.0 15.6 %collective-permute-start.21 = (bf16[2,4,672,128]{3,2,1,0:T(8,128)(2,1)S(1)}, bf16[2,4,672,128]{3,2,1,0:T(8,128)(2,1)S(1)}, u32[]{:S(2)}, u32[]{:S(2)}) collective-permute-start(bf16[2,4,672,128]{3,2,1,0:T(8,128)(2,1)S(1)} %collective-permute-done.17.refs_2_), channel_id=1, source_target_pairs={{0,4},{4,0},{8,12},{12,8},{16,20},{20,16},{24,28},{28,24},{1,5},{5... | collective-permute-start | bytes 4128776 | tf_op jit(solution)/shard_map/ppermute | solution.py:596
  166.0 15.5 %collective-permute-start.20 = (bf16[2,4,624,128]{3,2,1,0:T(8,128)(2,1)S(1)}, bf16[2,4,624,128]{3,2,1,0:T(8,128)(2,1)S(1)}, u32[]{:S(2)}, u32[]{:S(2)}) collective-permute-start(bf16[2,4,624,128]{3,2,1,0:T(8,128)(2,1)S(1)} %copy-done.2), channel_id=1, source_target_pairs={{0,4},{4,0},{8,12},{12,8},{16,20},{20,16},{24,28},{28,24},{1,5},{5... | collective-permute-start | bytes 3833864 | tf_op jit(solution)/shard_map/ppermute | solution.py:596
  166.5 15.0 %collective-permute-start.22 = (bf16[2,4,624,128]{3,2,1,0:T(8,128)(2,1)S(1)}, bf16[2,4,624,128]{3,2,1,0:T(8,128)(2,1)S(1)}, u32[]{:S(2)}, u32[]{:S(2)}) collective-permute-start(bf16[2,4,624,128]{3,2,1,0:T(8,128)(2,1)S(1)} %collective-permute-done.18.refs_3_), channel_id=1, source_target_pairs={{0,4},{4,0},{8,12},{12,8},{16,20},{20,16},{24,28},{28,24},{1,5},{5... | collective-permute-start | bytes 3833864 | tf_op jit(solution)/shard_map/ppermute | solution.py:596
  209.6 20.4 %all-to-all-start.4 = ((bf16[8,192,256]{2,1,0:T(8,128)(2,1)}), bf16[8,192,256]{2,1,0:T(8,128)(2,1)S(1)}, u32[]{:S(2)}, u32[]{:S(2)}) async-start(bf16[8,192,256]{2,1,0:T(8,128)(2,1)} %copy-done.4), calls=%async_computation.4 | async-start | bytes 1572864 | tf_op jit(solution)/shard_map/all_to_all | solution.py:702
  229.9 20.8 %collective-permute-start.23 = (bf16[4,4,672,128]{3,2,1,0:T(8,128)(2,1)}, bf16[4,4,672,128]{3,2,1,0:T(8,128)(2,1)}, u32[]{:S(2)}, u32[]{:S(2)}) collective-permute-start(bf16[4,4,672,128]{3,2,1,0:T(8,128)(2,1)} %get-tuple-element.145), channel_id=1, source_target_pairs={{0,4},{4,0},{8,12},{12,8},{16,20},{20,16},{24,28},{28,24},{1,5},{5... | collective-permute-start | bytes 8257544 | tf_op jit(solution)/shard_map/ppermute | solution.py:596
  230.4 20.4 %collective-permute-start.24 = (bf16[4,4,624,128]{3,2,1,0:T(8,128)(2,1)}, bf16[4,4,624,128]{3,2,1,0:T(8,128)(2,1)}, u32[]{:S(2)}, u32[]{:S(2)}) collective-permute-start(bf16[4,4,624,128]{3,2,1,0:T(8,128)(2,1)} %get-tuple-element.146), channel_id=1, source_target_pairs={{0,4},{4,0},{8,12},{12,8},{16,20},{20,16},{24,28},{28,24},{1,5},{5... | collective-permute-start | bytes 7667720 | tf_op jit(solution)/shard_map/ppermute | solution.py:596
  246.1 38.8 %all-to-all-start.5 = ((bf16[8,192,256]{2,1,0:T(8,128)(2,1)}), bf16[8,192,256]{2,1,0:T(8,128)(2,1)S(1)}, u32[]{:S(2)}, u32[]{:S(2)}) async-start(bf16[8,192,256]{2,1,0:T(8,128)(2,1)} %copy-done.3), calls=%async_computation.5 | async-start | bytes 1572864 | tf_op jit(solution)/shard_map/all_to_all | solution.py:702
  254.0 35.8 %collective-permute-start.26 = (bf16[2,4,624,128]{3,2,1,0:T(8,128)(2,1)}, bf16[2,4,624,128]{3,2,1,0:T(8,128)(2,1)}, u32[]{:S(2)}, u32[]{:S(2)}) collective-permute-start(bf16[2,4,624,128]{3,2,1,0:T(8,128)(2,1)} %add_convert_fusion.1), channel_id=1, source_target_pairs={{0,16},{4,20},{8,24},{12,28},{16,0},{20,4},{24,8},{28,12},{1,17},{... | collective-permute-start | bytes 3833864 | tf_op jit(solution)/shard_map/ppermute | solution.py:596
  259.0 33.1 %collective-permute-start.25 = (bf16[2,4,672,128]{3,2,1,0:T(8,128)(2,1)}, bf16[2,4,672,128]{3,2,1,0:T(8,128)(2,1)}, u32[]{:S(2)}, u32[]{:S(2)}) collective-permute-start(bf16[2,4,672,128]{3,2,1,0:T(8,128)(2,1)} %add_convert_fusion), channel_id=1, source_target_pairs={{0,8},{4,12},{8,0},{12,4},{16,24},{20,28},{24,16},{28,20},{1,9},{5... | collective-permute-start | bytes 4128776 | tf_op jit(solution)/shard_map/ppermute | solution.py:596
  292.1 38.6 %all-to-all-start.6 = ((bf16[8,384,256]{2,1,0:T(8,128)(2,1)}), bf16[8,384,256]{2,1,0:T(8,128)(2,1)S(1)}, u32[]{:S(2)}, u32[]{:S(2)}) async-start(bf16[8,384,256]{2,1,0:T(8,128)(2,1)} %attend_grad_1.1), calls=%async_computation.6 | async-start | bytes 3145728 | tf_op jit(solution)/shard_map/all_to_all | solution.py:702
  297.6 33.0 %collective-permute-start.27 = (bf16[4,672,128]{2,1,0:T(8,128)(2,1)S(1)}, bf16[4,672,128]{2,1,0:T(8,128)(2,1)}, u32[]{:S(2)}, u32[]{:S(2)}) collective-permute-start(bf16[4,672,128]{2,1,0:T(8,128)(2,1)S(1)} %fusion.2), channel_id=1, source_target_pairs={{0,16},{4,20},{8,24},{12,28},{16,0},{20,4},{24,8},{28,12},{1,17},{... | collective-permute-start | bytes 2064392 | tf_op jit(solution)/shard_map/ppermute | solution.py:596
  301.4 28.2 %collective-permute-start.28 = (bf16[4,624,128]{2,1,0:T(8,128)(2,1)S(1)}, bf16[4,624,128]{2,1,0:T(8,128)(2,1)S(1)}, u32[]{:S(2)}, u32[]{:S(2)}) collective-permute-start(bf16[4,624,128]{2,1,0:T(8,128)(2,1)S(1)} %fusion.4), channel_id=1, source_target_pairs={{0,8},{4,12},{8,0},{12,4},{16,24},{20,28},{24,16},{28,20},{1,9},{5... | collective-permute-start | bytes 1916936 | tf_op jit(solution)/shard_map/ppermute | solution.py:596
  346.3 9.9 %collective-permute-start.30 = (bf16[4,4,480,128]{3,2,1,0:T(8,128)(2,1)}, bf16[4,4,480,128]{3,2,1,0:T(8,128)(2,1)}, u32[]{:S(2)}, u32[]{:S(2)}) collective-permute-start(bf16[4,4,480,128]{3,2,1,0:T(8,128)(2,1)} %get-tuple-element.168), channel_id=1, source_target_pairs={{0,4},{4,0},{8,12},{12,8},{16,20},{20,16},{24,28},{28,24},{1,5},{5... | collective-permute-start | bytes 5898248 | tf_op jit(solution)/shard_map/ppermute | solution.py:596
  351.2 25.0 %collective-permute-start.29 = (bf16[2,1296,128]{2,1,0:T(8,128)(2,1)}, bf16[2,1296,128]{2,1,0:T(8,128)(2,1)S(1)}, u32[]{:S(2)}, u32[]{:S(2)}) collective-permute-start(bf16[2,1296,128]{2,1,0:T(8,128)(2,1)} %pad_maximum_fusion.4), channel_id=1, source_target_pairs={{0,1},{1,0},{2,3},{3,2},{4,5},{5,4},{6,7},{7,6},{8,9},{9,8},{10,11... | collective-permute-start | bytes 1990664 | tf_op jit(solution)/shard_map/ppermute | solution.py:780
  353.5 48.8 %all-to-all-start.7 = ((bf16[32,32,384]{2,1,0:T(8,128)(2,1)}), bf16[32,32,384]{2,1,0:T(8,128)(2,1)S(1)}, u32[]{:S(2)}, u32[]{:S(2)}) async-start(bf16[32,32,384]{2,1,0:T(8,128)(2,1)} %bitcast.50), calls=%async_computation.7 | async-start | bytes 1572864 | tf_op jit(solution)/shard_map/all_to_all | solution.py:702
  358.8 17.7 %collective-permute-start.32 = (bf16[4,480,128]{2,1,0:T(8,128)(2,1)S(1)}, bf16[4,480,128]{2,1,0:T(8,128)(2,1)S(1)}, u32[]{:S(2)}, u32[]{:S(2)}) collective-permute-start(bf16[4,480,128]{2,1,0:T(8,128)(2,1)S(1)} %get-tuple-element.199), channel_id=1, source_target_pairs={{0,8},{4,12},{8,0},{12,4},{16,24},{20,28},{24,16},{28,20},{1,9},{5... | collective-permute-start | bytes 1474568 | tf_op jit(solution)/shard_map/ppermute | solution.py:596
  360.5 27.8 %collective-permute-start.33 = (bf16[4,480,128]{2,1,0:T(8,128)(2,1)S(1)}, bf16[4,480,128]{2,1,0:T(8,128)(2,1)S(1)}, u32[]{:S(2)}, u32[]{:S(2)}) collective-permute-start(bf16[4,480,128]{2,1,0:T(8,128)(2,1)S(1)} %get-tuple-element.201), channel_id=1, source_target_pairs={{0,16},{4,20},{8,24},{12,28},{16,0},{20,4},{24,8},{28,12},{1,17},{... | collective-permute-start | bytes 1474568 | tf_op jit(solution)/shard_map/ppermute | solution.py:596
  362.0 27.8 %collective-permute-start.34 = (bf16[4,480,128]{2,1,0:T(8,128)(2,1)S(1)}, bf16[4,480,128]{2,1,0:T(8,128)(2,1)S(1)}, u32[]{:S(2)}, u32[]{:S(2)}) collective-permute-start(bf16[4,480,128]{2,1,0:T(8,128)(2,1)S(1)} %get-tuple-element.200), channel_id=1, source_target_pairs={{0,24},{4,28},{8,16},{12,20},{16,8},{20,12},{24,0},{28,4},{1,25},{... | collective-permute-start | bytes 1474568 | tf_op jit(solution)/shard_map/ppermute | solution.py:596
  376.4 19.3 %collective-permute-start.31 = (bf16[1296,128]{1,0:T(8,128)(2,1)S(1)}, bf16[1296,128]{1,0:T(8,128)(2,1)S(1)}, u32[]{:S(2)}, u32[]{:S(2)}) collective-permute-start(bf16[1296,128]{1,0:T(8,128)(2,1)S(1)} %fusion.9), channel_id=1, source_target_pairs={{0,2},{1,3},{2,0},{3,1},{4,6},{5,7},{6,4},{7,5},{8,10},{9,11},{10,... | collective-permute-start | bytes 995336 | tf_op jit(solution)/shard_map/ppermute | solution.py:780
  395.8 38.3 %collective-permute-start.38 = (bf16[1296,128]{1,0:T(8,128)(2,1)S(1)}, bf16[1296,128]{1,0:T(8,128)(2,1)S(1)}, u32[]{:S(2)}, u32[]{:S(2)}) collective-permute-start(bf16[1296,128]{1,0:T(8,128)(2,1)S(1)} %fusion.3), channel_id=1, source_target_pairs={{0,8},{4,12},{8,0},{12,4},{16,24},{20,28},{24,16},{28,20},{1,9},{5... | collective-permute-start | bytes 995336 | tf_op jit(solution)/shard_map/ppermute | solution.py:596
  397.3 36.8 %collective-permute-start.39 = (bf16[1296,128]{1,0:T(8,128)(2,1)S(1)}, bf16[1296,128]{1,0:T(8,128)(2,1)S(1)}, u32[]{:S(2)}, u32[]{:S(2)}) collective-permute-start(bf16[1296,128]{1,0:T(8,128)(2,1)S(1)} %fusion.3), channel_id=1, source_target_pairs={{0,16},{4,20},{8,24},{12,28},{16,0},{20,4},{24,8},{28,12},{1,17},{... | collective-permute-start | bytes 995336 | tf_op jit(solution)/shard_map/ppermute | solution.py:596
  397.9 18.3 %collective-permute-start.35 = (bf16[480,128]{1,0:T(8,128)(2,1)S(1)}, bf16[480,128]{1,0:T(8,128)(2,1)S(1)}, u32[]{:S(2)}, u32[]{:S(2)}) collective-permute-start(bf16[480,128]{1,0:T(8,128)(2,1)S(1)} %get-tuple-element.213), channel_id=1, source_target_pairs={{0,1},{1,0},{2,3},{3,2},{4,5},{5,4},{6,7},{7,6},{8,9},{9,8},{10,11... | collective-permute-start | bytes 368648 | tf_op jit(solution)/shard_map/ppermute | solution.py:780
  398.0 18.2 %collective-permute-start.36 = (bf16[480,128]{1,0:T(8,128)(2,1)S(1)}, bf16[480,128]{1,0:T(8,128)(2,1)S(1)}, u32[]{:S(2)}, u32[]{:S(2)}) collective-permute-start(bf16[480,128]{1,0:T(8,128)(2,1)S(1)} %get-tuple-element.212), channel_id=1, source_target_pairs={{0,2},{1,3},{2,0},{3,1},{4,6},{5,7},{6,4},{7,5},{8,10},{9,11},{10,... | collective-permute-start | bytes 368648 | tf_op jit(solution)/shard_map/ppermute | solution.py:780
  401.0 15.2 %collective-permute-start.37 = (bf16[480,128]{1,0:T(8,128)(2,1)S(1)}, bf16[480,128]{1,0:T(8,128)(2,1)S(1)}, u32[]{:S(2)}, u32[]{:S(2)}) collective-permute-start(bf16[480,128]{1,0:T(8,128)(2,1)S(1)} %get-tuple-element.211), channel_id=1, source_target_pairs={{0,3},{1,2},{2,1},{3,0},{4,7},{5,6},{6,5},{7,4},{8,11},{9,10},{10,... | collective-permute-start | bytes 368648 | tf_op jit(solution)/shard_map/ppermute | solution.py:780
  416.3 17.8 %collective-permute-start.40 = (bf16[1296,128]{1,0:T(8,128)(2,1)S(1)}, bf16[1296,128]{1,0:T(8,128)(2,1)S(1)}, u32[]{:S(2)}, u32[]{:S(2)}) collective-permute-start(bf16[1296,128]{1,0:T(8,128)(2,1)S(1)} %fusion.3), channel_id=1, source_target_pairs={{0,24},{4,28},{8,16},{12,20},{16,8},{20,12},{24,0},{28,4},{1,25},{... | collective-permute-start | bytes 995336 | tf_op jit(solution)/shard_map/ppermute | solution.py:596
  418.0 10.3 %collective-permute-start.41 = (bf16[480,128]{1,0:T(8,128)(2,1)S(1)}, bf16[480,128]{1,0:T(8,128)(2,1)S(1)}, u32[]{:S(2)}, u32[]{:S(2)}) collective-permute-start(bf16[480,128]{1,0:T(8,128)(2,1)S(1)} %add_convert_fusion.11), channel_id=1, source_target_pairs={{0,8},{4,12},{8,0},{12,4},{16,24},{20,28},{24,16},{28,20},{1,9},{5... | collective-permute-start | bytes 368648 | tf_op jit(solution)/shard_map/ppermute | solution.py:596
  (46 other events, 487.4 us)

commit v4 on v3

--- a/solution.py
+++ b/solution.py
@@ -117,34 +117,39 @@
     return jnp.concatenate(parts, axis=1)
 
 
-def read_rows_kernel(codes, bigram, trigram, out, spread, total):
+def swap(value):
+    return mm(eye(value.shape[1]), value, NT).astype(BF)
+
+
+def read_rows_kernel(codes, bigram, trigram, out, total):
     step = pl.program_id(0)
     width = bigram.shape[1]
+    slots = codes.shape[1]
 
     @pl.when(step == 0)
     def _():
-        for table in range(2):
-            wide(spread, codes, table)
         total[...] = jnp.zeros_like(total)
 
+    row = lax.broadcasted_iota(jnp.int32, (width, slots), 0) + (step * width + 1)
     for table, source in enumerate((bigram, trigram)):
-        hot = onehot_block(spread, table, step * width, width)
-        total[table] += mm(hot, source[...], NT)
+        hot = jnp.where(row == codes[table : table + 1, :], 1.0, 0.0).astype(BF)
+        total[table * E : (table + 1) * E, :] += mm(source[...], hot)
 
     @pl.when(step == pl.num_programs(0) - 1)
     def _():
-        out[...] = jnp.concatenate([total[0], total[1]], axis=1).astype(BF)
+        for begin in range(0, slots, 128):
+            out[begin : begin + 128, :] = swap(total[:, begin : begin + 128].astype(BF))
 
 
 def table_block(table_rows):
-    for width in (1280, 640, 512, 256, 128):
+    for width in (2560, 1280, 640, 512, 256, 128):
         if table_rows % width == 0:
             return width
     return table_rows
 
 
 def read_rows(codes, bigram_t, trigram_t):
-    slots = codes.shape[0]
+    slots = codes.shape[1]
     rows = bigram_t.shape[1]
     width = table_block(rows)
     table = pl.BlockSpec((E, width), lambda i: (0, i))
@@ -152,10 +157,10 @@
         read_rows_kernel,
         grid=(rows // width,),
         out_shape=jax.ShapeDtypeStruct((slots, 2 * E), BF),
-        in_specs=[pl.BlockSpec((slots, 2), lambda i: (0, 0)), table, table],
+        in_specs=[pl.BlockSpec((2, slots), lambda i: (0, 0)), table, table],
         out_specs=pl.BlockSpec((slots, 2 * E), lambda i: (0, 0)),
-        scratch_shapes=[pltpu.VMEM((2, slots, 128), F32), pltpu.VMEM((2, slots, E), F32)],
-        compiler_params=params(32),
+        scratch_shapes=[pltpu.VMEM((2 * E, slots), F32)],
+        compiler_params=params(40),
         cost_estimate=cost(17),
         name="read_rows",
     )(codes, bigram_t, trigram_t)
@@ -401,10 +406,6 @@
     return total + jnp.sum(tile.reshape(-1, 8, tile.shape[1]), axis=0)
 
 
-def swap(value):
-    return mm(eye(value.shape[1]), value, NT).astype(BF)
-
-
 def piece_of(order, j, piece):
     at = order[j]
     return at // 2, pl.ds(pl.multiple_of(lax.rem(at, 2) * piece, piece), piece)
@@ -877,21 +878,14 @@
     start, embed, hidden, send, joined, lookup, gains, t_s, g_s = refs[10:]
     core, chip, z = where[0], where[1], where[2]
     for blocks, tail, half in ((refs[:4], own_tail, core), (refs[4:8], other_tail, 1 - core)):
-        upper, lower = by_chip(*blocks)
         for m in range(4):
             zz = lax.rem(z + m, 4)
             for k in range(4):
-                begin = zz * 192 + (chip ^ k) * 48
-                for t, source, first, last, at in (
-                    (0, upper, 0, 48, 0),
-                    (1, upper, 48, 80, 0),
-                    (1, lower, 0, 16, 32),
-                    (2, lower, 16, 64, 0),
-                ):
-                    joined[
-                        pl.ds(aligned(begin + at), last - first),
-                        pl.ds(aligned(t * D + half * 384, 128), 384),
-                    ] = source[k][m, first:last, :]
+                rows = pl.ds(aligned(zz * 192 + (chip ^ k) * 48), 48)
+                for t in range(3):
+                    joined[rows, pl.ds(aligned(t * D + half * 384, 128), 384)] = blocks[k][
+                        m, t * 48 : (t + 1) * 48, :
+                    ]
             lookup[pl.ds(aligned(zz * 48), 48), pl.ds(aligned(half * 384, 128), 384)] = tail[
                 m, 0:48, :
             ]
@@ -1011,36 +1005,38 @@
         for blocks, half in ((blocks_own, core), (blocks_other, 1 - core))
     ]
 
-    def fill(which, begin):
+    def fill(which, j, take):
         for side in sides:
             for m in range(4):
                 for k in range(4):
                     rows = pl.ds(aligned(lax.rem(z + m, 4) * 192 + (chip ^ k) * 48), 48)
-                    for j in range(2):
-                        take = pl.ds(aligned((2 * step + j) * 48 - begin), 48)
-                        pair_s[side[2], rows, j * 128 : (j + 1) * 128] = side[which][k][m, take, :]
-
-    @pl.when(step < 7)
-    def _():
-        fill(0, 0)
-
-    @pl.when(step == 7)
-    def _():
-        fill(1, CUT)
-
-    m = lax.rem(step // 2 - z + 4, 4)
+                    pair_s[side[2], rows, j * 128 : (j + 1) * 128] = side[which][k][
+                        m, take, :
+                    ]
+
+    for j in range(4):
+        tile = pl.ds(aligned((4 * step + j) * 48), 48)
+        if j < 2:
+            fill(0, j, tile)
+            continue
+
+        @pl.when(step < 3)
+        def _():
+            fill(0, j, tile)
+
+        @pl.when(step == 3)
+        def _():
+            fill(1, j, slice((j - 2) * 48, (j - 1) * 48))
+
+    m = lax.rem(step - z + 4, 4)
     for k in range(4):
-        yx = chip ^ k
-
-        @pl.when(yx // 2 == lax.rem(step, 2))
-        def _():
-            rows = pl.ds(aligned(lax.rem(yx, 2) * 128), 128)
-            for _, lower, half in sides:
-                for j in range(3):
-                    begin = 768 + j * 128 - CUT
-                    w_down[rows, pl.ds(aligned(half * 384 + j * 128, 128), 128)] = lower[k][
-                        m, begin : begin + 128, :
-                    ]
+        rows = pl.ds(aligned((chip ^ k) * 128), 128)
+        for _, lower, side in sides:
+            for j in range(3):
+                begin = 768 + j * 128 - CUT
+                w_down[rows, pl.ds(aligned(side * 384 + j * 128, 128), 128)] = lower[k][
+                    m, begin : begin + 128, :
+                ]
 
     groups = HEADS // pairs
     wide_ = pairs * HD
@@ -1116,7 +1112,7 @@
 
 def mlp(pairs, where, came, start, gains, upstream, *blocks):
     tokens = start.shape[0]
-    width = 256
+    width = 512
     steps = FF // width
     whole = lambda shape: pl.BlockSpec(
         shape, lambda i: (0,) * len(shape), pipeline_mode=pl.Buffered(1)
@@ -1156,7 +1152,7 @@
             pltpu.VMEM((2, D, width), BF),
             pltpu.VMEM((width, D), BF),
         ],
-        compiler_params=params(40),
+        compiler_params=params(44),
         cost_estimate=cost(23),
         name="mlp",
     )(where, came, start, gains, upstream, *blocks)
@@ -1385,7 +1381,7 @@
             pltpu.VMEM((2, 3, E, 128), BF),
             pltpu.VMEM((2, 48, 128), BF),
         ],
-        compiler_params=params(48),
+        compiler_params=params(60),
         cost_estimate=cost(13),
         name="back",
     )(where, *operands)
@@ -1444,7 +1440,7 @@
     asked = exchange(requests, both)
     codes = jnp.stack([asked[:, :capacity].reshape(-1), asked[:, capacity:].reshape(-1)], axis=1)
     got = exchange(
-        read_rows(codes, bigram_table.T, trigram_table.T).reshape(devices, capacity, 2 * E), both
+        read_rows(codes.T, bigram_table.T, trigram_table.T).reshape(devices, capacity, 2 * E), both
     ).reshape(devices * capacity, 2 * E)
 
     lookup = gather_weight(lookup_weight)
@@ -1627,26 +1623,30 @@
     )
     along = spread_fsdp(first)
     column = jnp.stack([p[:144] for p in along])
-    tail = jnp.stack([p[144:] for p in along])
-    upper, lower = column[:, :80], column[:, 80:]
-    near = [over_ctx(upper, 2), over_ctx(lower, 4)]
-    codes = jnp.stack([asked[:, :capacity].reshape(-1), asked[:, capacity:].reshape(-1)], axis=1)
+    pieces_z = along
+    near = [over_ctx(column, 2), over_ctx(column, 4)]
+    codes = jnp.stack([asked[:, :capacity].reshape(-1), asked[:, capacity:].reshape(-1)])
     answer = read_rows(
-        after(codes, column, tail), in_hbm(bigram_table.T), in_hbm(trigram_table.T)
+        after(codes, column), in_hbm(bigram_table.T), in_hbm(trigram_table.T)
     )
     ready = after(second, column)
-    along = [along_fsdp(ready, k) for k in (1, 2, 3)]
-    answer, near, along = lax.optimization_barrier((answer, near, along))
+    early = [along_fsdp(ready, k) for k in (1, 3)]
+    answer, near, early = lax.optimization_barrier((answer, near, early))
     got = exchange(answer.reshape(devices, capacity, 2 * E), both)
-    first_near = [jnp.stack([upper, near[0]]), jnp.stack([lower, near[1]])]
-    first_far = [over_ctx(first_near[0], 4), over_ctx(first_near[1], 2)]
-    first_own = first_near + first_far
+    answer, column = lax.optimization_barrier((answer, column))
+    last = over_ctx(column, 6)
+    last, near, pieces_z, early = lax.optimization_barrier((last, near, pieces_z, early))
+    tail = jnp.stack([p[144:] for p in pieces_z])
+    first_own = [column, *near, last]
     first_other = [over_ctx(block, 1) for block in first_own]
     first_blocks = (*first_own, *first_other, tail, over_ctx(tail, 1))
-    along = [second] + [after(along[k], first_far) for k in (2, 1, 0)]
-    upper = jnp.stack([block[:CUT] for block in along])
-    lower = jnp.stack([block[CUT:] for block in along])
-    near = [over_ctx(upper, 2), over_ctx(lower, 4)]
+    three = [second, early[1], early[0]]
+    near = [
+        over_ctx(jnp.stack([block[:CUT] for block in three]), 2),
+        over_ctx(jnp.stack([block[CUT:] for block in three]), 4),
+    ]
+    got, ready = lax.optimization_barrier((got, ready))
+    late = along_fsdp(ready, 2)
     got = got.reshape(devices * capacity, 2 * E)
 
     order = jnp.sum(
@@ -1674,9 +1674,16 @@
         sin_t,
         *first_blocks,
     )
-    sent, near = lax.optimization_barrier((sent, near))
+    sent, near, late = lax.optimization_barrier((sent, near, late))
+    near_late = [over_ctx(late[:CUT], 2), over_ctx(late[CUT:], 4)]
     rows = exchange(sent, "ctx")
-    near_x, near_y = jnp.stack([upper, near[0]]), jnp.stack([lower, near[1]])
+    own_blocks = [three[0], three[1], late, three[2]]
+    near_x, near_y = (
+        jnp.stack([*[block[cut] for block in own_blocks], part[0], part[1], last, part[2]]).reshape(
+            2, 4, -1, 128
+        )
+        for cut, part, last in zip((slice(CUT), slice(CUT, None)), near, near_late)
+    )
     rows, near_x, near_y = lax.optimization_barrier((rows, near_x, near_y))
     far_y, far_x = over_ctx(near_x, 4), over_ctx(near_y, 2)
     others = [over_ctx(near_x, 1), over_ctx(near_y, 1)]
@@ -1715,13 +1722,9 @@
     grad_b, came_a, from_x, from_y = lax.optimization_barrier((grad_b, came_a, from_x, from_y))
     far_u = add_all(own_u[2], core_u[2], from_x[1]).astype(BF)
     far_l = add_all(own_l[2], core_l[2], from_y[1]).astype(BF)
+    came_b = exchange(grad_b, "ctx")
+    came_b, far_u, far_l = lax.optimization_barrier((came_b, far_u, far_l))
     from_far = [over_ctx(far_u, 4), over_ctx(far_l, 2)]
-    came_b = exchange(grad_b, "ctx")
-    came_b, from_far = lax.optimization_barrier((came_b, from_far))
-    sums_u = add_all(own_u[3], core_u[3], from_x[0], from_far[0]).astype(BF)
-    sums_l = add_all(own_l[3], core_l[3], from_y[0], from_far[1]).astype(BF)
-    from_z = over_fsdp(jnp.concatenate([sums_u[:2], sums_l[:2]], axis=1), 1)
-    total_m = jnp.concatenate([sums_u[2:], sums_l[2:]], axis=1)
     start_grad, send, own_j, other_j = back_pass(
         devices * capacity,
         where,
@@ -1738,6 +1741,11 @@
         target_row,
     )
     from_core = over_ctx(other_j, 1)
+    send, from_far = lax.optimization_barrier((send, from_far))
+    sums_u = add_all(own_u[3], core_u[3], from_x[0], from_far[0]).astype(BF)
+    sums_l = add_all(own_l[3], core_l[3], from_y[0], from_far[1]).astype(BF)
+    from_z = over_fsdp(jnp.concatenate([sums_u[:2], sums_l[:2]], axis=1), 1)
+    total_m = jnp.concatenate([sums_u[2:], sums_l[2:]], axis=1)
     arrived = exchange(send.reshape(devices, capacity, 2 * E), both)
     half_j = add_cores(own_j, from_core)
     from_chips = to_chips(half_j)
@@ -1749,11 +1757,11 @@
     from_z, kept = lax.optimization_barrier((from_z, total_j[0]))
     piece_m = add_blocks(near_m, [from_z])
     every_m = [over_ctx(piece_m, 2 * k) for k in (1, 2)]
-    late_codes, kept, piece_m = lax.optimization_barrier((codes, kept, piece_m))
+    late_codes, kept, piece_m = lax.optimization_barrier((codes.T, kept, piece_m))
     bigram_grad, trigram_grad = add_rows(
         late_codes, arrived.reshape(devices * capacity, 2 * E), table_rows
     )
-    bigram_grad, from_fsdp = lax.optimization_barrier((bigram_grad, from_fsdp))
+    bigram_grad, from_fsdp, every_m = lax.optimization_barrier((bigram_grad, from_fsdp, every_m))
     piece_j = add_blocks(kept, from_fsdp)
     every_j = to_chips([piece_j] * 4)
     piece_j, piece_m = lax.optimization_barrier((piece_j, piece_m))

time: 452 us -> 431 us (0.954)
  waiting for transfers between devices: 144 us -> 121 us
  local copies, waits for them, and re-layouts: 20.4 us -> 27.6 us
  Pallas kernels: 163 us -> 157 us
    ppermute x35 -> x36, waiting for transfers between devices: 80.9 us -> 57.7 us  [over_ctx(): return lax.ppermute(value, 'ctx', [(i, i ^ mask) for i in range(size)])]
    unnamed x86 -> x104, local copies, waits for them, and re-layouts: 14.6 us -> 20.9 us
    ppermute x5, waiting for transfers between devices: 19.4 us -> 14 us  [over_fsdp(): return lax.ppermute(value, 'fsdp', [(i, i ^ mask) for i in range(4)])]
    another operation x7 -> x3, other arithmetic: 7.35 us -> 2.37 us  [the longest x1 0.85 us: local_packed(): jnp.stack([block[:CUT] for block in three])]
    ppermute x35 -> x36, starting transfers between devices: 28.1 us -> 28.8 us  [over_ctx(): return lax.ppermute(value, 'ctx', [(i, i ^ mask) for i in range(size)])]
  transfers between devices with their start and end apart: 53 -> 54, of which waited for: 16 -> 18; matrix products, arithmetic and copies ran while one was open for 7% -> 10% of each run, Pallas kernels for 27% -> 30%
where the time goes in v4:
time: 431 us; the launch traced here: 423 us
  Pallas kernels  157 us (36%)
  waiting for transfers between devices  121 us (28%)
  starting transfers between devices  73.5 us (17%)
  local copies, waits for them, and re-layouts  27.6 us (6%)
  other arithmetic  26.8 us (6%)
  blocking collectives  15.3 us (4%)
    ppermute x36, waiting for transfers between devices, over_ctx(): return lax.ppermute(value, 'ctx', [(i, i ^ mask) for i in range(size)])  57.7 us
    all_to_all x7, waiting for transfers between devices, exchange(): return lax.all_to_all(values, axes, split_axis=0, concat_axis=0, tiled=True)  45.9 us
    pallas_call x2, Pallas kernels, attend_grad_short(): pl.pallas_call(functools.partial(attend_grad_short_kernel, pairs, begin,...  36.9 us
    ppermute x36, starting transfers between devices, over_ctx(): return lax.ppermute(value, 'ctx', [(i, i ^ mask) for i in range(size)])  28.8 us
    all_to_all x7, starting transfers between devices, exchange(): return lax.all_to_all(values, axes, split_axis=0, concat_axis=0, tiled=True)  27.2 us
    pallas_call x1, Pallas kernels, mlp(): pl.pallas_call(functools.partial(mlp_kernel, pairs), grid=(steps,), out_s...  23.7 us
    unnamed x104, local copies, waits for them, and re-layouts  20.9 us
    pallas_call x1, Pallas kernels, attend_short(): pl.pallas_call(functools.partial(attend_short_kernel, pairs, piece), out_...  17.6 us
  transfers between devices with their start and end apart: 54, of which 18 were waited for; matrix products, arithmetic and copies ran while one was open for 10% of the time, Pallas kernels for 30%

profile of v4, /device:TPU:0, one launch (start us, length us, event | category | flops | bytes accessed | tf_op | source)
XLA Modules:
  0.0 423.0 jit_solution(7613021402422987069)
XLA Ops:
  4.9 3.1 collective-permute-start.2
  8.0 2.6 collective-permute-start.1
  11.9 2.9 all-to-all-start
  15.6 1.9 fusion.12
  18.2 8.4 %all-to-all-done = s32[32,1,64]{2,1,0:T(1,128)S(1)} async-done(((s32[32,1,64]{2,1,0:T(1,128)}), s32[32,1,64]{2,1,0:T(1,128)S(1)}, u32[]{:S(2)}, u32[]{:S(2)}) %all-to-all-start) | async-done | bytes 8224 | tf_op jit(solution)/shard_map/all_to_all | solution.py:703
  29.6 3.2 collective-permute-start.6
  34.0 14.1 %read_rows.1 = bf16[1024,384]{1,0:T(8,128)(2,1)} custom-call(s32[2,1024]{1,0:T(2,128)S(1)} %pad_add_fusion.codes, bf16[192,12800]{1,0:T(8,128)(2,1)} %bitcast.155, bf16[192,12800]{1,0:T(8,128)(2,1)} %bitcast.156), custom_call_target="tpu_custom_call" | custom-call | flops 10200000512 | bytes 42500000 | tf_op jit(solution)/shard_map/read_rows/pallas_call | solution.py:156
  49.6 2.3 collective-permute-start.7
  52.7 2.6 all-to-all-start.1
  55.3 10.4 %collective-permute-done.7.refs_3_ = bf16[4,144,384]{2,1,0:T(8,128)(2,1)} collective-permute-done((bf16[4,144,384]{2,1,0:T(8,128)(2,1)}, bf16[4,144,384]{2,1,0:T(8,128)(2,1)}, u32[]{:S(2)}, u32[]{:S(2)}) %collective-permute-start.7) | collective-permute-done | bytes 442400 | tf_op jit(solution)/shard_map/ppermute | solution.py:597
  70.7 2.2 collective-permute-start.13
  76.4 2.1 collective-permute-start.15
  78.5 13.3 %front.1 = (f32[512,768]{1,0:T(8,128)}, bf16[512,192]{1,0:T(8,128)(2,1)}, bf16[512,768]{1,0:T(8,128)(2,1)}, bf16[8,576,256]{2,1,0:T(8,128)(2,1)}, bf16[768,2304]...) custom-call(s32[3]{0:T(128)} %copy-done.8, s32[2]{0:T(128)} %dynamic_slice.6.starts, ...), custom_call_target="tpu_custom_call" | custom-call | flops 5400000000 | bytes 22500000 | tf_op jit(solution)/shard_map/front/pallas_call | solution.py:953
  91.9 3.1 collective-permute-done.15
  97.6 3.9 all-to-all-start.2
  110.6 20.3 %all-to-all-done.2.rows = bf16[8,576,256]{2,1,0:T(8,128)(2,1)S(1)} async-done(((bf16[8,576,256]{2,1,0:T(8,128)(2,1)}), bf16[8,576,256]{2,1,0:T(8,128)(2,1)S(1)}, u32[]{:S(2)}, u32[]{:S(2)}) %all-to-all-start.2) | async-done | bytes 2359328 | tf_op jit(solution)/shard_map/all_to_all | solution.py:703
  132.1 17.6 %attend.1 = (bf16[8,192,256]{2,1,0:T(8,128)(2,1)S(1)}, f32[3,64,2048]{2,1,0:T(8,128)S(1)}, f32[3,1,2048]{2,1,0:T(1,128)S(1)}) custom-call(s32[16]{0:T(128)S(1)} %select_reduce_fusion.order, bf16[8,576,256]{2,1,0:T(8,128)(2,1)S(1)} %all-to-all-done.2.rows), custom_call_target="tpu_custom_call" | custom-call | flops 15000000512 | bytes 62500000 | tf_op jit(solution)/shard_map/attend/pallas_call | solution.py:465
  149.7 12.4 %collective-permute-done.19.refs_3_ = bf16[2,4,624,128]{3,2,1,0:T(8,128)(2,1)S(1)} collective-permute-done((bf16[2,4,624,128]{3,2,1,0:T(8,128)(2,1)}, bf16[2,4,624,128]{3,2,1,0:T(8,128)(2,1)S(1)}, u32[]{:S(2)}, u32[]{:S(2)}) %collective-permute-start.19) | collective-permute-done | bytes 1277984 | tf_op jit(solution)/shard_map/ppermute | solution.py:597
  162.7 15.3 %all_to_all.47.came = bf16[8,192,256]{2,1,0:T(8,128)(2,1)S(1)} all-to-all(bf16[8,192,256]{2,1,0:T(8,128)(2,1)S(1)} %get-tuple-element.150), channel_id=1, replica_groups=mesh['ctx'=8,'fsdp'=4] {'ctx'}, dimensions={0} | all-to-all | bytes 1572864 | tf_op jit(solution)/shard_map/all_to_all | solution.py:703
  179.6 23.7 %mlp.1 = (bf16[512,768]{1,0:T(8,128)(2,1)}, bf16[512,768]{1,0:T(8,128)(2,1)S(1)}, bf16[512,768]{1,0:T(8,128)(2,1)S(1)}, bf16[512,2048]{1,0:T(8,128)(2,1)}, bf16[...) custom-call(s32[3]{0:T(128)S(1)} %copy-done.9, ...), custom_call_target="tpu_custom_call" | custom-call | flops 13799999488 | bytes 57500000 | tf_op jit(solution)/shard_map/mlp/pallas_call | solution.py:1121
  206.6 4.1 all-to-all-start.4
  210.7 16.5 %weight_grads.1 = (bf16[4,4,672,128]{3,2,1,0:T(8,128)(2,1)}, bf16[4,4,624,128]{3,2,1,0:T(8,128)(2,1)}, bf16[4,4,672,128]{3,2,1,0:T(8,128)(2,1)}, bf16[4,4,624,128]{3,2,1,0:T(8,128)(2,1)}) custom-call(s32[3]{0:T(128)} %copy-done.8, bf16[512,768]{1,0:T(8,128)(2,1)} %copy-done.21, bf16[512,2048]{1,0:T(8,128)(2,1)} %get-tuple-element.159.gate, ...), custom_call_target="tpu_custom_call" | custom-call | flops 8999999488 | bytes 37500000 | tf_op jit(solution)/shard_map/weight_grads/pallas_call | solution.py:1245
  230.1 12.4 %attend_grad_0.1 = bf16[8,192,256]{2,1,0:T(8,128)(2,1)S(1)} custom-call(s32[16]{0:T(128)S(1)} %select_reduce_fusion.order, bf16[8,576,256]{2,1,0:T(8,128)(2,1)S(1)} %all-to-all-done.2.rows, bf16[8,192,256]{2,1,0:T(8,128)(2,1)S(1)} %all-to-all-done.4.grads, f32[3,64,2048]{2,1,0:T(8,128)S(1)} %copy-done.19, f32[3,1,2048]{2,1,0:T(1,128)S(1)} %get-tuple-element.171.logsum, ...), custom_call_target="tpu_custom_call" | custom-call | flops 8400000000 | bytes 35000000 | tf_op jit(solution)/shard_map/attend_grad_0/pallas_call | solution.py:583
  243.4 4.4 %all-to-all-start.5 = ((bf16[8,192,256]{2,1,0:T(8,128)(2,1)}), bf16[8,192,256]{2,1,0:T(8,128)(2,1)}, u32[]{:S(2)}, u32[]{:S(2)}) async-start(bf16[8,192,256]{2,1,0:T(8,128)(2,1)} %copy-done.1), calls=%async_computation.5 | async-start | bytes 1572864 | tf_op jit(solution)/shard_map/all_to_all | solution.py:703
  247.8 3.2 add_convert_fusion.1
  251.0 2.0 collective-permute-start.27
  253.0 2.9 add_convert_fusion
  257.4 24.5 %attend_grad_1.1 = bf16[8,384,256]{2,1,0:T(8,128)(2,1)} custom-call(s32[16]{0:T(128)S(1)} %select_reduce_fusion.order, bf16[8,576,256]{2,1,0:T(8,128)(2,1)} %copy-done, bf16[8,192,256]{2,1,0:T(8,128)(2,1)S(1)} %all-to-all-done.4.grads, f32[3,64,2048]{2,1,0:T(8,128)S(1)} %copy-done.20, f32[3,1,2048]{2,1,0:T(1,128)S(1)} %get-tuple-element.171.logsum, ...), custom_call_target="tpu_custom_call" | custom-call | flops 16800000000 | bytes 70000000 | tf_op jit(solution)/shard_map/attend_grad_1/pallas_call | solution.py:583
  281.9 4.9 %collective-permute-done.27 = bf16[2,4,624,128]{3,2,1,0:T(8,128)(2,1)} collective-permute-done((bf16[2,4,624,128]{3,2,1,0:T(8,128)(2,1)}, bf16[2,4,624,128]{3,2,1,0:T(8,128)(2,1)}, u32[]{:S(2)}, u32[]{:S(2)}) %collective-permute-start.27) | collective-permute-done | bytes 1277984 | tf_op jit(solution)/shard_map/ppermute | solution.py:597
  286.8 2.2 collective-permute-done.26
  289.0 4.5 %all-to-all-start.6 = ((bf16[8,384,256]{2,1,0:T(8,128)(2,1)}), bf16[8,384,256]{2,1,0:T(8,128)(2,1)}, u32[]{:S(2)}, u32[]{:S(2)}) async-start(bf16[8,384,256]{2,1,0:T(8,128)(2,1)} %attend_grad_1.1), calls=%async_computation.6 | async-start | bytes 3145728 | tf_op jit(solution)/shard_map/all_to_all | solution.py:703
  293.6 2.4 fusion.4
  296.0 2.7 fusion.2
  298.6 16.0 %all-to-all-done.6.came_b = bf16[8,384,256]{2,1,0:T(8,128)(2,1)} async-done(((bf16[8,384,256]{2,1,0:T(8,128)(2,1)}), bf16[8,384,256]{2,1,0:T(8,128)(2,1)}, u32[]{:S(2)}, u32[]{:S(2)}) %all-to-all-start.6) | async-done | bytes 1572896 | tf_op jit(solution)/shard_map/all_to_all | solution.py:703
  315.8 14.4 %back.1 = (f32[512,768]{1,0:T(8,128)}, bf16[1024,384]{1,0:T(8,128)(2,1)}, bf16[4,4,480,128]{3,2,1,0:T(8,128)(2,1)}, bf16[4,4,480,128]{3,2,1,0:T(8,128)(2,1)}) custom-call(s32[3]{0:T(128)} %copy-done.8, bf16[8,192,256]{2,1,0:T(8,128)(2,1)} %all-to-all-done.5.came_a, bf16[8,384,256]{2,1,0:T(8,128)(2,1)} %all-to-all-done.6.came_b, ...), custom_call_target="tpu_custom_call" | custom-call | flops 7800000000 | bytes 32500000 | tf_op jit(solution)/shard_map/back/pallas_call | solution.py:1368
  332.1 1.9 fusion
  335.0 4.8 %all-to-all-start.7 = ((bf16[32,32,384]{2,1,0:T(8,128)(2,1)}), bf16[32,32,384]{2,1,0:T(8,128)(2,1)S(1)}, u32[]{:S(2)}, u32[]{:S(2)}) async-start(bf16[32,32,384]{2,1,0:T(8,128)(2,1)} %bitcast.47), calls=%async_computation.7 | async-start | bytes 1572864 | tf_op jit(solution)/shard_map/all_to_all | solution.py:703
  339.8 3.5 fusion.6
  343.3 1.9 collective-permute-start.33
  347.0 12.7 %collective-permute-done.30 = bf16[2,1296,128]{2,1,0:T(8,128)(2,1)S(1)} collective-permute-done((bf16[2,1296,128]{2,1,0:T(8,128)(2,1)}, bf16[2,1296,128]{2,1,0:T(8,128)(2,1)S(1)}, u32[]{:S(2)}, u32[]{:S(2)}) %collective-permute-start.30) | collective-permute-done | bytes 663584 | tf_op jit(solution)/shard_map/ppermute | solution.py:781
  360.8 12.5 %collective-permute-done.34 = bf16[4,480,128]{2,1,0:T(8,128)(2,1)} collective-permute-done((bf16[4,480,128]{2,1,0:T(8,128)(2,1)}, bf16[4,480,128]{2,1,0:T(8,128)(2,1)}, u32[]{:S(2)}, u32[]{:S(2)}) %collective-permute-start.34) | collective-permute-done | bytes 491552 | tf_op jit(solution)/shard_map/ppermute | solution.py:597
  378.8 1.9 collective-permute-start.40
  380.7 2.8 collective-permute-start.37
  385.0 13.1 %add_rows.1 = (f32[192,12800]{1,0:T(8,128)}, f32[192,12800]{1,0:T(8,128)}) custom-call(s32[1024,2]{1,0:T(8,128)S(1)} %bitcast.128, bf16[1024,384]{1,0:T(8,128)(2,1)S(1)} %bitcast.127), custom_call_target="tpu_custom_call" | custom-call | flops 8400000000 | bytes 35000000 | tf_op jit(solution)/shard_map/add_rows/pallas_call | solution.py:189
  402.6 6.9 %collective-permute-done.42 = bf16[480,128]{1,0:T(8,128)(2,1)S(1)} collective-permute-done((bf16[480,128]{1,0:T(8,128)(2,1)S(1)}, bf16[480,128]{1,0:T(8,128)(2,1)S(1)}, u32[]{:S(2)}, u32[]{:S(2)}) %collective-permute-start.42) | collective-permute-done | bytes 122912 | tf_op jit(solution)/shard_map/ppermute | solution.py:597
  412.9 3.2 collective-permute-done.45.other
  416.2 2.5 unpack_first.1
  419.4 3.4 unpack_second.1
  (229 shorter events, 67.6 us)
Async XLA Ops:
  4.9 21.9 %collective-permute-start.2 = (bf16[208,384]{1,0:T(8,128)(2,1)S(1)}, bf16[208,384]{1,0:T(8,128)(2,1)S(1)}, u32[]{:S(2)}, u32[]{:S(2)}) collective-permute-start(bf16[208,384]{1,0:T(8,128)(2,1)S(1)} %get-tuple-element.137), channel_id=1, source_target_pairs={{0,1},{1,2},{2,3},{3,0},{4,5},{5,6},{6,7},{7,4},{8,9},{9,10},{10,1... | collective-permute-start | bytes 479240 | tf_op jit(solution)/shard_map/ppermute | solution.py:602
  8.0 19.5 %collective-permute-start.1 = (bf16[208,384]{1,0:T(8,128)(2,1)S(1)}, bf16[208,384]{1,0:T(8,128)(2,1)S(1)}, u32[]{:S(2)}, u32[]{:S(2)}) collective-permute-start(bf16[208,384]{1,0:T(8,128)(2,1)S(1)} %get-tuple-element.137), channel_id=1, source_target_pairs={{0,2},{1,3},{2,0},{3,1},{4,6},{5,7},{6,4},{7,5},{8,10},{9,11},{10,... | collective-permute-start | bytes 479240 | tf_op jit(solution)/shard_map/ppermute | solution.py:602
  10.6 17.6 %collective-permute-start = (bf16[208,384]{1,0:T(8,128)(2,1)S(1)}, bf16[208,384]{1,0:T(8,128)(2,1)S(1)}, u32[]{:S(2)}, u32[]{:S(2)}) collective-permute-start(bf16[208,384]{1,0:T(8,128)(2,1)S(1)} %get-tuple-element.137), channel_id=1, source_target_pairs={{0,3},{1,0},{2,1},{3,2},{4,7},{5,4},{6,5},{7,6},{8,11},{9,8},{10,9... | collective-permute-start | bytes 479240 | tf_op jit(solution)/shard_map/ppermute | solution.py:602
  11.9 14.6 %all-to-all-start = ((s32[32,1,64]{2,1,0:T(1,128)}), s32[32,1,64]{2,1,0:T(1,128)S(1)}, u32[]{:S(2)}, u32[]{:S(2)}) async-start(s32[32,1,64]{2,1,0:T(1,128)} %bitcast.5), calls=%async_computation | async-start | bytes 32768 | tf_op jit(solution)/shard_map/all_to_all | solution.py:703
  29.0 19.1 %collective-permute-start.5 = (bf16[1296,128]{1,0:T(8,128)(2,1)S(1)}, bf16[1296,128]{1,0:T(8,128)(2,1)S(1)}, u32[]{:S(2)}, u32[]{:S(2)}) collective-permute-start(bf16[1296,128]{1,0:T(8,128)(2,1)S(1)} %get-tuple-element.144), channel_id=1, source_target_pairs={{0,1},{1,2},{2,3},{3,0},{4,5},{5,6},{6,7},{7,4},{8,9},{9,10},{10,1... | collective-permute-start | bytes 995336 | tf_op jit(solution)/shard_map/ppermute | solution.py:602
  29.6 18.5 %collective-permute-start.6 = (bf16[1296,128]{1,0:T(8,128)(2,1)S(1)}, bf16[1296,128]{1,0:T(8,128)(2,1)S(1)}, u32[]{:S(2)}, u32[]{:S(2)}) collective-permute-start(bf16[1296,128]{1,0:T(8,128)(2,1)S(1)} %get-tuple-element.144), channel_id=1, source_target_pairs={{0,3},{1,0},{2,1},{3,2},{4,7},{5,4},{6,5},{7,6},{8,11},{9,8},{10,9... | collective-permute-start | bytes 995336 | tf_op jit(solution)/shard_map/ppermute | solution.py:602
  32.8 15.3 %collective-permute-start.3 = (bf16[4,144,384]{2,1,0:T(8,128)(2,1)}, bf16[4,144,384]{2,1,0:T(8,128)(2,1)S(1)}, u32[]{:S(2)}, u32[]{:S(2)}) collective-permute-start(bf16[4,144,384]{2,1,0:T(8,128)(2,1)} %pad_maximum_fusion.5.refs_0_), channel_id=1, source_target_pairs={{0,8},{4,12},{8,0},{12,4},{16,24},{20,28},{24,16},{28,20},{1,9},{5... | collective-permute-start | bytes 1327112 | tf_op jit(solution)/shard_map/ppermute | solution.py:597
  33.4 14.7 %collective-permute-start.4 = (bf16[4,144,384]{2,1,0:T(8,128)(2,1)}, bf16[4,144,384]{2,1,0:T(8,128)(2,1)S(1)}, u32[]{:S(2)}, u32[]{:S(2)}) collective-permute-start(bf16[4,144,384]{2,1,0:T(8,128)(2,1)} %pad_maximum_fusion.5.refs_0_), channel_id=1, source_target_pairs={{0,16},{4,20},{8,24},{12,28},{16,0},{20,4},{24,8},{28,12},{1,17},{... | collective-permute-start | bytes 1327112 | tf_op jit(solution)/shard_map/ppermute | solution.py:597
  49.6 16.1 %collective-permute-start.7 = (bf16[4,144,384]{2,1,0:T(8,128)(2,1)}, bf16[4,144,384]{2,1,0:T(8,128)(2,1)}, u32[]{:S(2)}, u32[]{:S(2)}) collective-permute-start(bf16[4,144,384]{2,1,0:T(8,128)(2,1)} %pad_maximum_fusion.5.refs_0_), channel_id=1, source_target_pairs={{0,24},{4,28},{8,16},{12,20},{16,8},{20,12},{24,0},{28,4},{1,25},{... | collective-permute-start | bytes 1327112 | tf_op jit(solution)/shard_map/ppermute | solution.py:597
  52.7 18.1 %collective-permute-start.8 = (bf16[4,144,384]{2,1,0:T(8,128)(2,1)}, bf16[4,144,384]{2,1,0:T(8,128)(2,1)}, u32[]{:S(2)}, u32[]{:S(2)}) collective-permute-start(bf16[4,144,384]{2,1,0:T(8,128)(2,1)} %pad_maximum_fusion.5.refs_0_), channel_id=1, source_target_pairs={{0,4},{4,0},{8,12},{12,8},{16,20},{20,16},{24,28},{28,24},{1,5},{5... | collective-permute-start | bytes 1327112 | tf_op jit(solution)/shard_map/ppermute | solution.py:597
  52.7 22.2 %all-to-all-start.1 = ((bf16[32,32,384]{2,1,0:T(8,128)(2,1)}), bf16[32,32,384]{2,1,0:T(8,128)(2,1)S(1)}, u32[]{:S(2)}, u32[]{:S(2)}) async-start(bf16[32,32,384]{2,1,0:T(8,128)(2,1)} %bitcast.13), calls=%async_computation.1 | async-start | bytes 1572864 | tf_op jit(solution)/shard_map/all_to_all | solution.py:703
  68.6 9.9 %collective-permute-start.11 = (bf16[4,144,384]{2,1,0:T(8,128)(2,1)}, bf16[4,144,384]{2,1,0:T(8,128)(2,1)}, u32[]{:S(2)}, u32[]{:S(2)}) collective-permute-start(bf16[4,144,384]{2,1,0:T(8,128)(2,1)} %collective-permute-done.7.refs_3_), channel_id=1, source_target_pairs={{0,4},{4,0},{8,12},{12,8},{16,20},{20,16},{24,28},{28,24},{1,5},{5... | collective-permute-start | bytes 1327112 | tf_op jit(solution)/shard_map/ppermute | solution.py:597
  70.7 21.1 %collective-permute-start.13 = (bf16[3,672,128]{2,1,0:T(8,128)(2,1)}, bf16[3,672,128]{2,1,0:T(8,128)(2,1)S(1)}, u32[]{:S(2)}, u32[]{:S(2)}) collective-permute-start(bf16[3,672,128]{2,1,0:T(8,128)(2,1)} %pad_maximum_fusion.2), channel_id=1, source_target_pairs={{0,8},{4,12},{8,0},{12,4},{16,24},{20,28},{24,16},{28,20},{1,9},{5... | collective-permute-start | bytes 1548296 | tf_op jit(solution)/shard_map/ppermute | solution.py:597
  74.9 16.9 %collective-permute-start.14 = (bf16[3,624,128]{2,1,0:T(8,128)(2,1)}, bf16[3,624,128]{2,1,0:T(8,128)(2,1)S(1)}, u32[]{:S(2)}, u32[]{:S(2)}) collective-permute-start(bf16[3,624,128]{2,1,0:T(8,128)(2,1)} %pad_maximum_fusion.4), channel_id=1, source_target_pairs={{0,16},{4,20},{8,24},{12,28},{16,0},{20,4},{24,8},{28,12},{1,17},{... | collective-permute-start | bytes 1437704 | tf_op jit(solution)/shard_map/ppermute | solution.py:597
  76.4 18.5 %collective-permute-start.15 = (bf16[1296,128]{1,0:T(8,128)(2,1)S(1)}, bf16[1296,128]{1,0:T(8,128)(2,1)S(1)}, u32[]{:S(2)}, u32[]{:S(2)}) collective-permute-start(bf16[1296,128]{1,0:T(8,128)(2,1)S(1)} %get-tuple-element.144), channel_id=1, source_target_pairs={{0,2},{1,3},{2,0},{3,1},{4,6},{5,7},{6,4},{7,5},{8,10},{9,11},{10,... | collective-permute-start | bytes 995336 | tf_op jit(solution)/shard_map/ppermute | solution.py:602
  95.0 11.0 %collective-permute-start.17 = (bf16[624,128]{1,0:T(8,128)(2,1)S(1)}, bf16[624,128]{1,0:T(8,128)(2,1)}, u32[]{:S(2)}, u32[]{:S(2)}) collective-permute-start(bf16[624,128]{1,0:T(8,128)(2,1)S(1)} %slice.214), channel_id=1, source_target_pairs={{0,16},{4,20},{8,24},{12,28},{16,0},{20,4},{24,8},{28,12},{1,17},{... | collective-permute-start | bytes 479240 | tf_op jit(solution)/shard_map/ppermute | solution.py:597
  95.9 12.5 %collective-permute-start.16 = (bf16[672,128]{1,0:T(8,128)(2,1)S(1)}, bf16[672,128]{1,0:T(8,128)(2,1)S(1)}, u32[]{:S(2)}, u32[]{:S(2)}) collective-permute-start(bf16[672,128]{1,0:T(8,128)(2,1)S(1)} %slice.211), channel_id=1, source_target_pairs={{0,8},{4,12},{8,0},{12,4},{16,24},{20,28},{24,16},{28,20},{1,9},{5... | collective-permute-start | bytes 516104 | tf_op jit(solution)/shard_map/ppermute | solution.py:597
  97.6 33.3 %all-to-all-start.2 = ((bf16[8,576,256]{2,1,0:T(8,128)(2,1)}), bf16[8,576,256]{2,1,0:T(8,128)(2,1)S(1)}, u32[]{:S(2)}, u32[]{:S(2)}) async-start(bf16[8,576,256]{2,1,0:T(8,128)(2,1)} %get-tuple-element.145), calls=%async_computation.2 | async-start | bytes 4718592 | tf_op jit(solution)/shard_map/all_to_all | solution.py:703
  130.9 31.2 %collective-permute-start.18 = (bf16[2,4,672,128]{3,2,1,0:T(8,128)(2,1)}, bf16[2,4,672,128]{3,2,1,0:T(8,128)(2,1)S(1)}, u32[]{:S(2)}, u32[]{:S(2)}) collective-permute-start(bf16[2,4,672,128]{3,2,1,0:T(8,128)(2,1)} %bitcast.145), channel_id=1, source_target_pairs={{0,16},{4,20},{8,24},{12,28},{16,0},{20,4},{24,8},{28,12},{1,17},{... | collective-permute-start | bytes 4128776 | tf_op jit(solution)/shard_map/ppermute | solution.py:597
  131.4 46.6 %collective-permute-start.20 = (bf16[2,4,672,128]{3,2,1,0:T(8,128)(2,1)}, bf16[2,4,672,128]{3,2,1,0:T(8,128)(2,1)S(1)}, u32[]{:S(2)}, u32[]{:S(2)}) collective-permute-start(bf16[2,4,672,128]{3,2,1,0:T(8,128)(2,1)} %bitcast.146), channel_id=1, source_target_pairs={{0,4},{4,0},{8,12},{12,8},{16,20},{20,16},{24,28},{28,24},{1,5},{5... | collective-permute-start | bytes 4128776 | tf_op jit(solution)/shard_map/ppermute | solution.py:597
  131.4 30.7 %collective-permute-start.19 = (bf16[2,4,624,128]{3,2,1,0:T(8,128)(2,1)}, bf16[2,4,624,128]{3,2,1,0:T(8,128)(2,1)S(1)}, u32[]{:S(2)}, u32[]{:S(2)}) collective-permute-start(bf16[2,4,624,128]{3,2,1,0:T(8,128)(2,1)} %bitcast.129), channel_id=1, source_target_pairs={{0,8},{4,12},{8,0},{12,4},{16,24},{20,28},{24,16},{28,20},{1,9},{5... | collective-permute-start | bytes 3833864 | tf_op jit(solution)/shard_map/ppermute | solution.py:597
  162.1 15.9 %collective-permute-start.22 = (bf16[2,4,672,128]{3,2,1,0:T(8,128)(2,1)S(1)}, bf16[2,4,672,128]{3,2,1,0:T(8,128)(2,1)S(1)}, u32[]{:S(2)}, u32[]{:S(2)}) collective-permute-start(bf16[2,4,672,128]{3,2,1,0:T(8,128)(2,1)S(1)} %collective-permute-done.18.refs_2_), channel_id=1, source_target_pairs={{0,4},{4,0},{8,12},{12,8},{16,20},{20,16},{24,28},{28,24},{1,5},{5... | collective-permute-start | bytes 4128776 | tf_op jit(solution)/shard_map/ppermute | solution.py:597
  162.2 15.9 %collective-permute-start.21 = (bf16[2,4,624,128]{3,2,1,0:T(8,128)(2,1)S(1)}, bf16[2,4,624,128]{3,2,1,0:T(8,128)(2,1)S(1)}, u32[]{:S(2)}, u32[]{:S(2)}) collective-permute-start(bf16[2,4,624,128]{3,2,1,0:T(8,128)(2,1)S(1)} %bitcast.130), channel_id=1, source_target_pairs={{0,4},{4,0},{8,12},{12,8},{16,20},{20,16},{24,28},{28,24},{1,5},{5... | collective-permute-start | bytes 3833864 | tf_op jit(solution)/shard_map/ppermute | solution.py:597
  162.7 15.4 %collective-permute-start.23 = (bf16[2,4,624,128]{3,2,1,0:T(8,128)(2,1)S(1)}, bf16[2,4,624,128]{3,2,1,0:T(8,128)(2,1)S(1)}, u32[]{:S(2)}, u32[]{:S(2)}) collective-permute-start(bf16[2,4,624,128]{3,2,1,0:T(8,128)(2,1)S(1)} %collective-permute-done.19.refs_3_), channel_id=1, source_target_pairs={{0,4},{4,0},{8,12},{12,8},{16,20},{20,16},{24,28},{28,24},{1,5},{5... | collective-permute-start | bytes 3833864 | tf_op jit(solution)/shard_map/ppermute | solution.py:597
  206.6 20.6 %all-to-all-start.4 = ((bf16[8,192,256]{2,1,0:T(8,128)(2,1)}), bf16[8,192,256]{2,1,0:T(8,128)(2,1)S(1)}, u32[]{:S(2)}, u32[]{:S(2)}) async-start(bf16[8,192,256]{2,1,0:T(8,128)(2,1)} %copy-done.2), calls=%async_computation.4 | async-start | bytes 1572864 | tf_op jit(solution)/shard_map/all_to_all | solution.py:703
  227.2 20.6 %collective-permute-start.24 = (bf16[4,4,672,128]{3,2,1,0:T(8,128)(2,1)}, bf16[4,4,672,128]{3,2,1,0:T(8,128)(2,1)}, u32[]{:S(2)}, u32[]{:S(2)}) collective-permute-start(bf16[4,4,672,128]{3,2,1,0:T(8,128)(2,1)} %get-tuple-element.168), channel_id=1, source_target_pairs={{0,4},{4,0},{8,12},{12,8},{16,20},{20,16},{24,28},{28,24},{1,5},{5... | collective-permute-start | bytes 8257544 | tf_op jit(solution)/shard_map/ppermute | solution.py:597
  227.6 20.1 %collective-permute-start.25 = (bf16[4,4,624,128]{3,2,1,0:T(8,128)(2,1)}, bf16[4,4,624,128]{3,2,1,0:T(8,128)(2,1)}, u32[]{:S(2)}, u32[]{:S(2)}) collective-permute-start(bf16[4,4,624,128]{3,2,1,0:T(8,128)(2,1)} %get-tuple-element.169), channel_id=1, source_target_pairs={{0,4},{4,0},{8,12},{12,8},{16,20},{20,16},{24,28},{28,24},{1,5},{5... | collective-permute-start | bytes 7667720 | tf_op jit(solution)/shard_map/ppermute | solution.py:597
  243.4 38.6 %all-to-all-start.5 = ((bf16[8,192,256]{2,1,0:T(8,128)(2,1)}), bf16[8,192,256]{2,1,0:T(8,128)(2,1)}, u32[]{:S(2)}, u32[]{:S(2)}) async-start(bf16[8,192,256]{2,1,0:T(8,128)(2,1)} %copy-done.1), calls=%async_computation.5 | async-start | bytes 1572864 | tf_op jit(solution)/shard_map/all_to_all | solution.py:703
  251.0 35.8 %collective-permute-start.27 = (bf16[2,4,624,128]{3,2,1,0:T(8,128)(2,1)}, bf16[2,4,624,128]{3,2,1,0:T(8,128)(2,1)}, u32[]{:S(2)}, u32[]{:S(2)}) collective-permute-start(bf16[2,4,624,128]{3,2,1,0:T(8,128)(2,1)} %add_convert_fusion.1), channel_id=1, source_target_pairs={{0,16},{4,20},{8,24},{12,28},{16,0},{20,4},{24,8},{28,12},{1,17},{... | collective-permute-start | bytes 3833864 | tf_op jit(solution)/shard_map/ppermute | solution.py:597
  255.9 33.1 %collective-permute-start.26 = (bf16[2,4,672,128]{3,2,1,0:T(8,128)(2,1)}, bf16[2,4,672,128]{3,2,1,0:T(8,128)(2,1)}, u32[]{:S(2)}, u32[]{:S(2)}) collective-permute-start(bf16[2,4,672,128]{3,2,1,0:T(8,128)(2,1)} %add_convert_fusion), channel_id=1, source_target_pairs={{0,8},{4,12},{8,0},{12,4},{16,24},{20,28},{24,16},{28,20},{1,9},{5... | collective-permute-start | bytes 4128776 | tf_op jit(solution)/shard_map/ppermute | solution.py:597
  289.0 25.6 %all-to-all-start.6 = ((bf16[8,384,256]{2,1,0:T(8,128)(2,1)}), bf16[8,384,256]{2,1,0:T(8,128)(2,1)}, u32[]{:S(2)}, u32[]{:S(2)}) async-start(bf16[8,384,256]{2,1,0:T(8,128)(2,1)} %attend_grad_1.1), calls=%async_computation.6 | async-start | bytes 3145728 | tf_op jit(solution)/shard_map/all_to_all | solution.py:703
  314.6 15.6 %collective-permute-start.28 = (bf16[4,672,128]{2,1,0:T(8,128)(2,1)}, bf16[4,672,128]{2,1,0:T(8,128)(2,1)S(1)}, u32[]{:S(2)}, u32[]{:S(2)}) collective-permute-start(bf16[4,672,128]{2,1,0:T(8,128)(2,1)} %fusion.2), channel_id=1, source_target_pairs={{0,16},{4,20},{8,24},{12,28},{16,0},{20,4},{24,8},{28,12},{1,17},{... | collective-permute-start | bytes 2064392 | tf_op jit(solution)/shard_map/ppermute | solution.py:597
  315.1 15.1 %collective-permute-start.29 = (bf16[4,624,128]{2,1,0:T(8,128)(2,1)}, bf16[4,624,128]{2,1,0:T(8,128)(2,1)}, u32[]{:S(2)}, u32[]{:S(2)}) collective-permute-start(bf16[4,624,128]{2,1,0:T(8,128)(2,1)} %fusion.4), channel_id=1, source_target_pairs={{0,8},{4,12},{8,0},{12,4},{16,24},{20,28},{24,16},{28,20},{1,9},{5... | collective-permute-start | bytes 1916936 | tf_op jit(solution)/shard_map/ppermute | solution.py:597
  334.9 24.8 %collective-permute-start.30 = (bf16[2,1296,128]{2,1,0:T(8,128)(2,1)}, bf16[2,1296,128]{2,1,0:T(8,128)(2,1)S(1)}, u32[]{:S(2)}, u32[]{:S(2)}) collective-permute-start(bf16[2,1296,128]{2,1,0:T(8,128)(2,1)} %pad_maximum_fusion.1), channel_id=1, source_target_pairs={{0,1},{1,0},{2,3},{3,2},{4,5},{5,4},{6,7},{7,6},{8,9},{9,8},{10,11... | collective-permute-start | bytes 1990664 | tf_op jit(solution)/shard_map/ppermute | solution.py:781
  335.0 50.1 %all-to-all-start.7 = ((bf16[32,32,384]{2,1,0:T(8,128)(2,1)}), bf16[32,32,384]{2,1,0:T(8,128)(2,1)S(1)}, u32[]{:S(2)}, u32[]{:S(2)}) async-start(bf16[32,32,384]{2,1,0:T(8,128)(2,1)} %bitcast.47), calls=%async_computation.7 | async-start | bytes 1572864 | tf_op jit(solution)/shard_map/all_to_all | solution.py:703
  343.3 17.5 %collective-permute-start.33 = (bf16[4,480,128]{2,1,0:T(8,128)(2,1)}, bf16[4,480,128]{2,1,0:T(8,128)(2,1)}, u32[]{:S(2)}, u32[]{:S(2)}) collective-permute-start(bf16[4,480,128]{2,1,0:T(8,128)(2,1)} %get-tuple-element.227), channel_id=1, source_target_pairs={{0,8},{4,12},{8,0},{12,4},{16,24},{20,28},{24,16},{28,20},{1,9},{5... | collective-permute-start | bytes 1474568 | tf_op jit(solution)/shard_map/ppermute | solution.py:597
  345.2 28.1 %collective-permute-start.34 = (bf16[4,480,128]{2,1,0:T(8,128)(2,1)}, bf16[4,480,128]{2,1,0:T(8,128)(2,1)}, u32[]{:S(2)}, u32[]{:S(2)}) collective-permute-start(bf16[4,480,128]{2,1,0:T(8,128)(2,1)} %get-tuple-element.229), channel_id=1, source_target_pairs={{0,16},{4,20},{8,24},{12,28},{16,0},{20,4},{24,8},{28,12},{1,17},{... | collective-permute-start | bytes 1474568 | tf_op jit(solution)/shard_map/ppermute | solution.py:597
  346.6 28.2 %collective-permute-start.35 = (bf16[4,480,128]{2,1,0:T(8,128)(2,1)}, bf16[4,480,128]{2,1,0:T(8,128)(2,1)}, u32[]{:S(2)}, u32[]{:S(2)}) collective-permute-start(bf16[4,480,128]{2,1,0:T(8,128)(2,1)} %get-tuple-element.228), channel_id=1, source_target_pairs={{0,24},{4,28},{8,16},{12,20},{16,8},{20,12},{24,0},{28,4},{1,25},{... | collective-permute-start | bytes 1474568 | tf_op jit(solution)/shard_map/ppermute | solution.py:597
  359.8 18.0 %collective-permute-start.32 = (bf16[1296,128]{1,0:T(8,128)(2,1)S(1)}, bf16[1296,128]{1,0:T(8,128)(2,1)S(1)}, u32[]{:S(2)}, u32[]{:S(2)}) collective-permute-start(bf16[1296,128]{1,0:T(8,128)(2,1)S(1)} %fusion.9), channel_id=1, source_target_pairs={{0,2},{1,3},{2,0},{3,1},{4,6},{5,7},{6,4},{7,5},{8,10},{9,11},{10,... | collective-permute-start | bytes 995336 | tf_op jit(solution)/shard_map/ppermute | solution.py:781
  377.9 20.2 %collective-permute-start.39 = (bf16[1296,128]{1,0:T(8,128)(2,1)S(1)}, bf16[1296,128]{1,0:T(8,128)(2,1)S(1)}, u32[]{:S(2)}, u32[]{:S(2)}) collective-permute-start(bf16[1296,128]{1,0:T(8,128)(2,1)S(1)} %fusion.3), channel_id=1, source_target_pairs={{0,8},{4,12},{8,0},{12,4},{16,24},{20,28},{24,16},{28,20},{1,9},{5... | collective-permute-start | bytes 995336 | tf_op jit(solution)/shard_map/ppermute | solution.py:597
  378.8 19.3 %collective-permute-start.40 = (bf16[1296,128]{1,0:T(8,128)(2,1)S(1)}, bf16[1296,128]{1,0:T(8,128)(2,1)S(1)}, u32[]{:S(2)}, u32[]{:S(2)}) collective-permute-start(bf16[1296,128]{1,0:T(8,128)(2,1)S(1)} %fusion.3), channel_id=1, source_target_pairs={{0,16},{4,20},{8,24},{12,28},{16,0},{20,4},{24,8},{28,12},{1,17},{... | collective-permute-start | bytes 995336 | tf_op jit(solution)/shard_map/ppermute | solution.py:597
  380.6 17.4 %collective-permute-start.36 = (bf16[480,128]{1,0:T(8,128)(2,1)S(1)}, bf16[480,128]{1,0:T(8,128)(2,1)S(1)}, u32[]{:S(2)}, u32[]{:S(2)}) collective-permute-start(bf16[480,128]{1,0:T(8,128)(2,1)S(1)} %get-tuple-element.237), channel_id=1, source_target_pairs={{0,1},{1,0},{2,3},{3,2},{4,5},{5,4},{6,7},{7,6},{8,9},{9,8},{10,11... | collective-permute-start | bytes 368648 | tf_op jit(solution)/shard_map/ppermute | solution.py:781
  380.7 17.4 %collective-permute-start.37 = (bf16[480,128]{1,0:T(8,128)(2,1)S(1)}, bf16[480,128]{1,0:T(8,128)(2,1)S(1)}, u32[]{:S(2)}, u32[]{:S(2)}) collective-permute-start(bf16[480,128]{1,0:T(8,128)(2,1)S(1)} %get-tuple-element.236), channel_id=1, source_target_pairs={{0,2},{1,3},{2,0},{3,1},{4,6},{5,7},{6,4},{7,5},{8,10},{9,11},{10,... | collective-permute-start | bytes 368648 | tf_op jit(solution)/shard_map/ppermute | solution.py:781
  383.5 14.6 %collective-permute-start.38 = (bf16[480,128]{1,0:T(8,128)(2,1)S(1)}, bf16[480,128]{1,0:T(8,128)(2,1)S(1)}, u32[]{:S(2)}, u32[]{:S(2)}) collective-permute-start(bf16[480,128]{1,0:T(8,128)(2,1)S(1)} %get-tuple-element.235), channel_id=1, source_target_pairs={{0,3},{1,2},{2,1},{3,0},{4,7},{5,6},{6,5},{7,4},{8,11},{9,10},{10,... | collective-permute-start | bytes 368648 | tf_op jit(solution)/shard_map/ppermute | solution.py:781
  398.2 13.8 %collective-permute-start.41 = (bf16[1296,128]{1,0:T(8,128)(2,1)S(1)}, bf16[1296,128]{1,0:T(8,128)(2,1)S(1)}, u32[]{:S(2)}, u32[]{:S(2)}) collective-permute-start(bf16[1296,128]{1,0:T(8,128)(2,1)S(1)} %fusion.3), channel_id=1, source_target_pairs={{0,24},{4,28},{8,16},{12,20},{16,8},{20,12},{24,0},{28,4},{1,25},{... | collective-permute-start | bytes 995336 | tf_op jit(solution)/shard_map/ppermute | solution.py:597
  399.1 10.4 %collective-permute-start.42 = (bf16[480,128]{1,0:T(8,128)(2,1)S(1)}, bf16[480,128]{1,0:T(8,128)(2,1)S(1)}, u32[]{:S(2)}, u32[]{:S(2)}) collective-permute-start(bf16[480,128]{1,0:T(8,128)(2,1)S(1)} %add_convert_fusion.11), channel_id=1, source_target_pairs={{0,8},{4,12},{8,0},{12,4},{16,24},{20,28},{24,16},{28,20},{1,9},{5... | collective-permute-start | bytes 368648 | tf_op jit(solution)/shard_map/ppermute | solution.py:597
  399.9 10.7 %collective-permute-start.43 = (bf16[480,128]{1,0:T(8,128)(2,1)S(1)}, bf16[480,128]{1,0:T(8,128)(2,1)S(1)}, u32[]{:S(2)}, u32[]{:S(2)}) collective-permute-start(bf16[480,128]{1,0:T(8,128)(2,1)S(1)} %add_convert_fusion.11), channel_id=1, source_target_pairs={{0,16},{4,20},{8,24},{12,28},{16,0},{20,4},{24,8},{28,12},{1,17},{... | collective-permute-start | bytes 368648 | tf_op jit(solution)/shard_map/ppermute | solution.py:597
  401.8 10.3 %collective-permute-start.44 = (bf16[480,128]{1,0:T(8,128)(2,1)S(1)}, bf16[480,128]{1,0:T(8,128)(2,1)S(1)}, u32[]{:S(2)}, u32[]{:S(2)}) collective-permute-start(bf16[480,128]{1,0:T(8,128)(2,1)S(1)} %add_convert_fusion.11), channel_id=1, source_target_pairs={{0,24},{4,28},{8,16},{12,20},{16,8},{20,12},{24,0},{28,4},{1,25},{... | collective-permute-start | bytes 368648 | tf_op jit(solution)/shard_map/ppermute | solution.py:597
  (50 other events, 461.5 us)

commit v5 on v4

--- a/solution.py
+++ b/solution.py
@@ -199,6 +199,40 @@
         compiler_params=params(32),
         cost_estimate=cost(14),
         name="add_rows",
+    )(codes, grads)
+
+
+def add_table_kernel(table, codes, grads, out, spread, turned):
+    step = pl.program_id(0)
+    width = out.shape[1]
+
+    @pl.when(step == 0)
+    def _():
+        wide(spread, codes, table)
+        row = lax.broadcasted_iota(jnp.int32, (E, 2 * E), 0) + table * E
+        column = lax.broadcasted_iota(jnp.int32, (E, 2 * E), 1)
+        pick = jnp.where(row == column, 1.0, 0.0).astype(BF)
+        turned[...] = mm(pick, grads[...], NT).astype(BF)
+
+    out[...] = mm(turned[...], onehot_block(spread, table, step * width, width))
+
+
+def add_table(table, codes, grads, rows):
+    slots = codes.shape[0]
+    width = table_block(rows)
+    return pl.pallas_call(
+        functools.partial(add_table_kernel, table),
+        grid=(rows // width,),
+        out_shape=jax.ShapeDtypeStruct((E, rows), F32),
+        in_specs=[
+            pl.BlockSpec((slots, 2), lambda i: (0, 0)),
+            pl.BlockSpec((slots, 2 * E), lambda i: (0, 0)),
+        ],
+        out_specs=pl.BlockSpec((E, width), lambda i: (0, i)),
+        scratch_shapes=[pltpu.VMEM((2, slots, 128), F32), pltpu.VMEM((E, slots), BF)],
+        compiler_params=params(40),
+        cost_estimate=cost(7),
+        name=f"add_table_{table}",
     )(codes, grads)
 
 
@@ -707,7 +741,9 @@
     return pl.multiple_of(value, by)
 
 
-def pack_weights_kernel(where, joined, output, lookup, gains, expand, contract, first, second):
+def pack_weights_kernel(
+    where, joined, output, lookup, gains, expand, contract, first, second, third
+):
     core, chip = where[0], where[1]
     rows = pl.ds(aligned(chip * 48), 48)
     for t in range(3):
@@ -720,12 +756,9 @@
             rows, pl.ds(aligned(core * FF + j * 128, 128), 128)
         ]
     for j in range(3):
-        second[768 + j * 128 : 896 + j * 128, :] = contract[
-            pl.ds(aligned(chip * 128), 128), pl.ds(aligned(core * 384 + j * 128, 128), 128)
-        ]
-        second[1152 + j * 48 : 1200 + j * 48, :] = output[
-            rows, pl.ds(aligned(core * 384 + j * 128, 128), 128)
-        ]
+        lanes = pl.ds(aligned(core * 384 + j * 128, 128), 128)
+        second[768 + j * 48 : 816 + j * 48, :] = output[rows, lanes]
+        third[j * 128 : (j + 1) * 128, :] = contract[pl.ds(aligned(chip * 128), 128), lanes]
 
 
 def pack_weights(where, *weights):
@@ -733,10 +766,11 @@
         pack_weights_kernel,
         out_shape=(
             jax.ShapeDtypeStruct((208, 384), BF),
-            jax.ShapeDtypeStruct((1296, 128), BF),
+            jax.ShapeDtypeStruct((912, 128), BF),
+            jax.ShapeDtypeStruct((384, 128), BF),
         ),
         in_specs=[smem()] + [vmem()] * 6,
-        out_specs=(vmem(),) * 2,
+        out_specs=(vmem(),) * 3,
         compiler_params=params(16),
         cost_estimate=cost(2),
         name="pack_weights",
@@ -744,6 +778,7 @@
 
 
 CUT = 14 * 48
+WCUT = 10 * 48
 
 
 def by_chip(near_x, near_y, far_y, far_x):
@@ -980,6 +1015,7 @@
     *refs,
 ):
     blocks_own, blocks_other = refs[:4], refs[4:8]
+    tall_own, tall_other = refs[8:10], refs[10:12]
     (
         result,
         hidden_out,
@@ -996,7 +1032,7 @@
         output,
         pair_s,
         w_down,
-    ) = refs[8:]
+    ) = refs[12:]
     step = pl.program_id(0)
     core, chip, z = where[0], where[1], where[2]
     gain = gains[1:2, :]
@@ -1015,28 +1051,29 @@
                     ]
 
     for j in range(4):
-        tile = pl.ds(aligned((4 * step + j) * 48), 48)
-        if j < 2:
-            fill(0, j, tile)
-            continue
-
-        @pl.when(step < 3)
+        split = 3 if j < 2 else 2
+        tile = (4 * step + j) * 48
+
+        @pl.when(step < split)
         def _():
-            fill(0, j, tile)
-
-        @pl.when(step == 3)
+            fill(0, j, pl.ds(aligned(tile), 48))
+
+        @pl.when(step >= split)
         def _():
-            fill(1, j, slice((j - 2) * 48, (j - 1) * 48))
-
-    m = lax.rem(step - z + 4, 4)
-    for k in range(4):
-        rows = pl.ds(aligned((chip ^ k) * 128), 128)
-        for _, lower, side in sides:
-            for j in range(3):
-                begin = 768 + j * 128 - CUT
-                w_down[rows, pl.ds(aligned(side * 384 + j * 128, 128), 128)] = lower[k][
-                    m, begin : begin + 128, :
-                ]
+            fill(1, j, pl.ds(aligned(tile - WCUT), 48))
+
+    turn = step ^ z
+    for odd in range(2):
+
+        @pl.when(lax.rem(turn, 2) == odd)
+        def _():
+            for blocks, side in ((tall_own, core), (tall_other, 1 - core)):
+                for k in range(4):
+                    rows = pl.ds(aligned((chip ^ k) * 128), 128)
+                    for j in range(3):
+                        w_down[rows, pl.ds(aligned(side * 384 + j * 128, 128), 128)] = blocks[odd][
+                            turn // 2, k, j * 128 : (j + 1) * 128, :
+                        ]
 
     groups = HEADS // pairs
     wide_ = pairs * HD
@@ -1049,7 +1086,7 @@
                 for k in range(4):
                     rows = pl.ds(aligned(lax.rem(z + m, 4) * 192 + (chip ^ k) * 48), 48)
                     for j in range(3):
-                        begin = 1152 + j * 48 - CUT
+                        begin = 768 + j * 48 - WCUT
                         output[rows, pl.ds(aligned(side * 384 + j * 128, 128), 128)] = lower[k][
                             m, begin : begin + 48, :
                         ]
@@ -1612,7 +1649,7 @@
     requests, target_row, target_col = placement(ids, table_rows, devices, capacity)
     asked = exchange(requests, both)
     gain_rows = jnp.pad(jnp.stack([attention_gain, feedforward_gain]), ((0, 14), (0, 192)))
-    first, second = pack_weights(
+    first, second, third = pack_weights(
         after(where, requests),
         joined_weight,
         output_weight,
@@ -1625,13 +1662,16 @@
     column = jnp.stack([p[:144] for p in along])
     pieces_z = along
     near = [over_ctx(column, 2), over_ctx(column, 4)]
+    tall = [over_ctx(third, 2), over_ctx(third, 4)]
+    asked, tall, third = lax.optimization_barrier((asked, tall, third))
+    tall.append(over_ctx(third, 6))
     codes = jnp.stack([asked[:, :capacity].reshape(-1), asked[:, capacity:].reshape(-1)])
     answer = read_rows(
         after(codes, column), in_hbm(bigram_table.T), in_hbm(trigram_table.T)
     )
     ready = after(second, column)
     early = [along_fsdp(ready, k) for k in (1, 3)]
-    answer, near, early = lax.optimization_barrier((answer, near, early))
+    answer, near, early, tall = lax.optimization_barrier((answer, near, early, tall))
     got = exchange(answer.reshape(devices, capacity, 2 * E), both)
     answer, column = lax.optimization_barrier((answer, column))
     last = over_ctx(column, 6)
@@ -1642,8 +1682,8 @@
     first_blocks = (*first_own, *first_other, tail, over_ctx(tail, 1))
     three = [second, early[1], early[0]]
     near = [
-        over_ctx(jnp.stack([block[:CUT] for block in three]), 2),
-        over_ctx(jnp.stack([block[CUT:] for block in three]), 4),
+        over_ctx(jnp.stack([block[:WCUT] for block in three]), 2),
+        over_ctx(jnp.stack([block[WCUT:] for block in three]), 4),
     ]
     got, ready = lax.optimization_barrier((got, ready))
     late = along_fsdp(ready, 2)
@@ -1674,22 +1714,28 @@
         sin_t,
         *first_blocks,
     )
-    sent, near, late = lax.optimization_barrier((sent, near, late))
-    near_late = [over_ctx(late[:CUT], 2), over_ctx(late[CUT:], 4)]
+    sent, near, late, tall = lax.optimization_barrier((sent, near, late, tall))
+    tall = jnp.stack([third] + tall)
+    tall = jnp.stack([tall, over_fsdp(tall, 2)])
+    near_late = [over_ctx(late[:WCUT], 2), over_ctx(late[WCUT:], 4)]
     rows = exchange(sent, "ctx")
     own_blocks = [three[0], three[1], late, three[2]]
     near_x, near_y = (
         jnp.stack([*[block[cut] for block in own_blocks], part[0], part[1], last, part[2]]).reshape(
             2, 4, -1, 128
         )
-        for cut, part, last in zip((slice(CUT), slice(CUT, None)), near, near_late)
-    )
-    rows, near_x, near_y = lax.optimization_barrier((rows, near_x, near_y))
+        for cut, part, last in zip((slice(WCUT), slice(WCUT, None)), near, near_late)
+    )
+    rows, near_x, near_y, tall = lax.optimization_barrier((rows, near_x, near_y, tall))
+    tall_odd = over_fsdp(tall, 1)
     far_y, far_x = over_ctx(near_x, 4), over_ctx(near_y, 2)
     others = [over_ctx(near_x, 1), over_ctx(near_y, 1)]
     attended_rows, attended_t, logsum = attend_short(order, rows, pairs, piece)
     came = exchange(attended_rows, "ctx")
-    far_y, far_x = after((far_y, far_x), attended_rows)
+    far_y, far_x, tall, tall_odd, attended_rows = lax.optimization_barrier(
+        (far_y, far_x, tall, tall_odd, attended_rows)
+    )
+    talls = [tall, tall_odd, over_ctx(tall, 1), over_ctx(tall_odd, 1)]
     others += [over_ctx(far_y, 1), over_ctx(far_x, 1)]
     upstream = cotangent.reshape(tokens, D)
     (
@@ -1702,7 +1748,7 @@
         second_gain_term,
         middle_grad,
         sent,
-    ) = mlp(pairs, where, came, start, gains, upstream, near_x, near_y, far_y, far_x, *others)
+    ) = mlp(pairs, where, came, start, gains, upstream, near_x, near_y, far_y, far_x, *others, *talls)
 
     grad_rows = exchange(sent, "ctx")
     own_u, own_l, other_u, other_l = weight_grads(
@@ -1757,16 +1803,16 @@
     from_z, kept = lax.optimization_barrier((from_z, total_j[0]))
     piece_m = add_blocks(near_m, [from_z])
     every_m = [over_ctx(piece_m, 2 * k) for k in (1, 2)]
-    late_codes, kept, piece_m = lax.optimization_barrier((codes.T, kept, piece_m))
-    bigram_grad, trigram_grad = add_rows(
-        late_codes, arrived.reshape(devices * capacity, 2 * E), table_rows
-    )
+    arrived = arrived.reshape(devices * capacity, 2 * E)
+    from_fsdp[0], late_codes = lax.optimization_barrier((from_fsdp[0], codes.T))
+    bigram_grad = add_table(0, late_codes, arrived, table_rows)
     bigram_grad, from_fsdp, every_m = lax.optimization_barrier((bigram_grad, from_fsdp, every_m))
+    every_m.append(over_ctx(piece_m, 6))
     piece_j = add_blocks(kept, from_fsdp)
     every_j = to_chips([piece_j] * 4)
-    piece_j, piece_m = lax.optimization_barrier((piece_j, piece_m))
-    every_m.append(over_ctx(piece_m, 6))
-    every_m, every_j = lax.optimization_barrier((every_m, every_j))
+    late_codes, piece_j = lax.optimization_barrier((late_codes, piece_j))
+    trigram_grad = add_table(1, late_codes, arrived, table_rows)
+    trigram_grad, every_m, every_j = lax.optimization_barrier((trigram_grad, every_m, every_j))
     blocks_m = jnp.stack([piece_m] + every_m)
     other_m = over_ctx(blocks_m, 1)
     blocks_j = jnp.stack([piece_j] + every_j)

time: 431 us -> 421 us (0.977)
  waiting for transfers between devices: 121 us -> 98.2 us
  starting transfers between devices: 73.5 us -> 81.3 us
    all_to_all x7, waiting for transfers between devices: 45.9 us -> 23.9 us  [exchange(): return lax.all_to_all(values, axes, split_axis=0, concat_axis=0, tiled=True)]
    ppermute x36 -> x41, starting transfers between devices: 28.8 us -> 34.3 us  [over_ctx(): return lax.ppermute(value, 'ctx', [(i, i ^ mask) for i in range(size)])]
    ppermute x36 -> x41, waiting for transfers between devices: 57.7 us -> 61.1 us  [over_ctx(): return lax.ppermute(value, 'ctx', [(i, i ^ mask) for i in range(size)])]
    pallas_call x1 -> x2, Pallas kernels: 13.1 us -> 15.9 us  [add_table(): pl.pallas_call(functools.partial(add_table_kernel, table), grid=(rows //...]
    ppermute x5 -> x7, waiting for transfers between devices: 14 us -> 13.2 us  [over_fsdp(): return lax.ppermute(value, 'fsdp', [(i, i ^ mask) for i in range(4)])]
    unnamed x104 -> x126, local copies, waits for them, and re-layouts: 20.9 us -> 20.9 us
  transfers between devices with their start and end apart: 54 -> 61, of which waited for: 18 -> 16; matrix products, arithmetic and copies ran while one was open for 10% -> 10% of each run, Pallas kernels for 30% -> 32%
where the time goes in v5:
time: 421 us; the launch traced here: 413 us
  Pallas kernels  161 us (38%)
  waiting for transfers between devices  98.2 us (23%)
  starting transfers between devices  81.3 us (19%)
  other arithmetic  28.2 us (7%)
  local copies, waits for them, and re-layouts  27.3 us (6%)
  blocking collectives  15.6 us (4%)
    ppermute x41, waiting for transfers between devices, over_ctx(): return lax.ppermute(value, 'ctx', [(i, i ^ mask) for i in range(size)])  61.1 us
    pallas_call x2, Pallas kernels, attend_grad_short(): pl.pallas_call(functools.partial(attend_grad_short_kernel, pairs, begin,...  36.9 us
    ppermute x41, starting transfers between devices, over_ctx(): return lax.ppermute(value, 'ctx', [(i, i ^ mask) for i in range(size)])  34.3 us
    all_to_all x7, starting transfers between devices, exchange(): return lax.all_to_all(values, axes, split_axis=0, concat_axis=0, tiled=True)  26.4 us
    pallas_call x1, Pallas kernels, mlp(): pl.pallas_call(functools.partial(mlp_kernel, pairs), grid=(steps,), out_s...  24 us
    all_to_all x7, waiting for transfers between devices, exchange(): return lax.all_to_all(values, axes, split_axis=0, concat_axis=0, tiled=True)  23.9 us
    unnamed x126, local copies, waits for them, and re-layouts  20.9 us
    pallas_call x1, Pallas kernels, attend_short(): pl.pallas_call(functools.partial(attend_short_kernel, pairs, piece), out_...  17.6 us
  transfers between devices with their start and end apart: 61, of which 16 were waited for; matrix products, arithmetic and copies ran while one was open for 10% of the time, Pallas kernels for 32%

profile of v5, /device:TPU:0, one launch (start us, length us, event | category | flops | bytes accessed | tf_op | source)
XLA Modules:
  0.0 413.5 jit_solution(1545656646413552586)
XLA Ops:
  4.9 3.1 collective-permute-start.4
  8.0 2.6 collective-permute-start.3
  14.9 2.5 all-to-all-start
  17.5 1.9 fusion.12
  20.2 6.3 %all-to-all-done = s32[32,1,64]{2,1,0:T(1,128)S(1)} async-done(((s32[32,1,64]{2,1,0:T(1,128)}), s32[32,1,64]{2,1,0:T(1,128)S(1)}, u32[]{:S(2)}, u32[]{:S(2)}) %all-to-all-start) | async-done | bytes 8224 | tf_op jit(solution)/shard_map/all_to_all | solution.py:737
  29.6 3.1 collective-permute-start.8
  35.6 14.1 %read_rows.1 = bf16[1024,384]{1,0:T(8,128)(2,1)} custom-call(s32[2,1024]{1,0:T(2,128)S(1)} %pad_add_fusion.codes, bf16[192,12800]{1,0:T(8,128)(2,1)} %bitcast.168, bf16[192,12800]{1,0:T(8,128)(2,1)} %bitcast.169), custom_call_target="tpu_custom_call" | custom-call | flops 10200000512 | bytes 42500000 | tf_op jit(solution)/shard_map/read_rows/pallas_call | solution.py:156
  51.9 2.8 all-to-all-start.1
  54.7 12.3 %collective-permute-done.10.refs_3_ = bf16[4,144,384]{2,1,0:T(8,128)(2,1)} collective-permute-done((bf16[4,144,384]{2,1,0:T(8,128)(2,1)S(1)}, bf16[4,144,384]{2,1,0:T(8,128)(2,1)}, u32[]{:S(2)}, u32[]{:S(2)}) %collective-permute-start.10) | collective-permute-done | bytes 442400 | tf_op jit(solution)/shard_map/ppermute | solution.py:631
  78.6 13.4 %front.1 = (f32[512,768]{1,0:T(8,128)}, bf16[512,192]{1,0:T(8,128)(2,1)}, bf16[512,768]{1,0:T(8,128)(2,1)}, bf16[8,576,256]{2,1,0:T(8,128)(2,1)}, bf16[768,2304]...) custom-call(s32[3]{0:T(128)} %copy-done.8, s32[2]{0:T(128)} %dynamic_slice.6.starts, ...), custom_call_target="tpu_custom_call" | custom-call | flops 5400000000 | bytes 22500000 | tf_op jit(solution)/shard_map/front/pallas_call | solution.py:988
  93.1 1.7 collective-permute-start.21
  94.8 3.9 all-to-all-start.2
  102.6 2.0 collective-permute-start.20
  109.9 19.6 %collective-permute-done.20 = bf16[432,128]{1,0:T(8,128)(2,1)S(1)} collective-permute-done((bf16[432,128]{1,0:T(8,128)(2,1)S(1)}, bf16[432,128]{1,0:T(8,128)(2,1)S(1)}, u32[]{:S(2)}, u32[]{:S(2)}) %collective-permute-start.20) | collective-permute-done | bytes 110624 | tf_op jit(solution)/shard_map/ppermute | solution.py:631
  135.8 17.6 %attend.1 = (bf16[8,192,256]{2,1,0:T(8,128)(2,1)S(1)}, f32[3,64,2048]{2,1,0:T(8,128)S(1)}, f32[3,1,2048]{2,1,0:T(1,128)S(1)}) custom-call(s32[16]{0:T(128)S(1)} %select_reduce_fusion.order, bf16[8,576,256]{2,1,0:T(8,128)(2,1)S(1)} %all-to-all-done.2.rows), custom_call_target="tpu_custom_call" | custom-call | flops 15000000512 | bytes 62500000 | tf_op jit(solution)/shard_map/attend/pallas_call | solution.py:499
  157.2 15.6 %all_to_all.47.came = bf16[8,192,256]{2,1,0:T(8,128)(2,1)S(1)} all-to-all(bf16[8,192,256]{2,1,0:T(8,128)(2,1)S(1)} %get-tuple-element.173), channel_id=1, replica_groups=mesh['ctx'=8,'fsdp'=4] {'ctx'}, dimensions={0} | all-to-all | bytes 1572864 | tf_op jit(solution)/shard_map/all_to_all | solution.py:737
  174.4 24.0 %mlp.1 = (bf16[512,768]{1,0:T(8,128)(2,1)}, bf16[512,768]{1,0:T(8,128)(2,1)S(1)}, bf16[512,768]{1,0:T(8,128)(2,1)S(1)}, bf16[512,2048]{1,0:T(8,128)(2,1)}, bf16[...) custom-call(s32[3]{0:T(128)S(1)} %copy-done.9, ...), custom_call_target="tpu_custom_call" | custom-call | flops 13799999488 | bytes 57500000 | tf_op jit(solution)/shard_map/mlp/pallas_call | solution.py:1158
  201.7 3.7 all-to-all-start.4
  205.4 16.6 %weight_grads.1 = (bf16[4,4,672,128]{3,2,1,0:T(8,128)(2,1)}, bf16[4,4,624,128]{3,2,1,0:T(8,128)(2,1)}, bf16[4,4,672,128]{3,2,1,0:T(8,128)(2,1)}, bf16[4,4,624,128]{3,2,1,0:T(8,128)(2,1)}) custom-call(s32[3]{0:T(128)} %copy-done.8, bf16[512,768]{1,0:T(8,128)(2,1)} %copy-done.21, bf16[512,2048]{1,0:T(8,128)(2,1)} %get-tuple-element.185.gate, ...), custom_call_target="tpu_custom_call" | custom-call | flops 8999999488 | bytes 37500000 | tf_op jit(solution)/shard_map/weight_grads/pallas_call | solution.py:1282
  224.8 12.4 %attend_grad_0.1 = bf16[8,192,256]{2,1,0:T(8,128)(2,1)S(1)} custom-call(s32[16]{0:T(128)S(1)} %select_reduce_fusion.order, bf16[8,576,256]{2,1,0:T(8,128)(2,1)S(1)} %all-to-all-done.2.rows, bf16[8,192,256]{2,1,0:T(8,128)(2,1)S(1)} %all-to-all-done.4.grads, f32[3,64,2048]{2,1,0:T(8,128)S(1)} %copy-done.19, f32[3,1,2048]{2,1,0:T(1,128)S(1)} %get-tuple-element.197.logsum, ...), custom_call_target="tpu_custom_call" | custom-call | flops 8400000000 | bytes 35000000 | tf_op jit(solution)/shard_map/attend_grad_0/pallas_call | solution.py:617
  238.1 4.4 %all-to-all-start.5 = ((bf16[8,192,256]{2,1,0:T(8,128)(2,1)}), bf16[8,192,256]{2,1,0:T(8,128)(2,1)}, u32[]{:S(2)}, u32[]{:S(2)}) async-start(bf16[8,192,256]{2,1,0:T(8,128)(2,1)} %copy-done.2), calls=%async_computation.5 | async-start | bytes 1572864 | tf_op jit(solution)/shard_map/all_to_all | solution.py:737
  242.6 3.2 add_convert_fusion.1
  245.8 2.0 collective-permute-start.34
  247.9 3.0 add_convert_fusion
  252.3 24.5 %attend_grad_1.1 = bf16[8,384,256]{2,1,0:T(8,128)(2,1)} custom-call(s32[16]{0:T(128)S(1)} %select_reduce_fusion.order, bf16[8,576,256]{2,1,0:T(8,128)(2,1)} %copy-done, bf16[8,192,256]{2,1,0:T(8,128)(2,1)S(1)} %all-to-all-done.4.grads, f32[3,64,2048]{2,1,0:T(8,128)S(1)} %copy-done.20, f32[3,1,2048]{2,1,0:T(1,128)S(1)} %get-tuple-element.197.logsum, ...), custom_call_target="tpu_custom_call" | custom-call | flops 16800000000 | bytes 70000000 | tf_op jit(solution)/shard_map/attend_grad_1/pallas_call | solution.py:617
  276.8 4.8 %collective-permute-done.34 = bf16[2,4,624,128]{3,2,1,0:T(8,128)(2,1)} collective-permute-done((bf16[2,4,624,128]{3,2,1,0:T(8,128)(2,1)}, bf16[2,4,624,128]{3,2,1,0:T(8,128)(2,1)}, u32[]{:S(2)}, u32[]{:S(2)}) %collective-permute-start.34) | collective-permute-done | bytes 1277984 | tf_op jit(solution)/shard_map/ppermute | solution.py:631
  281.7 2.2 collective-permute-done.33
  283.9 4.6 %all-to-all-start.6 = ((bf16[8,384,256]{2,1,0:T(8,128)(2,1)}), bf16[8,384,256]{2,1,0:T(8,128)(2,1)}, u32[]{:S(2)}, u32[]{:S(2)}) async-start(bf16[8,384,256]{2,1,0:T(8,128)(2,1)} %attend_grad_1.1), calls=%async_computation.6 | async-start | bytes 3145728 | tf_op jit(solution)/shard_map/all_to_all | solution.py:737
  288.4 2.5 fusion.4
  290.9 2.7 fusion.2
  293.5 15.9 %all-to-all-done.6.came_b = bf16[8,384,256]{2,1,0:T(8,128)(2,1)} async-done(((bf16[8,384,256]{2,1,0:T(8,128)(2,1)}), bf16[8,384,256]{2,1,0:T(8,128)(2,1)}, u32[]{:S(2)}, u32[]{:S(2)}) %all-to-all-start.6) | async-done | bytes 1572896 | tf_op jit(solution)/shard_map/all_to_all | solution.py:737
  310.6 14.5 %back.1 = (f32[512,768]{1,0:T(8,128)}, bf16[1024,384]{1,0:T(8,128)(2,1)}, bf16[4,4,480,128]{3,2,1,0:T(8,128)(2,1)}, bf16[4,4,480,128]{3,2,1,0:T(8,128)(2,1)}) custom-call(s32[3]{0:T(128)} %copy-done.8, bf16[8,192,256]{2,1,0:T(8,128)(2,1)} %all-to-all-done.5.came_a, bf16[8,384,256]{2,1,0:T(8,128)(2,1)} %all-to-all-done.6.came_b, ...), custom_call_target="tpu_custom_call" | custom-call | flops 7800000000 | bytes 32500000 | tf_op jit(solution)/shard_map/back/pallas_call | solution.py:1405
  325.1 1.8 fusion.1
  327.0 1.9 fusion
  330.9 4.4 %all-to-all-start.7 = ((bf16[32,32,384]{2,1,0:T(8,128)(2,1)}), bf16[32,32,384]{2,1,0:T(8,128)(2,1)S(1)}, u32[]{:S(2)}, u32[]{:S(2)}) async-start(bf16[32,32,384]{2,1,0:T(8,128)(2,1)} %bitcast.51), calls=%async_computation.7 | async-start | bytes 1572864 | tf_op jit(solution)/shard_map/all_to_all | solution.py:737
  335.4 3.5 fusion.5
  338.9 1.9 collective-permute-start.39
  342.6 11.8 %collective-permute-done.37 = bf16[2,1296,128]{2,1,0:T(8,128)(2,1)S(1)} collective-permute-done((bf16[2,1296,128]{2,1,0:T(8,128)(2,1)}, bf16[2,1296,128]{2,1,0:T(8,128)(2,1)S(1)}, u32[]{:S(2)}, u32[]{:S(2)}) %collective-permute-start.37) | collective-permute-done | bytes 663584 | tf_op jit(solution)/shard_map/ppermute | solution.py:816
  356.2 12.7 %collective-permute-done.40 = bf16[4,480,128]{2,1,0:T(8,128)(2,1)} collective-permute-done((bf16[4,480,128]{2,1,0:T(8,128)(2,1)}, bf16[4,480,128]{2,1,0:T(8,128)(2,1)}, u32[]{:S(2)}, u32[]{:S(2)}) %collective-permute-start.40) | collective-permute-done | bytes 491552 | tf_op jit(solution)/shard_map/ppermute | solution.py:631
  374.7 1.6 collective-permute-start.47
  377.3 2.5 collective-permute-start.43
  379.8 1.9 collective-permute-start.44
  381.7 7.9 %add_table_0.1 = f32[192,12800]{1,0:T(8,128)} custom-call(s32[1024,2]{1,0:T(8,128)S(1)} %bitcast.136, bf16[1024,384]{1,0:T(8,128)(2,1)S(1)} %bitcast.134), custom_call_target="tpu_custom_call" | custom-call | flops 4200000000 | bytes 17500000 | tf_op jit(solution)/shard_map/add_table_0/pallas_call | solution.py:223
  392.4 1.9 collective-permute-start.51
  394.3 7.9 %add_table_1.1 = f32[192,12800]{1,0:T(8,128)} custom-call(s32[1024,2]{1,0:T(8,128)S(1)} %bitcast.137, bf16[1024,384]{1,0:T(8,128)(2,1)S(1)} %bitcast.135), custom_call_target="tpu_custom_call" | custom-call | flops 4200000000 | bytes 17500000 | tf_op jit(solution)/shard_map/add_table_1/pallas_call | solution.py:223
  403.2 3.2 collective-permute-done.52.other
  406.4 2.5 unpack_first.1
  409.6 3.4 unpack_second.1
  (268 shorter events, 76.9 us)
Async XLA Ops:
  4.9 22.5 %collective-permute-start.4 = (bf16[208,384]{1,0:T(8,128)(2,1)S(1)}, bf16[208,384]{1,0:T(8,128)(2,1)S(1)}, u32[]{:S(2)}, u32[]{:S(2)}) collective-permute-start(bf16[208,384]{1,0:T(8,128)(2,1)S(1)} %get-tuple-element.154), channel_id=1, source_target_pairs={{0,1},{1,2},{2,3},{3,0},{4,5},{5,6},{6,7},{7,4},{8,9},{9,10},{10,1... | collective-permute-start | bytes 479240 | tf_op jit(solution)/shard_map/ppermute | solution.py:636
  8.0 20.1 %collective-permute-start.3 = (bf16[208,384]{1,0:T(8,128)(2,1)S(1)}, bf16[208,384]{1,0:T(8,128)(2,1)S(1)}, u32[]{:S(2)}, u32[]{:S(2)}) collective-permute-start(bf16[208,384]{1,0:T(8,128)(2,1)S(1)} %get-tuple-element.154), channel_id=1, source_target_pairs={{0,2},{1,3},{2,0},{3,1},{4,6},{5,7},{6,4},{7,5},{8,10},{9,11},{10,... | collective-permute-start | bytes 479240 | tf_op jit(solution)/shard_map/ppermute | solution.py:636
  10.6 18.2 %collective-permute-start.2 = (bf16[208,384]{1,0:T(8,128)(2,1)S(1)}, bf16[208,384]{1,0:T(8,128)(2,1)S(1)}, u32[]{:S(2)}, u32[]{:S(2)}) collective-permute-start(bf16[208,384]{1,0:T(8,128)(2,1)S(1)} %get-tuple-element.154), channel_id=1, source_target_pairs={{0,3},{1,0},{2,1},{3,2},{4,7},{5,4},{6,5},{7,6},{8,11},{9,8},{10,9... | collective-permute-start | bytes 479240 | tf_op jit(solution)/shard_map/ppermute | solution.py:636
  11.9 14.6 %collective-permute-start = (bf16[384,128]{1,0:T(8,128)(2,1)S(1)}, bf16[384,128]{1,0:T(8,128)(2,1)S(1)}, u32[]{:S(2)}, u32[]{:S(2)}) collective-permute-start(bf16[384,128]{1,0:T(8,128)(2,1)S(1)} %get-tuple-element.140), channel_id=1, source_target_pairs={{0,8},{4,12},{8,0},{12,4},{16,24},{20,28},{24,16},{28,20},{1,9},{5... | collective-permute-start | bytes 294920 | tf_op jit(solution)/shard_map/ppermute | solution.py:631
  13.4 13.1 %collective-permute-start.1 = (bf16[384,128]{1,0:T(8,128)(2,1)S(1)}, bf16[384,128]{1,0:T(8,128)(2,1)S(1)}, u32[]{:S(2)}, u32[]{:S(2)}) collective-permute-start(bf16[384,128]{1,0:T(8,128)(2,1)S(1)} %get-tuple-element.140), channel_id=1, source_target_pairs={{0,16},{4,20},{8,24},{12,28},{16,0},{20,4},{24,8},{28,12},{1,17},{... | collective-permute-start | bytes 294920 | tf_op jit(solution)/shard_map/ppermute | solution.py:631
  26.8 22.9 %collective-permute-start.9 = (bf16[384,128]{1,0:T(8,128)(2,1)S(1)}, bf16[384,128]{1,0:T(8,128)(2,1)S(1)}, u32[]{:S(2)}, u32[]{:S(2)}) collective-permute-start(bf16[384,128]{1,0:T(8,128)(2,1)S(1)} %get-tuple-element.140), channel_id=1, source_target_pairs={{0,24},{4,28},{8,16},{12,20},{16,8},{20,12},{24,0},{28,4},{1,25},{... | collective-permute-start | bytes 294920 | tf_op jit(solution)/shard_map/ppermute | solution.py:631
  28.8 20.9 %collective-permute-start.7 = (bf16[912,128]{1,0:T(8,128)(2,1)S(1)}, bf16[912,128]{1,0:T(8,128)(2,1)S(1)}, u32[]{:S(2)}, u32[]{:S(2)}) collective-permute-start(bf16[912,128]{1,0:T(8,128)(2,1)S(1)} %get-tuple-element.161), channel_id=1, source_target_pairs={{0,1},{1,2},{2,3},{3,0},{4,5},{5,6},{6,7},{7,4},{8,9},{9,10},{10,1... | collective-permute-start | bytes 700424 | tf_op jit(solution)/shard_map/ppermute | solution.py:636
  29.6 20.2 %collective-permute-start.8 = (bf16[912,128]{1,0:T(8,128)(2,1)S(1)}, bf16[912,128]{1,0:T(8,128)(2,1)S(1)}, u32[]{:S(2)}, u32[]{:S(2)}) collective-permute-start(bf16[912,128]{1,0:T(8,128)(2,1)S(1)} %get-tuple-element.161), channel_id=1, source_target_pairs={{0,3},{1,0},{2,1},{3,2},{4,7},{5,4},{6,5},{7,6},{8,11},{9,8},{10,9... | collective-permute-start | bytes 700424 | tf_op jit(solution)/shard_map/ppermute | solution.py:636
  32.7 17.0 %collective-permute-start.5 = (bf16[4,144,384]{2,1,0:T(8,128)(2,1)S(1)}, bf16[4,144,384]{2,1,0:T(8,128)(2,1)S(1)}, u32[]{:S(2)}, u32[]{:S(2)}) collective-permute-start(bf16[4,144,384]{2,1,0:T(8,128)(2,1)S(1)} %pad_maximum_fusion.4.refs_0_), channel_id=1, source_target_pairs={{0,8},{4,12},{8,0},{12,4},{16,24},{20,28},{24,16},{28,20},{1,9},{5... | collective-permute-start | bytes 1327112 | tf_op jit(solution)/shard_map/ppermute | solution.py:631
  34.2 15.6 %collective-permute-start.6 = (bf16[4,144,384]{2,1,0:T(8,128)(2,1)S(1)}, bf16[4,144,384]{2,1,0:T(8,128)(2,1)S(1)}, u32[]{:S(2)}, u32[]{:S(2)}) collective-permute-start(bf16[4,144,384]{2,1,0:T(8,128)(2,1)S(1)} %pad_maximum_fusion.4.refs_0_), channel_id=1, source_target_pairs={{0,16},{4,20},{8,24},{12,28},{16,0},{20,4},{24,8},{28,12},{1,17},{... | collective-permute-start | bytes 1327112 | tf_op jit(solution)/shard_map/ppermute | solution.py:631
  50.6 16.4 %collective-permute-start.10 = (bf16[4,144,384]{2,1,0:T(8,128)(2,1)S(1)}, bf16[4,144,384]{2,1,0:T(8,128)(2,1)}, u32[]{:S(2)}, u32[]{:S(2)}) collective-permute-start(bf16[4,144,384]{2,1,0:T(8,128)(2,1)S(1)} %pad_maximum_fusion.4.refs_0_), channel_id=1, source_target_pairs={{0,24},{4,28},{8,16},{12,20},{16,8},{20,12},{24,0},{28,4},{1,25},{... | collective-permute-start | bytes 1327112 | tf_op jit(solution)/shard_map/ppermute | solution.py:631
  51.8 22.4 %collective-permute-start.11 = (bf16[4,144,384]{2,1,0:T(8,128)(2,1)S(1)}, bf16[4,144,384]{2,1,0:T(8,128)(2,1)}, u32[]{:S(2)}, u32[]{:S(2)}) collective-permute-start(bf16[4,144,384]{2,1,0:T(8,128)(2,1)S(1)} %pad_maximum_fusion.4.refs_0_), channel_id=1, source_target_pairs={{0,4},{4,0},{8,12},{12,8},{16,20},{20,16},{24,28},{28,24},{1,5},{5... | collective-permute-start | bytes 1327112 | tf_op jit(solution)/shard_map/ppermute | solution.py:631
  51.9 22.4 %all-to-all-start.1 = ((bf16[32,32,384]{2,1,0:T(8,128)(2,1)}), bf16[32,32,384]{2,1,0:T(8,128)(2,1)S(1)}, u32[]{:S(2)}, u32[]{:S(2)}) async-start(bf16[32,32,384]{2,1,0:T(8,128)(2,1)} %bitcast.13), calls=%async_computation.1 | async-start | bytes 1572864 | tf_op jit(solution)/shard_map/all_to_all | solution.py:737
  74.3 17.6 %collective-permute-start.17 = (bf16[3,432,128]{2,1,0:T(8,128)(2,1)}, bf16[3,432,128]{2,1,0:T(8,128)(2,1)S(1)}, u32[]{:S(2)}, u32[]{:S(2)}) collective-permute-start(bf16[3,432,128]{2,1,0:T(8,128)(2,1)} %pad_maximum_fusion.8), channel_id=1, source_target_pairs={{0,16},{4,20},{8,24},{12,28},{16,0},{20,4},{24,8},{28,12},{1,17},{... | collective-permute-start | bytes 995336 | tf_op jit(solution)/shard_map/ppermute | solution.py:631
  75.8 16.2 %collective-permute-start.16 = (bf16[3,480,128]{2,1,0:T(8,128)(2,1)}, bf16[3,480,128]{2,1,0:T(8,128)(2,1)S(1)}, u32[]{:S(2)}, u32[]{:S(2)}) collective-permute-start(bf16[3,480,128]{2,1,0:T(8,128)(2,1)} %pad_maximum_fusion.6), channel_id=1, source_target_pairs={{0,8},{4,12},{8,0},{12,4},{16,24},{20,28},{24,16},{28,20},{1,9},{5... | collective-permute-start | bytes 1105928 | tf_op jit(solution)/shard_map/ppermute | solution.py:631
  77.3 14.7 %collective-permute-start.18 = (bf16[912,128]{1,0:T(8,128)(2,1)S(1)}, bf16[912,128]{1,0:T(8,128)(2,1)S(1)}, u32[]{:S(2)}, u32[]{:S(2)}) collective-permute-start(bf16[912,128]{1,0:T(8,128)(2,1)S(1)} %get-tuple-element.161), channel_id=1, source_target_pairs={{0,2},{1,3},{2,0},{3,1},{4,6},{5,7},{6,4},{7,5},{8,10},{9,11},{10,... | collective-permute-start | bytes 700424 | tf_op jit(solution)/shard_map/ppermute | solution.py:636
  93.1 38.1 %collective-permute-start.21 = (bf16[4,384,128]{2,1,0:T(8,128)(2,1)}, bf16[4,384,128]{2,1,0:T(8,128)(2,1)}, u32[]{:S(2)}, u32[]{:S(2)}) collective-permute-start(bf16[4,384,128]{2,1,0:T(8,128)(2,1)} %get-tuple-element.264), channel_id=1, source_target_pairs={{0,2},{1,3},{2,0},{3,1},{4,6},{5,7},{6,4},{7,5},{8,10},{9,11},{10,... | collective-permute-start | bytes 1179656 | tf_op jit(solution)/shard_map/ppermute | solution.py:816
  94.8 37.5 %all-to-all-start.2 = ((bf16[8,576,256]{2,1,0:T(8,128)(2,1)}), bf16[8,576,256]{2,1,0:T(8,128)(2,1)S(1)}, u32[]{:S(2)}, u32[]{:S(2)}) async-start(bf16[8,576,256]{2,1,0:T(8,128)(2,1)} %get-tuple-element.165), calls=%async_computation.2 | async-start | bytes 4718592 | tf_op jit(solution)/shard_map/all_to_all | solution.py:737
  102.6 27.0 %collective-permute-start.20 = (bf16[432,128]{1,0:T(8,128)(2,1)S(1)}, bf16[432,128]{1,0:T(8,128)(2,1)S(1)}, u32[]{:S(2)}, u32[]{:S(2)}) collective-permute-start(bf16[432,128]{1,0:T(8,128)(2,1)S(1)} %slice.214), channel_id=1, source_target_pairs={{0,16},{4,20},{8,24},{12,28},{16,0},{20,4},{24,8},{28,12},{1,17},{... | collective-permute-start | bytes 331784 | tf_op jit(solution)/shard_map/ppermute | solution.py:631
  104.6 25.3 %collective-permute-start.19 = (bf16[480,128]{1,0:T(8,128)(2,1)S(1)}, bf16[480,128]{1,0:T(8,128)(2,1)S(1)}, u32[]{:S(2)}, u32[]{:S(2)}) collective-permute-start(bf16[480,128]{1,0:T(8,128)(2,1)S(1)} %slice.211), channel_id=1, source_target_pairs={{0,8},{4,12},{8,0},{12,4},{16,24},{20,28},{24,16},{28,20},{1,9},{5... | collective-permute-start | bytes 368648 | tf_op jit(solution)/shard_map/ppermute | solution.py:631
  132.3 23.8 %collective-permute-start.22 = (bf16[2,4,480,128]{3,2,1,0:T(8,128)(2,1)}, bf16[2,4,480,128]{3,2,1,0:T(8,128)(2,1)S(1)}, u32[]{:S(2)}, u32[]{:S(2)}) collective-permute-start(bf16[2,4,480,128]{3,2,1,0:T(8,128)(2,1)} %bitcast.158), channel_id=1, source_target_pairs={{0,16},{4,20},{8,24},{12,28},{16,0},{20,4},{24,8},{28,12},{1,17},{... | collective-permute-start | bytes 2949128 | tf_op jit(solution)/shard_map/ppermute | solution.py:631
  133.9 38.9 %collective-permute-start.25 = (bf16[2,4,480,128]{3,2,1,0:T(8,128)(2,1)}, bf16[2,4,480,128]{3,2,1,0:T(8,128)(2,1)S(1)}, u32[]{:S(2)}, u32[]{:S(2)}) collective-permute-start(bf16[2,4,480,128]{3,2,1,0:T(8,128)(2,1)} %bitcast.159), channel_id=1, source_target_pairs={{0,4},{4,0},{8,12},{12,8},{16,20},{20,16},{24,28},{28,24},{1,5},{5... | collective-permute-start | bytes 2949128 | tf_op jit(solution)/shard_map/ppermute | solution.py:631
  133.9 22.3 %collective-permute-start.23 = (bf16[2,4,432,128]{3,2,1,0:T(8,128)(2,1)}, bf16[2,4,432,128]{3,2,1,0:T(8,128)(2,1)S(1)}, u32[]{:S(2)}, u32[]{:S(2)}) collective-permute-start(bf16[2,4,432,128]{3,2,1,0:T(8,128)(2,1)} %bitcast.140), channel_id=1, source_target_pairs={{0,8},{4,12},{8,0},{12,4},{16,24},{20,28},{24,16},{28,20},{1,9},{5... | collective-permute-start | bytes 2654216 | tf_op jit(solution)/shard_map/ppermute | solution.py:631
  134.4 22.3 %collective-permute-start.26 = (bf16[2,4,432,128]{3,2,1,0:T(8,128)(2,1)}, bf16[2,4,432,128]{3,2,1,0:T(8,128)(2,1)S(1)}, u32[]{:S(2)}, u32[]{:S(2)}) collective-permute-start(bf16[2,4,432,128]{3,2,1,0:T(8,128)(2,1)} %bitcast.141), channel_id=1, source_target_pairs={{0,4},{4,0},{8,12},{12,8},{16,20},{20,16},{24,28},{28,24},{1,5},{5... | collective-permute-start | bytes 2654216 | tf_op jit(solution)/shard_map/ppermute | solution.py:631
  134.7 19.9 %collective-permute-start.24 = (bf16[2,4,384,128]{3,2,1,0:T(8,128)(2,1)S(1)}, bf16[2,4,384,128]{3,2,1,0:T(8,128)(2,1)S(1)}, u32[]{:S(2)}, u32[]{:S(2)}) collective-permute-start(bf16[2,4,384,128]{3,2,1,0:T(8,128)(2,1)S(1)} %pad_maximum_fusion.1.refs_8_), channel_id=1, source_target_pairs={{0,1},{1,0},{2,3},{3,2},{4,5},{5,4},{6,7},{7,6},{8,9},{9,8},{10,11... | collective-permute-start | bytes 2359304 | tf_op jit(solution)/shard_map/ppermute | solution.py:816
  156.2 16.7 %collective-permute-start.27 = (bf16[2,4,480,128]{3,2,1,0:T(8,128)(2,1)S(1)}, bf16[2,4,480,128]{3,2,1,0:T(8,128)(2,1)S(1)}, u32[]{:S(2)}, u32[]{:S(2)}) collective-permute-start(bf16[2,4,480,128]{3,2,1,0:T(8,128)(2,1)S(1)} %collective-permute-done.22.refs_2_), channel_id=1, source_target_pairs={{0,4},{4,0},{8,12},{12,8},{16,20},{20,16},{24,28},{28,24},{1,5},{5... | collective-permute-start | bytes 2949128 | tf_op jit(solution)/shard_map/ppermute | solution.py:631
  156.2 16.7 %collective-permute-start.28 = (bf16[2,4,432,128]{3,2,1,0:T(8,128)(2,1)S(1)}, bf16[2,4,432,128]{3,2,1,0:T(8,128)(2,1)S(1)}, u32[]{:S(2)}, u32[]{:S(2)}) collective-permute-start(bf16[2,4,432,128]{3,2,1,0:T(8,128)(2,1)S(1)} %collective-permute-done.23.refs_3_), channel_id=1, source_target_pairs={{0,4},{4,0},{8,12},{12,8},{16,20},{20,16},{24,28},{28,24},{1,5},{5... | collective-permute-start | bytes 2654216 | tf_op jit(solution)/shard_map/ppermute | solution.py:631
  156.7 16.2 %collective-permute-start.29 = (bf16[2,4,384,128]{3,2,1,0:T(8,128)(2,1)S(1)}, bf16[2,4,384,128]{3,2,1,0:T(8,128)(2,1)S(1)}, u32[]{:S(2)}, u32[]{:S(2)}) collective-permute-start(bf16[2,4,384,128]{3,2,1,0:T(8,128)(2,1)S(1)} %pad_maximum_fusion.1.refs_8_), channel_id=1, source_target_pairs={{0,4},{4,0},{8,12},{12,8},{16,20},{20,16},{24,28},{28,24},{1,5},{5... | collective-permute-start | bytes 2359304 | tf_op jit(solution)/shard_map/ppermute | solution.py:631
  156.7 16.1 %collective-permute-start.30 = (bf16[2,4,384,128]{3,2,1,0:T(8,128)(2,1)S(1)}, bf16[2,4,384,128]{3,2,1,0:T(8,128)(2,1)S(1)}, u32[]{:S(2)}, u32[]{:S(2)}) collective-permute-start(bf16[2,4,384,128]{3,2,1,0:T(8,128)(2,1)S(1)} %collective-permute-done.24.refs_9_), channel_id=1, source_target_pairs={{0,4},{4,0},{8,12},{12,8},{16,20},{20,16},{24,28},{28,24},{1,5},{5... | collective-permute-start | bytes 2359304 | tf_op jit(solution)/shard_map/ppermute | solution.py:631
  201.7 20.3 %all-to-all-start.4 = ((bf16[8,192,256]{2,1,0:T(8,128)(2,1)}), bf16[8,192,256]{2,1,0:T(8,128)(2,1)S(1)}, u32[]{:S(2)}, u32[]{:S(2)}) async-start(bf16[8,192,256]{2,1,0:T(8,128)(2,1)} %copy-done.1), calls=%async_computation.4 | async-start | bytes 1572864 | tf_op jit(solution)/shard_map/all_to_all | solution.py:737
  222.0 20.6 %collective-permute-start.31 = (bf16[4,4,672,128]{3,2,1,0:T(8,128)(2,1)}, bf16[4,4,672,128]{3,2,1,0:T(8,128)(2,1)}, u32[]{:S(2)}, u32[]{:S(2)}) collective-permute-start(bf16[4,4,672,128]{3,2,1,0:T(8,128)(2,1)} %get-tuple-element.194), channel_id=1, source_target_pairs={{0,4},{4,0},{8,12},{12,8},{16,20},{20,16},{24,28},{28,24},{1,5},{5... | collective-permute-start | bytes 8257544 | tf_op jit(solution)/shard_map/ppermute | solution.py:631
  222.4 20.2 %collective-permute-start.32 = (bf16[4,4,624,128]{3,2,1,0:T(8,128)(2,1)}, bf16[4,4,624,128]{3,2,1,0:T(8,128)(2,1)}, u32[]{:S(2)}, u32[]{:S(2)}) collective-permute-start(bf16[4,4,624,128]{3,2,1,0:T(8,128)(2,1)} %get-tuple-element.195), channel_id=1, source_target_pairs={{0,4},{4,0},{8,12},{12,8},{16,20},{20,16},{24,28},{28,24},{1,5},{5... | collective-permute-start | bytes 7667720 | tf_op jit(solution)/shard_map/ppermute | solution.py:631
  238.1 38.7 %all-to-all-start.5 = ((bf16[8,192,256]{2,1,0:T(8,128)(2,1)}), bf16[8,192,256]{2,1,0:T(8,128)(2,1)}, u32[]{:S(2)}, u32[]{:S(2)}) async-start(bf16[8,192,256]{2,1,0:T(8,128)(2,1)} %copy-done.2), calls=%async_computation.5 | async-start | bytes 1572864 | tf_op jit(solution)/shard_map/all_to_all | solution.py:737
  245.8 35.8 %collective-permute-start.34 = (bf16[2,4,624,128]{3,2,1,0:T(8,128)(2,1)}, bf16[2,4,624,128]{3,2,1,0:T(8,128)(2,1)}, u32[]{:S(2)}, u32[]{:S(2)}) collective-permute-start(bf16[2,4,624,128]{3,2,1,0:T(8,128)(2,1)} %add_convert_fusion.1), channel_id=1, source_target_pairs={{0,16},{4,20},{8,24},{12,28},{16,0},{20,4},{24,8},{28,12},{1,17},{... | collective-permute-start | bytes 3833864 | tf_op jit(solution)/shard_map/ppermute | solution.py:631
  250.9 33.0 %collective-permute-start.33 = (bf16[2,4,672,128]{3,2,1,0:T(8,128)(2,1)}, bf16[2,4,672,128]{3,2,1,0:T(8,128)(2,1)}, u32[]{:S(2)}, u32[]{:S(2)}) collective-permute-start(bf16[2,4,672,128]{3,2,1,0:T(8,128)(2,1)} %add_convert_fusion), channel_id=1, source_target_pairs={{0,8},{4,12},{8,0},{12,4},{16,24},{20,28},{24,16},{28,20},{1,9},{5... | collective-permute-start | bytes 4128776 | tf_op jit(solution)/shard_map/ppermute | solution.py:631
  283.9 25.6 %all-to-all-start.6 = ((bf16[8,384,256]{2,1,0:T(8,128)(2,1)}), bf16[8,384,256]{2,1,0:T(8,128)(2,1)}, u32[]{:S(2)}, u32[]{:S(2)}) async-start(bf16[8,384,256]{2,1,0:T(8,128)(2,1)} %attend_grad_1.1), calls=%async_computation.6 | async-start | bytes 3145728 | tf_op jit(solution)/shard_map/all_to_all | solution.py:737
  309.5 15.6 %collective-permute-start.35 = (bf16[4,672,128]{2,1,0:T(8,128)(2,1)}, bf16[4,672,128]{2,1,0:T(8,128)(2,1)S(1)}, u32[]{:S(2)}, u32[]{:S(2)}) collective-permute-start(bf16[4,672,128]{2,1,0:T(8,128)(2,1)} %fusion.2), channel_id=1, source_target_pairs={{0,16},{4,20},{8,24},{12,28},{16,0},{20,4},{24,8},{28,12},{1,17},{... | collective-permute-start | bytes 2064392 | tf_op jit(solution)/shard_map/ppermute | solution.py:631
  310.0 15.1 %collective-permute-start.36 = (bf16[4,624,128]{2,1,0:T(8,128)(2,1)}, bf16[4,624,128]{2,1,0:T(8,128)(2,1)}, u32[]{:S(2)}, u32[]{:S(2)}) collective-permute-start(bf16[4,624,128]{2,1,0:T(8,128)(2,1)} %fusion.4), channel_id=1, source_target_pairs={{0,8},{4,12},{8,0},{12,4},{16,24},{20,28},{24,16},{28,20},{1,9},{5... | collective-permute-start | bytes 1916936 | tf_op jit(solution)/shard_map/ppermute | solution.py:631
  329.8 24.6 %collective-permute-start.37 = (bf16[2,1296,128]{2,1,0:T(8,128)(2,1)}, bf16[2,1296,128]{2,1,0:T(8,128)(2,1)S(1)}, u32[]{:S(2)}, u32[]{:S(2)}) collective-permute-start(bf16[2,1296,128]{2,1,0:T(8,128)(2,1)} %pad_maximum_fusion.2), channel_id=1, source_target_pairs={{0,1},{1,0},{2,3},{3,2},{4,5},{5,4},{6,7},{7,6},{8,9},{9,8},{10,11... | collective-permute-start | bytes 1990664 | tf_op jit(solution)/shard_map/ppermute | solution.py:816
  330.9 50.7 %all-to-all-start.7 = ((bf16[32,32,384]{2,1,0:T(8,128)(2,1)}), bf16[32,32,384]{2,1,0:T(8,128)(2,1)S(1)}, u32[]{:S(2)}, u32[]{:S(2)}) async-start(bf16[32,32,384]{2,1,0:T(8,128)(2,1)} %bitcast.51), calls=%async_computation.7 | async-start | bytes 1572864 | tf_op jit(solution)/shard_map/all_to_all | solution.py:737
  338.9 17.3 %collective-permute-start.39 = (bf16[4,480,128]{2,1,0:T(8,128)(2,1)}, bf16[4,480,128]{2,1,0:T(8,128)(2,1)}, u32[]{:S(2)}, u32[]{:S(2)}) collective-permute-start(bf16[4,480,128]{2,1,0:T(8,128)(2,1)} %get-tuple-element.254), channel_id=1, source_target_pairs={{0,8},{4,12},{8,0},{12,4},{16,24},{20,28},{24,16},{28,20},{1,9},{5... | collective-permute-start | bytes 1474568 | tf_op jit(solution)/shard_map/ppermute | solution.py:631
  340.8 28.1 %collective-permute-start.40 = (bf16[4,480,128]{2,1,0:T(8,128)(2,1)}, bf16[4,480,128]{2,1,0:T(8,128)(2,1)}, u32[]{:S(2)}, u32[]{:S(2)}) collective-permute-start(bf16[4,480,128]{2,1,0:T(8,128)(2,1)} %get-tuple-element.253), channel_id=1, source_target_pairs={{0,16},{4,20},{8,24},{12,28},{16,0},{20,4},{24,8},{28,12},{1,17},{... | collective-permute-start | bytes 1474568 | tf_op jit(solution)/shard_map/ppermute | solution.py:631
  342.3 28.2 %collective-permute-start.41 = (bf16[4,480,128]{2,1,0:T(8,128)(2,1)}, bf16[4,480,128]{2,1,0:T(8,128)(2,1)}, u32[]{:S(2)}, u32[]{:S(2)}) collective-permute-start(bf16[4,480,128]{2,1,0:T(8,128)(2,1)} %get-tuple-element.252), channel_id=1, source_target_pairs={{0,24},{4,28},{8,16},{12,20},{16,8},{20,12},{24,0},{28,4},{1,25},{... | collective-permute-start | bytes 1474568 | tf_op jit(solution)/shard_map/ppermute | solution.py:631
  354.5 19.1 %collective-permute-start.45 = (bf16[1296,128]{1,0:T(8,128)(2,1)S(1)}, bf16[1296,128]{1,0:T(8,128)(2,1)S(1)}, u32[]{:S(2)}, u32[]{:S(2)}) collective-permute-start(bf16[1296,128]{1,0:T(8,128)(2,1)S(1)} %fusion.10), channel_id=1, source_target_pairs={{0,2},{1,3},{2,0},{3,1},{4,6},{5,7},{6,4},{7,5},{8,10},{9,11},{10,... | collective-permute-start | bytes 995336 | tf_op jit(solution)/shard_map/ppermute | solution.py:816
  373.7 15.9 %collective-permute-start.46 = (bf16[1296,128]{1,0:T(8,128)(2,1)S(1)}, bf16[1296,128]{1,0:T(8,128)(2,1)S(1)}, u32[]{:S(2)}, u32[]{:S(2)}) collective-permute-start(bf16[1296,128]{1,0:T(8,128)(2,1)S(1)} %fusion.3), channel_id=1, source_target_pairs={{0,8},{4,12},{8,0},{12,4},{16,24},{20,28},{24,16},{28,20},{1,9},{5... | collective-permute-start | bytes 995336 | tf_op jit(solution)/shard_map/ppermute | solution.py:631
  374.7 15.9 %collective-permute-start.47 = (bf16[1296,128]{1,0:T(8,128)(2,1)S(1)}, bf16[1296,128]{1,0:T(8,128)(2,1)S(1)}, u32[]{:S(2)}, u32[]{:S(2)}) collective-permute-start(bf16[1296,128]{1,0:T(8,128)(2,1)S(1)} %fusion.3), channel_id=1, source_target_pairs={{0,16},{4,20},{8,24},{12,28},{16,0},{20,4},{24,8},{28,12},{1,17},{... | collective-permute-start | bytes 995336 | tf_op jit(solution)/shard_map/ppermute | solution.py:631
  376.4 25.9 %collective-permute-start.48 = (bf16[1296,128]{1,0:T(8,128)(2,1)S(1)}, bf16[1296,128]{1,0:T(8,128)(2,1)S(1)}, u32[]{:S(2)}, u32[]{:S(2)}) collective-permute-start(bf16[1296,128]{1,0:T(8,128)(2,1)S(1)} %fusion.3), channel_id=1, source_target_pairs={{0,24},{4,28},{8,16},{12,20},{16,8},{20,12},{24,0},{28,4},{1,25},{... | collective-permute-start | bytes 995336 | tf_op jit(solution)/shard_map/ppermute | solution.py:631
  377.3 12.3 %collective-permute-start.43 = (bf16[480,128]{1,0:T(8,128)(2,1)S(1)}, bf16[480,128]{1,0:T(8,128)(2,1)S(1)}, u32[]{:S(2)}, u32[]{:S(2)}) collective-permute-start(bf16[480,128]{1,0:T(8,128)(2,1)S(1)} %get-tuple-element.261), channel_id=1, source_target_pairs={{0,2},{1,3},{2,0},{3,1},{4,6},{5,7},{6,4},{7,5},{8,10},{9,11},{10,... | collective-permute-start | bytes 368648 | tf_op jit(solution)/shard_map/ppermute | solution.py:816
  (68 other events, 603.5 us)

commit v6 on v5

--- a/solution.py
+++ b/solution.py
@@ -499,8 +499,8 @@
     return pl.pallas_call(
         functools.partial(attend_short_kernel, pairs, piece),
         out_shape=(
-            jax.ShapeDtypeStruct((contexts, pairs * HD, tokens), BF),
-            jax.ShapeDtypeStruct((pairs, HD, length), F32),
+            pltpu.HBM((contexts, pairs * HD, tokens), BF),
+            pltpu.HBM((pairs, HD, length), F32),
             jax.ShapeDtypeStruct((pairs, 1, length), F32),
         ),
         in_specs=[smem(), vmem()],
@@ -616,7 +616,7 @@
     full = pltpu.VMEM((HD, length), F32)
     return pl.pallas_call(
         functools.partial(attend_grad_short_kernel, pairs, begin, count, piece),
-        out_shape=jax.ShapeDtypeStruct((contexts, 3 * count * HD, tokens), BF),
+        out_shape=pltpu.HBM((contexts, 3 * count * HD, tokens), BF),
         in_specs=[smem()] + [vmem()] * 6,
         out_specs=vmem(),
         scratch_shapes=[wide_] * 3 + [tall] * 2 + [full] * 2,
@@ -1159,15 +1159,15 @@
         functools.partial(mlp_kernel, pairs),
         grid=(steps,),
         out_shape=(
-            jax.ShapeDtypeStruct((tokens, D), BF),
-            jax.ShapeDtypeStruct((tokens, D), BF),
-            jax.ShapeDtypeStruct((tokens, D), BF),
+            pltpu.HBM((tokens, D), BF),
+            pltpu.HBM((tokens, D), BF),
+            pltpu.HBM((tokens, D), BF),
             jax.ShapeDtypeStruct((tokens, FF), BF),
             jax.ShapeDtypeStruct((tokens, FF), BF),
             jax.ShapeDtypeStruct((tokens, FF), BF),
             jax.ShapeDtypeStruct((1, D), F32),
             jax.ShapeDtypeStruct((tokens, D), F32),
-            jax.ShapeDtypeStruct(came.shape, BF),
+            pltpu.HBM(came.shape, BF),
         ),
         in_specs=[smem()] + [whole(x.shape) for x in (came, start, gains, upstream, *blocks)],
         out_specs=(
@@ -1714,7 +1714,8 @@
         sin_t,
         *first_blocks,
     )
-    sent, near, late, tall = lax.optimization_barrier((sent, near, late, tall))
+    sent, near, tall = lax.optimization_barrier((sent, near, tall))
+    near, late, tall = lax.optimization_barrier((near, late, tall))
     tall = jnp.stack([third] + tall)
     tall = jnp.stack([tall, over_fsdp(tall, 2)])
     near_late = [over_ctx(late[:WCUT], 2), over_ctx(late[WCUT:], 4)]
@@ -1757,7 +1758,7 @@
     other_u, other_l = after((other_u, other_l), grad_rows)
     core_u, core_l = over_ctx(other_u, 1), over_ctx(other_l, 1)
     part = functools.partial(attend_grad_short, order)
-    shared = (attended_t, logsum, cos_t, sin_t, pairs, piece)
+    shared = (in_hbm(attended_t), logsum, in_hbm(cos_t), in_hbm(sin_t), pairs, piece)
     grad_a = part(rows, grad_rows, *shared, 0, 1)
     came_a = exchange(grad_a, "ctx")
     core_u, core_l = after((core_u, core_l), grad_a)
@@ -1765,7 +1766,7 @@
     near_l = add_all(own_l[:2], core_l[:2]).astype(BF)
     from_x, from_y = over_ctx(near_u, 2), over_ctx(near_l, 4)
     grad_b = part(after(rows, near_u, near_l), grad_rows, *shared, 1, pairs - 1)
-    grad_b, came_a, from_x, from_y = lax.optimization_barrier((grad_b, came_a, from_x, from_y))
+    from_x, from_y, came_a = lax.optimization_barrier((from_x, from_y, came_a))
     far_u = add_all(own_u[2], core_u[2], from_x[1]).astype(BF)
     far_l = add_all(own_l[2], core_l[2], from_y[1]).astype(BF)
     came_b = exchange(grad_b, "ctx")

time: 421 us -> 406 us (0.964)
  local copies, waits for them, and re-layouts: 27.3 us -> 16 us
  waiting for transfers between devices: 98.2 us -> 93 us
    unnamed x126 -> x82, local copies, waits for them, and re-layouts: 20.9 us -> 12.5 us
  transfers between devices with their start and end apart: 61 -> 61, of which waited for: 16 -> 16; matrix products, arithmetic and copies ran while one was open for 10% -> 9% of each run, Pallas kernels for 32% -> 34%
where the time goes in v6:
time: 406 us; the launch traced here: 399 us
  Pallas kernels  164 us (40%)
  waiting for transfers between devices  93 us (23%)
  starting transfers between devices  82.1 us (20%)
  other arithmetic  25.7 us (6%)
  blocking collectives  16.5 us (4%)
  local copies, waits for them, and re-layouts  16 us (4%)
    ppermute x41, waiting for transfers between devices, over_ctx(): return lax.ppermute(value, 'ctx', [(i, i ^ mask) for i in range(size)])  57.1 us
    pallas_call x2, Pallas kernels, attend_grad_short(): pl.pallas_call(functools.partial(attend_grad_short_kernel, pairs, begin,...  38.6 us
    ppermute x41, starting transfers between devices, over_ctx(): return lax.ppermute(value, 'ctx', [(i, i ^ mask) for i in range(size)])  34.3 us
    all_to_all x7, starting transfers between devices, exchange(): return lax.all_to_all(values, axes, split_axis=0, concat_axis=0, tiled=True)  26.5 us
    pallas_call x1, Pallas kernels, mlp(): pl.pallas_call(functools.partial(mlp_kernel, pairs), grid=(steps,), out_s...  23.9 us
    all_to_all x7, waiting for transfers between devices, exchange(): return lax.all_to_all(values, axes, split_axis=0, concat_axis=0, tiled=True)  23.7 us
    pallas_call x1, Pallas kernels, attend_short(): pl.pallas_call(functools.partial(attend_short_kernel, pairs, piece), out_...  19 us
    all_to_all x1, blocking collectives, exchange(): return lax.all_to_all(values, axes, split_axis=0, concat_axis=0, tiled=True)  16.5 us
  transfers between devices with their start and end apart: 61, of which 16 were waited for; matrix products, arithmetic and copies ran while one was open for 9% of the time, Pallas kernels for 34%

profile of v6, /device:TPU:0, one launch (start us, length us, event | category | flops | bytes accessed | tf_op | source)
XLA Modules:
  0.0 398.8 jit_solution(13647766550967434943)
XLA Ops:
  4.9 3.1 collective-permute-start.4
  8.0 2.6 collective-permute-start.3
  14.9 2.5 all-to-all-start
  17.5 1.8 fusion.12
  20.1 6.4 %all-to-all-done = s32[32,1,64]{2,1,0:T(1,128)S(1)} async-done(((s32[32,1,64]{2,1,0:T(1,128)}), s32[32,1,64]{2,1,0:T(1,128)S(1)}, u32[]{:S(2)}, u32[]{:S(2)}) %all-to-all-start) | async-done | bytes 8224 | tf_op jit(solution)/shard_map/all_to_all | solution.py:737
  28.3 3.1 collective-permute-start.8
  34.3 14.1 %read_rows.1 = bf16[1024,384]{1,0:T(8,128)(2,1)} custom-call(s32[2,1024]{1,0:T(2,128)S(1)} %pad_add_fusion.codes, bf16[192,12800]{1,0:T(8,128)(2,1)} %bitcast.169, bf16[192,12800]{1,0:T(8,128)(2,1)} %bitcast.170), custom_call_target="tpu_custom_call" | custom-call | flops 10200000512 | bytes 42500000 | tf_op jit(solution)/shard_map/read_rows/pallas_call | solution.py:156
  50.5 2.8 all-to-all-start.1
  53.3 11.6 %collective-permute-done.10.refs_3_ = bf16[4,144,384]{2,1,0:T(8,128)(2,1)S(1)} collective-permute-done((bf16[4,144,384]{2,1,0:T(8,128)(2,1)S(1)}, bf16[4,144,384]{2,1,0:T(8,128)(2,1)S(1)}, u32[]{:S(2)}, u32[]{:S(2)}) %collective-permute-start.10) | collective-permute-done | bytes 442400 | tf_op jit(solution)/shard_map/ppermute | solution.py:631
  68.9 4.0 all-to-all-done.1
  77.2 13.3 %front.1 = (f32[512,768]{1,0:T(8,128)}, bf16[512,192]{1,0:T(8,128)(2,1)}, bf16[512,768]{1,0:T(8,128)(2,1)}, bf16[8,576,256]{2,1,0:T(8,128)(2,1)}, bf16[768,2304]...) custom-call(s32[3]{0:T(128)} %copy-done.2, s32[2]{0:T(128)} %dynamic_slice.6.starts, ...), custom_call_target="tpu_custom_call" | custom-call | flops 5400000000 | bytes 22500000 | tf_op jit(solution)/shard_map/front/pallas_call | solution.py:988
  91.2 3.9 all-to-all-start.2
  96.2 1.7 collective-permute-start.21
  99.3 2.0 collective-permute-start.20
  105.6 20.3 %collective-permute-done.20 = bf16[432,128]{1,0:T(8,128)(2,1)S(1)} collective-permute-done((bf16[432,128]{1,0:T(8,128)(2,1)S(1)}, bf16[432,128]{1,0:T(8,128)(2,1)S(1)}, u32[]{:S(2)}, u32[]{:S(2)}) %collective-permute-start.20) | collective-permute-done | bytes 110624 | tf_op jit(solution)/shard_map/ppermute | solution.py:631
  132.2 19.0 %attend.1 = (bf16[8,192,256]{2,1,0:T(8,128)(2,1)}, f32[3,64,2048]{2,1,0:T(8,128)}, f32[3,1,2048]{2,1,0:T(1,128)S(1)}) custom-call(s32[16]{0:T(128)S(1)} %select_reduce_fusion.order, bf16[8,576,256]{2,1,0:T(8,128)(2,1)S(1)} %all-to-all-done.2.rows), custom_call_target="tpu_custom_call" | custom-call | flops 15000000512 | bytes 62500000 | tf_op jit(solution)/shard_map/attend/pallas_call | solution.py:499
  153.2 16.5 %all_to_all.47.came = bf16[8,192,256]{2,1,0:T(8,128)(2,1)S(1)} all-to-all(bf16[8,192,256]{2,1,0:T(8,128)(2,1)} %get-tuple-element.182), channel_id=1, replica_groups=mesh['ctx'=8,'fsdp'=4] {'ctx'}, dimensions={0} | all-to-all | bytes 1572864 | tf_op jit(solution)/shard_map/all_to_all | solution.py:737
  171.0 23.9 %mlp.1 = (bf16[512,768]{1,0:T(8,128)(2,1)}, bf16[512,768]{1,0:T(8,128)(2,1)}, bf16[512,768]{1,0:T(8,128)(2,1)}, bf16[512,2048]{1,0:T(8,128)(2,1)}, bf16[512,2048...) custom-call(s32[3]{0:T(128)S(1)} %copy-done.3, ...), custom_call_target="tpu_custom_call" | custom-call | flops 13799999488 | bytes 57500000 | tf_op jit(solution)/shard_map/mlp/pallas_call | solution.py:1158
  195.0 3.7 all-to-all-start.4
  198.7 16.5 %weight_grads.1 = (bf16[4,4,672,128]{3,2,1,0:T(8,128)(2,1)}, bf16[4,4,624,128]{3,2,1,0:T(8,128)(2,1)}, bf16[4,4,672,128]{3,2,1,0:T(8,128)(2,1)}, bf16[4,4,624,128]{3,2,1,0:T(8,128)(2,1)}) custom-call(s32[3]{0:T(128)} %copy-done.2, bf16[512,768]{1,0:T(8,128)(2,1)} %get-tuple-element.193.hidden, bf16[512,2048]{1,0:T(8,128)(2,1)} %get-tuple-element.194.gate, ...), custom_call_target="tpu_custom_call" | custom-call | flops 8999999488 | bytes 37500000 | tf_op jit(solution)/shard_map/weight_grads/pallas_call | solution.py:1282
  215.8 14.3 %attend_grad_0.1 = bf16[8,192,256]{2,1,0:T(8,128)(2,1)} custom-call(s32[16]{0:T(128)S(1)} %select_reduce_fusion.order, bf16[8,576,256]{2,1,0:T(8,128)(2,1)S(1)} %all-to-all-done.2.rows, bf16[8,192,256]{2,1,0:T(8,128)(2,1)S(1)} %all-to-all-done.4.grads, f32[3,64,2048]{2,1,0:T(8,128)} %get-tuple-element.205.attended_t, ...), custom_call_target="tpu_custom_call" | custom-call | flops 8400000000 | bytes 35000000 | tf_op jit(solution)/shard_map/attend_grad_0/pallas_call | solution.py:617
  230.0 4.4 %all-to-all-start.5 = ((bf16[8,192,256]{2,1,0:T(8,128)(2,1)}), bf16[8,192,256]{2,1,0:T(8,128)(2,1)}, u32[]{:S(2)}, u32[]{:S(2)}) async-start(bf16[8,192,256]{2,1,0:T(8,128)(2,1)} %attend_grad_0.1), calls=%async_computation.5 | async-start | bytes 1572864 | tf_op jit(solution)/shard_map/all_to_all | solution.py:737
  234.5 3.3 add_convert_fusion.1
  237.8 2.0 collective-permute-start.34
  239.8 2.8 add_convert_fusion
  244.1 24.3 %attend_grad_1.1 = bf16[8,384,256]{2,1,0:T(8,128)(2,1)} custom-call(s32[16]{0:T(128)S(1)} %select_reduce_fusion.order, bf16[8,576,256]{2,1,0:T(8,128)(2,1)S(1)} %all-to-all-done.2.rows, bf16[8,192,256]{2,1,0:T(8,128)(2,1)S(1)} %all-to-all-done.4.grads, f32[3,64,2048]{2,1,0:T(8,128)} %get-tuple-element.205.attended_t, ...), custom_call_target="tpu_custom_call" | custom-call | flops 16800000000 | bytes 70000000 | tf_op jit(solution)/shard_map/attend_grad_1/pallas_call | solution.py:617
  268.4 4.7 %all-to-all-start.6 = ((bf16[8,384,256]{2,1,0:T(8,128)(2,1)}), bf16[8,384,256]{2,1,0:T(8,128)(2,1)}, u32[]{:S(2)}, u32[]{:S(2)}) async-start(bf16[8,384,256]{2,1,0:T(8,128)(2,1)} %attend_grad_1.1), calls=%async_computation.6 | async-start | bytes 3145728 | tf_op jit(solution)/shard_map/all_to_all | solution.py:737
  273.5 2.2 collective-permute-done.33
  275.8 2.4 fusion.4
  278.2 2.7 fusion.2
  280.9 13.3 %all-to-all-done.6.came_b = bf16[8,384,256]{2,1,0:T(8,128)(2,1)} async-done(((bf16[8,384,256]{2,1,0:T(8,128)(2,1)}), bf16[8,384,256]{2,1,0:T(8,128)(2,1)}, u32[]{:S(2)}, u32[]{:S(2)}) %all-to-all-start.6) | async-done | bytes 1572896 | tf_op jit(solution)/shard_map/all_to_all | solution.py:737
  295.3 14.5 %back.1 = (f32[512,768]{1,0:T(8,128)}, bf16[1024,384]{1,0:T(8,128)(2,1)}, bf16[4,4,480,128]{3,2,1,0:T(8,128)(2,1)}, bf16[4,4,480,128]{3,2,1,0:T(8,128)(2,1)}) custom-call(s32[3]{0:T(128)} %copy-done.2, bf16[8,192,256]{2,1,0:T(8,128)(2,1)} %all-to-all-done.5.came_a, bf16[8,384,256]{2,1,0:T(8,128)(2,1)} %all-to-all-done.6.came_b, ...), custom_call_target="tpu_custom_call" | custom-call | flops 7800000000 | bytes 32500000 | tf_op jit(solution)/shard_map/back/pallas_call | solution.py:1405
  309.8 1.8 fusion.1
  311.7 1.9 fusion
  316.0 4.4 %all-to-all-start.7 = ((bf16[32,32,384]{2,1,0:T(8,128)(2,1)}), bf16[32,32,384]{2,1,0:T(8,128)(2,1)S(1)}, u32[]{:S(2)}, u32[]{:S(2)}) async-start(bf16[32,32,384]{2,1,0:T(8,128)(2,1)} %bitcast.51), calls=%async_computation.7 | async-start | bytes 1572864 | tf_op jit(solution)/shard_map/all_to_all | solution.py:737
  320.5 3.5 fusion.5
  324.0 1.9 collective-permute-start.39
  327.7 11.3 %collective-permute-done.37 = bf16[2,1296,128]{2,1,0:T(8,128)(2,1)S(1)} collective-permute-done((bf16[2,1296,128]{2,1,0:T(8,128)(2,1)}, bf16[2,1296,128]{2,1,0:T(8,128)(2,1)S(1)}, u32[]{:S(2)}, u32[]{:S(2)}) %collective-permute-start.37) | collective-permute-done | bytes 663584 | tf_op jit(solution)/shard_map/ppermute | solution.py:816
  339.2 2.1 collective-permute-done.39
  341.3 12.7 %collective-permute-done.40 = bf16[4,480,128]{2,1,0:T(8,128)(2,1)} collective-permute-done((bf16[4,480,128]{2,1,0:T(8,128)(2,1)}, bf16[4,480,128]{2,1,0:T(8,128)(2,1)}, u32[]{:S(2)}, u32[]{:S(2)}) %collective-permute-start.40) | collective-permute-done | bytes 491552 | tf_op jit(solution)/shard_map/ppermute | solution.py:631
  362.0 2.9 collective-permute-start.43
  366.3 7.9 %add_table_0.1 = f32[192,12800]{1,0:T(8,128)} custom-call(s32[1024,2]{1,0:T(8,128)S(1)} %bitcast.136, bf16[1024,384]{1,0:T(8,128)(2,1)S(1)} %bitcast.134), custom_call_target="tpu_custom_call" | custom-call | flops 4200000000 | bytes 17500000 | tf_op jit(solution)/shard_map/add_table_0/pallas_call | solution.py:223
  374.3 1.8 collective-permute-done.47
  377.2 2.4 collective-permute-start.51
  379.7 7.9 %add_table_1.1 = f32[192,12800]{1,0:T(8,128)} custom-call(s32[1024,2]{1,0:T(8,128)S(1)} %bitcast.137, bf16[1024,384]{1,0:T(8,128)(2,1)S(1)} %bitcast.135), custom_call_target="tpu_custom_call" | custom-call | flops 4200000000 | bytes 17500000 | tf_op jit(solution)/shard_map/add_table_1/pallas_call | solution.py:223
  388.5 3.2 collective-permute-done.52.other
  391.8 2.5 unpack_first.1
  395.0 3.4 unpack_second.1
  (224 shorter events, 61.2 us)
Async XLA Ops:
  4.9 22.5 %collective-permute-start.4 = (bf16[208,384]{1,0:T(8,128)(2,1)S(1)}, bf16[208,384]{1,0:T(8,128)(2,1)S(1)}, u32[]{:S(2)}, u32[]{:S(2)}) collective-permute-start(bf16[208,384]{1,0:T(8,128)(2,1)S(1)} %get-tuple-element.158), channel_id=1, source_target_pairs={{0,1},{1,2},{2,3},{3,0},{4,5},{5,6},{6,7},{7,4},{8,9},{9,10},{10,1... | collective-permute-start | bytes 479240 | tf_op jit(solution)/shard_map/ppermute | solution.py:636
  8.0 19.4 %collective-permute-start.3 = (bf16[208,384]{1,0:T(8,128)(2,1)S(1)}, bf16[208,384]{1,0:T(8,128)(2,1)S(1)}, u32[]{:S(2)}, u32[]{:S(2)}) collective-permute-start(bf16[208,384]{1,0:T(8,128)(2,1)S(1)} %get-tuple-element.158), channel_id=1, source_target_pairs={{0,2},{1,3},{2,0},{3,1},{4,6},{5,7},{6,4},{7,5},{8,10},{9,11},{10,... | collective-permute-start | bytes 479240 | tf_op jit(solution)/shard_map/ppermute | solution.py:636
  10.6 16.9 %collective-permute-start.2 = (bf16[208,384]{1,0:T(8,128)(2,1)S(1)}, bf16[208,384]{1,0:T(8,128)(2,1)S(1)}, u32[]{:S(2)}, u32[]{:S(2)}) collective-permute-start(bf16[208,384]{1,0:T(8,128)(2,1)S(1)} %get-tuple-element.158), channel_id=1, source_target_pairs={{0,3},{1,0},{2,1},{3,2},{4,7},{5,4},{6,5},{7,6},{8,11},{9,8},{10,9... | collective-permute-start | bytes 479240 | tf_op jit(solution)/shard_map/ppermute | solution.py:636
  11.9 14.6 %collective-permute-start = (bf16[384,128]{1,0:T(8,128)(2,1)S(1)}, bf16[384,128]{1,0:T(8,128)(2,1)S(1)}, u32[]{:S(2)}, u32[]{:S(2)}) collective-permute-start(bf16[384,128]{1,0:T(8,128)(2,1)S(1)} %get-tuple-element.144), channel_id=1, source_target_pairs={{0,8},{4,12},{8,0},{12,4},{16,24},{20,28},{24,16},{28,20},{1,9},{5... | collective-permute-start | bytes 294920 | tf_op jit(solution)/shard_map/ppermute | solution.py:631
  13.4 13.1 %collective-permute-start.1 = (bf16[384,128]{1,0:T(8,128)(2,1)S(1)}, bf16[384,128]{1,0:T(8,128)(2,1)S(1)}, u32[]{:S(2)}, u32[]{:S(2)}) collective-permute-start(bf16[384,128]{1,0:T(8,128)(2,1)S(1)} %get-tuple-element.144), channel_id=1, source_target_pairs={{0,16},{4,20},{8,24},{12,28},{16,0},{20,4},{24,8},{28,12},{1,17},{... | collective-permute-start | bytes 294920 | tf_op jit(solution)/shard_map/ppermute | solution.py:631
  26.8 21.7 %collective-permute-start.9 = (bf16[384,128]{1,0:T(8,128)(2,1)S(1)}, bf16[384,128]{1,0:T(8,128)(2,1)S(1)}, u32[]{:S(2)}, u32[]{:S(2)}) collective-permute-start(bf16[384,128]{1,0:T(8,128)(2,1)S(1)} %get-tuple-element.144), channel_id=1, source_target_pairs={{0,24},{4,28},{8,16},{12,20},{16,8},{20,12},{24,0},{28,4},{1,25},{... | collective-permute-start | bytes 294920 | tf_op jit(solution)/shard_map/ppermute | solution.py:631
  27.6 20.9 %collective-permute-start.7 = (bf16[912,128]{1,0:T(8,128)(2,1)S(1)}, bf16[912,128]{1,0:T(8,128)(2,1)S(1)}, u32[]{:S(2)}, u32[]{:S(2)}) collective-permute-start(bf16[912,128]{1,0:T(8,128)(2,1)S(1)} %get-tuple-element.171), channel_id=1, source_target_pairs={{0,1},{1,2},{2,3},{3,0},{4,5},{5,6},{6,7},{7,4},{8,9},{9,10},{10,1... | collective-permute-start | bytes 700424 | tf_op jit(solution)/shard_map/ppermute | solution.py:636
  28.3 20.1 %collective-permute-start.8 = (bf16[912,128]{1,0:T(8,128)(2,1)S(1)}, bf16[912,128]{1,0:T(8,128)(2,1)S(1)}, u32[]{:S(2)}, u32[]{:S(2)}) collective-permute-start(bf16[912,128]{1,0:T(8,128)(2,1)S(1)} %get-tuple-element.171), channel_id=1, source_target_pairs={{0,3},{1,0},{2,1},{3,2},{4,7},{5,4},{6,5},{7,6},{8,11},{9,8},{10,9... | collective-permute-start | bytes 700424 | tf_op jit(solution)/shard_map/ppermute | solution.py:636
  31.4 17.0 %collective-permute-start.5 = (bf16[4,144,384]{2,1,0:T(8,128)(2,1)S(1)}, bf16[4,144,384]{2,1,0:T(8,128)(2,1)S(1)}, u32[]{:S(2)}, u32[]{:S(2)}) collective-permute-start(bf16[4,144,384]{2,1,0:T(8,128)(2,1)S(1)} %pad_maximum_fusion.4.refs_0_), channel_id=1, source_target_pairs={{0,8},{4,12},{8,0},{12,4},{16,24},{20,28},{24,16},{28,20},{1,9},{5... | collective-permute-start | bytes 1327112 | tf_op jit(solution)/shard_map/ppermute | solution.py:631
  32.9 15.6 %collective-permute-start.6 = (bf16[4,144,384]{2,1,0:T(8,128)(2,1)S(1)}, bf16[4,144,384]{2,1,0:T(8,128)(2,1)S(1)}, u32[]{:S(2)}, u32[]{:S(2)}) collective-permute-start(bf16[4,144,384]{2,1,0:T(8,128)(2,1)S(1)} %pad_maximum_fusion.4.refs_0_), channel_id=1, source_target_pairs={{0,16},{4,20},{8,24},{12,28},{16,0},{20,4},{24,8},{28,12},{1,17},{... | collective-permute-start | bytes 1327112 | tf_op jit(solution)/shard_map/ppermute | solution.py:631
  48.5 16.4 %collective-permute-start.10 = (bf16[4,144,384]{2,1,0:T(8,128)(2,1)S(1)}, bf16[4,144,384]{2,1,0:T(8,128)(2,1)S(1)}, u32[]{:S(2)}, u32[]{:S(2)}) collective-permute-start(bf16[4,144,384]{2,1,0:T(8,128)(2,1)S(1)} %pad_maximum_fusion.4.refs_0_), channel_id=1, source_target_pairs={{0,24},{4,28},{8,16},{12,20},{16,8},{20,12},{24,0},{28,4},{1,25},{... | collective-permute-start | bytes 1327112 | tf_op jit(solution)/shard_map/ppermute | solution.py:631
  50.5 22.5 %collective-permute-start.11 = (bf16[4,144,384]{2,1,0:T(8,128)(2,1)S(1)}, bf16[4,144,384]{2,1,0:T(8,128)(2,1)}, u32[]{:S(2)}, u32[]{:S(2)}) collective-permute-start(bf16[4,144,384]{2,1,0:T(8,128)(2,1)S(1)} %pad_maximum_fusion.4.refs_0_), channel_id=1, source_target_pairs={{0,4},{4,0},{8,12},{12,8},{16,20},{20,16},{24,28},{28,24},{1,5},{5... | collective-permute-start | bytes 1327112 | tf_op jit(solution)/shard_map/ppermute | solution.py:631
  50.5 22.4 %all-to-all-start.1 = ((bf16[32,32,384]{2,1,0:T(8,128)(2,1)}), bf16[32,32,384]{2,1,0:T(8,128)(2,1)S(1)}, u32[]{:S(2)}, u32[]{:S(2)}) async-start(bf16[32,32,384]{2,1,0:T(8,128)(2,1)} %bitcast.13), calls=%async_computation.1 | async-start | bytes 1572864 | tf_op jit(solution)/shard_map/all_to_all | solution.py:737
  72.9 17.5 %collective-permute-start.17 = (bf16[3,432,128]{2,1,0:T(8,128)(2,1)}, bf16[3,432,128]{2,1,0:T(8,128)(2,1)S(1)}, u32[]{:S(2)}, u32[]{:S(2)}) collective-permute-start(bf16[3,432,128]{2,1,0:T(8,128)(2,1)} %pad_maximum_fusion.8), channel_id=1, source_target_pairs={{0,16},{4,20},{8,24},{12,28},{16,0},{20,4},{24,8},{28,12},{1,17},{... | collective-permute-start | bytes 995336 | tf_op jit(solution)/shard_map/ppermute | solution.py:631
  74.4 16.1 %collective-permute-start.16 = (bf16[3,480,128]{2,1,0:T(8,128)(2,1)S(1)}, bf16[3,480,128]{2,1,0:T(8,128)(2,1)S(1)}, u32[]{:S(2)}, u32[]{:S(2)}) collective-permute-start(bf16[3,480,128]{2,1,0:T(8,128)(2,1)S(1)} %pad_maximum_fusion.6), channel_id=1, source_target_pairs={{0,8},{4,12},{8,0},{12,4},{16,24},{20,28},{24,16},{28,20},{1,9},{5... | collective-permute-start | bytes 1105928 | tf_op jit(solution)/shard_map/ppermute | solution.py:631
  75.9 19.2 %collective-permute-start.18 = (bf16[912,128]{1,0:T(8,128)(2,1)S(1)}, bf16[912,128]{1,0:T(8,128)(2,1)S(1)}, u32[]{:S(2)}, u32[]{:S(2)}) collective-permute-start(bf16[912,128]{1,0:T(8,128)(2,1)S(1)} %get-tuple-element.171), channel_id=1, source_target_pairs={{0,2},{1,3},{2,0},{3,1},{4,6},{5,7},{6,4},{7,5},{8,10},{9,11},{10,... | collective-permute-start | bytes 700424 | tf_op jit(solution)/shard_map/ppermute | solution.py:636
  91.2 37.4 %all-to-all-start.2 = ((bf16[8,576,256]{2,1,0:T(8,128)(2,1)}), bf16[8,576,256]{2,1,0:T(8,128)(2,1)S(1)}, u32[]{:S(2)}, u32[]{:S(2)}) async-start(bf16[8,576,256]{2,1,0:T(8,128)(2,1)} %get-tuple-element.168), calls=%async_computation.2 | async-start | bytes 4718592 | tf_op jit(solution)/shard_map/all_to_all | solution.py:737
  96.2 32.3 %collective-permute-start.21 = (bf16[4,384,128]{2,1,0:T(8,128)(2,1)S(1)}, bf16[4,384,128]{2,1,0:T(8,128)(2,1)S(1)}, u32[]{:S(2)}, u32[]{:S(2)}) collective-permute-start(bf16[4,384,128]{2,1,0:T(8,128)(2,1)S(1)} %get-tuple-element.272), channel_id=1, source_target_pairs={{0,2},{1,3},{2,0},{3,1},{4,6},{5,7},{6,4},{7,5},{8,10},{9,11},{10,... | collective-permute-start | bytes 1179656 | tf_op jit(solution)/shard_map/ppermute | solution.py:816
  99.3 26.6 %collective-permute-start.20 = (bf16[432,128]{1,0:T(8,128)(2,1)S(1)}, bf16[432,128]{1,0:T(8,128)(2,1)S(1)}, u32[]{:S(2)}, u32[]{:S(2)}) collective-permute-start(bf16[432,128]{1,0:T(8,128)(2,1)S(1)} %slice.214), channel_id=1, source_target_pairs={{0,16},{4,20},{8,24},{12,28},{16,0},{20,4},{24,8},{28,12},{1,17},{... | collective-permute-start | bytes 331784 | tf_op jit(solution)/shard_map/ppermute | solution.py:631
  101.3 25.9 %collective-permute-start.19 = (bf16[480,128]{1,0:T(8,128)(2,1)S(1)}, bf16[480,128]{1,0:T(8,128)(2,1)S(1)}, u32[]{:S(2)}, u32[]{:S(2)}) collective-permute-start(bf16[480,128]{1,0:T(8,128)(2,1)S(1)} %slice.211), channel_id=1, source_target_pairs={{0,8},{4,12},{8,0},{12,4},{16,24},{20,28},{24,16},{28,20},{1,9},{5... | collective-permute-start | bytes 368648 | tf_op jit(solution)/shard_map/ppermute | solution.py:631
  128.6 23.6 %collective-permute-start.22 = (bf16[2,4,480,128]{3,2,1,0:T(8,128)(2,1)}, bf16[2,4,480,128]{3,2,1,0:T(8,128)(2,1)S(1)}, u32[]{:S(2)}, u32[]{:S(2)}) collective-permute-start(bf16[2,4,480,128]{3,2,1,0:T(8,128)(2,1)} %bitcast.140), channel_id=1, source_target_pairs={{0,16},{4,20},{8,24},{12,28},{16,0},{20,4},{24,8},{28,12},{1,17},{... | collective-permute-start | bytes 2949128 | tf_op jit(solution)/shard_map/ppermute | solution.py:631
  129.2 40.5 %collective-permute-start.25 = (bf16[2,4,480,128]{3,2,1,0:T(8,128)(2,1)}, bf16[2,4,480,128]{3,2,1,0:T(8,128)(2,1)S(1)}, u32[]{:S(2)}, u32[]{:S(2)}) collective-permute-start(bf16[2,4,480,128]{3,2,1,0:T(8,128)(2,1)} %bitcast.141), channel_id=1, source_target_pairs={{0,4},{4,0},{8,12},{12,8},{16,20},{20,16},{24,28},{28,24},{1,5},{5... | collective-permute-start | bytes 2949128 | tf_op jit(solution)/shard_map/ppermute | solution.py:631
  129.2 22.3 %collective-permute-start.23 = (bf16[2,4,432,128]{3,2,1,0:T(8,128)(2,1)}, bf16[2,4,432,128]{3,2,1,0:T(8,128)(2,1)S(1)}, u32[]{:S(2)}, u32[]{:S(2)}) collective-permute-start(bf16[2,4,432,128]{3,2,1,0:T(8,128)(2,1)} %bitcast.143), channel_id=1, source_target_pairs={{0,8},{4,12},{8,0},{12,4},{16,24},{20,28},{24,16},{28,20},{1,9},{5... | collective-permute-start | bytes 2654216 | tf_op jit(solution)/shard_map/ppermute | solution.py:631
  130.5 22.2 %collective-permute-start.26 = (bf16[2,4,432,128]{3,2,1,0:T(8,128)(2,1)}, bf16[2,4,432,128]{3,2,1,0:T(8,128)(2,1)S(1)}, u32[]{:S(2)}, u32[]{:S(2)}) collective-permute-start(bf16[2,4,432,128]{3,2,1,0:T(8,128)(2,1)} %bitcast.144), channel_id=1, source_target_pairs={{0,4},{4,0},{8,12},{12,8},{16,20},{20,16},{24,28},{28,24},{1,5},{5... | collective-permute-start | bytes 2654216 | tf_op jit(solution)/shard_map/ppermute | solution.py:631
  130.7 20.5 %collective-permute-start.24 = (bf16[2,4,384,128]{3,2,1,0:T(8,128)(2,1)S(1)}, bf16[2,4,384,128]{3,2,1,0:T(8,128)(2,1)S(1)}, u32[]{:S(2)}, u32[]{:S(2)}) collective-permute-start(bf16[2,4,384,128]{3,2,1,0:T(8,128)(2,1)S(1)} %pad_maximum_fusion.1.refs_8_), channel_id=1, source_target_pairs={{0,1},{1,0},{2,3},{3,2},{4,5},{5,4},{6,7},{7,6},{8,9},{9,8},{10,11... | collective-permute-start | bytes 2359304 | tf_op jit(solution)/shard_map/ppermute | solution.py:816
  152.2 17.6 %collective-permute-start.27 = (bf16[2,4,480,128]{3,2,1,0:T(8,128)(2,1)S(1)}, bf16[2,4,480,128]{3,2,1,0:T(8,128)(2,1)S(1)}, u32[]{:S(2)}, u32[]{:S(2)}) collective-permute-start(bf16[2,4,480,128]{3,2,1,0:T(8,128)(2,1)S(1)} %collective-permute-done.22.refs_2_), channel_id=1, source_target_pairs={{0,4},{4,0},{8,12},{12,8},{16,20},{20,16},{24,28},{28,24},{1,5},{5... | collective-permute-start | bytes 2949128 | tf_op jit(solution)/shard_map/ppermute | solution.py:631
  152.2 17.6 %collective-permute-start.28 = (bf16[2,4,432,128]{3,2,1,0:T(8,128)(2,1)S(1)}, bf16[2,4,432,128]{3,2,1,0:T(8,128)(2,1)S(1)}, u32[]{:S(2)}, u32[]{:S(2)}) collective-permute-start(bf16[2,4,432,128]{3,2,1,0:T(8,128)(2,1)S(1)} %collective-permute-done.23.refs_3_), channel_id=1, source_target_pairs={{0,4},{4,0},{8,12},{12,8},{16,20},{20,16},{24,28},{28,24},{1,5},{5... | collective-permute-start | bytes 2654216 | tf_op jit(solution)/shard_map/ppermute | solution.py:631
  152.7 17.1 %collective-permute-start.29 = (bf16[2,4,384,128]{3,2,1,0:T(8,128)(2,1)S(1)}, bf16[2,4,384,128]{3,2,1,0:T(8,128)(2,1)S(1)}, u32[]{:S(2)}, u32[]{:S(2)}) collective-permute-start(bf16[2,4,384,128]{3,2,1,0:T(8,128)(2,1)S(1)} %pad_maximum_fusion.1.refs_8_), channel_id=1, source_target_pairs={{0,4},{4,0},{8,12},{12,8},{16,20},{20,16},{24,28},{28,24},{1,5},{5... | collective-permute-start | bytes 2359304 | tf_op jit(solution)/shard_map/ppermute | solution.py:631
  152.7 17.1 %collective-permute-start.30 = (bf16[2,4,384,128]{3,2,1,0:T(8,128)(2,1)S(1)}, bf16[2,4,384,128]{3,2,1,0:T(8,128)(2,1)S(1)}, u32[]{:S(2)}, u32[]{:S(2)}) collective-permute-start(bf16[2,4,384,128]{3,2,1,0:T(8,128)(2,1)S(1)} %collective-permute-done.24.refs_9_), channel_id=1, source_target_pairs={{0,4},{4,0},{8,12},{12,8},{16,20},{20,16},{24,28},{28,24},{1,5},{5... | collective-permute-start | bytes 2359304 | tf_op jit(solution)/shard_map/ppermute | solution.py:631
  195.0 20.2 %all-to-all-start.4 = ((bf16[8,192,256]{2,1,0:T(8,128)(2,1)}), bf16[8,192,256]{2,1,0:T(8,128)(2,1)S(1)}, u32[]{:S(2)}, u32[]{:S(2)}) async-start(bf16[8,192,256]{2,1,0:T(8,128)(2,1)} %get-tuple-element.202), calls=%async_computation.4 | async-start | bytes 1572864 | tf_op jit(solution)/shard_map/all_to_all | solution.py:737
  215.2 19.3 %collective-permute-start.31 = (bf16[4,4,672,128]{3,2,1,0:T(8,128)(2,1)}, bf16[4,4,672,128]{3,2,1,0:T(8,128)(2,1)}, u32[]{:S(2)}, u32[]{:S(2)}) collective-permute-start(bf16[4,4,672,128]{3,2,1,0:T(8,128)(2,1)} %get-tuple-element.203), channel_id=1, source_target_pairs={{0,4},{4,0},{8,12},{12,8},{16,20},{20,16},{24,28},{28,24},{1,5},{5... | collective-permute-start | bytes 8257544 | tf_op jit(solution)/shard_map/ppermute | solution.py:631
  215.7 18.8 %collective-permute-start.32 = (bf16[4,4,624,128]{3,2,1,0:T(8,128)(2,1)}, bf16[4,4,624,128]{3,2,1,0:T(8,128)(2,1)}, u32[]{:S(2)}, u32[]{:S(2)}) collective-permute-start(bf16[4,4,624,128]{3,2,1,0:T(8,128)(2,1)} %get-tuple-element.204), channel_id=1, source_target_pairs={{0,4},{4,0},{8,12},{12,8},{16,20},{20,16},{24,28},{28,24},{1,5},{5... | collective-permute-start | bytes 7667720 | tf_op jit(solution)/shard_map/ppermute | solution.py:631
  230.0 38.4 %all-to-all-start.5 = ((bf16[8,192,256]{2,1,0:T(8,128)(2,1)}), bf16[8,192,256]{2,1,0:T(8,128)(2,1)}, u32[]{:S(2)}, u32[]{:S(2)}) async-start(bf16[8,192,256]{2,1,0:T(8,128)(2,1)} %attend_grad_0.1), calls=%async_computation.5 | async-start | bytes 1572864 | tf_op jit(solution)/shard_map/all_to_all | solution.py:737
  237.8 35.8 %collective-permute-start.34 = (bf16[2,4,624,128]{3,2,1,0:T(8,128)(2,1)}, bf16[2,4,624,128]{3,2,1,0:T(8,128)(2,1)}, u32[]{:S(2)}, u32[]{:S(2)}) collective-permute-start(bf16[2,4,624,128]{3,2,1,0:T(8,128)(2,1)} %add_convert_fusion.1), channel_id=1, source_target_pairs={{0,16},{4,20},{8,24},{12,28},{16,0},{20,4},{24,8},{28,12},{1,17},{... | collective-permute-start | bytes 3833864 | tf_op jit(solution)/shard_map/ppermute | solution.py:631
  242.6 33.1 %collective-permute-start.33 = (bf16[2,4,672,128]{3,2,1,0:T(8,128)(2,1)}, bf16[2,4,672,128]{3,2,1,0:T(8,128)(2,1)}, u32[]{:S(2)}, u32[]{:S(2)}) collective-permute-start(bf16[2,4,672,128]{3,2,1,0:T(8,128)(2,1)} %add_convert_fusion), channel_id=1, source_target_pairs={{0,8},{4,12},{8,0},{12,4},{16,24},{20,28},{24,16},{28,20},{1,9},{5... | collective-permute-start | bytes 4128776 | tf_op jit(solution)/shard_map/ppermute | solution.py:631
  268.4 25.8 %all-to-all-start.6 = ((bf16[8,384,256]{2,1,0:T(8,128)(2,1)}), bf16[8,384,256]{2,1,0:T(8,128)(2,1)}, u32[]{:S(2)}, u32[]{:S(2)}) async-start(bf16[8,384,256]{2,1,0:T(8,128)(2,1)} %attend_grad_1.1), calls=%async_computation.6 | async-start | bytes 3145728 | tf_op jit(solution)/shard_map/all_to_all | solution.py:737
  294.2 15.6 %collective-permute-start.35 = (bf16[4,672,128]{2,1,0:T(8,128)(2,1)}, bf16[4,672,128]{2,1,0:T(8,128)(2,1)S(1)}, u32[]{:S(2)}, u32[]{:S(2)}) collective-permute-start(bf16[4,672,128]{2,1,0:T(8,128)(2,1)} %fusion.2), channel_id=1, source_target_pairs={{0,16},{4,20},{8,24},{12,28},{16,0},{20,4},{24,8},{28,12},{1,17},{... | collective-permute-start | bytes 2064392 | tf_op jit(solution)/shard_map/ppermute | solution.py:631
  294.7 15.1 %collective-permute-start.36 = (bf16[4,624,128]{2,1,0:T(8,128)(2,1)}, bf16[4,624,128]{2,1,0:T(8,128)(2,1)}, u32[]{:S(2)}, u32[]{:S(2)}) collective-permute-start(bf16[4,624,128]{2,1,0:T(8,128)(2,1)} %fusion.4), channel_id=1, source_target_pairs={{0,8},{4,12},{8,0},{12,4},{16,24},{20,28},{24,16},{28,20},{1,9},{5... | collective-permute-start | bytes 1916936 | tf_op jit(solution)/shard_map/ppermute | solution.py:631
  314.5 24.5 %collective-permute-start.37 = (bf16[2,1296,128]{2,1,0:T(8,128)(2,1)}, bf16[2,1296,128]{2,1,0:T(8,128)(2,1)S(1)}, u32[]{:S(2)}, u32[]{:S(2)}) collective-permute-start(bf16[2,1296,128]{2,1,0:T(8,128)(2,1)} %pad_maximum_fusion.2), channel_id=1, source_target_pairs={{0,1},{1,0},{2,3},{3,2},{4,5},{5,4},{6,7},{7,6},{8,9},{9,8},{10,11... | collective-permute-start | bytes 1990664 | tf_op jit(solution)/shard_map/ppermute | solution.py:816
  316.0 50.3 %all-to-all-start.7 = ((bf16[32,32,384]{2,1,0:T(8,128)(2,1)}), bf16[32,32,384]{2,1,0:T(8,128)(2,1)S(1)}, u32[]{:S(2)}, u32[]{:S(2)}) async-start(bf16[32,32,384]{2,1,0:T(8,128)(2,1)} %bitcast.51), calls=%async_computation.7 | async-start | bytes 1572864 | tf_op jit(solution)/shard_map/all_to_all | solution.py:737
  324.0 17.3 %collective-permute-start.39 = (bf16[4,480,128]{2,1,0:T(8,128)(2,1)}, bf16[4,480,128]{2,1,0:T(8,128)(2,1)}, u32[]{:S(2)}, u32[]{:S(2)}) collective-permute-start(bf16[4,480,128]{2,1,0:T(8,128)(2,1)} %get-tuple-element.262), channel_id=1, source_target_pairs={{0,8},{4,12},{8,0},{12,4},{16,24},{20,28},{24,16},{28,20},{1,9},{5... | collective-permute-start | bytes 1474568 | tf_op jit(solution)/shard_map/ppermute | solution.py:631
  325.9 28.1 %collective-permute-start.40 = (bf16[4,480,128]{2,1,0:T(8,128)(2,1)}, bf16[4,480,128]{2,1,0:T(8,128)(2,1)}, u32[]{:S(2)}, u32[]{:S(2)}) collective-permute-start(bf16[4,480,128]{2,1,0:T(8,128)(2,1)} %get-tuple-element.261), channel_id=1, source_target_pairs={{0,16},{4,20},{8,24},{12,28},{16,0},{20,4},{24,8},{28,12},{1,17},{... | collective-permute-start | bytes 1474568 | tf_op jit(solution)/shard_map/ppermute | solution.py:631
  327.3 28.3 %collective-permute-start.41 = (bf16[4,480,128]{2,1,0:T(8,128)(2,1)}, bf16[4,480,128]{2,1,0:T(8,128)(2,1)}, u32[]{:S(2)}, u32[]{:S(2)}) collective-permute-start(bf16[4,480,128]{2,1,0:T(8,128)(2,1)} %get-tuple-element.260), channel_id=1, source_target_pairs={{0,24},{4,28},{8,16},{12,20},{16,8},{20,12},{24,0},{28,4},{1,25},{... | collective-permute-start | bytes 1474568 | tf_op jit(solution)/shard_map/ppermute | solution.py:631
  339.1 19.1 %collective-permute-start.45 = (bf16[1296,128]{1,0:T(8,128)(2,1)S(1)}, bf16[1296,128]{1,0:T(8,128)(2,1)S(1)}, u32[]{:S(2)}, u32[]{:S(2)}) collective-permute-start(bf16[1296,128]{1,0:T(8,128)(2,1)S(1)} %fusion.10), channel_id=1, source_target_pairs={{0,2},{1,3},{2,0},{3,1},{4,6},{5,7},{6,4},{7,5},{8,10},{9,11},{10,... | collective-permute-start | bytes 995336 | tf_op jit(solution)/shard_map/ppermute | solution.py:816
  358.4 15.8 %collective-permute-start.46 = (bf16[1296,128]{1,0:T(8,128)(2,1)S(1)}, bf16[1296,128]{1,0:T(8,128)(2,1)S(1)}, u32[]{:S(2)}, u32[]{:S(2)}) collective-permute-start(bf16[1296,128]{1,0:T(8,128)(2,1)S(1)} %fusion.3), channel_id=1, source_target_pairs={{0,8},{4,12},{8,0},{12,4},{16,24},{20,28},{24,16},{28,20},{1,9},{5... | collective-permute-start | bytes 995336 | tf_op jit(solution)/shard_map/ppermute | solution.py:631
  359.8 16.2 %collective-permute-start.47 = (bf16[1296,128]{1,0:T(8,128)(2,1)S(1)}, bf16[1296,128]{1,0:T(8,128)(2,1)S(1)}, u32[]{:S(2)}, u32[]{:S(2)}) collective-permute-start(bf16[1296,128]{1,0:T(8,128)(2,1)S(1)} %fusion.3), channel_id=1, source_target_pairs={{0,16},{4,20},{8,24},{12,28},{16,0},{20,4},{24,8},{28,12},{1,17},{... | collective-permute-start | bytes 995336 | tf_op jit(solution)/shard_map/ppermute | solution.py:631
  361.3 26.3 %collective-permute-start.48 = (bf16[1296,128]{1,0:T(8,128)(2,1)S(1)}, bf16[1296,128]{1,0:T(8,128)(2,1)S(1)}, u32[]{:S(2)}, u32[]{:S(2)}) collective-permute-start(bf16[1296,128]{1,0:T(8,128)(2,1)S(1)} %fusion.3), channel_id=1, source_target_pairs={{0,24},{4,28},{8,16},{12,20},{16,8},{20,12},{24,0},{28,4},{1,25},{... | collective-permute-start | bytes 995336 | tf_op jit(solution)/shard_map/ppermute | solution.py:631
  362.0 12.2 %collective-permute-start.43 = (bf16[480,128]{1,0:T(8,128)(2,1)S(1)}, bf16[480,128]{1,0:T(8,128)(2,1)S(1)}, u32[]{:S(2)}, u32[]{:S(2)}) collective-permute-start(bf16[480,128]{1,0:T(8,128)(2,1)S(1)} %get-tuple-element.269), channel_id=1, source_target_pairs={{0,2},{1,3},{2,0},{3,1},{4,6},{5,7},{6,4},{7,5},{8,10},{9,11},{10,... | collective-permute-start | bytes 368648 | tf_op jit(solution)/shard_map/ppermute | solution.py:816
  (46 other events, 379.6 us)

commit v7 on v6

--- a/solution.py
+++ b/solution.py
@@ -1794,12 +1794,12 @@
     from_z = over_fsdp(jnp.concatenate([sums_u[:2], sums_l[:2]], axis=1), 1)
     total_m = jnp.concatenate([sums_u[2:], sums_l[2:]], axis=1)
     arrived = exchange(send.reshape(devices, capacity, 2 * E), both)
-    half_j = add_cores(own_j, from_core)
-    from_chips = to_chips(half_j)
-    from_z, kept = lax.optimization_barrier((from_z, half_j[0]))
+    half_j = [add_all(own_j[k], from_core[k]).astype(BF) for k in (1, 2, 3)]
+    from_chips = [over_ctx(block, 2 * k) for k, block in zip((1, 2, 3), half_j)]
+    from_z, own_j, from_core = lax.optimization_barrier((from_z, own_j, from_core))
     near_m, far_m = add_blocks(total_m[1], [from_z[0]]), add_blocks(total_m[0], [from_z[1]])
     from_z = over_fsdp(far_m, 2)
-    total_j = add_blocks(kept, from_chips)
+    total_j = add_all(own_j[0], from_core[0], *from_chips).astype(BF)
     from_fsdp = [over_fsdp(total_j[m], m) for m in (1, 2, 3)]
     from_z, kept = lax.optimization_barrier((from_z, total_j[0]))
     piece_m = add_blocks(near_m, [from_z])

time: 406 us -> 406 us (level)
  no operation moved by 1% of the time
where the time goes in v7:
time: 406 us; the launch traced here: 398 us
  Pallas kernels  164 us (40%)
  waiting for transfers between devices  92.8 us (23%)
  starting transfers between devices  82.1 us (20%)
  other arithmetic  25.4 us (6%)
  blocking collectives  16.5 us (4%)
  local copies, waits for them, and re-layouts  16 us (4%)
    ppermute x41, waiting for transfers between devices, over_ctx(): return lax.ppermute(value, 'ctx', [(i, i ^ mask) for i in range(size)])  56.3 us
    pallas_call x2, Pallas kernels, attend_grad_short(): pl.pallas_call(functools.partial(attend_grad_short_kernel, pairs, begin,...  38.6 us
    ppermute x41, starting transfers between devices, over_ctx(): return lax.ppermute(value, 'ctx', [(i, i ^ mask) for i in range(size)])  34.3 us
    all_to_all x7, starting transfers between devices, exchange(): return lax.all_to_all(values, axes, split_axis=0, concat_axis=0, tiled=True)  26.5 us
    pallas_call x1, Pallas kernels, mlp(): pl.pallas_call(functools.partial(mlp_kernel, pairs), grid=(steps,), out_s...  23.9 us
    all_to_all x7, waiting for transfers between devices, exchange(): return lax.all_to_all(values, axes, split_axis=0, concat_axis=0, tiled=True)  23.7 us
    pallas_call x1, Pallas kernels, attend_short(): pl.pallas_call(functools.partial(attend_short_kernel, pairs, piece), out_...  19 us
    all_to_all x1, blocking collectives, exchange(): return lax.all_to_all(values, axes, split_axis=0, concat_axis=0, tiled=True)  16.5 us
  transfers between devices with their start and end apart: 61, of which 16 were waited for; matrix products, arithmetic and copies ran while one was open for 9% of the time, Pallas kernels for 34%

profile of v7, /device:TPU:0, one launch (start us, length us, event | category | flops | bytes accessed | tf_op | source)
XLA Modules:
  0.0 398.4 jit_solution(3527948116108790609)
XLA Ops:
  4.9 3.1 collective-permute-start.4
  8.0 2.6 collective-permute-start.3
  14.9 2.5 all-to-all-start
  17.5 1.8 fusion.14
  20.1 6.4 %all-to-all-done = s32[32,1,64]{2,1,0:T(1,128)S(1)} async-done(((s32[32,1,64]{2,1,0:T(1,128)}), s32[32,1,64]{2,1,0:T(1,128)S(1)}, u32[]{:S(2)}, u32[]{:S(2)}) %all-to-all-start) | async-done | bytes 8224 | tf_op jit(solution)/shard_map/all_to_all | solution.py:737
  28.3 3.1 collective-permute-start.8
  34.3 14.1 %read_rows.1 = bf16[1024,384]{1,0:T(8,128)(2,1)} custom-call(s32[2,1024]{1,0:T(2,128)S(1)} %pad_add_fusion.codes, bf16[192,12800]{1,0:T(8,128)(2,1)} %bitcast.175, bf16[192,12800]{1,0:T(8,128)(2,1)} %bitcast.176), custom_call_target="tpu_custom_call" | custom-call | flops 10200000512 | bytes 42500000 | tf_op jit(solution)/shard_map/read_rows/pallas_call | solution.py:156
  50.5 2.8 all-to-all-start.1
  53.3 11.6 %collective-permute-done.10.refs_3_ = bf16[4,144,384]{2,1,0:T(8,128)(2,1)S(1)} collective-permute-done((bf16[4,144,384]{2,1,0:T(8,128)(2,1)S(1)}, bf16[4,144,384]{2,1,0:T(8,128)(2,1)S(1)}, u32[]{:S(2)}, u32[]{:S(2)}) %collective-permute-start.10) | collective-permute-done | bytes 442400 | tf_op jit(solution)/shard_map/ppermute | solution.py:631
  68.9 4.0 all-to-all-done.1
  77.2 13.3 %front.1 = (f32[512,768]{1,0:T(8,128)}, bf16[512,192]{1,0:T(8,128)(2,1)}, bf16[512,768]{1,0:T(8,128)(2,1)}, bf16[8,576,256]{2,1,0:T(8,128)(2,1)}, bf16[768,2304]...) custom-call(s32[3]{0:T(128)} %copy-done.2, s32[2]{0:T(128)} %dynamic_slice.6.starts, ...), custom_call_target="tpu_custom_call" | custom-call | flops 5400000000 | bytes 22500000 | tf_op jit(solution)/shard_map/front/pallas_call | solution.py:988
  91.2 3.9 all-to-all-start.2
  96.2 1.7 collective-permute-start.21
  99.3 2.0 collective-permute-start.20
  105.6 20.3 %collective-permute-done.20 = bf16[432,128]{1,0:T(8,128)(2,1)S(1)} collective-permute-done((bf16[432,128]{1,0:T(8,128)(2,1)S(1)}, bf16[432,128]{1,0:T(8,128)(2,1)S(1)}, u32[]{:S(2)}, u32[]{:S(2)}) %collective-permute-start.20) | collective-permute-done | bytes 110624 | tf_op jit(solution)/shard_map/ppermute | solution.py:631
  132.2 19.0 %attend.1 = (bf16[8,192,256]{2,1,0:T(8,128)(2,1)}, f32[3,64,2048]{2,1,0:T(8,128)}, f32[3,1,2048]{2,1,0:T(1,128)S(1)}) custom-call(s32[16]{0:T(128)S(1)} %select_reduce_fusion.order, bf16[8,576,256]{2,1,0:T(8,128)(2,1)S(1)} %all-to-all-done.2.rows), custom_call_target="tpu_custom_call" | custom-call | flops 15000000512 | bytes 62500000 | tf_op jit(solution)/shard_map/attend/pallas_call | solution.py:499
  153.2 16.5 %all_to_all.47.came = bf16[8,192,256]{2,1,0:T(8,128)(2,1)S(1)} all-to-all(bf16[8,192,256]{2,1,0:T(8,128)(2,1)} %get-tuple-element.183), channel_id=1, replica_groups=mesh['ctx'=8,'fsdp'=4] {'ctx'}, dimensions={0} | all-to-all | bytes 1572864 | tf_op jit(solution)/shard_map/all_to_all | solution.py:737
  171.0 23.9 %mlp.1 = (bf16[512,768]{1,0:T(8,128)(2,1)}, bf16[512,768]{1,0:T(8,128)(2,1)}, bf16[512,768]{1,0:T(8,128)(2,1)}, bf16[512,2048]{1,0:T(8,128)(2,1)}, bf16[512,2048...) custom-call(s32[3]{0:T(128)S(1)} %copy-done.3, ...), custom_call_target="tpu_custom_call" | custom-call | flops 13799999488 | bytes 57500000 | tf_op jit(solution)/shard_map/mlp/pallas_call | solution.py:1158
  195.0 3.7 all-to-all-start.4
  198.7 16.5 %weight_grads.1 = (bf16[4,4,672,128]{3,2,1,0:T(8,128)(2,1)}, bf16[4,4,624,128]{3,2,1,0:T(8,128)(2,1)}, bf16[4,4,672,128]{3,2,1,0:T(8,128)(2,1)}, bf16[4,4,624,128]{3,2,1,0:T(8,128)(2,1)}) custom-call(s32[3]{0:T(128)} %copy-done.2, bf16[512,768]{1,0:T(8,128)(2,1)} %get-tuple-element.194.hidden, bf16[512,2048]{1,0:T(8,128)(2,1)} %get-tuple-element.195.gate, ...), custom_call_target="tpu_custom_call" | custom-call | flops 8999999488 | bytes 37500000 | tf_op jit(solution)/shard_map/weight_grads/pallas_call | solution.py:1282
  215.8 14.3 %attend_grad_0.1 = bf16[8,192,256]{2,1,0:T(8,128)(2,1)} custom-call(s32[16]{0:T(128)S(1)} %select_reduce_fusion.order, bf16[8,576,256]{2,1,0:T(8,128)(2,1)S(1)} %all-to-all-done.2.rows, bf16[8,192,256]{2,1,0:T(8,128)(2,1)S(1)} %all-to-all-done.4.grads, f32[3,64,2048]{2,1,0:T(8,128)} %get-tuple-element.206.attended_t, ...), custom_call_target="tpu_custom_call" | custom-call | flops 8400000000 | bytes 35000000 | tf_op jit(solution)/shard_map/attend_grad_0/pallas_call | solution.py:617
  230.0 4.4 %all-to-all-start.5 = ((bf16[8,192,256]{2,1,0:T(8,128)(2,1)}), bf16[8,192,256]{2,1,0:T(8,128)(2,1)}, u32[]{:S(2)}, u32[]{:S(2)}) async-start(bf16[8,192,256]{2,1,0:T(8,128)(2,1)} %attend_grad_0.1), calls=%async_computation.5 | async-start | bytes 1572864 | tf_op jit(solution)/shard_map/all_to_all | solution.py:737
  234.5 3.3 add_convert_fusion.1
  237.8 2.0 collective-permute-start.34
  239.8 2.8 add_convert_fusion
  244.1 24.3 %attend_grad_1.1 = bf16[8,384,256]{2,1,0:T(8,128)(2,1)} custom-call(s32[16]{0:T(128)S(1)} %select_reduce_fusion.order, bf16[8,576,256]{2,1,0:T(8,128)(2,1)S(1)} %all-to-all-done.2.rows, bf16[8,192,256]{2,1,0:T(8,128)(2,1)S(1)} %all-to-all-done.4.grads, f32[3,64,2048]{2,1,0:T(8,128)} %get-tuple-element.206.attended_t, ...), custom_call_target="tpu_custom_call" | custom-call | flops 16800000000 | bytes 70000000 | tf_op jit(solution)/shard_map/attend_grad_1/pallas_call | solution.py:617
  268.4 4.7 %all-to-all-start.6 = ((bf16[8,384,256]{2,1,0:T(8,128)(2,1)}), bf16[8,384,256]{2,1,0:T(8,128)(2,1)}, u32[]{:S(2)}, u32[]{:S(2)}) async-start(bf16[8,384,256]{2,1,0:T(8,128)(2,1)} %attend_grad_1.1), calls=%async_computation.6 | async-start | bytes 3145728 | tf_op jit(solution)/shard_map/all_to_all | solution.py:737
  273.5 2.2 collective-permute-done.33
  275.8 2.4 fusion.7
  278.2 2.7 fusion.5
  280.9 13.3 %all-to-all-done.6.came_b = bf16[8,384,256]{2,1,0:T(8,128)(2,1)} async-done(((bf16[8,384,256]{2,1,0:T(8,128)(2,1)}), bf16[8,384,256]{2,1,0:T(8,128)(2,1)}, u32[]{:S(2)}, u32[]{:S(2)}) %all-to-all-start.6) | async-done | bytes 1572896 | tf_op jit(solution)/shard_map/all_to_all | solution.py:737
  295.3 14.5 %back.1 = (f32[512,768]{1,0:T(8,128)}, bf16[1024,384]{1,0:T(8,128)(2,1)}, bf16[4,4,480,128]{3,2,1,0:T(8,128)(2,1)}, bf16[4,4,480,128]{3,2,1,0:T(8,128)(2,1)}) custom-call(s32[3]{0:T(128)} %copy-done.2, bf16[8,192,256]{2,1,0:T(8,128)(2,1)} %all-to-all-done.5.came_a, bf16[8,384,256]{2,1,0:T(8,128)(2,1)} %all-to-all-done.6.came_b, ...), custom_call_target="tpu_custom_call" | custom-call | flops 7800000000 | bytes 32500000 | tf_op jit(solution)/shard_map/back/pallas_call | solution.py:1405
  309.8 1.8 fusion.1
  311.7 1.9 fusion
  316.0 4.4 %all-to-all-start.7 = ((bf16[32,32,384]{2,1,0:T(8,128)(2,1)}), bf16[32,32,384]{2,1,0:T(8,128)(2,1)S(1)}, u32[]{:S(2)}, u32[]{:S(2)}) async-start(bf16[32,32,384]{2,1,0:T(8,128)(2,1)} %bitcast.51), calls=%async_computation.7 | async-start | bytes 1572864 | tf_op jit(solution)/shard_map/all_to_all | solution.py:737
  320.5 3.1 fusion.8
  323.6 1.9 collective-permute-start.39
  327.3 11.7 %collective-permute-done.37 = bf16[2,1296,128]{2,1,0:T(8,128)(2,1)S(1)} collective-permute-done((bf16[2,1296,128]{2,1,0:T(8,128)(2,1)}, bf16[2,1296,128]{2,1,0:T(8,128)(2,1)S(1)}, u32[]{:S(2)}, u32[]{:S(2)}) %collective-permute-start.37) | collective-permute-done | bytes 663584 | tf_op jit(solution)/shard_map/ppermute | solution.py:816
  339.2 1.7 collective-permute-done.39
  340.9 12.7 %collective-permute-done.40 = bf16[4,480,128]{2,1,0:T(8,128)(2,1)} collective-permute-done((bf16[4,480,128]{2,1,0:T(8,128)(2,1)}, bf16[4,480,128]{2,1,0:T(8,128)(2,1)}, u32[]{:S(2)}, u32[]{:S(2)}) %collective-permute-start.40) | collective-permute-done | bytes 491552 | tf_op jit(solution)/shard_map/ppermute | solution.py:631
  355.3 1.8 fusion.4
  361.9 2.9 collective-permute-start.43
  366.3 7.9 %add_table_0.1 = f32[192,12800]{1,0:T(8,128)} custom-call(s32[1024,2]{1,0:T(8,128)S(1)} %bitcast.142, bf16[1024,384]{1,0:T(8,128)(2,1)S(1)} %bitcast.140), custom_call_target="tpu_custom_call" | custom-call | flops 4200000000 | bytes 17500000 | tf_op jit(solution)/shard_map/add_table_0/pallas_call | solution.py:223
  377.2 2.0 collective-permute-start.51
  379.3 7.9 %add_table_1.1 = f32[192,12800]{1,0:T(8,128)} custom-call(s32[1024,2]{1,0:T(8,128)S(1)} %bitcast.143, bf16[1024,384]{1,0:T(8,128)(2,1)S(1)} %bitcast.141), custom_call_target="tpu_custom_call" | custom-call | flops 4200000000 | bytes 17500000 | tf_op jit(solution)/shard_map/add_table_1/pallas_call | solution.py:223
  388.1 3.2 collective-permute-done.52.other
  391.4 2.5 unpack_first.1
  394.6 3.4 unpack_second.1
  (224 shorter events, 61.5 us)
Async XLA Ops:
  4.9 22.5 %collective-permute-start.4 = (bf16[208,384]{1,0:T(8,128)(2,1)S(1)}, bf16[208,384]{1,0:T(8,128)(2,1)S(1)}, u32[]{:S(2)}, u32[]{:S(2)}) collective-permute-start(bf16[208,384]{1,0:T(8,128)(2,1)S(1)} %get-tuple-element.159), channel_id=1, source_target_pairs={{0,1},{1,2},{2,3},{3,0},{4,5},{5,6},{6,7},{7,4},{8,9},{9,10},{10,1... | collective-permute-start | bytes 479240 | tf_op jit(solution)/shard_map/ppermute | solution.py:636
  8.0 19.4 %collective-permute-start.3 = (bf16[208,384]{1,0:T(8,128)(2,1)S(1)}, bf16[208,384]{1,0:T(8,128)(2,1)S(1)}, u32[]{:S(2)}, u32[]{:S(2)}) collective-permute-start(bf16[208,384]{1,0:T(8,128)(2,1)S(1)} %get-tuple-element.159), channel_id=1, source_target_pairs={{0,2},{1,3},{2,0},{3,1},{4,6},{5,7},{6,4},{7,5},{8,10},{9,11},{10,... | collective-permute-start | bytes 479240 | tf_op jit(solution)/shard_map/ppermute | solution.py:636
  10.6 16.9 %collective-permute-start.2 = (bf16[208,384]{1,0:T(8,128)(2,1)S(1)}, bf16[208,384]{1,0:T(8,128)(2,1)S(1)}, u32[]{:S(2)}, u32[]{:S(2)}) collective-permute-start(bf16[208,384]{1,0:T(8,128)(2,1)S(1)} %get-tuple-element.159), channel_id=1, source_target_pairs={{0,3},{1,0},{2,1},{3,2},{4,7},{5,4},{6,5},{7,6},{8,11},{9,8},{10,9... | collective-permute-start | bytes 479240 | tf_op jit(solution)/shard_map/ppermute | solution.py:636
  11.9 14.6 %collective-permute-start = (bf16[384,128]{1,0:T(8,128)(2,1)S(1)}, bf16[384,128]{1,0:T(8,128)(2,1)S(1)}, u32[]{:S(2)}, u32[]{:S(2)}) collective-permute-start(bf16[384,128]{1,0:T(8,128)(2,1)S(1)} %get-tuple-element.145), channel_id=1, source_target_pairs={{0,8},{4,12},{8,0},{12,4},{16,24},{20,28},{24,16},{28,20},{1,9},{5... | collective-permute-start | bytes 294920 | tf_op jit(solution)/shard_map/ppermute | solution.py:631
  13.4 13.1 %collective-permute-start.1 = (bf16[384,128]{1,0:T(8,128)(2,1)S(1)}, bf16[384,128]{1,0:T(8,128)(2,1)S(1)}, u32[]{:S(2)}, u32[]{:S(2)}) collective-permute-start(bf16[384,128]{1,0:T(8,128)(2,1)S(1)} %get-tuple-element.145), channel_id=1, source_target_pairs={{0,16},{4,20},{8,24},{12,28},{16,0},{20,4},{24,8},{28,12},{1,17},{... | collective-permute-start | bytes 294920 | tf_op jit(solution)/shard_map/ppermute | solution.py:631
  26.8 21.7 %collective-permute-start.9 = (bf16[384,128]{1,0:T(8,128)(2,1)S(1)}, bf16[384,128]{1,0:T(8,128)(2,1)S(1)}, u32[]{:S(2)}, u32[]{:S(2)}) collective-permute-start(bf16[384,128]{1,0:T(8,128)(2,1)S(1)} %get-tuple-element.145), channel_id=1, source_target_pairs={{0,24},{4,28},{8,16},{12,20},{16,8},{20,12},{24,0},{28,4},{1,25},{... | collective-permute-start | bytes 294920 | tf_op jit(solution)/shard_map/ppermute | solution.py:631
  27.6 20.9 %collective-permute-start.7 = (bf16[912,128]{1,0:T(8,128)(2,1)S(1)}, bf16[912,128]{1,0:T(8,128)(2,1)S(1)}, u32[]{:S(2)}, u32[]{:S(2)}) collective-permute-start(bf16[912,128]{1,0:T(8,128)(2,1)S(1)} %get-tuple-element.172), channel_id=1, source_target_pairs={{0,1},{1,2},{2,3},{3,0},{4,5},{5,6},{6,7},{7,4},{8,9},{9,10},{10,1... | collective-permute-start | bytes 700424 | tf_op jit(solution)/shard_map/ppermute | solution.py:636
  28.3 20.1 %collective-permute-start.8 = (bf16[912,128]{1,0:T(8,128)(2,1)S(1)}, bf16[912,128]{1,0:T(8,128)(2,1)S(1)}, u32[]{:S(2)}, u32[]{:S(2)}) collective-permute-start(bf16[912,128]{1,0:T(8,128)(2,1)S(1)} %get-tuple-element.172), channel_id=1, source_target_pairs={{0,3},{1,0},{2,1},{3,2},{4,7},{5,4},{6,5},{7,6},{8,11},{9,8},{10,9... | collective-permute-start | bytes 700424 | tf_op jit(solution)/shard_map/ppermute | solution.py:636
  31.4 17.0 %collective-permute-start.5 = (bf16[4,144,384]{2,1,0:T(8,128)(2,1)S(1)}, bf16[4,144,384]{2,1,0:T(8,128)(2,1)S(1)}, u32[]{:S(2)}, u32[]{:S(2)}) collective-permute-start(bf16[4,144,384]{2,1,0:T(8,128)(2,1)S(1)} %pad_maximum_fusion.4.refs_0_), channel_id=1, source_target_pairs={{0,8},{4,12},{8,0},{12,4},{16,24},{20,28},{24,16},{28,20},{1,9},{5... | collective-permute-start | bytes 1327112 | tf_op jit(solution)/shard_map/ppermute | solution.py:631
  32.9 15.6 %collective-permute-start.6 = (bf16[4,144,384]{2,1,0:T(8,128)(2,1)S(1)}, bf16[4,144,384]{2,1,0:T(8,128)(2,1)S(1)}, u32[]{:S(2)}, u32[]{:S(2)}) collective-permute-start(bf16[4,144,384]{2,1,0:T(8,128)(2,1)S(1)} %pad_maximum_fusion.4.refs_0_), channel_id=1, source_target_pairs={{0,16},{4,20},{8,24},{12,28},{16,0},{20,4},{24,8},{28,12},{1,17},{... | collective-permute-start | bytes 1327112 | tf_op jit(solution)/shard_map/ppermute | solution.py:631
  48.5 16.4 %collective-permute-start.10 = (bf16[4,144,384]{2,1,0:T(8,128)(2,1)S(1)}, bf16[4,144,384]{2,1,0:T(8,128)(2,1)S(1)}, u32[]{:S(2)}, u32[]{:S(2)}) collective-permute-start(bf16[4,144,384]{2,1,0:T(8,128)(2,1)S(1)} %pad_maximum_fusion.4.refs_0_), channel_id=1, source_target_pairs={{0,24},{4,28},{8,16},{12,20},{16,8},{20,12},{24,0},{28,4},{1,25},{... | collective-permute-start | bytes 1327112 | tf_op jit(solution)/shard_map/ppermute | solution.py:631
  50.5 22.5 %collective-permute-start.11 = (bf16[4,144,384]{2,1,0:T(8,128)(2,1)S(1)}, bf16[4,144,384]{2,1,0:T(8,128)(2,1)}, u32[]{:S(2)}, u32[]{:S(2)}) collective-permute-start(bf16[4,144,384]{2,1,0:T(8,128)(2,1)S(1)} %pad_maximum_fusion.4.refs_0_), channel_id=1, source_target_pairs={{0,4},{4,0},{8,12},{12,8},{16,20},{20,16},{24,28},{28,24},{1,5},{5... | collective-permute-start | bytes 1327112 | tf_op jit(solution)/shard_map/ppermute | solution.py:631
  50.5 22.4 %all-to-all-start.1 = ((bf16[32,32,384]{2,1,0:T(8,128)(2,1)}), bf16[32,32,384]{2,1,0:T(8,128)(2,1)S(1)}, u32[]{:S(2)}, u32[]{:S(2)}) async-start(bf16[32,32,384]{2,1,0:T(8,128)(2,1)} %bitcast.13), calls=%async_computation.1 | async-start | bytes 1572864 | tf_op jit(solution)/shard_map/all_to_all | solution.py:737
  72.9 17.5 %collective-permute-start.17 = (bf16[3,432,128]{2,1,0:T(8,128)(2,1)}, bf16[3,432,128]{2,1,0:T(8,128)(2,1)S(1)}, u32[]{:S(2)}, u32[]{:S(2)}) collective-permute-start(bf16[3,432,128]{2,1,0:T(8,128)(2,1)} %pad_maximum_fusion.8), channel_id=1, source_target_pairs={{0,16},{4,20},{8,24},{12,28},{16,0},{20,4},{24,8},{28,12},{1,17},{... | collective-permute-start | bytes 995336 | tf_op jit(solution)/shard_map/ppermute | solution.py:631
  74.4 16.1 %collective-permute-start.16 = (bf16[3,480,128]{2,1,0:T(8,128)(2,1)S(1)}, bf16[3,480,128]{2,1,0:T(8,128)(2,1)S(1)}, u32[]{:S(2)}, u32[]{:S(2)}) collective-permute-start(bf16[3,480,128]{2,1,0:T(8,128)(2,1)S(1)} %pad_maximum_fusion.6), channel_id=1, source_target_pairs={{0,8},{4,12},{8,0},{12,4},{16,24},{20,28},{24,16},{28,20},{1,9},{5... | collective-permute-start | bytes 1105928 | tf_op jit(solution)/shard_map/ppermute | solution.py:631
  75.9 19.2 %collective-permute-start.18 = (bf16[912,128]{1,0:T(8,128)(2,1)S(1)}, bf16[912,128]{1,0:T(8,128)(2,1)S(1)}, u32[]{:S(2)}, u32[]{:S(2)}) collective-permute-start(bf16[912,128]{1,0:T(8,128)(2,1)S(1)} %get-tuple-element.172), channel_id=1, source_target_pairs={{0,2},{1,3},{2,0},{3,1},{4,6},{5,7},{6,4},{7,5},{8,10},{9,11},{10,... | collective-permute-start | bytes 700424 | tf_op jit(solution)/shard_map/ppermute | solution.py:636
  91.2 37.4 %all-to-all-start.2 = ((bf16[8,576,256]{2,1,0:T(8,128)(2,1)}), bf16[8,576,256]{2,1,0:T(8,128)(2,1)S(1)}, u32[]{:S(2)}, u32[]{:S(2)}) async-start(bf16[8,576,256]{2,1,0:T(8,128)(2,1)} %get-tuple-element.169), calls=%async_computation.2 | async-start | bytes 4718592 | tf_op jit(solution)/shard_map/all_to_all | solution.py:737
  96.2 32.3 %collective-permute-start.21 = (bf16[4,384,128]{2,1,0:T(8,128)(2,1)S(1)}, bf16[4,384,128]{2,1,0:T(8,128)(2,1)S(1)}, u32[]{:S(2)}, u32[]{:S(2)}) collective-permute-start(bf16[4,384,128]{2,1,0:T(8,128)(2,1)S(1)} %get-tuple-element.273), channel_id=1, source_target_pairs={{0,2},{1,3},{2,0},{3,1},{4,6},{5,7},{6,4},{7,5},{8,10},{9,11},{10,... | collective-permute-start | bytes 1179656 | tf_op jit(solution)/shard_map/ppermute | solution.py:816
  99.3 26.6 %collective-permute-start.20 = (bf16[432,128]{1,0:T(8,128)(2,1)S(1)}, bf16[432,128]{1,0:T(8,128)(2,1)S(1)}, u32[]{:S(2)}, u32[]{:S(2)}) collective-permute-start(bf16[432,128]{1,0:T(8,128)(2,1)S(1)} %slice.214), channel_id=1, source_target_pairs={{0,16},{4,20},{8,24},{12,28},{16,0},{20,4},{24,8},{28,12},{1,17},{... | collective-permute-start | bytes 331784 | tf_op jit(solution)/shard_map/ppermute | solution.py:631
  101.3 25.9 %collective-permute-start.19 = (bf16[480,128]{1,0:T(8,128)(2,1)S(1)}, bf16[480,128]{1,0:T(8,128)(2,1)S(1)}, u32[]{:S(2)}, u32[]{:S(2)}) collective-permute-start(bf16[480,128]{1,0:T(8,128)(2,1)S(1)} %slice.211), channel_id=1, source_target_pairs={{0,8},{4,12},{8,0},{12,4},{16,24},{20,28},{24,16},{28,20},{1,9},{5... | collective-permute-start | bytes 368648 | tf_op jit(solution)/shard_map/ppermute | solution.py:631
  128.6 23.6 %collective-permute-start.22 = (bf16[2,4,480,128]{3,2,1,0:T(8,128)(2,1)}, bf16[2,4,480,128]{3,2,1,0:T(8,128)(2,1)S(1)}, u32[]{:S(2)}, u32[]{:S(2)}) collective-permute-start(bf16[2,4,480,128]{3,2,1,0:T(8,128)(2,1)} %bitcast.146), channel_id=1, source_target_pairs={{0,16},{4,20},{8,24},{12,28},{16,0},{20,4},{24,8},{28,12},{1,17},{... | collective-permute-start | bytes 2949128 | tf_op jit(solution)/shard_map/ppermute | solution.py:631
  129.2 40.5 %collective-permute-start.25 = (bf16[2,4,480,128]{3,2,1,0:T(8,128)(2,1)}, bf16[2,4,480,128]{3,2,1,0:T(8,128)(2,1)S(1)}, u32[]{:S(2)}, u32[]{:S(2)}) collective-permute-start(bf16[2,4,480,128]{3,2,1,0:T(8,128)(2,1)} %bitcast.147), channel_id=1, source_target_pairs={{0,4},{4,0},{8,12},{12,8},{16,20},{20,16},{24,28},{28,24},{1,5},{5... | collective-permute-start | bytes 2949128 | tf_op jit(solution)/shard_map/ppermute | solution.py:631
  129.2 22.3 %collective-permute-start.23 = (bf16[2,4,432,128]{3,2,1,0:T(8,128)(2,1)}, bf16[2,4,432,128]{3,2,1,0:T(8,128)(2,1)S(1)}, u32[]{:S(2)}, u32[]{:S(2)}) collective-permute-start(bf16[2,4,432,128]{3,2,1,0:T(8,128)(2,1)} %bitcast.149), channel_id=1, source_target_pairs={{0,8},{4,12},{8,0},{12,4},{16,24},{20,28},{24,16},{28,20},{1,9},{5... | collective-permute-start | bytes 2654216 | tf_op jit(solution)/shard_map/ppermute | solution.py:631
  130.5 22.2 %collective-permute-start.26 = (bf16[2,4,432,128]{3,2,1,0:T(8,128)(2,1)}, bf16[2,4,432,128]{3,2,1,0:T(8,128)(2,1)S(1)}, u32[]{:S(2)}, u32[]{:S(2)}) collective-permute-start(bf16[2,4,432,128]{3,2,1,0:T(8,128)(2,1)} %bitcast.150), channel_id=1, source_target_pairs={{0,4},{4,0},{8,12},{12,8},{16,20},{20,16},{24,28},{28,24},{1,5},{5... | collective-permute-start | bytes 2654216 | tf_op jit(solution)/shard_map/ppermute | solution.py:631
  130.7 20.5 %collective-permute-start.24 = (bf16[2,4,384,128]{3,2,1,0:T(8,128)(2,1)S(1)}, bf16[2,4,384,128]{3,2,1,0:T(8,128)(2,1)S(1)}, u32[]{:S(2)}, u32[]{:S(2)}) collective-permute-start(bf16[2,4,384,128]{3,2,1,0:T(8,128)(2,1)S(1)} %pad_maximum_fusion.1.refs_8_), channel_id=1, source_target_pairs={{0,1},{1,0},{2,3},{3,2},{4,5},{5,4},{6,7},{7,6},{8,9},{9,8},{10,11... | collective-permute-start | bytes 2359304 | tf_op jit(solution)/shard_map/ppermute | solution.py:816
  152.2 17.6 %collective-permute-start.27 = (bf16[2,4,480,128]{3,2,1,0:T(8,128)(2,1)S(1)}, bf16[2,4,480,128]{3,2,1,0:T(8,128)(2,1)S(1)}, u32[]{:S(2)}, u32[]{:S(2)}) collective-permute-start(bf16[2,4,480,128]{3,2,1,0:T(8,128)(2,1)S(1)} %collective-permute-done.22.refs_2_), channel_id=1, source_target_pairs={{0,4},{4,0},{8,12},{12,8},{16,20},{20,16},{24,28},{28,24},{1,5},{5... | collective-permute-start | bytes 2949128 | tf_op jit(solution)/shard_map/ppermute | solution.py:631
  152.2 17.6 %collective-permute-start.28 = (bf16[2,4,432,128]{3,2,1,0:T(8,128)(2,1)S(1)}, bf16[2,4,432,128]{3,2,1,0:T(8,128)(2,1)S(1)}, u32[]{:S(2)}, u32[]{:S(2)}) collective-permute-start(bf16[2,4,432,128]{3,2,1,0:T(8,128)(2,1)S(1)} %collective-permute-done.23.refs_3_), channel_id=1, source_target_pairs={{0,4},{4,0},{8,12},{12,8},{16,20},{20,16},{24,28},{28,24},{1,5},{5... | collective-permute-start | bytes 2654216 | tf_op jit(solution)/shard_map/ppermute | solution.py:631
  152.7 17.1 %collective-permute-start.29 = (bf16[2,4,384,128]{3,2,1,0:T(8,128)(2,1)S(1)}, bf16[2,4,384,128]{3,2,1,0:T(8,128)(2,1)S(1)}, u32[]{:S(2)}, u32[]{:S(2)}) collective-permute-start(bf16[2,4,384,128]{3,2,1,0:T(8,128)(2,1)S(1)} %pad_maximum_fusion.1.refs_8_), channel_id=1, source_target_pairs={{0,4},{4,0},{8,12},{12,8},{16,20},{20,16},{24,28},{28,24},{1,5},{5... | collective-permute-start | bytes 2359304 | tf_op jit(solution)/shard_map/ppermute | solution.py:631
  152.7 17.1 %collective-permute-start.30 = (bf16[2,4,384,128]{3,2,1,0:T(8,128)(2,1)S(1)}, bf16[2,4,384,128]{3,2,1,0:T(8,128)(2,1)S(1)}, u32[]{:S(2)}, u32[]{:S(2)}) collective-permute-start(bf16[2,4,384,128]{3,2,1,0:T(8,128)(2,1)S(1)} %collective-permute-done.24.refs_9_), channel_id=1, source_target_pairs={{0,4},{4,0},{8,12},{12,8},{16,20},{20,16},{24,28},{28,24},{1,5},{5... | collective-permute-start | bytes 2359304 | tf_op jit(solution)/shard_map/ppermute | solution.py:631
  195.0 20.2 %all-to-all-start.4 = ((bf16[8,192,256]{2,1,0:T(8,128)(2,1)}), bf16[8,192,256]{2,1,0:T(8,128)(2,1)S(1)}, u32[]{:S(2)}, u32[]{:S(2)}) async-start(bf16[8,192,256]{2,1,0:T(8,128)(2,1)} %get-tuple-element.203), calls=%async_computation.4 | async-start | bytes 1572864 | tf_op jit(solution)/shard_map/all_to_all | solution.py:737
  215.2 19.3 %collective-permute-start.31 = (bf16[4,4,672,128]{3,2,1,0:T(8,128)(2,1)}, bf16[4,4,672,128]{3,2,1,0:T(8,128)(2,1)}, u32[]{:S(2)}, u32[]{:S(2)}) collective-permute-start(bf16[4,4,672,128]{3,2,1,0:T(8,128)(2,1)} %get-tuple-element.204), channel_id=1, source_target_pairs={{0,4},{4,0},{8,12},{12,8},{16,20},{20,16},{24,28},{28,24},{1,5},{5... | collective-permute-start | bytes 8257544 | tf_op jit(solution)/shard_map/ppermute | solution.py:631
  215.7 18.8 %collective-permute-start.32 = (bf16[4,4,624,128]{3,2,1,0:T(8,128)(2,1)}, bf16[4,4,624,128]{3,2,1,0:T(8,128)(2,1)}, u32[]{:S(2)}, u32[]{:S(2)}) collective-permute-start(bf16[4,4,624,128]{3,2,1,0:T(8,128)(2,1)} %get-tuple-element.205), channel_id=1, source_target_pairs={{0,4},{4,0},{8,12},{12,8},{16,20},{20,16},{24,28},{28,24},{1,5},{5... | collective-permute-start | bytes 7667720 | tf_op jit(solution)/shard_map/ppermute | solution.py:631
  230.0 38.4 %all-to-all-start.5 = ((bf16[8,192,256]{2,1,0:T(8,128)(2,1)}), bf16[8,192,256]{2,1,0:T(8,128)(2,1)}, u32[]{:S(2)}, u32[]{:S(2)}) async-start(bf16[8,192,256]{2,1,0:T(8,128)(2,1)} %attend_grad_0.1), calls=%async_computation.5 | async-start | bytes 1572864 | tf_op jit(solution)/shard_map/all_to_all | solution.py:737
  237.8 35.8 %collective-permute-start.34 = (bf16[2,4,624,128]{3,2,1,0:T(8,128)(2,1)}, bf16[2,4,624,128]{3,2,1,0:T(8,128)(2,1)}, u32[]{:S(2)}, u32[]{:S(2)}) collective-permute-start(bf16[2,4,624,128]{3,2,1,0:T(8,128)(2,1)} %add_convert_fusion.1), channel_id=1, source_target_pairs={{0,16},{4,20},{8,24},{12,28},{16,0},{20,4},{24,8},{28,12},{1,17},{... | collective-permute-start | bytes 3833864 | tf_op jit(solution)/shard_map/ppermute | solution.py:631
  242.6 33.1 %collective-permute-start.33 = (bf16[2,4,672,128]{3,2,1,0:T(8,128)(2,1)}, bf16[2,4,672,128]{3,2,1,0:T(8,128)(2,1)}, u32[]{:S(2)}, u32[]{:S(2)}) collective-permute-start(bf16[2,4,672,128]{3,2,1,0:T(8,128)(2,1)} %add_convert_fusion), channel_id=1, source_target_pairs={{0,8},{4,12},{8,0},{12,4},{16,24},{20,28},{24,16},{28,20},{1,9},{5... | collective-permute-start | bytes 4128776 | tf_op jit(solution)/shard_map/ppermute | solution.py:631
  268.4 25.8 %all-to-all-start.6 = ((bf16[8,384,256]{2,1,0:T(8,128)(2,1)}), bf16[8,384,256]{2,1,0:T(8,128)(2,1)}, u32[]{:S(2)}, u32[]{:S(2)}) async-start(bf16[8,384,256]{2,1,0:T(8,128)(2,1)} %attend_grad_1.1), calls=%async_computation.6 | async-start | bytes 3145728 | tf_op jit(solution)/shard_map/all_to_all | solution.py:737
  294.2 15.6 %collective-permute-start.35 = (bf16[4,672,128]{2,1,0:T(8,128)(2,1)}, bf16[4,672,128]{2,1,0:T(8,128)(2,1)S(1)}, u32[]{:S(2)}, u32[]{:S(2)}) collective-permute-start(bf16[4,672,128]{2,1,0:T(8,128)(2,1)} %fusion.5), channel_id=1, source_target_pairs={{0,16},{4,20},{8,24},{12,28},{16,0},{20,4},{24,8},{28,12},{1,17},{... | collective-permute-start | bytes 2064392 | tf_op jit(solution)/shard_map/ppermute | solution.py:631
  294.7 15.1 %collective-permute-start.36 = (bf16[4,624,128]{2,1,0:T(8,128)(2,1)}, bf16[4,624,128]{2,1,0:T(8,128)(2,1)}, u32[]{:S(2)}, u32[]{:S(2)}) collective-permute-start(bf16[4,624,128]{2,1,0:T(8,128)(2,1)} %fusion.7), channel_id=1, source_target_pairs={{0,8},{4,12},{8,0},{12,4},{16,24},{20,28},{24,16},{28,20},{1,9},{5... | collective-permute-start | bytes 1916936 | tf_op jit(solution)/shard_map/ppermute | solution.py:631
  314.5 24.4 %collective-permute-start.37 = (bf16[2,1296,128]{2,1,0:T(8,128)(2,1)}, bf16[2,1296,128]{2,1,0:T(8,128)(2,1)S(1)}, u32[]{:S(2)}, u32[]{:S(2)}) collective-permute-start(bf16[2,1296,128]{2,1,0:T(8,128)(2,1)} %pad_maximum_fusion.2), channel_id=1, source_target_pairs={{0,1},{1,0},{2,3},{3,2},{4,5},{5,4},{6,7},{7,6},{8,9},{9,8},{10,11... | collective-permute-start | bytes 1990664 | tf_op jit(solution)/shard_map/ppermute | solution.py:816
  316.0 50.3 %all-to-all-start.7 = ((bf16[32,32,384]{2,1,0:T(8,128)(2,1)}), bf16[32,32,384]{2,1,0:T(8,128)(2,1)S(1)}, u32[]{:S(2)}, u32[]{:S(2)}) async-start(bf16[32,32,384]{2,1,0:T(8,128)(2,1)} %bitcast.51), calls=%async_computation.7 | async-start | bytes 1572864 | tf_op jit(solution)/shard_map/all_to_all | solution.py:737
  323.6 17.3 %collective-permute-start.39 = (bf16[4,480,128]{2,1,0:T(8,128)(2,1)}, bf16[4,480,128]{2,1,0:T(8,128)(2,1)S(1)}, u32[]{:S(2)}, u32[]{:S(2)}) collective-permute-start(bf16[4,480,128]{2,1,0:T(8,128)(2,1)} %get-tuple-element.261), channel_id=1, source_target_pairs={{0,8},{4,12},{8,0},{12,4},{16,24},{20,28},{24,16},{28,20},{1,9},{5... | collective-permute-start | bytes 1474568 | tf_op jit(solution)/shard_map/ppermute | solution.py:631
  325.5 28.1 %collective-permute-start.40 = (bf16[4,480,128]{2,1,0:T(8,128)(2,1)}, bf16[4,480,128]{2,1,0:T(8,128)(2,1)}, u32[]{:S(2)}, u32[]{:S(2)}) collective-permute-start(bf16[4,480,128]{2,1,0:T(8,128)(2,1)} %get-tuple-element.263), channel_id=1, source_target_pairs={{0,16},{4,20},{8,24},{12,28},{16,0},{20,4},{24,8},{28,12},{1,17},{... | collective-permute-start | bytes 1474568 | tf_op jit(solution)/shard_map/ppermute | solution.py:631
  326.9 28.4 %collective-permute-start.41 = (bf16[4,480,128]{2,1,0:T(8,128)(2,1)}, bf16[4,480,128]{2,1,0:T(8,128)(2,1)}, u32[]{:S(2)}, u32[]{:S(2)}) collective-permute-start(bf16[4,480,128]{2,1,0:T(8,128)(2,1)} %get-tuple-element.262), channel_id=1, source_target_pairs={{0,24},{4,28},{8,16},{12,20},{16,8},{20,12},{24,0},{28,4},{1,25},{... | collective-permute-start | bytes 1474568 | tf_op jit(solution)/shard_map/ppermute | solution.py:631
  339.1 19.2 %collective-permute-start.45 = (bf16[1296,128]{1,0:T(8,128)(2,1)S(1)}, bf16[1296,128]{1,0:T(8,128)(2,1)S(1)}, u32[]{:S(2)}, u32[]{:S(2)}) collective-permute-start(bf16[1296,128]{1,0:T(8,128)(2,1)S(1)} %fusion.12), channel_id=1, source_target_pairs={{0,2},{1,3},{2,0},{3,1},{4,6},{5,7},{6,4},{7,5},{8,10},{9,11},{10,... | collective-permute-start | bytes 995336 | tf_op jit(solution)/shard_map/ppermute | solution.py:816
  358.4 15.9 %collective-permute-start.46 = (bf16[1296,128]{1,0:T(8,128)(2,1)S(1)}, bf16[1296,128]{1,0:T(8,128)(2,1)S(1)}, u32[]{:S(2)}, u32[]{:S(2)}) collective-permute-start(bf16[1296,128]{1,0:T(8,128)(2,1)S(1)} %fusion.6), channel_id=1, source_target_pairs={{0,8},{4,12},{8,0},{12,4},{16,24},{20,28},{24,16},{28,20},{1,9},{5... | collective-permute-start | bytes 995336 | tf_op jit(solution)/shard_map/ppermute | solution.py:631
  359.7 16.0 %collective-permute-start.47 = (bf16[1296,128]{1,0:T(8,128)(2,1)S(1)}, bf16[1296,128]{1,0:T(8,128)(2,1)S(1)}, u32[]{:S(2)}, u32[]{:S(2)}) collective-permute-start(bf16[1296,128]{1,0:T(8,128)(2,1)S(1)} %fusion.6), channel_id=1, source_target_pairs={{0,16},{4,20},{8,24},{12,28},{16,0},{20,4},{24,8},{28,12},{1,17},{... | collective-permute-start | bytes 995336 | tf_op jit(solution)/shard_map/ppermute | solution.py:631
  361.3 25.9 %collective-permute-start.48 = (bf16[1296,128]{1,0:T(8,128)(2,1)S(1)}, bf16[1296,128]{1,0:T(8,128)(2,1)S(1)}, u32[]{:S(2)}, u32[]{:S(2)}) collective-permute-start(bf16[1296,128]{1,0:T(8,128)(2,1)S(1)} %fusion.6), channel_id=1, source_target_pairs={{0,24},{4,28},{8,16},{12,20},{16,8},{20,12},{24,0},{28,4},{1,25},{... | collective-permute-start | bytes 995336 | tf_op jit(solution)/shard_map/ppermute | solution.py:631
  361.9 12.3 %collective-permute-start.43 = (bf16[480,128]{1,0:T(8,128)(2,1)S(1)}, bf16[480,128]{1,0:T(8,128)(2,1)S(1)}, u32[]{:S(2)}, u32[]{:S(2)}) collective-permute-start(bf16[480,128]{1,0:T(8,128)(2,1)S(1)} %get-tuple-element.270), channel_id=1, source_target_pairs={{0,2},{1,3},{2,0},{3,1},{4,6},{5,7},{6,4},{7,5},{8,10},{9,11},{10,... | collective-permute-start | bytes 368648 | tf_op jit(solution)/shard_map/ppermute | solution.py:816
  (46 other events, 386.2 us)
